TPU v7x, 32 devices: a whole 2x2x4 slice. The times are simulated.
32 devices in a mesh: dp: 8 (over y, x, core), stream: 4 (over z).
Axes of the slice: x: 2, y: 2, z: 4, core: 2. Of those that a mesh axis runs over, the one named last changes fastest.
Arguments:
- history: bfloat16 [8, 4096, 2048], P(None, 'dp'), may hold values from -6 to 6
- mixing: float32 [4096, 4, 8], P('dp', 'stream'), may hold values from -2 to 2
- shard_offset: int32 [8], P('dp'), may hold values from 0 to 3584, as said below
- norm_gain: bfloat16 [4, 2048], P('stream'), may hold values from 0.099609375 to 1.8984375
- norm_bias: bfloat16 [4, 2048], P('stream'), may hold values from -1.75 to 1.75
- w_heads: bfloat16 [3, 2048, 2048], P(None, 'dp', 'stream'), may hold values from -0.125 to 0.125
- w_merge: bfloat16 [2048, 2048], P('stream', 'dp'), may hold values from -3 to 3
- w_up: bfloat16 [2048, 8192], P('dp', 'stream'), may hold values from -0.125 to 0.125
- w_down: bfloat16 [8192, 2048], P('stream', 'dp'), may hold values from -0.0625 to 0.0625
- mixer_first: bfloat16 [2048, 36], P('stream'), may hold values from -0.125 to 0.125
- mixer_second: bfloat16 [36, 4, 9], P(None, 'stream'), may hold values from -1 to 1
- out_cotangent: bfloat16 [4096, 2048], P('dp', 'stream'), may hold values from -6 to 6
- next_cotangent: float32 [4096, 4, 9], P('dp', 'stream'), may hold values from -6 to 6
Outputs:
- block_out: bfloat16 [4096, 2048], P('dp', 'stream')
- next_mixing: float32 [4096, 4, 9], P('dp', 'stream')
- grad_history: float32 [8, 4096, 2048], P('stream', 'dp')
- grad_mixing: float32 [4096, 4, 8], P('dp', 'stream')
- grad_gain: float32 [4, 2048], P('stream')
- grad_bias: float32 [4, 2048], P('stream')
- grad_heads: float32 [3, 2048, 2048], P(None, 'dp', 'stream')
- grad_merge: float32 [2048, 2048], P('stream', 'dp')
- grad_up: float32 [2048, 8192], P('dp', 'stream')
- grad_down: float32 [8192, 2048], P('stream', 'dp')
- grad_first: float32 [2048, 36], P('stream')
- grad_second: float32 [36, 4, 9], P(None, 'stream')
Inputs may be any that keep to these rules, and one draw needn't show every extreme that they name: `shard_offset`: sequences of 2048 and 4096 tokens are packed end to end, each new one starting at the first token of a shard; the first may have begun before the first token and the last may be cut off at the end. Entry i is the position, within its sequence, of the first token of shard i.
All inputs are finite; a program needn't handle non-finite values.
Results may differ from a plain program's by a relative error of at most 0.012.
Values may be sent and summed in bfloat16 or wider, within the bound.
No kernel may reach another device: no remote copies, remote signals or barrier semaphores. Data moves between devices by JAX's collectives and lax.ppermute only.
A program may use at most 256 MiB of HBM per device.

v0:
```python
import math

import jax
import jax.numpy as jnp
from jax import lax
from jax.sharding import PartitionSpec as P

HD = 128
ROT = 32
SEQ = 2048


def passed_along(shard, axis, by):
    peers = lax.axis_size(axis)
    pairs = [(i, i + by) for i in range(peers) if 0 <= i + by < peers]
    return lax.ppermute(shard, axis, pairs)


def rotate(vectors, positions, sign):
    half = ROT // 2
    counter = jnp.arange(half, dtype=jnp.float32)
    freqs = jnp.exp(counter * (-2.0 * math.log(10000.0) / ROT))
    angles = positions.astype(jnp.float32)[:, None] * freqs[None, :]
    cosine = jnp.cos(angles)[:, None, :]
    sine = sign * jnp.sin(angles)[:, None, :]
    first = vectors[..., :half]
    second = vectors[..., half:ROT]
    return jnp.concatenate(
        [first * cosine - second * sine, second * cosine + first * sine, vectors[..., ROT:]],
        axis=-1,
    )


def exact_gelu(vectors):
    return jax.nn.gelu(vectors, approximate=False)


def block_logits(queries, keys_block, diagonal):
    logits = jnp.einsum("qhd,khd->hqk", queries, keys_block, preferred_element_type=jnp.float32) * (
        1.0 / math.sqrt(queries.shape[-1])
    )
    if diagonal:
        counter = jnp.arange(queries.shape[0], dtype=jnp.int32)
        allowed = counter[None, :] <= counter[:, None]
        logits = jnp.where(allowed[None], logits, -1e30)
    return logits


def keep_same(state):
    return state


def body(
    history,
    mixing,
    shard_offset,
    norm_gain,
    norm_bias,
    w_heads,
    w_merge,
    w_up,
    w_down,
    mixer_first,
    mixer_second,
    out_cotangent,
    next_cotangent,
):
    member = lax.axis_index("stream")
    members = lax.axis_size("stream")
    data_index = lax.axis_index("dp")
    last_flag = (member == members - 1).astype(jnp.float32)
    entries = history.shape[0]
    tokens = history.shape[1]
    width = history.shape[2]
    head_size = HD
    factor = 1.0 / math.sqrt(head_size)
    highest = lax.Precision.HIGHEST
    mix_here = mixing[:, 0, :]
    stream = jnp.zeros((tokens, width), jnp.float32)
    for entry in range(entries):
        stream = stream + mix_here[:, entry : entry + 1] * history[entry]
    center = stream - jnp.mean(stream, axis=-1, keepdims=True)
    inv_std = lax.rsqrt(jnp.mean(center * center, axis=-1, keepdims=True) + 1e-05)
    unit = center * inv_std
    gain = norm_gain[0].astype(jnp.float32)
    normed = (unit * gain + norm_bias[0].astype(jnp.float32)).astype(jnp.bfloat16)
    all_normed = lax.all_gather(normed[None], "stream", axis=0, tiled=True)
    full_heads, full_merge, full_up, full_down = (
        lax.all_gather(w_heads, "dp", axis=1, tiled=True),
        lax.all_gather(w_merge, "dp", axis=1, tiled=True),
        lax.all_gather(w_up, "dp", axis=0, tiled=True),
        lax.all_gather(w_down, "dp", axis=1, tiled=True),
    )
    projected = [
        jnp.dot(all_normed[index], full_heads[index], preferred_element_type=jnp.float32)
        for index in range(3)
    ]
    heads_here = projected[0].shape[1] // head_size
    positions = shard_offset[0] + jnp.arange(tokens, dtype=jnp.int32)

    def split_heads(matrix):
        return matrix.reshape(tokens, heads_here, head_size)

    queries = rotate(split_heads(projected[0]), positions, 1.0).astype(jnp.bfloat16)
    keys = rotate(split_heads(projected[1]), positions, 1.0).astype(jnp.bfloat16)
    values = split_heads(projected[2]).astype(jnp.bfloat16)
    pairs = [jnp.stack([keys, values])]
    reach = 2 * SEQ // tokens
    for back in range(1, reach):
        pairs.append(passed_along(pairs[0], "dp", back))
    usable = [(shard_offset[0] >= back * tokens) & (data_index >= back) for back in range(reach)]
    first_logits = block_logits(queries, keys, True)
    top = jnp.max(first_logits, axis=-1)
    total = jnp.sum(jnp.exp(first_logits - top[..., None]), axis=-1)
    for back in range(1, reach):

        def widen(state, block=pairs[back][0]):
            logits = block_logits(queries, block, False)
            new_top = jnp.maximum(state[0], jnp.max(logits, axis=-1))
            summed = state[1] * jnp.exp(state[0] - new_top) + jnp.sum(
                jnp.exp(logits - new_top[..., None]), axis=-1
            )
            return (new_top, summed)

        top, total = lax.cond(usable[back], widen, keep_same, (top, total))
    log_total = top + jnp.log(total)

    def weights_of(block, diagonal):
        return jnp.exp(block_logits(queries, block, diagonal) - log_total[..., None])

    attended = jnp.zeros((tokens, heads_here, head_size), jnp.float32)
    for back in range(reach):

        def accumulate(current, block=pairs[back], diagonal=back == 0):
            probs = weights_of(block[0], diagonal).astype(jnp.bfloat16)
            return current + jnp.einsum(
                "hqk,khd->qhd", probs, block[1], preferred_element_type=jnp.float32
            )

        attended = lax.cond(usable[back], accumulate, keep_same, attended)
    attended_low = attended.reshape(tokens, -1).astype(jnp.bfloat16)
    up = jnp.dot(all_normed[3], full_up, preferred_element_type=jnp.float32)
    hidden, gelu_back = jax.vjp(exact_gelu, up)
    hidden_low = hidden.astype(jnp.bfloat16)
    branches = (
        jnp.dot(attended_low, full_merge, preferred_element_type=jnp.float32)
        + jnp.dot(hidden_low, full_down, preferred_element_type=jnp.float32)
        + last_flag * stream
    )
    out_cols = lax.psum_scatter(branches, "stream", scatter_dimension=1, tiled=True)
    block_out = out_cols.astype(jnp.bfloat16)
    out_float = block_out.astype(jnp.float32)
    square_part = jnp.sum(out_float * out_float, axis=-1)
    proj_part = jnp.dot(block_out, mixer_first, preferred_element_type=jnp.float32)
    square_sum, proj = lax.psum((square_part, proj_part), "stream")
    scale_rows = lax.rsqrt(square_sum / width + 1e-06)
    mixer, mixer_gelu_back = jax.vjp(exact_gelu, scale_rows[:, None] * proj)
    second_here = mixer_second[:, 0, :].astype(jnp.float32)
    next_here = jnp.dot(mixer, second_here, precision=highest, preferred_element_type=jnp.float32)
    next_back = next_cotangent[:, 0, :]
    mixer_part = jnp.dot(
        next_back, second_here.T, precision=highest, preferred_element_type=jnp.float32
    )
    mixer_grad = lax.psum(mixer_part, "stream")
    pre_grad = mixer_gelu_back(mixer_grad)[0]
    proj_grad = (scale_rows[:, None] * pre_grad).astype(jnp.bfloat16)
    scale_grad = jnp.sum(pre_grad * proj, axis=-1)
    second_local = jnp.dot(
        mixer.T, next_back, precision=highest, preferred_element_type=jnp.float32
    )
    first_local = jnp.einsum("td,tc->dc", block_out, proj_grad, preferred_element_type=jnp.float32)
    out_total = (
        out_cotangent.astype(jnp.float32)
        + jnp.einsum("tc,dc->td", proj_grad, mixer_first, preferred_element_type=jnp.float32)
        - (scale_rows * scale_rows * scale_rows * scale_grad)[:, None] * out_float / width
    )
    grad_out = out_total.astype(jnp.bfloat16)
    grad_out_full = lax.all_gather(grad_out, "stream", axis=1, tiled=True)
    back_heads, back_merge, back_up, back_down = (full_heads, full_merge, full_up, full_down)
    hidden_grad = jnp.einsum(
        "td,fd->tf", grad_out_full, back_down, preferred_element_type=jnp.float32
    )
    up_grad = gelu_back(hidden_grad)[0].astype(jnp.bfloat16)
    down_full_grad = jnp.einsum(
        "tf,td->fd", hidden_low, grad_out_full, preferred_element_type=jnp.float32
    )
    up_full_grad = jnp.einsum(
        "td,tf->df", all_normed[3], up_grad, preferred_element_type=jnp.float32
    )
    merge_full_grad = jnp.einsum(
        "te,td->ed", attended_low, grad_out_full, preferred_element_type=jnp.float32
    )
    attended_grad = (
        jnp.einsum("td,ed->te", grad_out_full, back_merge, preferred_element_type=jnp.float32)
        .astype(jnp.bfloat16)
        .reshape(tokens, heads_here, head_size)
    )
    delta = jnp.zeros((heads_here, tokens), jnp.float32)
    for back in range(reach):

        def gather_delta(current, block=pairs[back], diagonal=back == 0):
            probs = weights_of(block[0], diagonal)
            prob_grad = jnp.einsum(
                "qhd,khd->hqk", attended_grad, block[1], preferred_element_type=jnp.float32
            )
            return current + jnp.sum(probs * prob_grad, axis=-1)

        delta = lax.cond(usable[back], gather_delta, keep_same, delta)

    def skip_block(current):
        return (current, jnp.zeros((2, tokens, heads_here, head_size), jnp.float32))

    query_grad = jnp.zeros((tokens, heads_here, head_size), jnp.float32)
    key_value_grad = jnp.zeros((2, tokens, heads_here, head_size), jnp.float32)
    for back in range(reach):

        def spread(current, block=pairs[back], diagonal=back == 0):
            probs = weights_of(block[0], diagonal)
            prob_grad = jnp.einsum(
                "qhd,khd->hqk", attended_grad, block[1], preferred_element_type=jnp.float32
            )
            score_grad = (probs * (prob_grad - delta[..., None])).astype(jnp.bfloat16)
            query_part = (
                current
                + jnp.einsum(
                    "hqk,khd->qhd", score_grad, block[0], preferred_element_type=jnp.float32
                )
                * factor
            )
            key_part = (
                jnp.einsum("hqk,qhd->khd", score_grad, queries, preferred_element_type=jnp.float32)
                * factor
            )
            value_part = jnp.einsum(
                "hqk,qhd->khd",
                probs.astype(jnp.bfloat16),
                attended_grad,
                preferred_element_type=jnp.float32,
            )
            return (query_part, jnp.stack([key_part, value_part]))

        query_grad, pair_grad = lax.cond(usable[back], spread, skip_block, query_grad)
        if back == 0:
            key_value_grad = pair_grad
        else:
            key_value_grad = key_value_grad + passed_along(pair_grad, "dp", -back)
    pre_grads = (
        rotate(query_grad, positions, -1.0).astype(jnp.bfloat16).reshape(tokens, -1),
        rotate(key_value_grad[0], positions, -1.0).astype(jnp.bfloat16).reshape(tokens, -1),
        key_value_grad[1].astype(jnp.bfloat16).reshape(tokens, -1),
    )
    project_grads = jnp.stack(
        [
            jnp.einsum(
                "td,te->de", all_normed[index], pre_grads[index], preferred_element_type=jnp.float32
            )
            for index in range(3)
        ]
    )
    normed_parts = jnp.stack(
        [
            jnp.einsum(
                "te,de->td", pre_grads[index], back_heads[index], preferred_element_type=jnp.float32
            )
            for index in range(3)
        ]
        + [jnp.einsum("tf,df->td", up_grad, back_up, preferred_element_type=jnp.float32)]
    )
    normed_grad = lax.psum_scatter(normed_parts, "stream", scatter_dimension=0, tiled=True)[0]
    gain_local = jnp.sum(normed_grad * unit, axis=0)
    bias_local = jnp.sum(normed_grad, axis=0)
    scaled = normed_grad * gain
    stream_grad = inv_std * (
        scaled
        - jnp.mean(scaled, axis=-1, keepdims=True)
        - unit * jnp.mean(scaled * unit, axis=-1, keepdims=True)
    ) + last_flag * grad_out_full.astype(jnp.float32)
    grad_mixing = jnp.stack(
        [jnp.sum(stream_grad * history[entry], axis=-1) for entry in range(entries)], axis=-1
    )[:, None, :]
    grad_history = lax.psum_scatter(
        jnp.transpose(mix_here)[:, :, None] * stream_grad[None],
        "stream",
        scatter_dimension=0,
        tiled=True,
    )
    grad_heads, grad_merge, grad_up, grad_down = (
        lax.psum_scatter(project_grads, "dp", scatter_dimension=1, tiled=True),
        lax.psum_scatter(merge_full_grad, "dp", scatter_dimension=1, tiled=True),
        lax.psum_scatter(up_full_grad, "dp", scatter_dimension=0, tiled=True),
        lax.psum_scatter(down_full_grad, "dp", scatter_dimension=1, tiled=True),
    )
    grad_gain, grad_bias, grad_first, grad_second = lax.psum(
        (gain_local[None], bias_local[None], first_local, second_local[:, None, :]), "dp"
    )
    return (
        block_out,
        next_here[:, None, :],
        grad_history,
        grad_mixing,
        grad_gain,
        grad_bias,
        grad_heads,
        grad_merge,
        grad_up,
        grad_down,
        grad_first,
        grad_second,
    )


def solution(mesh):
    in_specs = (
        P(None, "dp", None),
        P("dp", "stream", None),
        P("dp"),
        P("stream", None),
        P("stream", None),
        P(None, "dp", "stream"),
        P("stream", "dp"),
        P("dp", "stream"),
        P("stream", "dp"),
        P("stream", None),
        P(None, "stream", None),
        P("dp", "stream"),
        P("dp", "stream", None),
    )
    out_specs = (
        P("dp", "stream"),
        P("dp", "stream", None),
        P("stream", "dp", None),
        P("dp", "stream", None),
        P("stream", None),
        P("stream", None),
        P(None, "dp", "stream"),
        P("stream", "dp"),
        P("dp", "stream"),
        P("stream", "dp"),
        P("stream", None),
        P(None, "stream", None),
    )
    return jax.shard_map(body, mesh=mesh, in_specs=in_specs, out_specs=out_specs, check_vma=False)
```

profile of v0, /device:TPU:0, one launch (start us, length us, event | category | flops | bytes accessed | tf_op | source)
XLA Modules:
  0.0 2197.4 jit_solution(2177624863093289873)
XLA Ops:
  10.5 8.0 fusion.247
  23.0 6.3 fusion.180
  32.1 25.9 %all-gather.9.cloned.1.call-done = bf16[3,2048,512]{2,1,0:T(8,128)(2,1)} async-done(((bf16[3,256,512]{2,1,0:T(8,128)(2,1)}), bf16[3,2048,512]{2,1,0:T(8,128)(2,1)}) %all-gather.9.cloned.1.call-update) | async-done | bytes 6291472 | tf_op jit(solution)/shard_map/all_gather | solution.py:89
  58.1 5.7 slice_bitcast_fusion.103
  63.8 4.0 copy.279
  67.8 4.1 copy.275
  71.9 4.1 copy.276
  75.9 133.9 %all-gather.7.cloned.1.call-done = bf16[4,512,2048]{2,1,0:T(8,128)(2,1)} async-done(((bf16[1,512,2048]{2,1,0:T(8,128)(2,1)}), bf16[4,512,2048]{2,1,0:T(8,128)(2,1)}) %all-gather.7.cloned.1.call-update) | async-done | bytes 8388624 | tf_op jit(solution)/shard_map/all_gather | solution.py:87
  209.8 3.6 fusion.206
  213.5 3.3 fusion.202
  217.0 3.3 fusion.221
  221.5 3.5 collective-permute-start.1
  227.6 3.6 collective-permute-start.4
  239.6 12.8 collective-permute-done.1
  252.3 6.4 collective-permute-start.5
  261.8 13.0 collective-permute-done.2
  276.7 65.7 %collective-permute-done.3 = bf16[2,512,4,128]{1,3,2,0:T(8,128)(2,1)} collective-permute-done((bf16[2,512,4,128]{1,3,2,0:T(8,128)(2,1)}, bf16[2,512,4,128]{1,3,2,0:T(8,128)(2,1)}, u32[]{:S(2)}, u32[]{:S(2)}) %collective-permute-start.3) | collective-permute-done | bytes 1048608 | tf_op jit(solution)/shard_map/ppermute | solution.py:16
  348.0 11.0 conditional.37
  359.0 4.0 conditional.38
  359.1 3.9 fusion.2
  363.1 4.6 conditional.45
  369.1 18.4 multiply_convert_fusion.8
  387.5 16.7 all-gather.15.cloned.1.call-done
  404.1 10.5 fusion.252
  414.6 19.3 all-gather.11.cloned.1.call-done
  434.0 7.5 multiply_add_fusion.8
  443.1 75.4 %reduce-scatter.8.cloned.1.call-done = f32[512,512]{1,0:T(8,128)} async-done(((f32[512,2048]{1,0:T(8,128)}), f32[512,512]{1,0:T(8,128)}) %reduce-scatter.8.cloned.1.call-update) | async-done | bytes 1048592 | tf_op jit(solution)/shard_map/reduce_scatter | solution.py:150
  519.9 11.0 psum.49
  531.9 33.3 %all-reduce.7.cloned.1.call-done = (f32[512,36]{0,1:T(8,128)}, f32[512,36]{0,1:T(8,128)}) async-done(((f32[512,36]{0,1:T(8,128)}, f32[512,36]{0,1:T(8,128)}), (f32[512,36]{0,1:T(8,128)}, f32[512,36]{0,1:T(8,128)})) %all-reduce.7.cloned.1.call-update) | async-done | bytes 147472 | tf_op jit(solution)/shard_map/psum | solution.py:155
  570.1 45.3 %all-gather.17.cloned.1.call-done = bf16[512,2048]{1,0:T(8,128)(2,1)} async-done(((bf16[512,512]{1,0:T(8,128)(2,1)}), bf16[512,2048]{1,0:T(8,128)(2,1)}) %all-gather.17.cloned.1.call-update) | async-done | bytes 2097168 | tf_op jit(solution)/shard_map/all_gather | solution.py:178
  615.5 3.5 convolution_convert_fusion
  619.0 3.6 conditional.46
  622.9 11.3 conditional.54
  631.2 2.9 copy.455
  637.6 4.6 conditional.57
  643.7 4.6 conditional.59
  649.9 7.0 conditional.61
  661.2 2.9 copy.372
  665.4 2.9 copy.366
  668.3 2.9 copy.368
  674.2 2.9 copy.370
  684.3 58.5 %collective-permute-done.13 = f32[2,512,4,128]{1,3,2,0:T(8,128)} collective-permute-done((f32[2,512,4,128]{1,3,2,0:T(8,128)}, f32[2,512,4,128]{1,3,2,0:T(8,128)}, u32[]{:S(2)}, u32[]{:S(2)}) %collective-permute-start.13) | collective-permute-done | bytes 2097184 | tf_op jit(solution)/shard_map/ppermute | solution.py:16
  745.4 13.4 add_convert_fusion
  758.9 7.9 convolution_bitcast_fusion.6
  766.8 62.5 %collective-permute-done.11 = f32[2,512,4,128]{1,3,2,0:T(8,128)S(1)} collective-permute-done((f32[2,512,4,128]{1,3,2,0:T(8,128)}, f32[2,512,4,128]{1,3,2,0:T(8,128)S(1)}, u32[]{:S(2)}, u32[]{:S(2)}) %collective-permute-start.11) | collective-permute-done | bytes 2097184 | tf_op jit(solution)/shard_map/ppermute | solution.py:16
  829.3 6.2 add_add_fusion
  839.9 6.1 pad_maximum_fusion.8
  848.0 4.8 fusion.254
  853.1 2.9 convolution_bitcast_fusion.1
  856.0 2.9 convolution_bitcast_fusion.2
  858.9 2.9 convolution_bitcast_fusion
  861.9 5.1 pad_maximum_fusion.9
  867.0 12.5 fusion.209
  879.9 12.5 fusion.255
  892.5 295.0 %reduce-scatter.10.cloned.1.call-done = f32[1,512,2048]{2,1,0:T(8,128)} async-done(((f32[4,512,2048]{2,1,0:T(8,128)}), f32[1,512,2048]{2,1,0:T(8,128)}) %reduce-scatter.10.cloned.1.call-update) | async-done | bytes 4194320 | tf_op jit(solution)/shard_map/reduce_scatter | solution.py:269
  1187.5 5.1 fusion.189
  1193.4 9.1 fusion.187
  1202.5 11.2 broadcast_multiply_fusion
  1218.0 24.2 %all-reduce = (f32[1,2048]{1,0:T(1,128)}, f32[1,2048]{1,0:T(1,128)}, f32[36,1,9]{0,2,1:T(8,128)S(1)}) all-reduce(f32[1,2048]{1,0:T(1,128)S(1)} %bitcast.672, f32[1,2048]{1,0:T(1,128)S(1)} %bitcast.673, f32[36,1,9]{0,2,1:T(8,128)S(1)} %convolution_bitcast_fusion.8), channel_id=1, replica_groups=mesh['dp'=8,'stream'=4] {'dp'}, use_global_device_ids=true, to_apply=%region_107.108 | all-reduce | flops 4420 | bytes 35360 | tf_op jit(solution)/shard_map/psum | solution.py:293
  1243.4 54.0 %reduce-scatter.16.cloned.1.call-done = f32[512,256]{1,0:T(8,128)} async-done(((f32[512,2048]{1,0:T(8,128)}), f32[512,256]{1,0:T(8,128)}) %reduce-scatter.16.cloned.1.call-update) | async-done | bytes 524304 | tf_op jit(solution)/shard_map/reduce_scatter | solution.py:289
  1297.5 96.0 %reduce-scatter.14.cloned.1.call-done = f32[3,256,512]{2,1,0:T(8,128)} async-done(((f32[3,2048,512]{2,1,0:T(8,128)}), f32[3,256,512]{2,1,0:T(8,128)}) %reduce-scatter.14.cloned.1.call-update) | async-done | bytes 1572880 | tf_op jit(solution)/shard_map/reduce_scatter | solution.py:288
  1393.5 120.4 %reduce-scatter.18.cloned.1.call-done = f32[256,2048]{1,0:T(8,128)} async-done(((f32[2048,2048]{1,0:T(8,128)}), f32[256,2048]{1,0:T(8,128)}) %reduce-scatter.18.cloned.1.call-update) | async-done | bytes 2097168 | tf_op jit(solution)/shard_map/reduce_scatter | solution.py:290
  1513.9 120.0 %reduce-scatter.20.cloned.1.call-done = f32[2048,256]{1,0:T(8,128)} async-done(((f32[2048,2048]{1,0:T(8,128)}), f32[2048,256]{1,0:T(8,128)}) %reduce-scatter.20.cloned.1.call-update) | async-done | bytes 2097168 | tf_op jit(solution)/shard_map/reduce_scatter | solution.py:291
  1633.9 555.0 %reduce-scatter.12.cloned.1.call-done = f32[2,512,2048]{2,1,0:T(8,128)} async-done(((f32[8,512,2048]{2,1,0:T(8,128)}), f32[2,512,2048]{2,1,0:T(8,128)}) %reduce-scatter.12.cloned.1.call-update) | async-done | bytes 8388624 | tf_op jit(solution)/shard_map/reduce_scatter | solution.py:281
  (237 shorter events, 105.0 us)
Async XLA Ops:
  7.2 523.7 %copy-start = (bf16[512,36]{0,1:T(8,128)(2,1)S(1)}, bf16[512,36]{0,1:T(8,128)(2,1)}, u32[]{:S(2)}) copy-start(bf16[512,36]{0,1:T(8,128)(2,1)} %param.84) | copy-start | bytes 110596
  7.2 50.9 %all-gather.9.cloned.1.call-start = ((), (), s32[]{:S(2)}) async-start(), calls=%async_computation.8 | async-start | bytes 7077888 | tf_op jit(solution)/shard_map/all_gather | solution.py:89
  7.9 201.9 %all-gather.7.cloned.1.call-start = ((), (), s32[]{:S(2)}) async-start(), calls=%async_computation.7 | async-start | bytes 10485760 | tf_op jit(solution)/shard_map/all_gather | solution.py:87
  8.7 12.5 copy-start.38
  10.4 12.6 copy-start.2
  18.4 2.2 copy-start.3
  18.4 10.8 copy-start.44
  21.2 8.1 copy-start.46
  29.3 339.8 %all-gather.13.cloned.1.call-start = ((), (), s32[]{:S(2)}) async-start(), calls=%async_computation.10 | async-start | bytes 9437184 | tf_op jit(solution)/shard_map/all_gather | solution.py:91
  30.0 374.1 %all-gather.15.cloned.1.call-start = ((), (), s32[]{:S(2)}) async-start(), calls=%async_computation.11 | async-start | bytes 9437184 | tf_op jit(solution)/shard_map/all_gather | solution.py:92
  30.6 403.4 %all-gather.11.cloned.1.call-start = ((), (), s32[]{:S(2)}) async-start(), calls=%async_computation.9 | async-start | bytes 2359296 | tf_op jit(solution)/shard_map/all_gather | solution.py:90
  32.1 184.7 %copy-start.34 = (f32[512,16]{0,1:T(8,128)}, f32[512,16]{0,1:T(8,128)S(1)}, u32[]{:S(2)}) copy-start(f32[512,16]{0,1:T(8,128)S(1)} %get-tuple-element.1182) | copy-start | bytes 98308
  209.8 3.7 copy-start.24
  213.5 3.3 copy-start.31
  213.5 3.5 copy-start.23
  216.8 3.5 copy-start.25
  220.3 1.1 copy-start.28
  221.5 30.9 %collective-permute-start.1 = (bf16[2,512,4,128]{1,3,2,0:T(8,128)(2,1)}, bf16[2,512,4,128]{1,3,2,0:T(8,128)(2,1)S(1)}, u32[]{:S(2)}, u32[]{:S(2)}) collective-permute-start(bf16[2,512,4,128]{1,3,2,0:T(8,128)(2,1)} %pad_maximum_fusion.10), channel_id=1, source_target_pairs={{0,8},{4,12},{8,16},{12,20},{16,24},{20,28},{1,9},{5,13},{9,17},{1... | collective-permute-start | bytes 3145736 | tf_op jit(solution)/shard_map/ppermute | solution.py:16
  225.0 293.5 %reduce-scatter.8.cloned.1.call-start = ((), (), s32[]{:S(2)}) async-start(), calls=%async_computation.12 | async-start | bytes 5242880 | tf_op jit(solution)/shard_map/reduce_scatter | solution.py:150
  227.6 116.6 %collective-permute-start.4 = (bf16[2,512,4,128]{1,3,2,0:T(8,128)(2,1)}, bf16[2,512,4,128]{1,3,2,0:T(8,128)(2,1)}, u32[]{:S(2)}, u32[]{:S(2)}) collective-permute-start(bf16[2,512,4,128]{1,3,2,0:T(8,128)(2,1)} %pad_maximum_fusion.10), channel_id=1, source_target_pairs={{0,20},{4,24},{8,28},{1,21},{5,25},{9,29},{2,22},{6,26},{10,30},{3... | collective-permute-start | bytes 3145736 | tf_op jit(solution)/shard_map/ppermute | solution.py:16
  231.2 111.1 %collective-permute-start.3 = (bf16[2,512,4,128]{1,3,2,0:T(8,128)(2,1)}, bf16[2,512,4,128]{1,3,2,0:T(8,128)(2,1)}, u32[]{:S(2)}, u32[]{:S(2)}) collective-permute-start(bf16[2,512,4,128]{1,3,2,0:T(8,128)(2,1)} %pad_maximum_fusion.10), channel_id=1, source_target_pairs={{0,16},{4,20},{8,24},{12,28},{1,17},{5,21},{9,25},{13,29},{2,18},{... | collective-permute-start | bytes 3145736 | tf_op jit(solution)/shard_map/ppermute | solution.py:16
  233.5 41.3 %collective-permute-start.2 = (bf16[2,512,4,128]{1,3,2,0:T(8,128)(2,1)}, bf16[2,512,4,128]{1,3,2,0:T(8,128)(2,1)}, u32[]{:S(2)}, u32[]{:S(2)}) collective-permute-start(bf16[2,512,4,128]{1,3,2,0:T(8,128)(2,1)} %pad_maximum_fusion.10), channel_id=1, source_target_pairs={{0,12},{4,16},{8,20},{12,24},{16,28},{1,13},{5,17},{9,21},{13,25},... | collective-permute-start | bytes 3145736 | tf_op jit(solution)/shard_map/ppermute | solution.py:16
  235.8 23.8 %collective-permute-start = (bf16[2,512,4,128]{1,3,2,0:T(8,128)(2,1)}, bf16[2,512,4,128]{1,3,2,0:T(8,128)(2,1)S(1)}, u32[]{:S(2)}, u32[]{:S(2)}) collective-permute-start(bf16[2,512,4,128]{1,3,2,0:T(8,128)(2,1)} %pad_maximum_fusion.10), channel_id=1, source_target_pairs={{0,4},{4,8},{8,12},{12,16},{16,20},{20,24},{24,28},{1,5},{5,9},{9,... | collective-permute-start | bytes 3145736 | tf_op jit(solution)/shard_map/ppermute | solution.py:16
  239.6 119.5 %copy-start.8 = (bf16[512,4,128]{0,2,1:T(8,128)(2,1)}, bf16[512,4,128]{0,2,1:T(8,128)(2,1)S(1)}, u32[]{:S(2)}) copy-start(bf16[512,4,128]{0,2,1:T(8,128)(2,1)S(1)} %get-tuple-element.1187) | copy-start | bytes 1572868
  252.3 370.2 %copy-start.6 = (bf16[2,512,4,128]{1,3,2,0:T(8,128)(2,1)}, bf16[2,512,4,128]{1,3,2,0:T(8,128)(2,1)S(1)}, u32[]{:S(2)}) copy-start(bf16[2,512,4,128]{1,3,2,0:T(8,128)(2,1)S(1)} %collective-permute-done.1) | copy-start | bytes 3145732
  252.3 93.8 %collective-permute-start.5 = (bf16[2,512,4,128]{1,3,2,0:T(8,128)(2,1)}, bf16[2,512,4,128]{1,3,2,0:T(8,128)(2,1)}, u32[]{:S(2)}, u32[]{:S(2)}) collective-permute-start(bf16[2,512,4,128]{1,3,2,0:T(8,128)(2,1)} %pad_maximum_fusion.10), channel_id=1, source_target_pairs={{0,24},{4,28},{1,25},{5,29},{2,26},{6,30},{3,27},{7,31}} | collective-permute-start | bytes 3145736 | tf_op jit(solution)/shard_map/ppermute | solution.py:16
  259.6 1.4 copy-start.7
  259.6 88.4 %collective-permute-start.6 = (bf16[2,512,4,128]{1,3,2,0:T(8,128)(2,1)}, bf16[2,512,4,128]{1,3,2,0:T(8,128)(2,1)S(1)}, u32[]{:S(2)}, u32[]{:S(2)}) collective-permute-start(bf16[2,512,4,128]{1,3,2,0:T(8,128)(2,1)} %pad_maximum_fusion.10), channel_id=1, source_target_pairs={{0,28},{1,29},{2,30},{3,31}} | collective-permute-start | bytes 3145736 | tf_op jit(solution)/shard_map/ppermute | solution.py:16
  369.1 64.9 %copy-start.19 = (bf16[512,4,128]{0,2,1:T(8,128)(2,1)}, bf16[512,4,128]{0,2,1:T(8,128)(2,1)S(1)}, u32[]{:S(2)}) copy-start(bf16[512,4,128]{0,2,1:T(8,128)(2,1)S(1)} %copy.312) | copy-start | bytes 1572868
  441.6 123.7 %all-reduce.7.cloned.1.call-start = ((), (), s32[]{:S(2)}) async-start(), calls=%async_computation.21 | async-start | bytes 327680 | tf_op jit(solution)/shard_map/psum | solution.py:155
  519.9 50.2 %copy-start.17 = (bf16[512,512]{1,0:T(8,128)(2,1)}, bf16[512,512]{1,0:T(8,128)(2,1)S(1)}, u32[]{:S(2)}) copy-start(bf16[512,512]{1,0:T(8,128)(2,1)S(1)} %get-tuple-element.1248) | copy-start | bytes 1572868
  531.8 83.6 %all-gather.17.cloned.1.call-start = ((), (), s32[]{:S(2)}) async-start(), calls=%async_computation.13 | async-start | bytes 2621440 | tf_op jit(solution)/shard_map/all_gather | solution.py:178
  531.9 87.1 %copy-start.42 = (f32[512]{0:T(512)}, f32[512]{0:T(512)S(1)}, u32[]{:S(2)}) copy-start(f32[512]{0:T(512)S(1)} %add_rsqrt_fusion) | copy-start | bytes 6148
  569.9 617.6 %reduce-scatter.10.cloned.1.call-start = ((), (), s32[]{:S(2)}) async-start(), calls=%async_computation.14 | async-start | bytes 20971520 | tf_op jit(solution)/shard_map/reduce_scatter | solution.py:269
  619.0 2.0 copy-start.29
  624.8 1.6 copy-start.30
  626.5 2.6 copy-start.9
  659.9 83.0 %collective-permute-start.13 = (f32[2,512,4,128]{1,3,2,0:T(8,128)}, f32[2,512,4,128]{1,3,2,0:T(8,128)}, u32[]{:S(2)}, u32[]{:S(2)}) collective-permute-start(f32[2,512,4,128]{1,3,2,0:T(8,128)} %copy.373), channel_id=1, source_target_pairs={{28,0},{29,1},{30,2},{31,3}} | collective-permute-start | bytes 6291464 | tf_op jit(solution)/shard_map/ppermute | solution.py:16
  664.1 80.0 %collective-permute-start.12 = (f32[2,512,4,128]{1,3,2,0:T(8,128)}, f32[2,512,4,128]{1,3,2,0:T(8,128)}, u32[]{:S(2)}, u32[]{:S(2)}) collective-permute-start(f32[2,512,4,128]{1,3,2,0:T(8,128)} %copy.372), channel_id=1, source_target_pairs={{24,0},{28,4},{25,1},{29,5},{26,2},{30,6},{27,3},{31,7}} | collective-permute-start | bytes 6291464 | tf_op jit(solution)/shard_map/ppermute | solution.py:16
  680.4 148.9 %collective-permute-start.11 = (f32[2,512,4,128]{1,3,2,0:T(8,128)}, f32[2,512,4,128]{1,3,2,0:T(8,128)S(1)}, u32[]{:S(2)}, u32[]{:S(2)}) collective-permute-start(f32[2,512,4,128]{1,3,2,0:T(8,128)} %copy.371), channel_id=1, source_target_pairs={{20,0},{24,4},{28,8},{21,1},{25,5},{29,9},{22,2},{26,6},{30,10},{2... | collective-permute-start | bytes 6291464 | tf_op jit(solution)/shard_map/ppermute | solution.py:16
  681.7 147.6 %collective-permute-start.10 = (f32[2,512,4,128]{1,3,2,0:T(8,128)}, f32[2,512,4,128]{1,3,2,0:T(8,128)S(1)}, u32[]{:S(2)}, u32[]{:S(2)}) collective-permute-start(f32[2,512,4,128]{1,3,2,0:T(8,128)} %copy.370), channel_id=1, source_target_pairs={{16,0},{20,4},{24,8},{28,12},{17,1},{21,5},{25,9},{29,13},{18,2},{... | collective-permute-start | bytes 6291464 | tf_op jit(solution)/shard_map/ppermute | solution.py:16
  683.0 146.3 %collective-permute-start.9 = (f32[2,512,4,128]{1,3,2,0:T(8,128)}, f32[2,512,4,128]{1,3,2,0:T(8,128)}, u32[]{:S(2)}, u32[]{:S(2)}) collective-permute-start(f32[2,512,4,128]{1,3,2,0:T(8,128)} %copy.369), channel_id=1, source_target_pairs={{12,0},{16,4},{20,8},{24,12},{28,16},{13,1},{17,5},{21,9},{25,13},... | collective-permute-start | bytes 6291464 | tf_op jit(solution)/shard_map/ppermute | solution.py:16
  742.8 86.5 %collective-permute-start.8 = (f32[2,512,4,128]{1,3,2,0:T(8,128)}, f32[2,512,4,128]{1,3,2,0:T(8,128)}, u32[]{:S(2)}, u32[]{:S(2)}) collective-permute-start(f32[2,512,4,128]{1,3,2,0:T(8,128)} %copy.368), channel_id=1, source_target_pairs={{8,0},{12,4},{16,8},{20,12},{24,16},{28,20},{9,1},{13,5},{17,9},{2... | collective-permute-start | bytes 6291464 | tf_op jit(solution)/shard_map/ppermute | solution.py:16
  744.1 85.2 %collective-permute-start.7 = (f32[2,512,4,128]{1,3,2,0:T(8,128)}, f32[2,512,4,128]{1,3,2,0:T(8,128)}, u32[]{:S(2)}, u32[]{:S(2)}) collective-permute-start(f32[2,512,4,128]{1,3,2,0:T(8,128)} %copy.366), channel_id=1, source_target_pairs={{4,0},{8,4},{12,8},{16,12},{20,16},{24,20},{28,24},{5,1},{9,5},{13... | collective-permute-start | bytes 6291464 | tf_op jit(solution)/shard_map/ppermute | solution.py:16
  745.4 90.5 %slice-start = ((s8[6291456]{0:T(1024)(128)(4,1)}), s8[2097152]{0:T(1024)(128)(4,1)S(1)}, s32[]{:S(2)}) async-start(s8[6291456]{0:T(1024)(128)(4,1)} %bitcast.651), calls=%async_computation.22 | async-start | bytes 4194304
  758.9 77.1 %slice-start.1 = ((s8[6291456]{0:T(1024)(128)(4,1)}), s8[4194304]{0:T(1024)(128)(4,1)S(1)}, s32[]{:S(2)}) async-start(s8[6291456]{0:T(1024)(128)(4,1)} %bitcast.651), calls=%async_computation.23 | async-start | bytes 8388608
  829.3 6.5 copy-start.35
  829.3 6.5 copy-start.40
  846.0 1.0 copy-start.43
  846.0 2.0 copy-start.20
  846.0 397.4 %all-reduce.5.cloned.1.call-start = ((), (), s32[]{:S(2)}) async-start(), calls=%async_computation.20 | async-start | bytes 163840 | tf_op jit(solution)/shard_map/psum | solution.py:293
  847.9 449.6 %reduce-scatter.16.cloned.1.call-start = ((), (), s32[]{:S(2)}) async-start(), calls=%async_computation.17 | async-start | bytes 4718592 | tf_op jit(solution)/shard_map/reduce_scatter | solution.py:289
  852.8 540.7 %reduce-scatter.14.cloned.1.call-start = ((), (), s32[]{:S(2)}) async-start(), calls=%async_computation.16 | async-start | bytes 14155776 | tf_op jit(solution)/shard_map/reduce_scatter | solution.py:288
  867.0 646.9 %reduce-scatter.18.cloned.1.call-start = ((), (), s32[]{:S(2)}) async-start(), calls=%async_computation.18 | async-start | bytes 18874368 | tf_op jit(solution)/shard_map/reduce_scatter | solution.py:290
  879.6 754.3 %reduce-scatter.20.cloned.1.call-start = ((), (), s32[]{:S(2)}) async-start(), calls=%async_computation.19 | async-start | bytes 18874368 | tf_op jit(solution)/shard_map/reduce_scatter | solution.py:291
  892.4 295.0 %copy-start.39 = (f32[1,2048]{1,0:T(1,128)S(1)}, f32[1,2048]{1,0:T(1,128)}, u32[]{:S(2)}) copy-start(f32[1,2048]{1,0:T(1,128)} %copy-done.38) | copy-start | bytes 24580
  892.4 295.0 %copy-start.45 = (f32[512]{0:T(512)S(1)}, f32[512]{0:T(512)}, u32[]{:S(2)}) copy-start(f32[512]{0:T(512)} %copy-done.44) | copy-start | bytes 6148
  892.4 295.0 %copy-start.47 = (f32[512]{0:T(512)S(1)}, f32[512]{0:T(512)}, u32[]{:S(2)}) copy-start(f32[512]{0:T(512)} %copy-done.46) | copy-start | bytes 6148
  892.5 1296.4 %reduce-scatter.12.cloned.1.call-start = ((), (), s32[]{:S(2)}) async-start(), calls=%async_computation.15 | async-start | bytes 41943040 | tf_op jit(solution)/shard_map/reduce_scatter | solution.py:281
  1187.5 5.1 copy-start.4
  1187.5 5.9 copy-start.5
  1193.4 9.1 copy-start.41
  1213.7 1.7 copy-start.37
  1213.7 976.7 %copy-start.1 = (bf16[512,36]{0,1:T(8,128)(2,1)S(1)}, bf16[512,36]{0,1:T(8,128)(2,1)}, u32[]{:S(2)}) copy-start(bf16[512,36]{0,1:T(8,128)(2,1)} %param.84) | copy-start | bytes 110596
  (8 other events, 6.9 us)
Sparse Core Ops, SparseCore 0:
  9.9 48.1 all-gather.8
  60.2 149.5 all-gather.6
  211.7 119.3 all-gather.12
  332.9 71.2 all-gather.14
  405.9 28.0 all-gather.10
  441.7 76.7 reduce-scatter.7
  531.9 33.2 all-reduce.6
  570.0 45.3 all-gather.16
  846.2 341.2 reduce-scatter.9
  1190.4 51.2 all-reduce.4
  1245.6 51.8 reduce-scatter.15
  1301.4 92.0 reduce-scatter.13
  1397.6 116.1 reduce-scatter.17
  1517.9 115.9 reduce-scatter.19
  1636.7 552.1 reduce-scatter.11
where the time goes:
time: 2200 us
  waiting for transfers between devices  1800 us (82%)
  matrix products  134 us (6%)
  local copies, waits for them, and re-layouts  77.9 us (4%)
  other arithmetic  69.5 us (3%)
  blocking collectives  35.2 us (2%)
  starting transfers between devices  31.5 us (1%)
  loops' own time  28.2 us (1%)
    reduce_scatter x1, waiting for transfers between devices, body(): lax.psum_scatter(jnp.transpose(mix_here)[:, :, None] * stream_grad[None],...  555 us
    reduce_scatter x1, waiting for transfers between devices, body(): lax.psum_scatter(normed_parts, 'stream', scatter_dimension=0, tiled=True)[0]  295 us
    ppermute x14, waiting for transfers between devices, passed_along(): return lax.ppermute(shard, axis, pairs)  213 us
    all_gather x1, waiting for transfers between devices, body(): all_normed = lax.all_gather(normed[None], 'stream', axis=0, tiled=True)  134 us
    reduce_scatter x1, waiting for transfers between devices, body(): lax.psum_scatter(up_full_grad, 'dp', scatter_dimension=0, tiled=True)  120 us
    reduce_scatter x1, waiting for transfers between devices, body(): lax.psum_scatter(down_full_grad, 'dp', scatter_dimension=1, tiled=True)  120 us
    reduce_scatter x1, waiting for transfers between devices, body(): lax.psum_scatter(project_grads, 'dp', scatter_dimension=1, tiled=True)  96 us
    reduce_scatter x1, waiting for transfers between devices, body(): lax.psum_scatter(branches, 'stream', scatter_dimension=1, tiled=True)  75.4 us
  transfers between devices with their start and end apart: 29, of which 18 were waited for; matrix products, arithmetic and copies ran while one was open for 10% of the time, Pallas kernels for 0%

commit v1 on v0

v1 whole, which is shorter than its diff:
```python
import math

import jax
import jax.numpy as jnp
from jax import lax
from jax.experimental import pallas as pl
from jax.experimental.pallas import tpu as pltpu
from jax.sharding import PartitionSpec as P

HD = 128
ROT = 32
SEQ = 2048


def passed_along(shard, axis, by):
    peers = lax.axis_size(axis)
    pairs = [(i, i + by) for i in range(peers) if 0 <= i + by < peers]
    return lax.ppermute(shard, axis, pairs)


def rotate(vectors, positions, sign):
    half = ROT // 2
    counter = jnp.arange(half, dtype=jnp.float32)
    freqs = jnp.exp(counter * (-2.0 * math.log(10000.0) / ROT))
    angles = positions.astype(jnp.float32)[:, None] * freqs[None, :]
    cosine = jnp.cos(angles)[:, None, :]
    sine = sign * jnp.sin(angles)[:, None, :]
    first = vectors[..., :half]
    second = vectors[..., half:ROT]
    return jnp.concatenate(
        [first * cosine - second * sine, second * cosine + first * sine, vectors[..., ROT:]],
        axis=-1,
    )


def exact_gelu(vectors):
    return jax.nn.gelu(vectors, approximate=False)


def block_logits(queries, keys_block, diagonal):
    logits = jnp.einsum("qhd,khd->hqk", queries, keys_block, preferred_element_type=jnp.float32) * (
        1.0 / math.sqrt(queries.shape[-1])
    )
    if diagonal:
        counter = jnp.arange(queries.shape[0], dtype=jnp.int32)
        allowed = counter[None, :] <= counter[:, None]
        logits = jnp.where(allowed[None], logits, -1e30)
    return logits


def keep_same(state):
    return state


BF = jnp.bfloat16
F32 = jnp.float32
OUTWARD = [(0, 1), (3, 2)]
MIDDLE = [(1, 2), (2, 1)]
INWARD = [(1, 0), (2, 3)]


def dot(left, right):
    return jnp.dot(left, right, preferred_element_type=F32)


def dot_rows(left, right):
    return lax.dot_general(left, right, (((0,), (0,)), ((), ())), preferred_element_type=F32)


def dot_cols(left, right):
    return lax.dot_general(left, right, (((1,), (1,)), ((), ())), preferred_element_type=F32)


def partner(shard, bit):
    peers = lax.axis_size("dp")
    return lax.ppermute(shard, "dp", [(i, i ^ bit) for i in range(peers)])


def line_hop(shard, pairs):
    return lax.ppermute(shard, "stream", pairs)


def after(value, *others):
    return lax.optimization_barrier((value, *others))[0]


def gather_weights(shards):
    peers = lax.axis_size("dp")
    if peers != 8:
        return [lax.all_gather(shard, "dp", axis=0) for shard in shards]
    index = lax.axis_index("dp")
    full = []
    ahead = None
    for shard in shards:
        if ahead is not None:
            shard = after(shard, *ahead)
        by_x = partner(shard, 2)
        by_y = partner(shard, 4)
        ahead = (by_x, by_y)
        cut = max(range(shard.ndim - 1), key=lambda dim: shard.shape[dim])
        half = shard.shape[cut] // 2
        low = lax.slice_in_dim(by_y, 0, half, axis=cut)
        high = lax.slice_in_dim(by_x, half, 2 * half, axis=cut)
        pieces = [
            (shard, 0, 0),
            (by_x, 2, 0),
            (by_y, 4, 0),
            (partner(low, 2), 6, 0),
            (partner(high, 4), 6, half),
        ]
        pieces += [(partner(piece, 1), code ^ 1, start) for piece, code, start in pieces]
        whole = jnp.zeros((peers, *shard.shape), shard.dtype)
        for piece, code, start in pieces:
            place = [jnp.int32(0)] * (shard.ndim + 1)
            place[0] = index ^ code
            place[cut + 1] = jnp.int32(start)
            whole = lax.dynamic_update_slice(whole, piece[None], place)
        full.append(whole)
    return full


def rope_tables(positions, sign):
    half = ROT // 2
    lane = jnp.arange(HD, dtype=jnp.int32)
    counter = (lane % half).astype(F32)
    freqs = jnp.exp(counter * (-2.0 * math.log(10000.0) / ROT))
    angles = positions.astype(F32)[:, None] * freqs[None, :]
    cosine = jnp.where(lane < ROT, jnp.cos(angles), 1.0)
    sine = sign * jnp.sin(angles)
    up = jnp.where(lane < half, -sine, 0.0)
    down = jnp.where((lane >= half) & (lane < ROT), sine, 0.0)
    return jnp.stack([cosine, up, down])


def turned(block, tables):
    half = ROT // 2
    return (
        block * tables[0]
        + pltpu.roll(block, HD - half, 1) * tables[1]
        + pltpu.roll(block, half, 1) * tables[2]
    )


def make_streams(history, mix_rows, gains, biases):
    entries, tokens, width = history.shape
    streams = gains.shape[0]
    rows, sub, lanes = min(64, tokens), 16, 512

    def kernel(hist, mix, gain, bias, normed, unit, inv, last, scratch):
        def step(r, carry):
            here = pl.ds(pl.multiple_of(r * sub, sub), sub)
            weights = mix[here, :]
            columns = [
                [weights[:, s * entries + j : s * entries + j + 1] for j in range(entries)]
                for s in range(streams)
            ]
            for lane in range(0, width, lanes):
                span = slice(lane, lane + lanes)
                sums = [None] * streams
                for j in range(entries):
                    part = hist[j, here, span].astype(F32)
                    for s in range(streams):
                        term = columns[s][j] * part
                        sums[s] = term if j == 0 else sums[s] + term
                for s in range(streams):
                    scratch[s, :, span] = sums[s]
            stds = []
            for s in range(streams):
                values = scratch[s]
                center = values - jnp.sum(values, axis=-1, keepdims=True) * (1.0 / width)
                var = jnp.sum(center * center, axis=-1, keepdims=True) * (1.0 / width)
                std = lax.rsqrt(var + 1e-05)
                stds.append(std)
                scaled = center * std
                unit[s, here, :] = scaled.astype(BF)
                normed[s, here, :] = (scaled * gain[s : s + 1] + bias[s : s + 1]).astype(BF)
            last[here, :] = scratch[streams - 1]
            inv[here, :] = jnp.concatenate(stds, axis=-1)
            return carry

        lax.fori_loop(0, rows // sub, step, 0)

    wide = jax.ShapeDtypeStruct((streams, tokens, width), BF)
    return pl.pallas_call(
        kernel,
        grid=(tokens // rows,),
        in_specs=[
            pl.BlockSpec((entries, rows, width), lambda i: (0, i, 0)),
            pl.BlockSpec((rows, streams * entries), lambda i: (i, 0)),
            pl.BlockSpec((streams, width), lambda i: (0, 0)),
            pl.BlockSpec((streams, width), lambda i: (0, 0)),
        ],
        out_specs=[
            pl.BlockSpec((streams, rows, width), lambda i: (0, i, 0)),
            pl.BlockSpec((streams, rows, width), lambda i: (0, i, 0)),
            pl.BlockSpec((rows, streams), lambda i: (i, 0)),
            pl.BlockSpec((rows, width), lambda i: (i, 0)),
        ],
        out_shape=[
            wide,
            wide,
            jax.ShapeDtypeStruct((tokens, streams), F32),
            jax.ShapeDtypeStruct((tokens, width), F32),
        ],
        scratch_shapes=[pltpu.VMEM((streams, sub, width), F32)],
        name="make_streams",
    )(history, mix_rows, gains, biases)


def project(normed, w_heads, tables):
    _, tokens, width = normed.shape
    columns = w_heads.shape[3]
    heads, half = columns // HD, tokens // 2

    def kernel(x, w, table, out):
        flat = dot(x[0], w[...].reshape(width, columns))
        turn = pl.program_id(0) < 2

        def put(head, block):
            out[2 * head, 0] = block[:half].astype(BF)
            out[2 * head + 1, 0] = block[half:].astype(BF)

        @pl.when(turn)
        def _():
            for head in range(heads):
                put(head, turned(flat[:, head * HD : (head + 1) * HD], table[...]))

        @pl.when(jnp.logical_not(turn))
        def _():
            for head in range(heads):
                put(head, flat[:, head * HD : (head + 1) * HD])

    return pl.pallas_call(
        kernel,
        grid=(3,),
        in_specs=[
            pl.BlockSpec((1, tokens, width), lambda c: (c, 0, 0)),
            pl.BlockSpec((w_heads.shape[0], 1, w_heads.shape[2], columns), lambda c: (0, c, 0, 0)),
            pl.BlockSpec((3, tokens, HD), lambda c: (0, 0, 0)),
        ],
        out_specs=pl.BlockSpec((2 * heads, 1, half, HD), lambda c: (0, c, 0, 0)),
        out_shape=jax.ShapeDtypeStruct((2 * heads, 3, half, HD), BF),
        name="project",
    )(normed, w_heads, tables)


def attend(own, other, first_key, side):
    shards, _, half, _ = own.shape
    factor = 1.0 / math.sqrt(HD)

    def kernel(first, part, mine, theirs, out, exact, norm):
        s = pl.program_id(0)
        query = mine[s, 0]

        def fold(state, keys, values, mask):
            top, total, acc = state
            logits = dot_cols(query, keys) * factor
            if mask is not None:
                logits = jnp.where(mask, logits, -1e30)
            new_top = jnp.maximum(top, jnp.max(logits, axis=-1, keepdims=True))
            probs = jnp.exp(logits - new_top)
            keep = jnp.exp(top - new_top)
            return (
                new_top,
                total * keep + jnp.sum(probs, axis=-1, keepdims=True),
                acc * keep + dot(probs.astype(BF), values),
            )

        row = lax.broadcasted_iota(jnp.int32, (half, half), 0)
        col = lax.broadcasted_iota(jnp.int32, (half, half), 1)
        state = (
            jnp.full((half, 1), -1e30, F32),
            jnp.zeros((half, 1), F32),
            jnp.zeros((half, HD), F32),
        )
        state = fold(state, mine[s, 1], mine[s, 2], col <= row)
        state = lax.fori_loop(
            0, part[0], lambda i, st: fold(st, theirs[s, 0], theirs[s, 1], None), state
        )

        def shard_step(b, st):
            st = fold(st, mine[b, 1], mine[b, 2], None)
            return fold(st, theirs[b, 0], theirs[b, 1], None)

        top, total, acc = lax.fori_loop(first[s], s, shard_step, state)
        result = acc / total
        out[0] = result.astype(BF)
        exact[0] = result
        norm[0] = top + jnp.log(total)

    return pl.pallas_call(
        kernel,
        grid_spec=pltpu.PrefetchScalarGridSpec(
            num_scalar_prefetch=2,
            grid=(shards,),
            in_specs=[
                pl.BlockSpec((shards, 3, half, HD), lambda s, *_: (0, 0, 0, 0)),
                pl.BlockSpec((shards, 2, half, HD), lambda s, *_: (0, 0, 0, 0)),
            ],
            out_specs=[
                pl.BlockSpec((1, half, HD), lambda s, *_: (s, 0, 0)),
                pl.BlockSpec((1, half, HD), lambda s, *_: (s, 0, 0)),
                pl.BlockSpec((1, half, 1), lambda s, *_: (s, 0, 0)),
            ],
        ),
        out_shape=[
            jax.ShapeDtypeStruct((shards, half, HD), BF),
            jax.ShapeDtypeStruct((shards, half, HD), F32),
            jax.ShapeDtypeStruct((shards, half, 1), F32),
        ],
        name="attend",
    )(first_key, side, own, other)


def attend_back(own, other, grads, exact, norm, first_key, side):
    shards, _, half, _ = own.shape
    factor = 1.0 / math.sqrt(HD)

    def kernel(first, part, mine, theirs, grad_ref, exact_ref, norm_ref, kept, given, sums):
        s = pl.program_id(0)
        query = mine[s, 0]
        grad = grad_ref[s]
        delta = jnp.sum(grad.astype(F32) * exact_ref[0], axis=-1, keepdims=True)
        level = norm_ref[0]
        lowered = grad

        @pl.when(s == 0)
        def _():
            sums[...] = jnp.zeros_like(sums)

        def fold(query_grad, keys, values, mask, slot, b):
            logits = dot_cols(query, keys) * factor
            probs = jnp.exp(logits - level)
            if mask is not None:
                probs = jnp.where(mask, probs, 0.0)
            score = (probs * (dot_cols(grad, values) - delta)).astype(BF)
            sums[slot, b] += dot_rows(score, query)
            sums[slot + 1, b] += dot_rows(probs.astype(BF), lowered)
            return query_grad + dot(score, keys)

        row = lax.broadcasted_iota(jnp.int32, (half, half), 0)
        col = lax.broadcasted_iota(jnp.int32, (half, half), 1)
        total = fold(jnp.zeros((half, HD), F32), mine[s, 1], mine[s, 2], col <= row, 0, s)
        total = lax.fori_loop(
            0, part[0], lambda i, q: fold(q, theirs[s, 0], theirs[s, 1], None, 2, s), total
        )

        def shard_step(b, q):
            q = fold(q, mine[b, 1], mine[b, 2], None, 0, b)
            return fold(q, theirs[b, 0], theirs[b, 1], None, 2, b)

        total = lax.fori_loop(first[s], s, shard_step, total)
        kept[s, 0] = (total * factor).astype(BF)

        @pl.when(s == shards - 1)
        def _():
            for b in range(shards):
                kept[b, 1] = (sums[0, b] * factor).astype(BF)
                kept[b, 2] = sums[1, b].astype(BF)
                given[b, 0] = (sums[2, b] * factor).astype(BF)
                given[b, 1] = sums[3, b].astype(BF)

    whole = lambda n: pl.BlockSpec((shards, n, half, HD), lambda s, *_: (0, 0, 0, 0))
    return pl.pallas_call(
        kernel,
        grid_spec=pltpu.PrefetchScalarGridSpec(
            num_scalar_prefetch=2,
            grid=(shards,),
            in_specs=[
                whole(3),
                whole(2),
                pl.BlockSpec((shards, half, HD), lambda s, *_: (0, 0, 0)),
                pl.BlockSpec((1, half, HD), lambda s, *_: (s, 0, 0)),
                pl.BlockSpec((1, half, 1), lambda s, *_: (s, 0, 0)),
            ],
            out_specs=[whole(3), whole(2)],
            scratch_shapes=[pltpu.VMEM((4, shards, half, HD), F32)],
        ),
        out_shape=[
            jax.ShapeDtypeStruct((shards, 3, half, HD), BF),
            jax.ShapeDtypeStruct((shards, 2, half, HD), BF),
        ],
        name="attend_back",
    )(first_key, side, own, other, grads, exact, norm)


def norm_back(grad, unit, inv, gain, extra):
    width = grad.shape[1]
    scaled = grad * gain
    mean = jnp.sum(scaled, axis=-1, keepdims=True) * (1.0 / width)
    slope = jnp.sum(scaled * unit, axis=-1, keepdims=True) * (1.0 / width)
    result = inv * (scaled - mean - unit * slope)
    return result if extra is None else result + extra


def heads_back(parts, w_heads, normed, unit, inv, gains, tables):
    _, tokens, width = normed.shape
    columns = w_heads.shape[3]
    heads, half = columns // HD, tokens // 2
    block = min(128, tokens)

    def kernel(part, w, x, u, istd, gain, table, stream, weight, stats, grad, wide):
        c = pl.program_id(0)
        turn = c < 2

        def take(head):
            return jnp.concatenate([part[2 * head, 0], part[2 * head + 1, 0]], axis=0).astype(F32)

        @pl.when(turn)
        def _():
            for head in range(heads):
                grad[:, head * HD : (head + 1) * HD] = turned(take(head), table[...]).astype(BF)

        @pl.when(jnp.logical_not(turn))
        def _():
            for head in range(heads):
                grad[:, head * HD : (head + 1) * HD] = take(head).astype(BF)

        wide[...] = dot_cols(grad[...], w[...].reshape(width, columns))
        weight[0] = dot_rows(x[0], grad[...]).astype(BF)
        stats[...] = jnp.zeros_like(stats)
        column = lax.broadcasted_iota(jnp.int32, (block, istd.shape[1]), 1)

        def step(r, carry):
            here = pl.ds(pl.multiple_of(r * block, block), block)
            values = wide[here, :]
            units = u[0, here, :].astype(F32)
            std = jnp.sum(jnp.where(column == c, istd[here, :], 0.0), axis=-1, keepdims=True)
            stream[0, here, :] = norm_back(values, units, std, gain[0], None).astype(BF)
            stats[0, 0:1] += jnp.sum(values * units, axis=0, keepdims=True)
            stats[0, 1:2] += jnp.sum(values, axis=0, keepdims=True)
            return carry

        lax.fori_loop(0, tokens // block, step, 0)

    return pl.pallas_call(
        kernel,
        grid=(3,),
        in_specs=[
            pl.BlockSpec((2 * heads, 1, half, HD), lambda c: (0, c, 0, 0)),
            pl.BlockSpec((w_heads.shape[0], 1, w_heads.shape[2], columns), lambda c: (0, c, 0, 0)),
            pl.BlockSpec((1, tokens, width), lambda c: (c, 0, 0)),
            pl.BlockSpec((1, tokens, width), lambda c: (c, 0, 0)),
            pl.BlockSpec((tokens, inv.shape[1]), lambda c: (0, 0)),
            pl.BlockSpec((1, 1, width), lambda c: (c, 0, 0)),
            pl.BlockSpec((3, tokens, HD), lambda c: (0, 0, 0)),
        ],
        out_specs=[
            pl.BlockSpec((1, tokens, width), lambda c: (c, 0, 0)),
            pl.BlockSpec((1, width, columns), lambda c: (c, 0, 0)),
            pl.BlockSpec((1, 2, width), lambda c: (c, 0, 0)),
        ],
        out_shape=[
            jax.ShapeDtypeStruct((3, tokens, width), BF),
            jax.ShapeDtypeStruct((3, width, columns), BF),
            jax.ShapeDtypeStruct((3, 2, width), F32),
        ],
        scratch_shapes=[pltpu.VMEM((tokens, columns), BF), pltpu.VMEM((tokens, width), F32)],
        name="heads_back",
    )(parts, w_heads, normed, unit, inv, gains[:, None, :], tables)


def last_back(grad, unit, inv, gain, extra, flag):
    tokens, width = grad.shape
    block = min(128, tokens)

    def kernel(g, u, istd, gain_ref, e, flag_ref, stream, stats):
        @pl.when(pl.program_id(0) == 0)
        def _():
            stats[...] = jnp.zeros_like(stats)

        values = g[...]
        units = u[...].astype(F32)
        std = istd[...][:, -1:]
        added = e[...].astype(F32) * flag_ref[0]
        stream[...] = norm_back(values, units, std, gain_ref[...], added).astype(BF)
        stats[0:1] += jnp.sum(values * units, axis=0, keepdims=True)
        stats[1:2] += jnp.sum(values, axis=0, keepdims=True)

    row = lambda n: pl.BlockSpec((block, n), lambda i: (i, 0))
    return pl.pallas_call(
        kernel,
        grid=(tokens // block,),
        in_specs=[
            row(width),
            row(width),
            row(inv.shape[1]),
            pl.BlockSpec((1, width), lambda i: (0, 0)),
            row(width),
            pl.BlockSpec(memory_space=pltpu.SMEM),
        ],
        out_specs=[row(width), pl.BlockSpec((2, width), lambda i: (0, 0))],
        out_shape=[
            jax.ShapeDtypeStruct((tokens, width), BF),
            jax.ShapeDtypeStruct((2, width), F32),
        ],
        name="last_back",
    )(grad, unit, inv, gain, extra, flag)


def mixing_back(heads_part, last_part, history):
    entries, tokens, width = history.shape
    streams = heads_part.shape[0] + 1
    rows, sub, lanes = min(64, tokens), 16, 256

    def kernel(first, last, hist, out):
        def step(r, carry):
            here = pl.ds(pl.multiple_of(r * sub, sub), sub)
            for s in range(streams):
                sums = [None] * entries
                for lane in range(0, width, lanes):
                    span = slice(lane, lane + lanes)
                    part = first[s, here, span] if s < streams - 1 else last[here, span]
                    part = part.astype(F32)
                    for j in range(entries):
                        term = part * hist[j, here, span].astype(F32)
                        sums[j] = term if lane == 0 else sums[j] + term
                columns = [jnp.sum(item, axis=-1, keepdims=True) for item in sums]
                out[s, here, :] = jnp.concatenate(columns, axis=-1)
            return carry

        lax.fori_loop(0, rows // sub, step, 0)

    return pl.pallas_call(
        kernel,
        grid=(tokens // rows,),
        in_specs=[
            pl.BlockSpec((streams - 1, rows, width), lambda i: (0, i, 0)),
            pl.BlockSpec((rows, width), lambda i: (i, 0)),
            pl.BlockSpec((entries, rows, width), lambda i: (0, i, 0)),
        ],
        out_specs=pl.BlockSpec((streams, rows, entries), lambda i: (0, i, 0)),
        out_shape=jax.ShapeDtypeStruct((streams, tokens, entries), F32),
        name="mixing_back",
    )(heads_part, last_part, history)


def far_attend(queries, keys, values, shard_offset):
    tokens, heads_here, head_size = queries.shape
    data_index = lax.axis_index("dp")
    pairs = [jnp.stack([keys, values])]
    reach = 2 * SEQ // tokens
    for back in range(1, reach):
        pairs.append(passed_along(pairs[0], "dp", back))
    usable = [(shard_offset[0] >= back * tokens) & (data_index >= back) for back in range(reach)]
    first_logits = block_logits(queries, keys, True)
    top = jnp.max(first_logits, axis=-1)
    total = jnp.sum(jnp.exp(first_logits - top[..., None]), axis=-1)
    for back in range(1, reach):

        def widen(state, block=pairs[back][0]):
            logits = block_logits(queries, block, False)
            new_top = jnp.maximum(state[0], jnp.max(logits, axis=-1))
            summed = state[1] * jnp.exp(state[0] - new_top) + jnp.sum(
                jnp.exp(logits - new_top[..., None]), axis=-1
            )
            return (new_top, summed)

        top, total = lax.cond(usable[back], widen, keep_same, (top, total))
    log_total = top + jnp.log(total)
    attended = jnp.zeros((tokens, heads_here, head_size), F32)
    for back in range(reach):

        def accumulate(current, block=pairs[back], diagonal=back == 0):
            probs = jnp.exp(block_logits(queries, block[0], diagonal) - log_total[..., None])
            return current + jnp.einsum(
                "hqk,khd->qhd", probs.astype(BF), block[1], preferred_element_type=F32
            )

        attended = lax.cond(usable[back], accumulate, keep_same, attended)
    return attended, (pairs, usable, log_total)


def far_attend_back(queries, attended_grad, kept):
    tokens, heads_here, head_size = queries.shape
    factor = 1.0 / math.sqrt(head_size)
    pairs, usable, log_total = kept
    reach = len(pairs)

    def weights_of(block, diagonal):
        return jnp.exp(block_logits(queries, block, diagonal) - log_total[..., None])

    def prob_grads(block):
        return jnp.einsum("qhd,khd->hqk", attended_grad, block[1], preferred_element_type=F32)

    delta = jnp.zeros((heads_here, tokens), F32)
    for back in range(reach):

        def gather_delta(current, block=pairs[back], diagonal=back == 0):
            return current + jnp.sum(weights_of(block[0], diagonal) * prob_grads(block), axis=-1)

        delta = lax.cond(usable[back], gather_delta, keep_same, delta)

    def skip_block(current):
        return (current, jnp.zeros((2, tokens, heads_here, head_size), F32))

    query_grad = jnp.zeros((tokens, heads_here, head_size), F32)
    key_value_grad = jnp.zeros((2, tokens, heads_here, head_size), F32)
    for back in range(reach):

        def spread(current, block=pairs[back], diagonal=back == 0):
            probs = weights_of(block[0], diagonal)
            score_grad = (probs * (prob_grads(block) - delta[..., None])).astype(BF)
            query_part = (
                current
                + jnp.einsum("hqk,khd->qhd", score_grad, block[0], preferred_element_type=F32)
                * factor
            )
            key_part = (
                jnp.einsum("hqk,qhd->khd", score_grad, queries, preferred_element_type=F32)
                * factor
            )
            value_part = jnp.einsum(
                "hqk,qhd->khd", probs.astype(BF), attended_grad, preferred_element_type=F32
            )
            return (query_part, jnp.stack([key_part, value_part]))

        query_grad, pair_grad = lax.cond(usable[back], spread, skip_block, query_grad)
        if back == 0:
            key_value_grad = pair_grad
        else:
            key_value_grad = key_value_grad + passed_along(pair_grad, "dp", -back)
    return jnp.concatenate([query_grad[None], key_value_grad])


def merge_branches(attended, hidden, w_merge, w_down, stream, flag):
    tokens, inner = attended.shape
    shards, units, cols = w_down.shape
    if cols % 128:
        merged = jnp.einsum("te,ned->tnd", attended, w_merge, preferred_element_type=F32)
        merged = merged + jnp.einsum("tf,nfd->tnd", hidden, w_down, preferred_element_type=F32)
        return merged.reshape(tokens, -1) + flag * stream

    def kernel(a, h, wm, wd, st, flag_ref, out):
        out[...] = dot(a[...], wm[0]) + dot(h[...], wd[0]) + flag_ref[0] * st[...]

    return pl.pallas_call(
        kernel,
        grid=(shards,),
        in_specs=[
            pl.BlockSpec((tokens, inner), lambda n: (0, 0)),
            pl.BlockSpec((tokens, units), lambda n: (0, 0)),
            pl.BlockSpec((1, inner, cols), lambda n: (n, 0, 0)),
            pl.BlockSpec((1, units, cols), lambda n: (n, 0, 0)),
            pl.BlockSpec((tokens, cols), lambda n: (0, n)),
            pl.BlockSpec(memory_space=pltpu.SMEM),
        ],
        out_specs=pl.BlockSpec((tokens, cols), lambda n: (0, n)),
        out_shape=jax.ShapeDtypeStruct((tokens, shards * cols), F32),
        name="merge_branches",
    )(attended, hidden, w_merge, w_down, stream, flag)


def back_through(grad, stacked, slope):
    tokens = grad.shape[0]
    shards, units, cols = stacked.shape
    if cols % 128:
        split = grad.reshape(tokens, shards, cols)
        total = jnp.einsum("tnd,nfd->tf", split, stacked, preferred_element_type=F32)
        return (total if slope is None else total * slope.astype(F32)).astype(BF)

    def kernel(*refs):
        g, w = refs[:2]
        out, acc = refs[-2:]
        n = pl.program_id(0)
        part = dot_cols(g[...], w[0])

        @pl.when(n == 0)
        def _():
            acc[...] = part

        @pl.when(n > 0)
        def _():
            acc[...] += part

        @pl.when(n == shards - 1)
        def _():
            total = acc[...]
            if slope is not None:
                total = total * refs[2][...].astype(F32)
            out[...] = total.astype(BF)

    specs = [
        pl.BlockSpec((tokens, cols), lambda n: (0, n)),
        pl.BlockSpec((1, units, cols), lambda n: (n, 0, 0)),
    ]
    args = [grad, stacked]
    if slope is not None:
        specs.append(pl.BlockSpec((tokens, units), lambda n: (0, 0)))
        args.append(slope)
    return pl.pallas_call(
        kernel,
        grid=(shards,),
        in_specs=specs,
        out_specs=pl.BlockSpec((tokens, units), lambda n: (0, 0)),
        out_shape=jax.ShapeDtypeStruct((tokens, units), BF),
        scratch_shapes=[pltpu.VMEM((tokens, units), F32)],
        name="back_through",
    )(*args)


def body(
    history,
    mixing,
    shard_offset,
    norm_gain,
    norm_bias,
    w_heads,
    w_merge,
    w_up,
    w_down,
    mixer_first,
    mixer_second,
    out_cotangent,
    next_cotangent,
):
    member = lax.axis_index("stream")
    members = lax.axis_size("stream")
    shards = lax.axis_size("dp")
    index = lax.axis_index("dp")
    entries, tokens, width = history.shape
    heads_here = w_heads.shape[2] // HD
    half = tokens // 2
    highest = lax.Precision.HIGHEST
    flag = (member == members - 1).astype(F32)
    flags = flag.reshape(1)
    near = shards == 8 and heads_here * 2 == shards and tokens * shards == 2 * SEQ

    mix_all = lax.all_gather(mixing[:, 0, :], "stream", axis=0)
    norms = lax.all_gather(jnp.concatenate([norm_gain, norm_bias]), "stream", axis=0)
    gains, biases = norms[:, 0].astype(F32), norms[:, 1].astype(F32)
    mix_rows = jnp.transpose(mix_all, (1, 0, 2)).reshape(tokens, members * entries)
    spread = jnp.broadcast_to(shard_offset[:, None], (8, 128))
    offsets = lax.all_gather(spread, "dp", axis=0)[:, 0, 0]
    first_full = lax.all_gather(mixer_first, "stream", axis=0, tiled=True)
    second_full = lax.all_gather(mixer_second[:, 0, :], "stream", axis=0).astype(F32)
    next_full = lax.all_gather(next_cotangent[:, 0, :], "stream", axis=0)
    cotangent = lax.all_gather(out_cotangent, "stream", axis=1, tiled=True)
    full_heads, full_up, full_merge, full_down = gather_weights([w_heads, w_up, w_merge, w_down])
    flat_up = full_up.reshape(width, -1)

    normed, unit, inv, stream = make_streams(history, mix_rows, gains, biases)
    positions = shard_offset[0] + jnp.arange(tokens, dtype=jnp.int32)
    projected = project(normed, full_heads, rope_tables(positions, 1.0))
    if near:
        side = (index % 2).astype(jnp.int32).reshape(1)
        place = jnp.arange(shards, dtype=jnp.int32)
        first_key = jnp.maximum(place - offsets // tokens, 0).astype(jnp.int32)
        own = lax.all_to_all(projected, "dp", 0, 0, tiled=True)
        other = partner(own[:, 1:], 1)
        result, exact, level = attend(own, other, first_key, side)
        back = lax.all_to_all(result, "dp", 0, 0, tiled=True)
        attended = jnp.transpose(back.reshape(heads_here, tokens, HD), (1, 0, 2)).reshape(tokens, -1)
    else:
        split = projected.reshape(heads_here, 2, 3, half, HD)
        split = jnp.transpose(split, (2, 1, 3, 0, 4)).reshape(3, tokens, heads_here, HD)
        result, kept = far_attend(split[0], split[1], split[2], shard_offset)
        attended = result.reshape(tokens, -1).astype(BF)

    up = dot(normed[members - 1], flat_up)
    hidden, gelu_back = jax.vjp(exact_gelu, up)
    hidden = hidden.astype(BF)
    slope = gelu_back(jnp.ones_like(up))[0].astype(BF)
    share = merge_branches(attended, hidden, full_merge, full_down, stream, flags)

    inner = (member == 1) | (member == 2)
    pieces = []
    count = 4
    for i in range(count):
        part = lax.slice_in_dim(share, i * tokens // count, (i + 1) * tokens // count)
        one = line_hop(part.astype(BF), OUTWARD)
        nearer = part + one.astype(F32)
        two = line_hop(nearer.astype(BF), MIDDLE)
        total = (nearer + two.astype(F32)).astype(BF)
        pieces.append(jnp.where(inner, total, line_hop(total, INWARD)))
    block_full = jnp.concatenate(pieces)

    mine = member * (width // members)
    block_out = lax.dynamic_slice_in_dim(block_full, mine, width // members, axis=1)
    out_float = block_full.astype(F32)
    scale = lax.rsqrt(jnp.sum(out_float * out_float, axis=-1) / width + 1e-06)
    proj = dot(block_full, first_full)
    mixer, mixer_back = jax.vjp(exact_gelu, scale[:, None] * proj)
    second_here = mixer_second[:, 0, :].astype(F32)
    next_here = jnp.dot(mixer, second_here, precision=highest, preferred_element_type=F32)
    mixer_grad = jnp.einsum(
        "stn,scn->tc", next_full, second_full, precision=highest, preferred_element_type=F32
    )
    pre_grad = mixer_back(mixer_grad)[0]
    proj_grad = (scale[:, None] * pre_grad).astype(BF)
    scale_grad = jnp.sum(pre_grad * proj, axis=-1)
    second_local = jnp.dot(
        mixer.T, next_cotangent[:, 0, :], precision=highest, preferred_element_type=F32
    )
    first_local = dot_rows(block_out, proj_grad)
    grad_out = (
        cotangent.astype(F32)
        + dot_cols(proj_grad, first_full)
        - (scale * scale * scale * scale_grad)[:, None] * out_float / width
    ).astype(BF)

    attended_grad = back_through(grad_out, full_merge, None)
    if near:
        sent = attended_grad.reshape(tokens, heads_here, HD)
        sent = jnp.transpose(sent, (1, 0, 2)).reshape(shards, half, HD)
        grads = lax.all_to_all(sent, "dp", 0, 0, tiled=True)
        kept_grads, given = attend_back(own, other, grads, exact, level, first_key, side)
        taken = partner(given, 1)
        summed = kept_grads[:, 1:].astype(F32) + taken.astype(F32)
        packed = jnp.concatenate([kept_grads[:, :1], summed.astype(BF)], axis=1)
        parts = lax.all_to_all(packed, "dp", 0, 0, tiled=True)
    else:
        grads = far_attend_back(split[0], attended_grad.reshape(tokens, heads_here, HD), kept)
        parts = grads.reshape(3, 2, half, heads_here, HD)
        parts = jnp.transpose(parts, (3, 1, 0, 2, 4)).reshape(2 * heads_here, 3, half, HD)

    up_grad = back_through(grad_out, full_down, slope)
    down_grad = dot_rows(hidden, grad_out).astype(BF)
    merge_grad = dot_rows(attended, grad_out).astype(BF)
    last_normed = dot_cols(up_grad, flat_up)
    last_share, last_stats = last_back(
        last_normed, unit[members - 1], inv, gains[members - 1 :], grad_out, flags
    )
    up_back = dot_rows(normed[members - 1], up_grad).astype(BF)
    heads_share, heads_grad, heads_stats = heads_back(
        parts, full_heads, normed, unit, inv, gains, rope_tables(positions, -1.0)
    )

    grad_down = lax.psum_scatter(down_grad, "dp", scatter_dimension=1, tiled=True).astype(F32)
    grad_merge = lax.psum_scatter(merge_grad, "dp", scatter_dimension=1, tiled=True).astype(F32)
    grad_up = lax.psum_scatter(up_back, "dp", scatter_dimension=0, tiled=True).astype(F32)
    grad_heads = lax.psum_scatter(heads_grad, "dp", scatter_dimension=1, tiled=True).astype(F32)

    shares = [last_share] + [heads_share[c] for c in range(members - 1)]
    order = [members - 1] + list(range(members - 1))
    ones, twos = [], []
    for item in shares:
        one = line_hop(item, OUTWARD)
        ones.append(one)
        twos.append(line_hop((item.astype(F32) + one.astype(F32)).astype(BF), MIDDLE))
    each = entries // members
    target = jnp.where(member == 1, 0, members - 1)

    def weights_for(owner):
        block = lax.dynamic_slice_in_dim(mix_all, owner * each, each, axis=2)
        return [[block[s, :, e : e + 1] for s in order] for e in range(each)]

    def weighted(weights, values):
        sums = []
        for e in range(each):
            total = weights[e][0] * values[0]
            for weight, value in zip(weights[e][1:], values[1:]):
                total = total + weight * value
            sums.append(total)
        return jnp.stack(sums)

    there, here = weights_for(target), weights_for(member)
    history_parts = []
    for i in range(count):
        low, high = i * tokens // count, (i + 1) * tokens // count
        cut = lambda array: lax.slice_in_dim(array, low, high).astype(F32)
        rows = lambda weights: [[w[low:high] for w in line] for line in weights]
        inward = [cut(item) + cut(two) for item, two in zip(shares, twos)]
        three = line_hop(weighted(rows(there), inward).astype(BF), INWARD)
        sums = [value + cut(one) for value, one in zip(inward, ones)]
        history_parts.append(weighted(rows(here), sums) + three.astype(F32))
    grad_history = jnp.concatenate(history_parts, axis=1)

    mix_parts = mixing_back(heads_share, last_share, history)
    mix_parts = lax.all_to_all(mix_parts, "stream", 0, 0, tiled=True)
    grad_mixing = jnp.sum(mix_parts, axis=0)[:, None, :]

    stats = jnp.concatenate([heads_stats, last_stats[None]])
    stats = jnp.sum(lax.all_to_all(stats, "stream", 0, 0, tiled=True), axis=0)
    stats = jnp.sum(lax.all_gather(stats, "dp", axis=0), axis=0)
    grad_first = jnp.sum(lax.all_gather(first_local, "dp", axis=0), axis=0)
    grad_second = jnp.sum(lax.all_gather(second_local, "dp", axis=0), axis=0)
    return (
        block_out,
        next_here[:, None, :],
        grad_history,
        grad_mixing,
        stats[:1],
        stats[1:],
        grad_heads,
        grad_merge,
        grad_up,
        grad_down,
        grad_first,
        grad_second[:, None, :],
    )


def solution(mesh):
    in_specs = (
        P(None, "dp", None),
        P("dp", "stream", None),
        P("dp"),
        P("stream", None),
        P("stream", None),
        P(None, "dp", "stream"),
        P("stream", "dp"),
        P("dp", "stream"),
        P("stream", "dp"),
        P("stream", None),
        P(None, "stream", None),
        P("dp", "stream"),
        P("dp", "stream", None),
    )
    out_specs = (
        P("dp", "stream"),
        P("dp", "stream", None),
        P("stream", "dp", None),
        P("dp", "stream", None),
        P("stream", None),
        P("stream", None),
        P(None, "dp", "stream"),
        P("stream", "dp"),
        P("dp", "stream"),
        P("stream", "dp"),
        P("stream", None),
        P(None, "stream", None),
    )
    return jax.shard_map(body, mesh=mesh, in_specs=in_specs, out_specs=out_specs, check_vma=False)
```

time: 2200 us -> 1100 us (0.50)
  waiting for transfers between devices: 1800 us -> 405 us
  blocking collectives: 35.2 us -> 196 us
  Pallas kernels: 0 us -> 151 us
  matrix products: 134 us -> 53.7 us
  starting transfers between devices: 31.5 us -> 95.2 us
  loops' own time: 28.2 us -> 0 us
    reduce_scatter x7 -> x4, waiting for transfers between devices: 1320 us -> 0.01 us  [the longest x1 0.01 us: body(): lax.psum_scatter(merge_grad, 'dp', scatter_dimension=1, tiled=True)]
    all_gather x6 -> x1, waiting for transfers between devices: 241 us -> 0.02 us  [body(): cotangent = lax.all_gather(out_cotangent, 'stream', axis=1, tiled=True)]
    all_gather x0 -> x8, blocking collectives: none -> 164 us  [the longest x1 62 us: body(): next_full = lax.all_gather(next_cotangent[:, 0, :], 'stream', axis=0)]
    pallas_call x0 -> x10, Pallas kernels: none -> 151 us  [the longest x1 22.9 us: attend_back(): pl.pallas_call(kernel, grid_spec=pltpu.PrefetchScalarGridSpec(num_scalar_...]
    all_to_all x0 -> x5, waiting for transfers between devices: none -> 109 us  [the longest x1 98.2 us: body(): stats = jnp.sum(lax.all_to_all(stats, 'stream', 0, 0, tiled=True), axis=0)]
    ppermute x14 -> x62, waiting for transfers between devices: 213 us -> 296 us  [the longest x24 236 us: line_hop(): return lax.ppermute(shard, 'stream', pairs)]
    dot_general x33 -> x11, matrix products: 134 us -> 53.7 us  [the longest x4 20.4 us: dot_rows(): lax.dot_general(left, right, (((0,), (0,)), ((), ())), preferred_element_...]
    ppermute x14 -> x62, starting transfers between devices: 30.3 us -> 70.9 us  [the longest x24 39.9 us: line_hop(): return lax.ppermute(shard, 'stream', pairs)]
  transfers between devices with their start and end apart: 29 -> 72, of which waited for: 18 -> 28; matrix products, arithmetic and copies ran while one was open for 10% -> 19% of each run, Pallas kernels for 0% -> 12%
where the time goes in v1:
time: 1100 us; the launch traced here: 1090 us
  waiting for transfers between devices  405 us (37%)
  blocking collectives  196 us (18%)
  Pallas kernels  151 us (14%)
  starting transfers between devices  95.2 us (9%)
  other arithmetic  91.1 us (8%)
  local copies, waits for them, and re-layouts  80.4 us (7%)
  matrix products  53.7 us (5%)
  between operations  16.8 us (2%)
    ppermute x24, waiting for transfers between devices, line_hop(): return lax.ppermute(shard, 'stream', pairs)  236 us
    all_to_all x1, waiting for transfers between devices, body(): stats = jnp.sum(lax.all_to_all(stats, 'stream', 0, 0, tiled=True), axis=0)  98.2 us
    all_gather x1, blocking collectives, body(): next_full = lax.all_gather(next_cotangent[:, 0, :], 'stream', axis=0)  62 us
    ppermute x38, waiting for transfers between devices, partner(): return lax.ppermute(shard, 'dp', [(i, i ^ bit) for i in range(peers)])  59.7 us
    another operation x20, other arithmetic, weighted(): return jnp.stack(sums)  52.3 us
    ppermute x24, starting transfers between devices, line_hop(): return lax.ppermute(shard, 'stream', pairs)  39.9 us
    dynamic_update_slice x40, local copies, waits for them, and re-layouts, gather_weights(): whole = lax.dynamic_update_slice(whole, piece[None], place)  37.1 us
    all_gather x1, blocking collectives, body(): first_full = lax.all_gather(mixer_first, 'stream', axis=0, tiled=True)  33.2 us
  transfers between devices with their start and end apart: 72, of which 28 were waited for; matrix products, arithmetic and copies ran while one was open for 19% of the time, Pallas kernels for 12%

profile of v1, /device:TPU:0, one launch (start us, length us, event | category | flops | bytes accessed | tf_op | source)
XLA Modules:
  0.0 1088.0 jit_solution(265611792182814151)
XLA Ops:
  12.5 13.4 %all-gather.8 = bf16[4,2,2048]{2,1,0:T(2,128)(2,1)S(1)} all-gather(bf16[1,2,2048]{2,1,0:T(2,128)(2,1)S(1)} %maximum_bitcast_fusion), channel_id=5, replica_groups=mesh['dp'=8,'stream'=4] {'stream'}, dimensions={0}, use_global_device_ids=true | all-gather | bytes 40960 | tf_op jit(solution)/shard_map/all_gather | solution.py:730
  26.6 13.4 %all-gather.1 = f32[2048,1,8]{0,2,1:T(8,128)S(1)} all-gather(f32[512,1,8]{0,2,1:T(8,128)} %param.14), channel_id=4, replica_groups=mesh['dp'=8,'stream'=4] {'stream'}, dimensions={0}, use_global_device_ids=true | all-gather | bytes 81920 | tf_op jit(solution)/shard_map/all_gather | solution.py:729
  44.1 6.4 all-reduce
  50.5 22.6 %make_streams.1 = (bf16[4,512,2048]{2,1,0:T(8,128)(2,1)}, bf16[4,512,2048]{2,1,0:T(8,128)(2,1)}, f32[512,4]{1,0:T(8,128)}, f32[512,2048]{1,0:T(8,128)}) custom-call(bf16[8,512,2048]{2,1,0:T(8,128)(2,1)} %hist.3, f32[512,32]{1,0:T(8,128)} %copy.36.mix, f32[4,2048]{1,0:T(4,128)} %bitcast.474, f32[4,2048]{1,0:T(4,128)} %fusion.48.bias), custom_call_target="tpu_custom_call" | custom-call | tf_op jit(solution)/shard_map/make_streams/pallas_call | solution.py:184
  88.3 23.7 %collective-permute-done.2 = bf16[3,128,512]{2,1,0:T(8,128)(2,1)S(1)} collective-permute-done((bf16[3,128,512]{2,1,0:T(8,128)(2,1)S(1)}, bf16[3,128,512]{2,1,0:T(8,128)(2,1)S(1)}, u32[]{:S(2)}, u32[]{:S(2)}) %collective-permute-start.2) | collective-permute-done | bytes 393248 | tf_op jit(solution)/shard_map/ppermute | solution.py:76
  120.0 8.9 project.1
  128.9 3.8 all-to-all-start
  132.7 6.4 collective-permute-done.11
  139.1 5.6 collective-permute-start.19
  152.8 6.1 collective-permute-done.19
  165.5 6.9 collective-permute-done.21
  173.9 3.6 collective-permute-done.22
  191.4 16.9 %add_convert_fusion.4 = (bf16[512,2048]{1,0:T(8,128)(2,1)}, f32[512,2048]{1,0:T(8,128)S(1)}, f32[512,2048]{1,0:T(8,128)S(1)}) fusion(bf16[2048,2048]{1,0:T(8,128)(2,1)S(1)} %bitcast.463, bf16[4,512,2048]{2,1,0:T(8,128)(2,1)} %get-tuple-element.29.x), kind=kOutput, calls=%fused_computation.15 | convolution fusion | flops 4367319040 | bytes 20971520 | tf_op jit(solution)/shard_map/dot_general | solution.py:63
  219.7 6.7 collective-permute-done.30
  234.0 17.4 %attend.1 = (bf16[8,256,128]{2,1,0:T(8,128)(2,1)}, f32[8,256,128]{2,1,0:T(8,128)}, f32[8,256,1]{2,1,0:T(8,128)}) custom-call(s32[8]{0:T(128)} %subtract_maximum_fusion.first, s32[1]{0:T(128)} %bitcast.1.part, bf16[8,3,256,128]{3,2,1,0:T(8,128)(2,1)} %copy-done.4, bf16[8,2,256,128]{3,2,1,0:T(8,128)(2,1)} %copy-done.9), custom_call_target="tpu_custom_call" | custom-call | tf_op jit(solution)/shard_map/attend/pallas_call | solution.py:291
  251.4 5.9 all-to-all-start.1
  263.4 3.6 all-to-all-done.1
  268.2 13.1 %merge_branches.1 = f32[512,2048]{1,0:T(8,128)} custom-call(bf16[512,512]{1,0:T(8,128)(2,1)} %bitcast.467, bf16[512,2048]{1,0:T(8,128)(2,1)} %multiply_convert_fusion.h, bf16[8,512,256]{2,1,0:T(8,128)(2,1)} %copy-done.6, bf16[8,2048,256]{2,1,0:T(8,128)(2,1)} %bitcast_dynamic-update-slice_fusion.18.wd.refs_1_, f32[512,2048]{1,0:T(8,128)} %get-tuple-element.34.st, ...), custom_call_target="tpu_custom_call" | custom-call | tf_op jit(solution)/shard_map/merge_branches/pallas_call | solution.py:637
  291.4 8.3 collective-permute-done.37
  299.6 11.2 %collective-permute-done.40 = bf16[128,2048]{1,0:T(8,128)(2,1)S(1)} collective-permute-done((bf16[128,2048]{1,0:T(8,128)(2,1)S(1)}, bf16[128,2048]{1,0:T(8,128)(2,1)S(1)}, u32[]{:S(2)}, u32[]{:S(2)}) %collective-permute-start.40) | collective-permute-done | bytes 524320 | tf_op jit(solution)/shard_map/ppermute | solution.py:80
  310.9 11.2 %collective-permute-done.43 = bf16[128,2048]{1,0:T(8,128)(2,1)S(1)} collective-permute-done((bf16[128,2048]{1,0:T(8,128)(2,1)S(1)}, bf16[128,2048]{1,0:T(8,128)(2,1)S(1)}, u32[]{:S(2)}, u32[]{:S(2)}) %collective-permute-start.43) | collective-permute-done | bytes 524320 | tf_op jit(solution)/shard_map/ppermute | solution.py:80
  322.1 8.4 collective-permute-done.46
  336.7 62.0 %all-gather.3 = f32[2048,1,9]{0,1,2:T(1,128)S(1)} all-gather(f32[512,1,9]{0,1,2:T(1,128)S(1)} %copy-done.18), channel_id=6, replica_groups=mesh['dp'=8,'stream'=4] {'stream'}, dimensions={0}, use_global_device_ids=true | all-gather | bytes 92160 | tf_op jit(solution)/shard_map/all_gather | solution.py:737
  399.7 14.1 %all-gather.4 = bf16[144,1,9]{2,1,0:T(2,128)(2,1)S(1)} all-gather(bf16[36,1,9]{2,1,0:T(2,128)(2,1)S(1)} %copy.38), channel_id=7, replica_groups=mesh['dp'=8,'stream'=4] {'stream'}, dimensions={0}, use_global_device_ids=true | all-gather | bytes 3240 | tf_op jit(solution)/shard_map/all_gather | solution.py:736
  415.3 33.2 %all_gather.46 = bf16[2048,36]{0,1:T(8,128)(2,1)S(1)} all-gather(bf16[512,36]{0,1:T(8,128)(2,1)S(1)} %copy-done.23), channel_id=1, replica_groups=mesh['dp'=8,'stream'=4] {'stream'}, dimensions={0}, use_global_device_ids=true | all-gather | bytes 184320 | tf_op jit(solution)/shard_map/all_gather | solution.py:735
  451.2 13.9 %collective-permute-done.45 = bf16[128,2048]{1,0:T(8,128)(2,1)S(1)} collective-permute-done((bf16[128,2048]{1,0:T(8,128)(2,1)S(1)}, bf16[128,2048]{1,0:T(8,128)(2,1)S(1)}, u32[]{:S(2)}, u32[]{:S(2)}) %collective-permute-start.45) | collective-permute-done | bytes 524320 | tf_op jit(solution)/shard_map/ppermute | solution.py:80
  465.2 7.0 collective-permute-done.48
  474.3 4.2 fusion.3.refs_0_.e
  478.5 7.4 back_through.3
  487.8 4.2 all-to-all-start.2
  494.7 7.0 all-to-all-done.2.grad_ref
  502.5 22.9 %attend_back.1 = (bf16[8,3,256,128]{3,2,1,0:T(8,128)(2,1)}, bf16[8,2,256,128]{3,2,1,0:T(8,128)(2,1)}) custom-call(s32[8]{0:T(128)} %subtract_maximum_fusion.first, s32[1]{0:T(128)} %bitcast.1.part, bf16[8,3,256,128]{3,2,1,0:T(8,128)(2,1)} %copy-done.4, bf16[8,2,256,128]{3,2,1,0:T(8,128)(2,1)} %copy-done.9, bf16[8,256,128]{2,1,0:T(8,128)(2,1)} %copy-done.13, ...), custom_call_target="tpu_custom_call" | custom-call | tf_op jit(solution)/shard_map/attend_back/pallas_call | solution.py:364
  531.3 25.2 %all_to_all.30.part = bf16[8,3,256,128]{3,2,1,0:T(8,128)(2,1)} all-to-all(bf16[8,3,256,128]{3,2,1,0:T(8,128)(2,1)S(1)} %pad_maximum_fusion.2), channel_id=1, replica_groups=mesh['dp'=8,'stream'=4] {'dp'}, dimensions={0} | all-to-all | bytes 3145728 | tf_op jit(solution)/shard_map/all_to_all | solution.py:811
  556.5 20.2 %heads_back.1 = (bf16[3,512,2048]{2,1,0:T(8,128)(2,1)}, bf16[3,2048,512]{2,1,0:T(8,128)(2,1)}, f32[3,2,2048]{2,1,0:T(2,128)}) custom-call(bf16[8,3,256,128]{3,2,1,0:T(8,128)(2,1)} %all_to_all.30.part, bf16[8,3,256,512]{3,2,1,0:T(8,128)(2,1)} %bitcast_dynamic-update-slice_fusion.26.w, bf16[4,512,2048]{2,1,0:T(8,128)(2,1)} %get-tuple-element.29.x, ...), custom_call_target="tpu_custom_call" | custom-call | tf_op jit(solution)/shard_map/heads_back/pallas_call | solution.py:436
  576.9 8.5 convolution_convert_fusion
  586.7 3.5 slice_bitcast_fusion.3.u
  590.1 13.7 %back_through.2 = bf16[512,2048]{1,0:T(8,128)(2,1)} custom-call(bf16[512,2048]{1,0:T(8,128)(2,1)} %fusion.3.refs_0_.e, bf16[8,2048,256]{2,1,0:T(8,128)(2,1)} %bitcast_dynamic-update-slice_fusion.18.wd.refs_1_, bf16[512,2048]{1,0:T(8,128)(2,1)} %get-tuple-element.82.refs_2_), custom_call_target="tpu_custom_call" | custom-call | tf_op jit(solution)/shard_map/back_through/pallas_call | solution.py:691
  603.8 10.7 fusion.90.g
  614.5 6.5 last_back.1
  623.7 6.4 slice_bitcast_fusion.2
  639.4 8.5 all-gather.10
  650.6 10.3 all-gather.6
  661.3 7.4 collective-permute-done.49
  668.7 3.7 add_convert_fusion.3
  674.5 39.1 %collective-permute-done.52 = bf16[512,2048]{1,0:T(8,128)(2,1)} collective-permute-done((bf16[512,2048]{1,0:T(8,128)(2,1)}, bf16[512,2048]{1,0:T(8,128)(2,1)}, u32[]{:S(2)}, u32[]{:S(2)}) %collective-permute-start.52) | collective-permute-done | bytes 2097184 | tf_op jit(solution)/shard_map/ppermute | solution.py:80
  713.6 44.9 %collective-permute-done.54 = bf16[512,2048]{1,0:T(8,128)(2,1)} collective-permute-done((bf16[512,2048]{1,0:T(8,128)(2,1)}, bf16[512,2048]{1,0:T(8,128)(2,1)}, u32[]{:S(2)}, u32[]{:S(2)}) %collective-permute-start.54) | collective-permute-done | bytes 2097184 | tf_op jit(solution)/shard_map/ppermute | solution.py:80
  758.5 43.7 %collective-permute-done.56 = bf16[512,2048]{1,0:T(8,128)(2,1)} collective-permute-done((bf16[512,2048]{1,0:T(8,128)(2,1)}, bf16[512,2048]{1,0:T(8,128)(2,1)}, u32[]{:S(2)}, u32[]{:S(2)}) %collective-permute-start.56) | collective-permute-done | bytes 2097184 | tf_op jit(solution)/shard_map/ppermute | solution.py:80
  802.3 7.6 add_convert_fusion.2
  816.0 8.4 convolution_convert_fusion.1
  825.1 7.0 all-to-all-start.5
  833.0 18.1 %mixing_back.1 = f32[4,512,8]{2,1,0:T(8,128)} custom-call(bf16[3,512,2048]{2,1,0:T(8,128)(2,1)} %get-tuple-element.42.first, bf16[512,2048]{1,0:T(8,128)(2,1)} %get-tuple-element.37.last, bf16[8,512,2048]{2,1,0:T(8,128)(2,1)} %hist.3), custom_call_target="tpu_custom_call" | custom-call | tf_op jit(solution)/shard_map/mixing_back/pallas_call | solution.py:524
  853.4 98.2 %all-to-all-done.5 = f32[4,2,2048]{2,1,0:T(2,128)S(1)} async-done(((f32[4,2,2048]{2,1,0:T(2,128)}), f32[4,2,2048]{2,1,0:T(2,128)S(1)}, u32[]{:S(2)}, u32[]{:S(2)}) %all-to-all-start.5) | async-done | bytes 65568 | tf_op jit(solution)/shard_map/all_to_all | solution.py:874
  955.7 9.2 all-gather.9
  993.9 4.1 add_bitcast_fusion.7
  998.1 4.1 add_bitcast_fusion.6
  1002.3 4.1 add_bitcast_fusion.5
  1006.5 4.1 add_bitcast_fusion.4
  1010.7 4.1 add_bitcast_fusion.3
  1014.9 4.1 add_bitcast_fusion.2
  1019.1 4.1 add_bitcast_fusion.1
  1023.3 4.1 add_bitcast_fusion
  1028.0 19.3 %collective-permute-done.60 = bf16[2,128,2048]{2,1,0:T(8,128)(2,1)S(1)} collective-permute-done((bf16[2,128,2048]{2,1,0:T(8,128)(2,1)S(1)}, bf16[2,128,2048]{2,1,0:T(8,128)(2,1)S(1)}, u32[]{:S(2)}, u32[]{:S(2)}) %collective-permute-start.60) | collective-permute-done | bytes 1048608 | tf_op jit(solution)/shard_map/ppermute | solution.py:80
  1047.5 21.6 %collective-permute-done.61 = bf16[2,128,2048]{2,1,0:T(8,128)(2,1)S(1)} collective-permute-done((bf16[2,128,2048]{2,1,0:T(8,128)(2,1)S(1)}, bf16[2,128,2048]{2,1,0:T(8,128)(2,1)S(1)}, u32[]{:S(2)}, u32[]{:S(2)}) %collective-permute-start.61) | collective-permute-done | bytes 1048608 | tf_op jit(solution)/shard_map/ppermute | solution.py:80
  1069.4 3.9 pad_maximum_fusion
  (451 shorter events, 193.7 us)
Async XLA Ops:
  7.2 73.0 %collective-permute-start = (bf16[3,256,512]{2,1,0:T(8,128)(2,1)}, bf16[3,256,512]{2,1,0:T(8,128)(2,1)S(1)}, u32[]{:S(2)}, u32[]{:S(2)}) collective-permute-start(bf16[3,256,512]{2,1,0:T(8,128)(2,1)} %param.18), channel_id=1, source_target_pairs={{0,8},{4,12},{8,0},{12,4},{16,24},{20,28},{24,16},{28,20},{1,9},{5... | collective-permute-start | bytes 2359304 | tf_op jit(solution)/shard_map/ppermute | solution.py:76
  10.2 70.0 %collective-permute-start.1 = (bf16[3,256,512]{2,1,0:T(8,128)(2,1)}, bf16[3,256,512]{2,1,0:T(8,128)(2,1)S(1)}, u32[]{:S(2)}, u32[]{:S(2)}) collective-permute-start(bf16[3,256,512]{2,1,0:T(8,128)(2,1)} %param.18), channel_id=1, source_target_pairs={{0,16},{4,20},{8,24},{12,28},{16,0},{20,4},{24,8},{28,12},{1,17},{... | collective-permute-start | bytes 2359304 | tf_op jit(solution)/shard_map/ppermute | solution.py:76
  11.7 103.2 %collective-permute-start.4 = (bf16[3,256,512]{2,1,0:T(8,128)(2,1)}, bf16[3,256,512]{2,1,0:T(8,128)(2,1)S(1)}, u32[]{:S(2)}, u32[]{:S(2)}) collective-permute-start(bf16[3,256,512]{2,1,0:T(8,128)(2,1)} %param.18), channel_id=1, source_target_pairs={{0,4},{4,0},{8,12},{12,8},{16,20},{20,16},{24,28},{28,24},{1,5},{5... | collective-permute-start | bytes 2359304 | tf_op jit(solution)/shard_map/ppermute | solution.py:76
  80.2 52.5 %collective-permute-start.10 = (bf16[256,2048]{1,0:T(8,128)(2,1)}, bf16[256,2048]{1,0:T(8,128)(2,1)S(1)}, u32[]{:S(2)}, u32[]{:S(2)}) collective-permute-start(bf16[256,2048]{1,0:T(8,128)(2,1)} %param.20), channel_id=1, source_target_pairs={{0,8},{4,12},{8,0},{12,4},{16,24},{20,28},{24,16},{28,20},{1,9},{5... | collective-permute-start | bytes 3145736 | tf_op jit(solution)/shard_map/ppermute | solution.py:76
  83.8 28.1 %collective-permute-start.2 = (bf16[3,128,512]{2,1,0:T(8,128)(2,1)S(1)}, bf16[3,128,512]{2,1,0:T(8,128)(2,1)S(1)}, u32[]{:S(2)}, u32[]{:S(2)}) collective-permute-start(bf16[3,128,512]{2,1,0:T(8,128)(2,1)S(1)} %slice.727), channel_id=1, source_target_pairs={{0,8},{4,12},{8,0},{12,4},{16,24},{20,28},{24,16},{28,20},{1,9},{5... | collective-permute-start | bytes 1179656 | tf_op jit(solution)/shard_map/ppermute | solution.py:76
  84.8 28.0 %collective-permute-start.3 = (bf16[3,128,512]{2,1,0:T(8,128)(2,1)S(1)}, bf16[3,128,512]{2,1,0:T(8,128)(2,1)S(1)}, u32[]{:S(2)}, u32[]{:S(2)}) collective-permute-start(bf16[3,128,512]{2,1,0:T(8,128)(2,1)S(1)} %slice.728), channel_id=1, source_target_pairs={{0,16},{4,20},{8,24},{12,28},{16,0},{20,4},{24,8},{28,12},{1,17},{... | collective-permute-start | bytes 1179656 | tf_op jit(solution)/shard_map/ppermute | solution.py:76
  86.3 29.8 %collective-permute-start.5 = (bf16[3,256,512]{2,1,0:T(8,128)(2,1)S(1)}, bf16[3,256,512]{2,1,0:T(8,128)(2,1)S(1)}, u32[]{:S(2)}, u32[]{:S(2)}) collective-permute-start(bf16[3,256,512]{2,1,0:T(8,128)(2,1)S(1)} %collective-permute-done), channel_id=1, source_target_pairs={{0,4},{4,0},{8,12},{12,8},{16,20},{20,16},{24,28},{28,24},{1,5},{5... | collective-permute-start | bytes 2359304 | tf_op jit(solution)/shard_map/ppermute | solution.py:76
  111.9 5.4 collective-permute-start.6
  112.7 26.4 %collective-permute-start.11 = (bf16[256,2048]{1,0:T(8,128)(2,1)}, bf16[256,2048]{1,0:T(8,128)(2,1)}, u32[]{:S(2)}, u32[]{:S(2)}) collective-permute-start(bf16[256,2048]{1,0:T(8,128)(2,1)} %param.20), channel_id=1, source_target_pairs={{0,16},{4,20},{8,24},{12,28},{16,0},{20,4},{24,8},{28,12},{1,17},{... | collective-permute-start | bytes 3145736 | tf_op jit(solution)/shard_map/ppermute | solution.py:76
  114.9 71.4 %collective-permute-start.14 = (bf16[256,2048]{1,0:T(8,128)(2,1)}, bf16[256,2048]{1,0:T(8,128)(2,1)}, u32[]{:S(2)}, u32[]{:S(2)}) collective-permute-start(bf16[256,2048]{1,0:T(8,128)(2,1)} %param.20), channel_id=1, source_target_pairs={{0,4},{4,0},{8,12},{12,8},{16,20},{20,16},{24,28},{28,24},{1,5},{5... | collective-permute-start | bytes 3145736 | tf_op jit(solution)/shard_map/ppermute | solution.py:76
  116.1 2.4 collective-permute-start.7
  128.9 81.8 %all-to-all-start = ((bf16[8,3,256,128]{3,2,1,0:T(8,128)(2,1)}), bf16[8,3,256,128]{3,2,1,0:T(8,128)(2,1)S(1)}, u32[]{:S(2)}, u32[]{:S(2)}) async-start(bf16[8,3,256,128]{3,2,1,0:T(8,128)(2,1)} %project.1), calls=%async_computation | async-start | bytes 3145728 | tf_op jit(solution)/shard_map/all_to_all | solution.py:749
  139.1 19.8 %collective-permute-start.19 = (bf16[512,256]{1,0:T(8,128)(2,1)S(1)}, bf16[512,256]{1,0:T(8,128)(2,1)S(1)}, u32[]{:S(2)}, u32[]{:S(2)}) collective-permute-start(bf16[512,256]{1,0:T(8,128)(2,1)S(1)} %copy-done.16), channel_id=1, source_target_pairs={{0,8},{4,12},{8,0},{12,4},{16,24},{20,28},{24,16},{28,20},{1,9},{5... | collective-permute-start | bytes 786440 | tf_op jit(solution)/shard_map/ppermute | solution.py:76
  144.7 16.5 %collective-permute-start.20 = (bf16[512,256]{1,0:T(8,128)(2,1)S(1)}, bf16[512,256]{1,0:T(8,128)(2,1)S(1)}, u32[]{:S(2)}, u32[]{:S(2)}) collective-permute-start(bf16[512,256]{1,0:T(8,128)(2,1)S(1)} %copy-done.16), channel_id=1, source_target_pairs={{0,16},{4,20},{8,24},{12,28},{16,0},{20,4},{24,8},{28,12},{1,17},{... | collective-permute-start | bytes 786440 | tf_op jit(solution)/shard_map/ppermute | solution.py:76
  146.5 31.0 %collective-permute-start.23 = (bf16[512,256]{1,0:T(8,128)(2,1)S(1)}, bf16[512,256]{1,0:T(8,128)(2,1)}, u32[]{:S(2)}, u32[]{:S(2)}) collective-permute-start(bf16[512,256]{1,0:T(8,128)(2,1)S(1)} %copy-done.16), channel_id=1, source_target_pairs={{0,4},{4,0},{8,12},{12,8},{16,20},{20,16},{24,28},{28,24},{1,5},{5... | collective-permute-start | bytes 786440 | tf_op jit(solution)/shard_map/ppermute | solution.py:76
  148.4 31.4 %collective-permute-start.12 = (bf16[128,2048]{1,0:T(8,128)(2,1)}, bf16[128,2048]{1,0:T(8,128)(2,1)}, u32[]{:S(2)}, u32[]{:S(2)}) collective-permute-start(bf16[128,2048]{1,0:T(8,128)(2,1)} %slice.730), channel_id=1, source_target_pairs={{0,8},{4,12},{8,0},{12,4},{16,24},{20,28},{24,16},{28,20},{1,9},{5... | collective-permute-start | bytes 1572872 | tf_op jit(solution)/shard_map/ppermute | solution.py:76
  158.9 22.7 %collective-permute-start.13 = (bf16[128,2048]{1,0:T(8,128)(2,1)}, bf16[128,2048]{1,0:T(8,128)(2,1)}, u32[]{:S(2)}, u32[]{:S(2)}) collective-permute-start(bf16[128,2048]{1,0:T(8,128)(2,1)} %slice.731), channel_id=1, source_target_pairs={{0,16},{4,20},{8,24},{12,28},{16,0},{20,4},{24,8},{28,12},{1,17},{... | collective-permute-start | bytes 1572872 | tf_op jit(solution)/shard_map/ppermute | solution.py:76
  161.9 10.5 collective-permute-start.21
  172.4 5.1 collective-permute-start.22
  179.0 9.4 collective-permute-start.15
  179.4 9.3 collective-permute-start.16
  179.8 33.5 %collective-permute-start.28 = (bf16[2048,256]{1,0:T(8,128)(2,1)}, bf16[2048,256]{1,0:T(8,128)(2,1)}, u32[]{:S(2)}, u32[]{:S(2)}) collective-permute-start(bf16[2048,256]{1,0:T(8,128)(2,1)} %param.21), channel_id=1, source_target_pairs={{0,8},{4,12},{8,0},{12,4},{16,24},{20,28},{24,16},{28,20},{1,9},{5... | collective-permute-start | bytes 3145736 | tf_op jit(solution)/shard_map/ppermute | solution.py:76
  184.8 26.2 %collective-permute-start.29 = (bf16[2048,256]{1,0:T(8,128)(2,1)}, bf16[2048,256]{1,0:T(8,128)(2,1)}, u32[]{:S(2)}, u32[]{:S(2)}) collective-permute-start(bf16[2048,256]{1,0:T(8,128)(2,1)} %param.21), channel_id=1, source_target_pairs={{0,16},{4,20},{8,24},{12,28},{16,0},{20,4},{24,8},{28,12},{1,17},{... | collective-permute-start | bytes 3145736 | tf_op jit(solution)/shard_map/ppermute | solution.py:76
  186.3 44.4 %collective-permute-start.32 = (bf16[2048,256]{1,0:T(8,128)(2,1)}, bf16[2048,256]{1,0:T(8,128)(2,1)}, u32[]{:S(2)}, u32[]{:S(2)}) collective-permute-start(bf16[2048,256]{1,0:T(8,128)(2,1)} %param.21), channel_id=1, source_target_pairs={{0,4},{4,0},{8,12},{12,8},{16,20},{20,16},{24,28},{28,24},{1,5},{5... | collective-permute-start | bytes 3145736 | tf_op jit(solution)/shard_map/ppermute | solution.py:76
  188.6 2.7 collective-permute-start.18
  210.8 22.3 %collective-permute-start.9 = (bf16[8,2,256,128]{3,2,1,0:T(8,128)(2,1)S(1)}, bf16[8,2,256,128]{3,2,1,0:T(8,128)(2,1)S(1)}, u32[]{:S(2)}, u32[]{:S(2)}) collective-permute-start(bf16[8,2,256,128]{3,2,1,0:T(8,128)(2,1)S(1)} %slice.729), channel_id=1, source_target_pairs={{0,4},{4,0},{8,12},{12,8},{16,20},{20,16},{24,28},{28,24},{1,5},{5... | collective-permute-start | bytes 3145736 | tf_op jit(solution)/shard_map/ppermute | solution.py:76
  212.3 14.1 %collective-permute-start.30 = (bf16[1024,256]{1,0:T(8,128)(2,1)S(1)}, bf16[1024,256]{1,0:T(8,128)(2,1)}, u32[]{:S(2)}, u32[]{:S(2)}) collective-permute-start(bf16[1024,256]{1,0:T(8,128)(2,1)S(1)} %slice.734), channel_id=1, source_target_pairs={{0,8},{4,12},{8,0},{12,4},{16,24},{20,28},{24,16},{28,20},{1,9},{5... | collective-permute-start | bytes 1572872 | tf_op jit(solution)/shard_map/ppermute | solution.py:76
  214.4 14.0 %collective-permute-start.31 = (bf16[1024,256]{1,0:T(8,128)(2,1)S(1)}, bf16[1024,256]{1,0:T(8,128)(2,1)}, u32[]{:S(2)}, u32[]{:S(2)}) collective-permute-start(bf16[1024,256]{1,0:T(8,128)(2,1)S(1)} %slice.735), channel_id=1, source_target_pairs={{0,16},{4,20},{8,24},{12,28},{16,0},{20,4},{24,8},{28,12},{1,17},{... | collective-permute-start | bytes 1572872 | tf_op jit(solution)/shard_map/ppermute | solution.py:76
  215.2 42.1 %collective-permute-start.33 = (bf16[2048,256]{1,0:T(8,128)(2,1)}, bf16[2048,256]{1,0:T(8,128)(2,1)}, u32[]{:S(2)}, u32[]{:S(2)}) collective-permute-start(bf16[2048,256]{1,0:T(8,128)(2,1)} %collective-permute-done.28), channel_id=1, source_target_pairs={{0,4},{4,0},{8,12},{12,8},{16,20},{20,16},{24,28},{28,24},{1,5},{5... | collective-permute-start | bytes 3145736 | tf_op jit(solution)/shard_map/ppermute | solution.py:76
  226.4 33.2 %collective-permute-start.34 = (bf16[2048,256]{1,0:T(8,128)(2,1)}, bf16[2048,256]{1,0:T(8,128)(2,1)S(1)}, u32[]{:S(2)}, u32[]{:S(2)}) collective-permute-start(bf16[2048,256]{1,0:T(8,128)(2,1)} %collective-permute-done.29), channel_id=1, source_target_pairs={{0,4},{4,0},{8,12},{12,8},{16,20},{20,16},{24,28},{28,24},{1,5},{5... | collective-permute-start | bytes 3145736 | tf_op jit(solution)/shard_map/ppermute | solution.py:76
  228.3 32.3 %collective-permute-start.35 = (bf16[1024,256]{1,0:T(8,128)(2,1)}, bf16[1024,256]{1,0:T(8,128)(2,1)S(1)}, u32[]{:S(2)}, u32[]{:S(2)}) collective-permute-start(bf16[1024,256]{1,0:T(8,128)(2,1)} %collective-permute-done.30), channel_id=1, source_target_pairs={{0,4},{4,0},{8,12},{12,8},{16,20},{20,16},{24,28},{28,24},{1,5},{5... | collective-permute-start | bytes 1572872 | tf_op jit(solution)/shard_map/ppermute | solution.py:76
  230.7 30.8 %collective-permute-start.36 = (bf16[1024,256]{1,0:T(8,128)(2,1)}, bf16[1024,256]{1,0:T(8,128)(2,1)}, u32[]{:S(2)}, u32[]{:S(2)}) collective-permute-start(bf16[1024,256]{1,0:T(8,128)(2,1)} %collective-permute-done.31), channel_id=1, source_target_pairs={{0,4},{4,0},{8,12},{12,8},{16,20},{20,16},{24,28},{28,24},{1,5},{5... | collective-permute-start | bytes 1572872 | tf_op jit(solution)/shard_map/ppermute | solution.py:76
  251.4 15.6 %all-to-all-start.1 = ((bf16[8,256,128]{2,1,0:T(8,128)(2,1)}), bf16[8,256,128]{2,1,0:T(8,128)(2,1)S(1)}, u32[]{:S(2)}, u32[]{:S(2)}) async-start(bf16[8,256,128]{2,1,0:T(8,128)(2,1)} %get-tuple-element.30), calls=%async_computation.1 | async-start | bytes 1048576 | tf_op jit(solution)/shard_map/all_to_all | solution.py:752
  257.2 217.0 %all-gather.13.cloned.1.call-start = ((), (), s32[]{:S(2)}) async-start(), calls=%async_computation.10 | async-start | bytes 2621440 | tf_op jit(solution)/shard_map/all_gather | solution.py:738
  283.9 15.7 %collective-permute-start.37 = (bf16[128,2048]{1,0:T(8,128)(2,1)S(1)}, bf16[128,2048]{1,0:T(8,128)(2,1)S(1)}, u32[]{:S(2)}, u32[]{:S(2)}) collective-permute-start(bf16[128,2048]{1,0:T(8,128)(2,1)S(1)} %get-tuple-element.100), channel_id=1, source_target_pairs={{0,1},{3,2},{4,5},{7,6},{8,9},{11,10},{12,13},{15,14},{16,17},{19,... | collective-permute-start | bytes 1572872 | tf_op jit(solution)/shard_map/ppermute | solution.py:80
  287.4 23.5 %collective-permute-start.40 = (bf16[128,2048]{1,0:T(8,128)(2,1)S(1)}, bf16[128,2048]{1,0:T(8,128)(2,1)S(1)}, u32[]{:S(2)}, u32[]{:S(2)}) collective-permute-start(bf16[128,2048]{1,0:T(8,128)(2,1)S(1)} %get-tuple-element.103), channel_id=1, source_target_pairs={{0,1},{3,2},{4,5},{7,6},{8,9},{11,10},{12,13},{15,14},{16,17},{19,... | collective-permute-start | bytes 1572872 | tf_op jit(solution)/shard_map/ppermute | solution.py:80
  288.7 33.4 %collective-permute-start.43 = (bf16[128,2048]{1,0:T(8,128)(2,1)S(1)}, bf16[128,2048]{1,0:T(8,128)(2,1)S(1)}, u32[]{:S(2)}, u32[]{:S(2)}) collective-permute-start(bf16[128,2048]{1,0:T(8,128)(2,1)S(1)} %get-tuple-element.102), channel_id=1, source_target_pairs={{0,1},{3,2},{4,5},{7,6},{8,9},{11,10},{12,13},{15,14},{16,17},{19,... | collective-permute-start | bytes 1572872 | tf_op jit(solution)/shard_map/ppermute | solution.py:80
  290.0 40.5 %collective-permute-start.46 = (bf16[128,2048]{1,0:T(8,128)(2,1)S(1)}, bf16[128,2048]{1,0:T(8,128)(2,1)S(1)}, u32[]{:S(2)}, u32[]{:S(2)}) collective-permute-start(bf16[128,2048]{1,0:T(8,128)(2,1)S(1)} %get-tuple-element.101), channel_id=1, source_target_pairs={{0,1},{3,2},{4,5},{7,6},{8,9},{11,10},{12,13},{15,14},{16,17},{19,... | collective-permute-start | bytes 1572872 | tf_op jit(solution)/shard_map/ppermute | solution.py:80
  331.3 3.0 collective-permute-start.38
  332.0 2.3 collective-permute-start.41
  335.4 115.7 %collective-permute-start.39 = (bf16[128,2048]{1,0:T(8,128)(2,1)S(1)}, bf16[128,2048]{1,0:T(8,128)(2,1)S(1)}, u32[]{:S(2)}, u32[]{:S(2)}) collective-permute-start(bf16[128,2048]{1,0:T(8,128)(2,1)S(1)} %get-tuple-element.92), channel_id=1, source_target_pairs={{1,0},{2,3},{5,4},{6,7},{9,8},{10,11},{13,12},{14,15},{17,16},{18,... | collective-permute-start | bytes 1572872 | tf_op jit(solution)/shard_map/ppermute | solution.py:80
  414.0 37.2 %collective-permute-start.42 = (bf16[128,2048]{1,0:T(8,128)(2,1)S(1)}, bf16[128,2048]{1,0:T(8,128)(2,1)S(1)}, u32[]{:S(2)}, u32[]{:S(2)}) collective-permute-start(bf16[128,2048]{1,0:T(8,128)(2,1)S(1)} %get-tuple-element.95), channel_id=1, source_target_pairs={{1,0},{2,3},{5,4},{6,7},{9,8},{10,11},{13,12},{14,15},{17,16},{18,... | collective-permute-start | bytes 1572872 | tf_op jit(solution)/shard_map/ppermute | solution.py:80
  448.5 16.7 %collective-permute-start.45 = (bf16[128,2048]{1,0:T(8,128)(2,1)S(1)}, bf16[128,2048]{1,0:T(8,128)(2,1)S(1)}, u32[]{:S(2)}, u32[]{:S(2)}) collective-permute-start(bf16[128,2048]{1,0:T(8,128)(2,1)S(1)} %get-tuple-element.94), channel_id=1, source_target_pairs={{1,0},{2,3},{5,4},{6,7},{9,8},{10,11},{13,12},{14,15},{17,16},{18,... | collective-permute-start | bytes 1572872 | tf_op jit(solution)/shard_map/ppermute | solution.py:80
  449.8 22.5 %collective-permute-start.48 = (bf16[128,2048]{1,0:T(8,128)(2,1)S(1)}, bf16[128,2048]{1,0:T(8,128)(2,1)S(1)}, u32[]{:S(2)}, u32[]{:S(2)}) collective-permute-start(bf16[128,2048]{1,0:T(8,128)(2,1)S(1)} %get-tuple-element.93), channel_id=1, source_target_pairs={{1,0},{2,3},{5,4},{6,7},{9,8},{10,11},{13,12},{14,15},{17,16},{18,... | collective-permute-start | bytes 1572872 | tf_op jit(solution)/shard_map/ppermute | solution.py:80
  487.8 13.9 %all-to-all-start.2 = ((bf16[8,256,128]{2,1,0:T(8,128)(2,1)}), bf16[8,256,128]{2,1,0:T(8,128)(2,1)S(1)}, u32[]{:S(2)}, u32[]{:S(2)}) async-start(bf16[8,256,128]{2,1,0:T(8,128)(2,1)} %bitcast.61), calls=%async_computation.2 | async-start | bytes 1048576 | tf_op jit(solution)/shard_map/all_to_all | solution.py:806
  491.9 474.5 %reduce-scatter.7.cloned.1.call-start = ((), (), s32[]{:S(2)}) async-start(), calls=%async_computation.12 | async-start | bytes 2359296 | tf_op jit(solution)/shard_map/reduce_scatter | solution.py:830
  494.6 578.6 %reduce-scatter.5.cloned.1.call-start = ((), (), s32[]{:S(2)}) async-start(), calls=%async_computation.11 | async-start | bytes 7077888 | tf_op jit(solution)/shard_map/reduce_scatter | solution.py:832
  525.3 4.3 collective-permute-start.51
  576.8 499.0 %reduce-scatter.11.cloned.1.call-start = ((), (), s32[]{:S(2)}) async-start(), calls=%async_computation.14 | async-start | bytes 9437184 | tf_op jit(solution)/shard_map/reduce_scatter | solution.py:829
  621.0 47.7 %collective-permute-start.49 = (bf16[512,2048]{1,0:T(8,128)(2,1)}, bf16[512,2048]{1,0:T(8,128)(2,1)}, u32[]{:S(2)}, u32[]{:S(2)}) collective-permute-start(bf16[512,2048]{1,0:T(8,128)(2,1)} %get-tuple-element.37.last), channel_id=1, source_target_pairs={{0,1},{3,2},{4,5},{7,6},{8,9},{11,10},{12,13},{15,14},{16,17},{19,... | collective-permute-start | bytes 6291464 | tf_op jit(solution)/shard_map/ppermute | solution.py:80
  630.1 83.5 %collective-permute-start.52 = (bf16[512,2048]{1,0:T(8,128)(2,1)}, bf16[512,2048]{1,0:T(8,128)(2,1)}, u32[]{:S(2)}, u32[]{:S(2)}) collective-permute-start(bf16[512,2048]{1,0:T(8,128)(2,1)} %get-tuple-element.89), channel_id=1, source_target_pairs={{0,1},{3,2},{4,5},{7,6},{8,9},{11,10},{12,13},{15,14},{16,17},{19,... | collective-permute-start | bytes 6291464 | tf_op jit(solution)/shard_map/ppermute | solution.py:80
  632.9 125.6 %collective-permute-start.54 = (bf16[512,2048]{1,0:T(8,128)(2,1)}, bf16[512,2048]{1,0:T(8,128)(2,1)}, u32[]{:S(2)}, u32[]{:S(2)}) collective-permute-start(bf16[512,2048]{1,0:T(8,128)(2,1)} %get-tuple-element.91), channel_id=1, source_target_pairs={{0,1},{3,2},{4,5},{7,6},{8,9},{11,10},{12,13},{15,14},{16,17},{19,... | collective-permute-start | bytes 6291464 | tf_op jit(solution)/shard_map/ppermute | solution.py:80
  635.6 166.7 %collective-permute-start.56 = (bf16[512,2048]{1,0:T(8,128)(2,1)}, bf16[512,2048]{1,0:T(8,128)(2,1)}, u32[]{:S(2)}, u32[]{:S(2)}) collective-permute-start(bf16[512,2048]{1,0:T(8,128)(2,1)} %get-tuple-element.90), channel_id=1, source_target_pairs={{0,1},{3,2},{4,5},{7,6},{8,9},{11,10},{12,13},{15,14},{16,17},{19,... | collective-permute-start | bytes 6291464 | tf_op jit(solution)/shard_map/ppermute | solution.py:80
  672.4 296.0 %collective-permute-start.50 = (bf16[512,2048]{1,0:T(8,128)(2,1)}, bf16[512,2048]{1,0:T(8,128)(2,1)}, u32[]{:S(2)}, u32[]{:S(2)}) collective-permute-start(bf16[512,2048]{1,0:T(8,128)(2,1)} %add_convert_fusion.3), channel_id=1, source_target_pairs={{1,2},{2,1},{5,6},{6,5},{9,10},{10,9},{13,14},{14,13},{17,18},{18,... | collective-permute-start | bytes 6291464 | tf_op jit(solution)/shard_map/ppermute | solution.py:80
  809.9 158.5 %collective-permute-start.53 = (bf16[512,2048]{1,0:T(8,128)(2,1)}, bf16[512,2048]{1,0:T(8,128)(2,1)}, u32[]{:S(2)}, u32[]{:S(2)}) collective-permute-start(bf16[512,2048]{1,0:T(8,128)(2,1)} %get-tuple-element.86), channel_id=1, source_target_pairs={{1,2},{2,1},{5,6},{6,5},{9,10},{10,9},{13,14},{14,13},{17,18},{18,... | collective-permute-start | bytes 6291464 | tf_op jit(solution)/shard_map/ppermute | solution.py:80
  811.9 156.5 %collective-permute-start.55 = (bf16[512,2048]{1,0:T(8,128)(2,1)}, bf16[512,2048]{1,0:T(8,128)(2,1)}, u32[]{:S(2)}, u32[]{:S(2)}) collective-permute-start(bf16[512,2048]{1,0:T(8,128)(2,1)} %get-tuple-element.88), channel_id=1, source_target_pairs={{1,2},{2,1},{5,6},{6,5},{9,10},{10,9},{13,14},{14,13},{17,18},{18,... | collective-permute-start | bytes 6291464 | tf_op jit(solution)/shard_map/ppermute | solution.py:80
  813.9 154.5 %collective-permute-start.57 = (bf16[512,2048]{1,0:T(8,128)(2,1)}, bf16[512,2048]{1,0:T(8,128)(2,1)}, u32[]{:S(2)}, u32[]{:S(2)}) collective-permute-start(bf16[512,2048]{1,0:T(8,128)(2,1)} %get-tuple-element.87), channel_id=1, source_target_pairs={{1,2},{2,1},{5,6},{6,5},{9,10},{10,9},{13,14},{14,13},{17,18},{18,... | collective-permute-start | bytes 6291464 | tf_op jit(solution)/shard_map/ppermute | solution.py:80
  825.1 126.5 %all-to-all-start.5 = ((f32[4,2,2048]{2,1,0:T(2,128)}), f32[4,2,2048]{2,1,0:T(2,128)S(1)}, u32[]{:S(2)}, u32[]{:S(2)}) async-start(f32[4,2,2048]{2,1,0:T(2,128)} %pad_maximum_fusion.9), calls=%async_computation.5 | async-start | bytes 131072 | tf_op jit(solution)/shard_map/all_to_all | solution.py:874
  832.1 246.3 %reduce-scatter.9.cloned.1.call-start = ((), (), s32[]{:S(2)}) async-start(), calls=%async_computation.13 | async-start | bytes 9437184 | tf_op jit(solution)/shard_map/reduce_scatter | solution.py:831
  951.6 13.4 %all-to-all-start.4 = ((f32[4,512,8]{1,2,0:T(8,128)}), f32[4,512,8]{1,2,0:T(8,128)S(1)}, u32[]{:S(2)}, u32[]{:S(2)}) async-start(f32[4,512,8]{1,2,0:T(8,128)} %copy.43), calls=%async_computation.4 | async-start | bytes 131072 | tf_op jit(solution)/shard_map/all_to_all | solution.py:870
  974.4 53.0 %collective-permute-start.58 = (bf16[2,128,2048]{2,1,0:T(8,128)(2,1)S(1)}, bf16[2,128,2048]{2,1,0:T(8,128)(2,1)S(1)}, u32[]{:S(2)}, u32[]{:S(2)}) collective-permute-start(bf16[2,128,2048]{2,1,0:T(8,128)(2,1)S(1)} %pad_maximum_fusion.3), channel_id=1, source_target_pairs={{1,0},{2,3},{5,4},{6,7},{9,8},{10,11},{13,12},{14,15},{17,16},{18,... | collective-permute-start | bytes 3145736 | tf_op jit(solution)/shard_map/ppermute | solution.py:80
  980.4 47.3 %collective-permute-start.59 = (bf16[2,128,2048]{2,1,0:T(8,128)(2,1)S(1)}, bf16[2,128,2048]{2,1,0:T(8,128)(2,1)S(1)}, u32[]{:S(2)}, u32[]{:S(2)}) collective-permute-start(bf16[2,128,2048]{2,1,0:T(8,128)(2,1)S(1)} %pad_maximum_fusion.4), channel_id=1, source_target_pairs={{1,0},{2,3},{5,4},{6,7},{9,8},{10,11},{13,12},{14,15},{17,16},{18,... | collective-permute-start | bytes 3145736 | tf_op jit(solution)/shard_map/ppermute | solution.py:80
  986.4 60.8 %collective-permute-start.60 = (bf16[2,128,2048]{2,1,0:T(8,128)(2,1)S(1)}, bf16[2,128,2048]{2,1,0:T(8,128)(2,1)S(1)}, u32[]{:S(2)}, u32[]{:S(2)}) collective-permute-start(bf16[2,128,2048]{2,1,0:T(8,128)(2,1)S(1)} %pad_maximum_fusion.5), channel_id=1, source_target_pairs={{1,0},{2,3},{5,4},{6,7},{9,8},{10,11},{13,12},{14,15},{17,16},{18,... | collective-permute-start | bytes 3145736 | tf_op jit(solution)/shard_map/ppermute | solution.py:80
  992.4 76.7 %collective-permute-start.61 = (bf16[2,128,2048]{2,1,0:T(8,128)(2,1)S(1)}, bf16[2,128,2048]{2,1,0:T(8,128)(2,1)S(1)}, u32[]{:S(2)}, u32[]{:S(2)}) collective-permute-start(bf16[2,128,2048]{2,1,0:T(8,128)(2,1)S(1)} %pad_maximum_fusion.6), channel_id=1, source_target_pairs={{1,0},{2,3},{5,4},{6,7},{9,8},{10,11},{13,12},{14,15},{17,16},{18,... | collective-permute-start | bytes 3145736 | tf_op jit(solution)/shard_map/ppermute | solution.py:80
  (105 other events, 2217.5 us)
Sparse Core Ops, SparseCore 0:
  336.8 99.9 all-gather.12
  496.0 41.6 reduce-scatter.6
  576.9 59.9 reduce-scatter.4
  640.3 71.2 reduce-scatter.10
  836.1 71.9 reduce-scatter.8

commit v2 on v1

--- a/solution.py
+++ b/solution.py
@@ -84,39 +84,65 @@
     return lax.optimization_barrier((value, *others))[0]
 
 
-def gather_weights(shards):
-    peers = lax.axis_size("dp")
-    if peers != 8:
-        return [lax.all_gather(shard, "dp", axis=0) for shard in shards]
-    index = lax.axis_index("dp")
-    full = []
-    ahead = None
-    for shard in shards:
-        if ahead is not None:
-            shard = after(shard, *ahead)
-        by_x = partner(shard, 2)
-        by_y = partner(shard, 4)
-        ahead = (by_x, by_y)
-        cut = max(range(shard.ndim - 1), key=lambda dim: shard.shape[dim])
+class Gathered:
+    def __init__(self, shard, direct=False):
+        self.shard = shard
+        self.peers = lax.axis_size("dp")
+        if self.peers != 8:
+            self.by_x = self.by_y = shard
+            return
+        self.cut = max(range(shard.ndim - 1), key=lambda dim: shard.shape[dim])
+        self.by_x = partner(shard, 2)
+        self.by_y = partner(shard, 4)
+        self.across = partner(shard, 6) if direct else None
+
+    def whole(self, *earlier):
+        shard = self.shard
+        if self.peers != 8:
+            return lax.all_gather(shard, "dp", axis=0)
+        index = lax.axis_index("dp")
+        cut = self.cut
         half = shard.shape[cut] // 2
-        low = lax.slice_in_dim(by_y, 0, half, axis=cut)
-        high = lax.slice_in_dim(by_x, half, 2 * half, axis=cut)
-        pieces = [
-            (shard, 0, 0),
-            (by_x, 2, 0),
-            (by_y, 4, 0),
-            (partner(low, 2), 6, 0),
-            (partner(high, 4), 6, half),
-        ]
+        pieces = [(shard, 0, 0), (self.by_x, 2, 0), (self.by_y, 4, 0)]
+        if self.across is None:
+            low = lax.slice_in_dim(self.by_y, 0, half, axis=cut)
+            high = lax.slice_in_dim(self.by_x, half, 2 * half, axis=cut)
+            if earlier:
+                low, high = after(low, *earlier), after(high, *earlier)
+            pieces += [(partner(low, 2), 6, 0), (partner(high, 4), 6, half)]
+        else:
+            pieces.append((self.across, 6, 0))
         pieces += [(partner(piece, 1), code ^ 1, start) for piece, code, start in pieces]
-        whole = jnp.zeros((peers, *shard.shape), shard.dtype)
+        whole = jnp.zeros((self.peers, *shard.shape), shard.dtype)
         for piece, code, start in pieces:
             place = [jnp.int32(0)] * (shard.ndim + 1)
             place[0] = index ^ code
             place[cut + 1] = jnp.int32(start)
             whole = lax.dynamic_update_slice(whole, piece[None], place)
-        full.append(whole)
-    return full
+        return whole
+
+
+def along_line(count, first, second, third):
+    ones, twos, threes = [], [], []
+    for step in range(count + 2):
+        if step < count:
+            gates = []
+            if step >= 2:
+                gates.append(ones[step - 2])
+            if step >= 3:
+                gates.append(twos[step - 3])
+            if step >= 4:
+                gates.append(threes[step - 4])
+            ones.append(line_hop(first(step, gates), OUTWARD))
+        if 0 <= step - 1 < count:
+            twos.append(line_hop(second(step - 1, ones[step - 1]), MIDDLE))
+        if 0 <= step - 2 < count:
+            threes.append(line_hop(third(step - 2, ones[step - 2], twos[step - 2]), INWARD))
+    return ones, twos, threes
+
+
+def gated(value, gates):
+    return after(value, *gates) if gates else value
 
 
 def rope_tables(positions, sign):
@@ -393,13 +419,14 @@
     return result if extra is None else result + extra
 
 
-def heads_back(parts, w_heads, normed, unit, inv, gains, tables):
+def heads_back(parts, w_heads, normed, unit, inv, gains, tables, count):
     _, tokens, width = normed.shape
     columns = w_heads.shape[3]
     heads, half = columns // HD, tokens // 2
-    block = min(128, tokens)
-
-    def kernel(part, w, x, u, istd, gain, table, stream, weight, stats, grad, wide):
+    block = tokens // count
+
+    def kernel(part, w, x, u, istd, gain, table, *refs):
+        pieces, (stream, weight, stats, grad, wide) = refs[:count], refs[count:]
         c = pl.program_id(0)
         turn = c < 2
 
@@ -421,17 +448,16 @@
         stats[...] = jnp.zeros_like(stats)
         column = lax.broadcasted_iota(jnp.int32, (block, istd.shape[1]), 1)
 
-        def step(r, carry):
-            here = pl.ds(pl.multiple_of(r * block, block), block)
+        for r in range(count):
+            here = slice(r * block, (r + 1) * block)
             values = wide[here, :]
             units = u[0, here, :].astype(F32)
             std = jnp.sum(jnp.where(column == c, istd[here, :], 0.0), axis=-1, keepdims=True)
-            stream[0, here, :] = norm_back(values, units, std, gain[0], None).astype(BF)
+            result = norm_back(values, units, std, gain[0], None).astype(BF)
+            stream[0, here, :] = result
+            pieces[r][0] = result
             stats[0, 0:1] += jnp.sum(values * units, axis=0, keepdims=True)
             stats[0, 1:2] += jnp.sum(values, axis=0, keepdims=True)
-            return carry
-
-        lax.fori_loop(0, tokens // block, step, 0)
 
     return pl.pallas_call(
         kernel,
@@ -445,12 +471,14 @@
             pl.BlockSpec((1, 1, width), lambda c: (c, 0, 0)),
             pl.BlockSpec((3, tokens, HD), lambda c: (0, 0, 0)),
         ],
-        out_specs=[
+        out_specs=[pl.BlockSpec((1, block, width), lambda c: (c, 0, 0))] * count
+        + [
             pl.BlockSpec((1, tokens, width), lambda c: (c, 0, 0)),
             pl.BlockSpec((1, width, columns), lambda c: (c, 0, 0)),
             pl.BlockSpec((1, 2, width), lambda c: (c, 0, 0)),
         ],
-        out_shape=[
+        out_shape=[jax.ShapeDtypeStruct((3, block, width), BF)] * count
+        + [
             jax.ShapeDtypeStruct((3, tokens, width), BF),
             jax.ShapeDtypeStruct((3, width, columns), BF),
             jax.ShapeDtypeStruct((3, 2, width), F32),
@@ -621,6 +649,90 @@
         else:
             key_value_grad = key_value_grad + passed_along(pair_grad, "dp", -back)
     return jnp.concatenate([query_grad[None], key_value_grad])
+
+
+def mix_block(i, coefficients, shares, last_share, extras, last_extras, arrived, whole):
+    streams, block, width = shares.shape
+    each = coefficients.shape[1] // (streams + 1)
+    groups = 1 + len(extras)
+    final = arrived is not None
+    lanes = 512
+
+    def kernel(*refs):
+        weights = refs[0][...]
+        heads, lasts = refs[1 : 1 + groups], refs[1 + groups : 1 + 2 * groups]
+        out = refs[-1]
+        columns = [weights[:, n : n + 1] for n in range(weights.shape[1])]
+        for lane in range(0, width, lanes):
+            span = slice(lane, lane + lanes)
+            values = []
+            for s in range(streams + 1):
+                picks = [r[s, :, span] if s < streams else l[:, span] for r, l in zip(heads, lasts)]
+                total = picks[0].astype(F32)
+                for pick in picks[1:]:
+                    total = total + pick.astype(F32)
+                values.append(total)
+            for e in range(each):
+                total = columns[e * (streams + 1)] * values[0]
+                for s in range(1, streams + 1):
+                    total = total + columns[e * (streams + 1) + s] * values[s]
+                if final:
+                    total = total + refs[1 + 2 * groups][e, :, span].astype(F32)
+                out[e, :, span] = total.astype(out.dtype)
+
+    piece = pl.BlockSpec((streams, block, width), lambda n: (0, 0, 0))
+    row = pl.BlockSpec((block, width), lambda n: (i, 0))
+    small = pl.BlockSpec((each, block, width), lambda n: (0, 0, 0))
+    specs = [pl.BlockSpec((block, coefficients.shape[1]), lambda n: (i, 0))]
+    specs += [piece] * groups + [row] * groups
+    args = [coefficients, shares, *extras, last_share, *last_extras]
+    alias = {}
+    if final:
+        specs.append(small)
+        args.append(arrived)
+        if whole is not None:
+            specs.append(pl.BlockSpec(memory_space=pl.ANY))
+            args.append(whole)
+            alias = {len(args) - 1: 0}
+        out_spec = pl.BlockSpec((each, block, width), lambda n: (0, i, 0))
+        out_shape = jax.ShapeDtypeStruct((each, coefficients.shape[0], width), F32)
+    else:
+        out_spec, out_shape = small, jax.ShapeDtypeStruct((each, block, width), BF)
+    return pl.pallas_call(
+        kernel,
+        grid=(1,),
+        in_specs=specs,
+        out_specs=out_spec,
+        out_shape=out_shape,
+        input_output_aliases=alias,
+        name="mix_final" if final else "mix_inward",
+    )(*args)
+
+
+def hidden_units(x, w_up):
+    tokens, width = x.shape
+    units = w_up.shape[1]
+    block = min(512, units)
+
+    def kernel(x_ref, w, out, slope):
+        up = dot(x_ref[...], w[...])
+        inside = 0.5 * (1.0 + lax.erf(up * math.sqrt(0.5)))
+        out[...] = (up * inside).astype(BF)
+        bell = jnp.exp(-0.5 * up * up) * (1.0 / math.sqrt(2.0 * math.pi))
+        slope[...] = (inside + up * bell).astype(BF)
+
+    column = pl.BlockSpec((tokens, block), lambda i: (0, i))
+    return pl.pallas_call(
+        kernel,
+        grid=(units // block,),
+        in_specs=[
+            pl.BlockSpec((tokens, width), lambda i: (0, 0)),
+            pl.BlockSpec((width, block), lambda i: (0, i)),
+        ],
+        out_specs=[column, column],
+        out_shape=[jax.ShapeDtypeStruct((tokens, units), BF)] * 2,
+        name="hidden_units",
+    )(x, w_up)
 
 
 def merge_branches(attended, hidden, w_merge, w_down, stream, flag):
@@ -726,54 +838,81 @@
     flags = flag.reshape(1)
     near = shards == 8 and heads_here * 2 == shards and tokens * shards == 2 * SEQ
 
-    mix_all = lax.all_gather(mixing[:, 0, :], "stream", axis=0)
-    norms = lax.all_gather(jnp.concatenate([norm_gain, norm_bias]), "stream", axis=0)
-    gains, biases = norms[:, 0].astype(F32), norms[:, 1].astype(F32)
+    got_heads = Gathered(w_heads, direct=near)
+    got_up = Gathered(after(w_up, got_heads.shard))
+    got_merge = Gathered(w_merge)
+    cotangent = lax.all_gather(out_cotangent, "stream", axis=1, tiled=True)
+    lanes = jnp.concatenate([norm_gain, norm_bias]).astype(F32).reshape(tokens, -1)
+    packed = lax.all_gather(jnp.concatenate([mixing[:, 0, :], lanes], axis=1), "stream", axis=0)
+    mix_all = packed[:, :, :entries]
+    norms = packed[:, :, entries:].reshape(members, 2, width)
+    gains, biases = norms[:, 0], norms[:, 1]
     mix_rows = jnp.transpose(mix_all, (1, 0, 2)).reshape(tokens, members * entries)
-    spread = jnp.broadcast_to(shard_offset[:, None], (8, 128))
-    offsets = lax.all_gather(spread, "dp", axis=0)[:, 0, 0]
-    first_full = lax.all_gather(mixer_first, "stream", axis=0, tiled=True)
-    second_full = lax.all_gather(mixer_second[:, 0, :], "stream", axis=0).astype(F32)
-    next_full = lax.all_gather(next_cotangent[:, 0, :], "stream", axis=0)
-    cotangent = lax.all_gather(out_cotangent, "stream", axis=1, tiled=True)
-    full_heads, full_up, full_merge, full_down = gather_weights([w_heads, w_up, w_merge, w_down])
-    flat_up = full_up.reshape(width, -1)
 
     normed, unit, inv, stream = make_streams(history, mix_rows, gains, biases)
+    full_heads = got_heads.whole()
     positions = shard_offset[0] + jnp.arange(tokens, dtype=jnp.int32)
     projected = project(normed, full_heads, rope_tables(positions, 1.0))
+
+    first_rows = mixer_first.astype(F32).reshape(tokens, -1)
+    second_flat = mixer_second[:, 0, :].astype(F32).reshape(-1)
+    hidden_count = mixer_second.shape[0]
+    lines = -(-second_flat.shape[0] // tokens)
+    second_rows = jnp.pad(second_flat, (0, lines * tokens - second_flat.shape[0]))
+    rest = jnp.concatenate(
+        [next_cotangent[:, 0, :], first_rows, second_rows.reshape(tokens, lines)], axis=1
+    )
+    rest = lax.all_gather(after(rest, projected), "stream", axis=0)
+    outputs = next_cotangent.shape[2]
+    cut = outputs + first_rows.shape[1]
+    next_full = rest[:, :, :outputs]
+    first_full = rest[:, :, outputs:cut].astype(BF).reshape(width, -1)
+    second_full = rest[:, :, cut:].reshape(members, -1)[:, : second_flat.shape[0]]
+    second_full = second_full.reshape(members, hidden_count, outputs)
+
     if near:
+        spread = after(jnp.broadcast_to(shard_offset[:, None], (8, 128)), projected)
+        offsets = lax.all_gather(spread, "dp", axis=0)[:, 0, 0]
         side = (index % 2).astype(jnp.int32).reshape(1)
         place = jnp.arange(shards, dtype=jnp.int32)
         first_key = jnp.maximum(place - offsets // tokens, 0).astype(jnp.int32)
         own = lax.all_to_all(projected, "dp", 0, 0, tiled=True)
+        own = after(own, next_full, first_full, second_full, cotangent)
+        got_down = Gathered(after(w_down, own))
         other = partner(own[:, 1:], 1)
+        full_up = got_up.whole()
+        full_merge = got_merge.whole()
         result, exact, level = attend(own, other, first_key, side)
         back = lax.all_to_all(result, "dp", 0, 0, tiled=True)
         attended = jnp.transpose(back.reshape(heads_here, tokens, HD), (1, 0, 2)).reshape(tokens, -1)
     else:
+        got_down = Gathered(w_down)
+        full_up = got_up.whole()
+        full_merge = got_merge.whole()
         split = projected.reshape(heads_here, 2, 3, half, HD)
         split = jnp.transpose(split, (2, 1, 3, 0, 4)).reshape(3, tokens, heads_here, HD)
         result, kept = far_attend(split[0], split[1], split[2], shard_offset)
         attended = result.reshape(tokens, -1).astype(BF)
-
-    up = dot(normed[members - 1], flat_up)
-    hidden, gelu_back = jax.vjp(exact_gelu, up)
-    hidden = hidden.astype(BF)
-    slope = gelu_back(jnp.ones_like(up))[0].astype(BF)
+    full_down = got_down.whole()
+    flat_up = full_up.reshape(width, -1)
+    hidden, slope = hidden_units(normed[members - 1], flat_up)
+    attended = after(attended, hidden)
     share = merge_branches(attended, hidden, full_merge, full_down, stream, flags)
 
     inner = (member == 1) | (member == 2)
-    pieces = []
     count = 4
-    for i in range(count):
-        part = lax.slice_in_dim(share, i * tokens // count, (i + 1) * tokens // count)
-        one = line_hop(part.astype(BF), OUTWARD)
-        nearer = part + one.astype(F32)
-        two = line_hop(nearer.astype(BF), MIDDLE)
-        total = (nearer + two.astype(F32)).astype(BF)
-        pieces.append(jnp.where(inner, total, line_hop(total, INWARD)))
-    block_full = jnp.concatenate(pieces)
+    rows = [lax.slice_in_dim(share, i * tokens // count, (i + 1) * tokens // count) for i in range(count)]
+    totals = {}
+
+    def middle(i, one):
+        return (rows[i] + one.astype(F32)).astype(BF)
+
+    def ends(i, one, two):
+        totals[i] = (rows[i] + one.astype(F32) + two.astype(F32)).astype(BF)
+        return totals[i]
+
+    _, _, arrived = along_line(count, lambda i, gates: gated(rows[i].astype(BF), gates), middle, ends)
+    block_full = jnp.concatenate([jnp.where(inner, totals[i], arrived[i]) for i in range(count)])
 
     mine = member * (width // members)
     block_out = lax.dynamic_slice_in_dim(block_full, mine, width // members, axis=1)
@@ -800,81 +939,90 @@
     ).astype(BF)
 
     attended_grad = back_through(grad_out, full_merge, None)
+    up_grad = back_through(grad_out, full_down, slope)
+    merge_grad = dot_rows(attended, grad_out).astype(BF)
     if near:
         sent = attended_grad.reshape(tokens, heads_here, HD)
         sent = jnp.transpose(sent, (1, 0, 2)).reshape(shards, half, HD)
         grads = lax.all_to_all(sent, "dp", 0, 0, tiled=True)
+        grads = after(grads, up_grad)
         kept_grads, given = attend_back(own, other, grads, exact, level, first_key, side)
         taken = partner(given, 1)
         summed = kept_grads[:, 1:].astype(F32) + taken.astype(F32)
-        packed = jnp.concatenate([kept_grads[:, :1], summed.astype(BF)], axis=1)
-        parts = lax.all_to_all(packed, "dp", 0, 0, tiled=True)
+        pair = jnp.concatenate([kept_grads[:, :1], summed.astype(BF)], axis=1)
+        parts = lax.all_to_all(pair, "dp", 0, 0, tiled=True)
+        up_grad = after(up_grad, pair)
     else:
         grads = far_attend_back(split[0], attended_grad.reshape(tokens, heads_here, HD), kept)
         parts = grads.reshape(3, 2, half, heads_here, HD)
         parts = jnp.transpose(parts, (3, 1, 0, 2, 4)).reshape(2 * heads_here, 3, half, HD)
 
-    up_grad = back_through(grad_out, full_down, slope)
-    down_grad = dot_rows(hidden, grad_out).astype(BF)
-    merge_grad = dot_rows(attended, grad_out).astype(BF)
     last_normed = dot_cols(up_grad, flat_up)
     last_share, last_stats = last_back(
         last_normed, unit[members - 1], inv, gains[members - 1 :], grad_out, flags
     )
-    up_back = dot_rows(normed[members - 1], up_grad).astype(BF)
-    heads_share, heads_grad, heads_stats = heads_back(
-        parts, full_heads, normed, unit, inv, gains, rope_tables(positions, -1.0)
+    last_one = line_hop(last_share, OUTWARD)
+    down_grad = dot_rows(after(hidden, last_share), grad_out).astype(BF)
+    parts = after(parts, last_share, down_grad)
+    blocks = 8
+    *pieces, heads_share, heads_grad, heads_stats = heads_back(
+        parts, full_heads, normed, unit, inv, gains, rope_tables(positions, -1.0), blocks
     )
-
+    last_two = line_hop((last_share.astype(F32) + last_one.astype(F32)).astype(BF), MIDDLE)
+    up_back = dot_rows(normed[members - 1], after(up_grad, heads_share)).astype(BF)
+
+    grad_merge = lax.psum_scatter(merge_grad, "dp", scatter_dimension=1, tiled=True).astype(F32)
     grad_down = lax.psum_scatter(down_grad, "dp", scatter_dimension=1, tiled=True).astype(F32)
-    grad_merge = lax.psum_scatter(merge_grad, "dp", scatter_dimension=1, tiled=True).astype(F32)
+    grad_heads = lax.psum_scatter(heads_grad, "dp", scatter_dimension=1, tiled=True).astype(F32)
     grad_up = lax.psum_scatter(up_back, "dp", scatter_dimension=0, tiled=True).astype(F32)
-    grad_heads = lax.psum_scatter(heads_grad, "dp", scatter_dimension=1, tiled=True).astype(F32)
-
-    shares = [last_share] + [heads_share[c] for c in range(members - 1)]
-    order = [members - 1] + list(range(members - 1))
-    ones, twos = [], []
-    for item in shares:
-        one = line_hop(item, OUTWARD)
-        ones.append(one)
-        twos.append(line_hop((item.astype(F32) + one.astype(F32)).astype(BF), MIDDLE))
+
     each = entries // members
-    target = jnp.where(member == 1, 0, members - 1)
 
     def weights_for(owner):
         block = lax.dynamic_slice_in_dim(mix_all, owner * each, each, axis=2)
-        return [[block[s, :, e : e + 1] for s in order] for e in range(each)]
-
-    def weighted(weights, values):
-        sums = []
-        for e in range(each):
-            total = weights[e][0] * values[0]
-            for weight, value in zip(weights[e][1:], values[1:]):
-                total = total + weight * value
-            sums.append(total)
-        return jnp.stack(sums)
-
-    there, here = weights_for(target), weights_for(member)
-    history_parts = []
-    for i in range(count):
-        low, high = i * tokens // count, (i + 1) * tokens // count
-        cut = lambda array: lax.slice_in_dim(array, low, high).astype(F32)
-        rows = lambda weights: [[w[low:high] for w in line] for line in weights]
-        inward = [cut(item) + cut(two) for item, two in zip(shares, twos)]
-        three = line_hop(weighted(rows(there), inward).astype(BF), INWARD)
-        sums = [value + cut(one) for value, one in zip(inward, ones)]
-        history_parts.append(weighted(rows(here), sums) + three.astype(F32))
-    grad_history = jnp.concatenate(history_parts, axis=1)
-
-    mix_parts = mixing_back(heads_share, last_share, history)
-    mix_parts = lax.all_to_all(mix_parts, "stream", 0, 0, tiled=True)
-    grad_mixing = jnp.sum(mix_parts, axis=0)[:, None, :]
-
-    stats = jnp.concatenate([heads_stats, last_stats[None]])
-    stats = jnp.sum(lax.all_to_all(stats, "stream", 0, 0, tiled=True), axis=0)
-    stats = jnp.sum(lax.all_gather(stats, "dp", axis=0), axis=0)
-    grad_first = jnp.sum(lax.all_gather(first_local, "dp", axis=0), axis=0)
-    grad_second = jnp.sum(lax.all_gather(second_local, "dp", axis=0), axis=0)
+        return jnp.transpose(block, (1, 2, 0)).reshape(tokens, each * members)
+
+    there = weights_for(jnp.where(member == 1, 0, members - 1))
+    here = weights_for(member)
+    extra = {}
+
+    def first_hop(i, gates):
+        if i == 1:
+            mix_parts = mixing_back(heads_share, last_share, history)
+            stats = jnp.concatenate([heads_stats, last_stats[None]])
+            both = jnp.concatenate([mix_parts, stats.reshape(members, tokens, -1)], axis=2)
+            extra["both"] = jnp.sum(lax.all_to_all(both, "stream", 0, 0, tiled=True), axis=0)
+        if i == 4:
+            sums = extra["both"][:, entries:]
+            second_sums = jnp.pad(second_local.reshape(-1), (0, lines * tokens - second_flat.shape[0]))
+            local = jnp.concatenate(
+                [sums, first_local.reshape(tokens, -1), second_sums.reshape(tokens, lines)], axis=1
+            )
+            extra["all"] = jnp.sum(lax.all_gather(local, "dp", axis=0), axis=0)
+            gates = gates + [extra["both"]]
+        if i == 7:
+            gates = gates + [extra["all"]]
+        return gated(pieces[i], gates)
+
+    def second_hop(i, one):
+        return (pieces[i].astype(F32) + one.astype(F32)).astype(BF)
+
+    def third_hop(i, one, two):
+        return mix_block(i, there, pieces[i], last_share, [two], [last_two], None, None)
+
+    ones, twos, threes = along_line(blocks, first_hop, second_hop, third_hop)
+    grad_history = None
+    for i in range(blocks):
+        grad_history = mix_block(
+            i, here, pieces[i], last_share, [ones[i], twos[i]], [last_one, last_two], threes[i], grad_history
+        )
+
+    grad_mixing = extra["both"][:, :entries][:, None, :]
+    sums = extra["all"]
+    spans = 2 * width // tokens
+    stats = sums[:, :spans].reshape(2, width)
+    grad_first = sums[:, spans:-lines].reshape(mixer_first.shape)
+    grad_second = sums[:, -lines:].reshape(-1)[: second_flat.shape[0]].reshape(hidden_count, outputs)
     return (
         block_out,
         next_here[:, None, :],

time: 1100 us -> 882 us (0.80)
  the two profiles are of different devices: /device:TPU:0 before, /device:TPU:8 now
where the time goes in v2:
time: 882 us; the launch traced here: 870 us
  waiting for transfers between devices  270 us (31%)
  Pallas kernels  213 us (24%)
  starting transfers between devices  129 us (15%)
  local copies, waits for them, and re-layouts  111 us (13%)
  blocking collectives  55.9 us (6%)
  other arithmetic  40 us (5%)
  matrix products  35.1 us (4%)
  between operations  16.2 us (2%)
    ppermute x38, waiting for transfers between devices, line_hop(): return lax.ppermute(shard, 'stream', pairs)  220 us
    ppermute x38, starting transfers between devices, line_hop(): return lax.ppermute(shard, 'stream', pairs)  82.9 us
    pallas_call x16, Pallas kernels, mix_block(): pl.pallas_call(kernel, grid=(1,), in_specs=specs, out_specs=out_spec, out...  52.1 us
    dynamic_update_slice x38, local copies, waits for them, and re-layouts, whole(): whole = lax.dynamic_update_slice(whole, piece[None], place)  44.9 us
    ppermute x36, waiting for transfers between devices, partner(): return lax.ppermute(shard, 'dp', [(i, i ^ bit) for i in range(peers)])  42.7 us
    pallas_call x1, Pallas kernels, attend_back(): pl.pallas_call(kernel, grid_spec=pltpu.PrefetchScalarGridSpec(num_scalar_...  25.2 us
    ppermute x36, starting transfers between devices, partner(): return lax.ppermute(shard, 'dp', [(i, i ^ bit) for i in range(peers)])  24.2 us
    pallas_call x1, Pallas kernels, make_streams(): pl.pallas_call(kernel, grid=(tokens // rows,), in_specs=[pl.BlockSpec((en...  22.6 us
  transfers between devices with their start and end apart: 84, of which 31 were waited for; matrix products, arithmetic and copies ran while one was open for 18% of the time, Pallas kernels for 19%

profile of v2, /device:TPU:8, one launch (start us, length us, event | category | flops | bytes accessed | tf_op | source)
XLA Modules:
  0.0 869.9 jit_solution(5995452791913479896)
XLA Ops:
  16.3 14.6 %all-gather = f32[2048,16]{0,1:T(8,128)S(1)} all-gather(f32[512,16]{0,1:T(8,128)S(1)} %pad_maximum_fusion.6), channel_id=2, replica_groups=mesh['dp'=8,'stream'=4] {'stream'}, dimensions={0}, use_global_device_ids=true | all-gather | bytes 163840 | tf_op jit(solution)/shard_map/all_gather | solution.py:846
  34.5 22.6 %make_streams.1 = (bf16[4,512,2048]{2,1,0:T(8,128)(2,1)}, bf16[4,512,2048]{2,1,0:T(8,128)(2,1)}, f32[512,4]{1,0:T(8,128)}, f32[512,2048]{1,0:T(8,128)}) custom-call(bf16[8,512,2048]{2,1,0:T(8,128)(2,1)} %hist.3, f32[512,32]{1,0:T(8,128)} %copy.145.mix, f32[4,2048]{1,0:T(4,128)} %get-tuple-element.196.gain, f32[4,2048]{1,0:T(4,128)} %get-tuple-element.195.bias), custom_call_target="tpu_custom_call" | custom-call | tf_op jit(solution)/shard_map/make_streams/pallas_call | solution.py:210
  60.5 4.4 broadcast_in_dim.192
  68.3 3.4 broadcast_in_dim.178
  73.3 5.4 collective-permute-done.19
  79.1 4.6 collective-permute-done.20
  96.9 17.7 %collective-permute-done.9 = bf16[256,2048]{1,0:T(8,128)(2,1)} collective-permute-done((bf16[256,2048]{1,0:T(8,128)(2,1)S(1)}, bf16[256,2048]{1,0:T(8,128)(2,1)}, u32[]{:S(2)}, u32[]{:S(2)}) %collective-permute-start.9) | collective-permute-done | bytes 1048608 | tf_op jit(solution)/shard_map/ppermute | solution.py:76
  121.3 7.4 collective-permute-done.10
  137.6 8.8 %project.1 = bf16[8,3,256,128]{3,2,1,0:T(8,128)(2,1)} custom-call(bf16[4,512,2048]{2,1,0:T(8,128)(2,1)} %get-tuple-element.55.x, bf16[8,3,256,512]{3,2,1,0:T(8,128)(2,1)} %bitcast_dynamic-update-slice_fusion.12.w, f32[3,512,128]{2,1,0:T(8,128)} %get-tuple-element.174.table), custom_call_target="tpu_custom_call" | custom-call | tf_op jit(solution)/shard_map/project/pallas_call | solution.py:259
  146.4 3.6 all-to-all-start
  150.0 15.5 %all-gather.2 = f32[2048,46]{0,1:T(8,128)S(1)} all-gather(f32[512,46]{0,1:T(8,128)S(1)} %pad_maximum_fusion.4), channel_id=4, replica_groups=mesh['dp'=8,'stream'=4] {'stream'}, dimensions={0}, use_global_device_ids=true | all-gather | bytes 471040 | tf_op jit(solution)/shard_map/all_gather | solution.py:865
  167.3 9.7 %all-gather.1 = s32[64,128]{1,0:T(8,128)S(1)} all-gather(s32[8,128]{1,0:T(8,128)S(1)} %broadcast_in_dim.177), channel_id=3, replica_groups=mesh['dp'=8,'stream'=4] {'dp'}, dimensions={0}, use_global_device_ids=true | all-gather | bytes 36864 | tf_op jit(solution)/shard_map/all_gather | solution.py:875
  189.4 10.0 %hidden_units.1 = (bf16[512,2048]{1,0:T(8,128)(2,1)}, bf16[512,2048]{1,0:T(8,128)(2,1)}) custom-call(bf16[512,2048]{1,0:T(8,128)(2,1)} %slice_bitcast_fusion.1.x_ref, bf16[2048,2048]{1,0:T(8,128)(2,1)} %bitcast.30.w), custom_call_target="tpu_custom_call" | custom-call | tf_op jit(solution)/shard_map/hidden_units/pallas_call | solution.py:725
  199.9 3.9 broadcast_in_dim.214
  206.1 3.3 collective-permute-done.27
  216.2 19.1 %attend.1 = (bf16[8,256,128]{2,1,0:T(8,128)(2,1)}, f32[8,256,128]{2,1,0:T(8,128)}, f32[8,256,1]{2,1,0:T(8,128)}) custom-call(s32[8]{0:T(128)} %subtract_maximum_fusion.first, s32[1]{0:T(128)} %bitcast.14.part, bf16[8,3,256,128]{3,2,1,0:T(8,128)(2,1)} %copy-done.4, bf16[8,2,256,128]{3,2,1,0:T(8,128)(2,1)} %copy-done.14), custom_call_target="tpu_custom_call" | custom-call | tf_op jit(solution)/shard_map/attend/pallas_call | solution.py:317
  235.2 4.6 all-to-all-start.1
  245.6 3.9 all-to-all-done.1
  261.4 13.1 %merge_branches.1 = f32[512,2048]{1,0:T(8,128)} custom-call(bf16[512,512]{1,0:T(8,128)(2,1)} %bitcast.173, bf16[512,2048]{1,0:T(8,128)(2,1)} %get-tuple-element.77.h, bf16[8,512,256]{2,1,0:T(8,128)(2,1)} %copy-done.7, bf16[8,2048,256]{2,1,0:T(8,128)(2,1)} %bitcast_dynamic-update-slice_fusion.20.wd.refs_1_, f32[512,2048]{1,0:T(8,128)} %get-tuple-element.64.st, ...), custom_call_target="tpu_custom_call" | custom-call | tf_op jit(solution)/shard_map/merge_branches/pallas_call | solution.py:749
  279.7 14.1 %collective-permute-done.35 = bf16[128,2048]{1,0:T(8,128)(2,1)S(1)} collective-permute-done((bf16[128,2048]{1,0:T(8,128)(2,1)S(1)}, bf16[128,2048]{1,0:T(8,128)(2,1)S(1)}, u32[]{:S(2)}, u32[]{:S(2)}) %collective-permute-start.35) | collective-permute-done | bytes 524320 | tf_op jit(solution)/shard_map/ppermute | solution.py:80
  295.1 9.9 %collective-permute-done.38 = bf16[128,2048]{1,0:T(8,128)(2,1)S(1)} collective-permute-done((bf16[128,2048]{1,0:T(8,128)(2,1)S(1)}, bf16[128,2048]{1,0:T(8,128)(2,1)S(1)}, u32[]{:S(2)}, u32[]{:S(2)}) %collective-permute-start.38) | collective-permute-done | bytes 524320 | tf_op jit(solution)/shard_map/ppermute | solution.py:80
  305.0 10.2 %collective-permute-done.41 = bf16[128,2048]{1,0:T(8,128)(2,1)S(1)} collective-permute-done((bf16[128,2048]{1,0:T(8,128)(2,1)S(1)}, bf16[128,2048]{1,0:T(8,128)(2,1)S(1)}, u32[]{:S(2)}, u32[]{:S(2)}) %collective-permute-start.41) | collective-permute-done | bytes 524320 | tf_op jit(solution)/shard_map/ppermute | solution.py:80
  318.4 12.2 %collective-permute-done.36 = bf16[128,2048]{1,0:T(8,128)(2,1)S(1)} collective-permute-done((bf16[128,2048]{1,0:T(8,128)(2,1)S(1)}, bf16[128,2048]{1,0:T(8,128)(2,1)S(1)}, u32[]{:S(2)}, u32[]{:S(2)}) %collective-permute-start.36) | collective-permute-done | bytes 524320 | tf_op jit(solution)/shard_map/ppermute | solution.py:80
  337.7 6.8 collective-permute-done.44
  348.6 11.2 %collective-permute-done.42 = bf16[128,2048]{1,0:T(8,128)(2,1)S(1)} collective-permute-done((bf16[128,2048]{1,0:T(8,128)(2,1)S(1)}, bf16[128,2048]{1,0:T(8,128)(2,1)S(1)}, u32[]{:S(2)}, u32[]{:S(2)}) %collective-permute-start.42) | collective-permute-done | bytes 524320 | tf_op jit(solution)/shard_map/ppermute | solution.py:80
  359.8 8.5 collective-permute-done.45
  375.2 7.8 collective-permute-done.37
  383.1 11.2 %collective-permute-done.40 = bf16[128,2048]{1,0:T(8,128)(2,1)S(1)} collective-permute-done((bf16[128,2048]{1,0:T(8,128)(2,1)S(1)}, bf16[128,2048]{1,0:T(8,128)(2,1)S(1)}, u32[]{:S(2)}, u32[]{:S(2)}) %collective-permute-start.40) | collective-permute-done | bytes 524320 | tf_op jit(solution)/shard_map/ppermute | solution.py:80
  394.3 11.2 %collective-permute-done.43 = bf16[128,2048]{1,0:T(8,128)(2,1)S(1)} collective-permute-done((bf16[128,2048]{1,0:T(8,128)(2,1)S(1)}, bf16[128,2048]{1,0:T(8,128)(2,1)S(1)}, u32[]{:S(2)}, u32[]{:S(2)}) %collective-permute-start.43) | collective-permute-done | bytes 524320 | tf_op jit(solution)/shard_map/ppermute | solution.py:80
  405.5 7.9 collective-permute-done.46
  418.8 7.2 back_through.2
  428.0 3.5 all-to-all-start.2
  431.5 13.4 %back_through.3 = bf16[512,2048]{1,0:T(8,128)(2,1)} custom-call(bf16[512,2048]{1,0:T(8,128)(2,1)} %fusion.3.refs_0_.e, bf16[8,2048,256]{2,1,0:T(8,128)(2,1)} %bitcast_dynamic-update-slice_fusion.20.wd.refs_1_, bf16[512,2048]{1,0:T(8,128)(2,1)} %get-tuple-element.67.refs_2_), custom_call_target="tpu_custom_call" | custom-call | tf_op jit(solution)/shard_map/back_through/pallas_call | solution.py:803
  445.7 25.2 %attend_back.1 = (bf16[8,3,256,128]{3,2,1,0:T(8,128)(2,1)}, bf16[8,2,256,128]{3,2,1,0:T(8,128)(2,1)}) custom-call(s32[8]{0:T(128)} %subtract_maximum_fusion.first, s32[1]{0:T(128)} %bitcast.14.part, bf16[8,3,256,128]{3,2,1,0:T(8,128)(2,1)} %copy-done.4, bf16[8,2,256,128]{3,2,1,0:T(8,128)(2,1)} %copy-done.14, bf16[8,256,128]{2,1,0:T(8,128)(2,1)} %copy-done.27, ...), custom_call_target="tpu_custom_call" | custom-call | tf_op jit(solution)/shard_map/attend_back/pallas_call | solution.py:390
  470.9 4.7 collective-permute-start.47
  487.1 4.3 all-to-all-start.3
  491.7 9.9 %fusion.39.g = f32[512,2048]{1,0:T(8,128)} fusion(bf16[512,2048]{1,0:T(8,128)(2,1)S(1)} %copy-done.23, bf16[2048,2048]{1,0:T(8,128)(2,1)} %bitcast.30.w), kind=kOutput, calls=%fused_computation.166 | convolution fusion | flops 4294967296 | bytes 14680064 | tf_op jit(solution)/shard_map/dot_general | solution.py:71
  501.6 6.8 last_back.1
  508.4 8.4 convolution_convert_fusion.1
  517.7 17.2 %heads_back.1 = (bf16[3,64,2048]{2,1,0:T(8,128)(2,1)}, bf16[3,64,2048]{2,1,0:T(8,128)(2,1)}, bf16[3,64,2048]{2,1,0:T(8,128)(2,1)}, bf16[3,64,2048]{2,1,0:T(8,128...) custom-call(bf16[8,3,256,128]{3,2,1,0:T(8,128)(2,1)} %all-to-all-don, ...), custom_call_target="tpu_custom_call" | custom-call | tf_op jit(solution)/shard_map/heads_back/pallas_call | solution.py:462
  536.5 8.4 convolution_convert_fusion
  549.9 47.6 %collective-permute-done.55.refs_5_ = bf16[512,2048]{1,0:T(8,128)(2,1)S(1)} collective-permute-done((bf16[512,2048]{1,0:T(8,128)(2,1)S(1)}, bf16[512,2048]{1,0:T(8,128)(2,1)S(1)}, u32[]{:S(2)}, u32[]{:S(2)}) %collective-permute-start.55) | collective-permute-done | bytes 2097184 | tf_op jit(solution)/shard_map/ppermute | solution.py:80
  599.7 3.5 collective-permute-start.56
  604.5 9.9 %collective-permute-done.49.refs_2_ = bf16[3,64,2048]{2,1,0:T(8,128)(2,1)S(1)} collective-permute-done((bf16[3,64,2048]{2,1,0:T(8,128)(2,1)}, bf16[3,64,2048]{2,1,0:T(8,128)(2,1)S(1)}, u32[]{:S(2)}, u32[]{:S(2)}) %collective-permute-start.49) | collective-permute-done | bytes 786464 | tf_op jit(solution)/shard_map/ppermute | solution.py:80
  615.6 3.5 collective-permute-start.50
  619.4 17.5 %mixing_back.1 = f32[4,512,8]{2,1,0:T(8,128)} custom-call(bf16[3,512,2048]{2,1,0:T(8,128)(2,1)} %get-tuple-element.89.first, bf16[512,2048]{1,0:T(8,128)(2,1)} %get-tuple-element.76.refs_3_.last.refs_4_, bf16[8,512,2048]{2,1,0:T(8,128)(2,1)} %hist.3), custom_call_target="tpu_custom_call" | custom-call | tf_op jit(solution)/shard_map/mixing_back/pallas_call | solution.py:552
  648.2 5.5 all-to-all-start.4
  653.8 14.9 %collective-permute-done.50.refs_2_.refs_3_ = bf16[3,64,2048]{2,1,0:T(8,128)(2,1)} collective-permute-done((bf16[3,64,2048]{2,1,0:T(8,128)(2,1)}, bf16[3,64,2048]{2,1,0:T(8,128)(2,1)}, u32[]{:S(2)}, u32[]{:S(2)}) %collective-permute-start.50) | collective-permute-done | bytes 786464 | tf_op jit(solution)/shard_map/ppermute | solution.py:80
  675.1 5.4 collective-permute-start.59
  693.5 5.9 collective-permute-start.57
  720.4 4.2 collective-permute-done.62.refs_2_.refs_3_
  733.7 16.1 %all-gather.3 = f32[4096,45]{0,1:T(8,128)S(1)} all-gather(f32[512,45]{0,1:T(8,128)S(1)} %pad_maximum_fusion.5), channel_id=5, replica_groups=mesh['dp'=8,'stream'=4] {'dp'}, dimensions={0}, use_global_device_ids=true | all-gather | bytes 829440 | tf_op jit(solution)/shard_map/all_gather | solution.py:1001
  758.2 3.5 collective-permute-start.69
  761.7 11.1 %collective-permute-done.64.refs_2_ = bf16[3,64,2048]{2,1,0:T(8,128)(2,1)S(1)} collective-permute-done((bf16[3,64,2048]{2,1,0:T(8,128)(2,1)S(1)}, bf16[3,64,2048]{2,1,0:T(8,128)(2,1)S(1)}, u32[]{:S(2)}, u32[]{:S(2)}) %collective-permute-start.64) | collective-permute-done | bytes 786464 | tf_op jit(solution)/shard_map/ppermute | solution.py:80
  785.0 9.0 %collective-permute-done.69.refs_2_.refs_3_ = bf16[3,64,2048]{2,1,0:T(8,128)(2,1)S(1)} collective-permute-done((bf16[3,64,2048]{2,1,0:T(8,128)(2,1)}, bf16[3,64,2048]{2,1,0:T(8,128)(2,1)S(1)}, u32[]{:S(2)}, u32[]{:S(2)}) %collective-permute-start.69) | collective-permute-done | bytes 786464 | tf_op jit(solution)/shard_map/ppermute | solution.py:80
  799.2 11.1 %collective-permute-done.65.refs_2_.refs_3_ = bf16[3,64,2048]{2,1,0:T(8,128)(2,1)S(1)} collective-permute-done((bf16[3,64,2048]{2,1,0:T(8,128)(2,1)}, bf16[3,64,2048]{2,1,0:T(8,128)(2,1)S(1)}, u32[]{:S(2)}, u32[]{:S(2)}) %collective-permute-start.65) | collective-permute-done | bytes 786464 | tf_op jit(solution)/shard_map/ppermute | solution.py:80
  822.6 3.6 mix_final.8.refs_8_
  826.2 3.6 mix_final.9.refs_8_
  829.9 3.6 mix_final.10.refs_8_
  833.5 3.6 mix_final.11.refs_8_
  838.0 3.6 mix_final.12.refs_8_
  842.4 3.6 mix_final.13.refs_8_
  846.9 3.6 mix_final.14.refs_8_
  851.3 3.6 mix_final.15
  (412 shorter events, 260.0 us)
Async XLA Ops:
  7.2 175.2 %all-gather.6.cloned.1.call-start = ((), (), s32[]{:S(2)}) async-start(), calls=%async_computation.9 | async-start | bytes 2621440 | tf_op jit(solution)/shard_map/all_gather | solution.py:844
  7.3 82.3 %collective-permute-start = (bf16[3,256,512]{2,1,0:T(8,128)(2,1)}, bf16[3,256,512]{2,1,0:T(8,128)(2,1)}, u32[]{:S(2)}, u32[]{:S(2)}) collective-permute-start(bf16[3,256,512]{2,1,0:T(8,128)(2,1)} %param.18), channel_id=1, source_target_pairs={{0,8},{4,12},{8,0},{12,4},{16,24},{20,28},{24,16},{28,20},{1,9},{5... | collective-permute-start | bytes 2359304 | tf_op jit(solution)/shard_map/ppermute | solution.py:76
  8.8 83.6 %collective-permute-start.1 = (bf16[3,256,512]{2,1,0:T(8,128)(2,1)}, bf16[3,256,512]{2,1,0:T(8,128)(2,1)}, u32[]{:S(2)}, u32[]{:S(2)}) collective-permute-start(bf16[3,256,512]{2,1,0:T(8,128)(2,1)} %param.18), channel_id=1, source_target_pairs={{0,16},{4,20},{8,24},{12,28},{16,0},{20,4},{24,8},{28,12},{1,17},{... | collective-permute-start | bytes 2359304 | tf_op jit(solution)/shard_map/ppermute | solution.py:76
  10.3 84.2 %collective-permute-start.2 = (bf16[3,256,512]{2,1,0:T(8,128)(2,1)}, bf16[3,256,512]{2,1,0:T(8,128)(2,1)S(1)}, u32[]{:S(2)}, u32[]{:S(2)}) collective-permute-start(bf16[3,256,512]{2,1,0:T(8,128)(2,1)} %param.18), channel_id=1, source_target_pairs={{0,24},{4,28},{8,16},{12,20},{16,8},{20,12},{24,0},{28,4},{1,25},{... | collective-permute-start | bytes 2359304 | tf_op jit(solution)/shard_map/ppermute | solution.py:76
  10.8 61.9 %collective-permute-start.17 = (bf16[512,256]{1,0:T(8,128)(2,1)}, bf16[512,256]{1,0:T(8,128)(2,1)S(1)}, u32[]{:S(2)}, u32[]{:S(2)}) collective-permute-start(bf16[512,256]{1,0:T(8,128)(2,1)} %param.19), channel_id=1, source_target_pairs={{0,8},{4,12},{8,0},{12,4},{16,24},{20,28},{24,16},{28,20},{1,9},{5... | collective-permute-start | bytes 786440 | tf_op jit(solution)/shard_map/ppermute | solution.py:76
  12.3 60.4 %collective-permute-start.18 = (bf16[512,256]{1,0:T(8,128)(2,1)}, bf16[512,256]{1,0:T(8,128)(2,1)S(1)}, u32[]{:S(2)}, u32[]{:S(2)}) collective-permute-start(bf16[512,256]{1,0:T(8,128)(2,1)} %param.19), channel_id=1, source_target_pairs={{0,16},{4,20},{8,24},{12,28},{16,0},{20,4},{24,8},{28,12},{1,17},{... | collective-permute-start | bytes 786440 | tf_op jit(solution)/shard_map/ppermute | solution.py:76
  89.1 28.3 %collective-permute-start.8 = (bf16[256,2048]{1,0:T(8,128)(2,1)S(1)}, bf16[256,2048]{1,0:T(8,128)(2,1)S(1)}, u32[]{:S(2)}, u32[]{:S(2)}) collective-permute-start(bf16[256,2048]{1,0:T(8,128)(2,1)S(1)} %copy-done.28), channel_id=1, source_target_pairs={{0,8},{4,12},{8,0},{12,4},{16,24},{20,28},{24,16},{28,20},{1,9},{5... | collective-permute-start | bytes 3145736 | tf_op jit(solution)/shard_map/ppermute | solution.py:76
  89.6 25.1 %collective-permute-start.9 = (bf16[256,2048]{1,0:T(8,128)(2,1)S(1)}, bf16[256,2048]{1,0:T(8,128)(2,1)}, u32[]{:S(2)}, u32[]{:S(2)}) collective-permute-start(bf16[256,2048]{1,0:T(8,128)(2,1)S(1)} %copy-done.28), channel_id=1, source_target_pairs={{0,16},{4,20},{8,24},{12,28},{16,0},{20,4},{24,8},{28,12},{1,17},{... | collective-permute-start | bytes 3145736 | tf_op jit(solution)/shard_map/ppermute | solution.py:76
  92.4 40.7 %collective-permute-start.12 = (bf16[256,2048]{1,0:T(8,128)(2,1)S(1)}, bf16[256,2048]{1,0:T(8,128)(2,1)S(1)}, u32[]{:S(2)}, u32[]{:S(2)}) collective-permute-start(bf16[256,2048]{1,0:T(8,128)(2,1)S(1)} %copy-done.28), channel_id=1, source_target_pairs={{0,4},{4,0},{8,12},{12,8},{16,20},{20,16},{24,28},{28,24},{1,5},{5... | collective-permute-start | bytes 3145736 | tf_op jit(solution)/shard_map/ppermute | solution.py:76
  94.5 39.6 %collective-permute-start.4 = (bf16[3,256,512]{2,1,0:T(8,128)(2,1)}, bf16[3,256,512]{2,1,0:T(8,128)(2,1)S(1)}, u32[]{:S(2)}, u32[]{:S(2)}) collective-permute-start(bf16[3,256,512]{2,1,0:T(8,128)(2,1)} %collective-permute-done), channel_id=1, source_target_pairs={{0,4},{4,0},{8,12},{12,8},{16,20},{20,16},{24,28},{28,24},{1,5},{5... | collective-permute-start | bytes 2359304 | tf_op jit(solution)/shard_map/ppermute | solution.py:76
  95.9 39.7 %collective-permute-start.5 = (bf16[3,256,512]{2,1,0:T(8,128)(2,1)}, bf16[3,256,512]{2,1,0:T(8,128)(2,1)S(1)}, u32[]{:S(2)}, u32[]{:S(2)}) collective-permute-start(bf16[3,256,512]{2,1,0:T(8,128)(2,1)} %collective-permute-done.1), channel_id=1, source_target_pairs={{0,4},{4,0},{8,12},{12,8},{16,20},{20,16},{24,28},{28,24},{1,5},{5... | collective-permute-start | bytes 2359304 | tf_op jit(solution)/shard_map/ppermute | solution.py:76
  130.7 47.1 %collective-permute-start.13 = (bf16[256,2048]{1,0:T(8,128)(2,1)S(1)}, bf16[256,2048]{1,0:T(8,128)(2,1)}, u32[]{:S(2)}, u32[]{:S(2)}) collective-permute-start(bf16[256,2048]{1,0:T(8,128)(2,1)S(1)} %collective-permute-done.8), channel_id=1, source_target_pairs={{0,4},{4,0},{8,12},{12,8},{16,20},{20,16},{24,28},{28,24},{1,5},{5... | collective-permute-start | bytes 3145736 | tf_op jit(solution)/shard_map/ppermute | solution.py:76
  133.1 47.1 %collective-permute-start.14 = (bf16[256,2048]{1,0:T(8,128)(2,1)}, bf16[256,2048]{1,0:T(8,128)(2,1)}, u32[]{:S(2)}, u32[]{:S(2)}) collective-permute-start(bf16[256,2048]{1,0:T(8,128)(2,1)} %collective-permute-done.9), channel_id=1, source_target_pairs={{0,4},{4,0},{8,12},{12,8},{16,20},{20,16},{24,28},{28,24},{1,5},{5... | collective-permute-start | bytes 3145736 | tf_op jit(solution)/shard_map/ppermute | solution.py:76
  134.2 51.5 %collective-permute-start.15 = (bf16[128,2048]{1,0:T(8,128)(2,1)}, bf16[128,2048]{1,0:T(8,128)(2,1)}, u32[]{:S(2)}, u32[]{:S(2)}) collective-permute-start(bf16[128,2048]{1,0:T(8,128)(2,1)} %collective-permute-done.10), channel_id=1, source_target_pairs={{0,4},{4,0},{8,12},{12,8},{16,20},{20,16},{24,28},{28,24},{1,5},{5... | collective-permute-start | bytes 1572872 | tf_op jit(solution)/shard_map/ppermute | solution.py:76
  135.6 51.9 %collective-permute-start.16 = (bf16[128,2048]{1,0:T(8,128)(2,1)}, bf16[128,2048]{1,0:T(8,128)(2,1)}, u32[]{:S(2)}, u32[]{:S(2)}) collective-permute-start(bf16[128,2048]{1,0:T(8,128)(2,1)} %collective-permute-done.11), channel_id=1, source_target_pairs={{0,4},{4,0},{8,12},{12,8},{16,20},{20,16},{24,28},{28,24},{1,5},{5... | collective-permute-start | bytes 1572872 | tf_op jit(solution)/shard_map/ppermute | solution.py:76
  146.4 36.1 %all-to-all-start = ((bf16[8,3,256,128]{3,2,1,0:T(8,128)(2,1)}), bf16[8,3,256,128]{3,2,1,0:T(8,128)(2,1)S(1)}, u32[]{:S(2)}, u32[]{:S(2)}) async-start(bf16[8,3,256,128]{3,2,1,0:T(8,128)(2,1)} %project.1), calls=%async_computation | async-start | bytes 3145728 | tf_op jit(solution)/shard_map/all_to_all | solution.py:879
  182.4 29.5 %collective-permute-start.26 = (bf16[2048,256]{1,0:T(8,128)(2,1)}, bf16[2048,256]{1,0:T(8,128)(2,1)}, u32[]{:S(2)}, u32[]{:S(2)}) collective-permute-start(bf16[2048,256]{1,0:T(8,128)(2,1)} %param.21), channel_id=1, source_target_pairs={{0,8},{4,12},{8,0},{12,4},{16,24},{20,28},{24,16},{28,20},{1,9},{5... | collective-permute-start | bytes 3145736 | tf_op jit(solution)/shard_map/ppermute | solution.py:76
  184.0 25.4 %collective-permute-start.27 = (bf16[2048,256]{1,0:T(8,128)(2,1)}, bf16[2048,256]{1,0:T(8,128)(2,1)}, u32[]{:S(2)}, u32[]{:S(2)}) collective-permute-start(bf16[2048,256]{1,0:T(8,128)(2,1)} %param.21), channel_id=1, source_target_pairs={{0,16},{4,20},{8,24},{12,28},{16,0},{20,4},{24,8},{28,12},{1,17},{... | collective-permute-start | bytes 3145736 | tf_op jit(solution)/shard_map/ppermute | solution.py:76
  185.6 29.5 %collective-permute-start.7 = (bf16[8,2,256,128]{3,2,1,0:T(8,128)(2,1)}, bf16[8,2,256,128]{3,2,1,0:T(8,128)(2,1)S(1)}, u32[]{:S(2)}, u32[]{:S(2)}) collective-permute-start(bf16[8,2,256,128]{3,2,1,0:T(8,128)(2,1)} %slice.120), channel_id=1, source_target_pairs={{0,4},{4,0},{8,12},{12,8},{16,20},{20,16},{24,28},{28,24},{1,5},{5... | collective-permute-start | bytes 3145736 | tf_op jit(solution)/shard_map/ppermute | solution.py:76
  199.5 55.7 %collective-permute-start.30 = (bf16[2048,256]{1,0:T(8,128)(2,1)}, bf16[2048,256]{1,0:T(8,128)(2,1)}, u32[]{:S(2)}, u32[]{:S(2)}) collective-permute-start(bf16[2048,256]{1,0:T(8,128)(2,1)} %param.21), channel_id=1, source_target_pairs={{0,4},{4,0},{8,12},{12,8},{16,20},{20,16},{24,28},{28,24},{1,5},{5... | collective-permute-start | bytes 3145736 | tf_op jit(solution)/shard_map/ppermute | solution.py:76
  211.3 39.6 %collective-permute-start.28 = (bf16[1024,256]{1,0:T(8,128)(2,1)}, bf16[1024,256]{1,0:T(8,128)(2,1)}, u32[]{:S(2)}, u32[]{:S(2)}) collective-permute-start(bf16[1024,256]{1,0:T(8,128)(2,1)} %slice.158), channel_id=1, source_target_pairs={{0,8},{4,12},{8,0},{12,4},{16,24},{20,28},{24,16},{28,20},{1,9},{5... | collective-permute-start | bytes 1572872 | tf_op jit(solution)/shard_map/ppermute | solution.py:76
  213.8 37.1 %collective-permute-start.29 = (bf16[1024,256]{1,0:T(8,128)(2,1)}, bf16[1024,256]{1,0:T(8,128)(2,1)}, u32[]{:S(2)}, u32[]{:S(2)}) collective-permute-start(bf16[1024,256]{1,0:T(8,128)(2,1)} %slice.159), channel_id=1, source_target_pairs={{0,16},{4,20},{8,24},{12,28},{16,0},{20,4},{24,8},{28,12},{1,17},{... | collective-permute-start | bytes 1572872 | tf_op jit(solution)/shard_map/ppermute | solution.py:76
  239.8 17.6 %collective-permute-start.31 = (bf16[2048,256]{1,0:T(8,128)(2,1)}, bf16[2048,256]{1,0:T(8,128)(2,1)S(1)}, u32[]{:S(2)}, u32[]{:S(2)}) collective-permute-start(bf16[2048,256]{1,0:T(8,128)(2,1)} %collective-permute-done.26), channel_id=1, source_target_pairs={{0,4},{4,0},{8,12},{12,8},{16,20},{20,16},{24,28},{28,24},{1,5},{5... | collective-permute-start | bytes 3145736 | tf_op jit(solution)/shard_map/ppermute | solution.py:76
  241.0 17.5 %collective-permute-start.32 = (bf16[2048,256]{1,0:T(8,128)(2,1)}, bf16[2048,256]{1,0:T(8,128)(2,1)S(1)}, u32[]{:S(2)}, u32[]{:S(2)}) collective-permute-start(bf16[2048,256]{1,0:T(8,128)(2,1)} %collective-permute-done.27), channel_id=1, source_target_pairs={{0,4},{4,0},{8,12},{12,8},{16,20},{20,16},{24,28},{28,24},{1,5},{5... | collective-permute-start | bytes 3145736 | tf_op jit(solution)/shard_map/ppermute | solution.py:76
  277.1 16.7 %collective-permute-start.35 = (bf16[128,2048]{1,0:T(8,128)(2,1)S(1)}, bf16[128,2048]{1,0:T(8,128)(2,1)S(1)}, u32[]{:S(2)}, u32[]{:S(2)}) collective-permute-start(bf16[128,2048]{1,0:T(8,128)(2,1)S(1)} %get-tuple-element.170), channel_id=1, source_target_pairs={{0,1},{3,2},{4,5},{7,6},{8,9},{11,10},{12,13},{15,14},{16,17},{19,... | collective-permute-start | bytes 1572872 | tf_op jit(solution)/shard_map/ppermute | solution.py:80
  278.4 26.6 %collective-permute-start.38 = (bf16[128,2048]{1,0:T(8,128)(2,1)S(1)}, bf16[128,2048]{1,0:T(8,128)(2,1)S(1)}, u32[]{:S(2)}, u32[]{:S(2)}) collective-permute-start(bf16[128,2048]{1,0:T(8,128)(2,1)S(1)} %get-tuple-element.169), channel_id=1, source_target_pairs={{0,1},{3,2},{4,5},{7,6},{8,9},{11,10},{12,13},{15,14},{16,17},{19,... | collective-permute-start | bytes 1572872 | tf_op jit(solution)/shard_map/ppermute | solution.py:80
  293.8 21.5 %collective-permute-start.41 = (bf16[128,2048]{1,0:T(8,128)(2,1)S(1)}, bf16[128,2048]{1,0:T(8,128)(2,1)S(1)}, u32[]{:S(2)}, u32[]{:S(2)}) collective-permute-start(bf16[128,2048]{1,0:T(8,128)(2,1)S(1)} %get-tuple-element.65), channel_id=1, source_target_pairs={{0,1},{3,2},{4,5},{7,6},{8,9},{11,10},{12,13},{15,14},{16,17},{19,... | collective-permute-start | bytes 1572872 | tf_op jit(solution)/shard_map/ppermute | solution.py:80
  334.8 25.0 %collective-permute-start.42 = (bf16[128,2048]{1,0:T(8,128)(2,1)S(1)}, bf16[128,2048]{1,0:T(8,128)(2,1)S(1)}, u32[]{:S(2)}, u32[]{:S(2)}) collective-permute-start(bf16[128,2048]{1,0:T(8,128)(2,1)S(1)} %get-tuple-element.166), channel_id=1, source_target_pairs={{1,2},{2,1},{5,6},{6,5},{9,10},{10,9},{13,14},{14,13},{17,18},{18,... | collective-permute-start | bytes 1572872 | tf_op jit(solution)/shard_map/ppermute | solution.py:80
  344.6 23.7 %collective-permute-start.45 = (bf16[128,2048]{1,0:T(8,128)(2,1)S(1)}, bf16[128,2048]{1,0:T(8,128)(2,1)S(1)}, u32[]{:S(2)}, u32[]{:S(2)}) collective-permute-start(bf16[128,2048]{1,0:T(8,128)(2,1)S(1)} %fusion.9), channel_id=1, source_target_pairs={{1,2},{2,1},{5,6},{6,5},{9,10},{10,9},{13,14},{14,13},{17,18},{18,... | collective-permute-start | bytes 1572872 | tf_op jit(solution)/shard_map/ppermute | solution.py:80
  370.7 23.5 %collective-permute-start.40 = (bf16[128,2048]{1,0:T(8,128)(2,1)S(1)}, bf16[128,2048]{1,0:T(8,128)(2,1)S(1)}, u32[]{:S(2)}, u32[]{:S(2)}) collective-permute-start(bf16[128,2048]{1,0:T(8,128)(2,1)S(1)} %get-tuple-element.163), channel_id=1, source_target_pairs={{1,0},{2,3},{5,4},{6,7},{9,8},{10,11},{13,12},{14,15},{17,16},{18,... | collective-permute-start | bytes 1572872 | tf_op jit(solution)/shard_map/ppermute | solution.py:80
  372.1 33.4 %collective-permute-start.43 = (bf16[128,2048]{1,0:T(8,128)(2,1)S(1)}, bf16[128,2048]{1,0:T(8,128)(2,1)S(1)}, u32[]{:S(2)}, u32[]{:S(2)}) collective-permute-start(bf16[128,2048]{1,0:T(8,128)(2,1)S(1)} %get-tuple-element.162), channel_id=1, source_target_pairs={{1,0},{2,3},{5,4},{6,7},{9,8},{10,11},{13,12},{14,15},{17,16},{18,... | collective-permute-start | bytes 1572872 | tf_op jit(solution)/shard_map/ppermute | solution.py:80
  373.4 40.0 %collective-permute-start.46 = (bf16[128,2048]{1,0:T(8,128)(2,1)S(1)}, bf16[128,2048]{1,0:T(8,128)(2,1)S(1)}, u32[]{:S(2)}, u32[]{:S(2)}) collective-permute-start(bf16[128,2048]{1,0:T(8,128)(2,1)S(1)} %get-tuple-element.161), channel_id=1, source_target_pairs={{1,0},{2,3},{5,4},{6,7},{9,8},{10,11},{13,12},{14,15},{17,16},{18,... | collective-permute-start | bytes 1572872 | tf_op jit(solution)/shard_map/ppermute | solution.py:80
  428.0 16.9 %all-to-all-start.2 = ((bf16[8,256,128]{2,1,0:T(8,128)(2,1)}), bf16[8,256,128]{2,1,0:T(8,128)(2,1)S(1)}, u32[]{:S(2)}, u32[]{:S(2)}) async-start(bf16[8,256,128]{2,1,0:T(8,128)(2,1)} %bitcast.57), calls=%async_computation.2 | async-start | bytes 1048576 | tf_op jit(solution)/shard_map/all_to_all | solution.py:947
  431.5 389.3 %reduce-scatter.7.cloned.1.call-start = ((), (), s32[]{:S(2)}) async-start(), calls=%async_computation.11 | async-start | bytes 2359296 | tf_op jit(solution)/shard_map/reduce_scatter | solution.py:974
  487.1 30.6 %all-to-all-start.3 = ((bf16[8,3,256,128]{3,2,1,0:T(8,128)(2,1)}), bf16[8,3,256,128]{3,2,1,0:T(8,128)(2,1)}, u32[]{:S(2)}, u32[]{:S(2)}) async-start(bf16[8,3,256,128]{3,2,1,0:T(8,128)(2,1)} %pad_maximum_fusion.1), calls=%async_computation.3 | async-start | bytes 3145728 | tf_op jit(solution)/shard_map/all_to_all | solution.py:953
  491.4 363.5 %reduce-scatter.5.cloned.1.call-start = ((), (), s32[]{:S(2)}) async-start(), calls=%async_computation.10 | async-start | bytes 7077888 | tf_op jit(solution)/shard_map/reduce_scatter | solution.py:976
  534.9 322.5 %reduce-scatter.11.cloned.1.call-start = ((), (), s32[]{:S(2)}) async-start(), calls=%async_computation.13 | async-start | bytes 9437184 | tf_op jit(solution)/shard_map/reduce_scatter | solution.py:975
  535.5 324.6 %reduce-scatter.9.cloned.1.call-start = ((), (), s32[]{:S(2)}) async-start(), calls=%async_computation.12 | async-start | bytes 9437184 | tf_op jit(solution)/shard_map/reduce_scatter | solution.py:977
  546.8 50.7 %collective-permute-start.55 = (bf16[512,2048]{1,0:T(8,128)(2,1)S(1)}, bf16[512,2048]{1,0:T(8,128)(2,1)S(1)}, u32[]{:S(2)}, u32[]{:S(2)}) collective-permute-start(bf16[512,2048]{1,0:T(8,128)(2,1)S(1)} %copy-done), channel_id=1, source_target_pairs={{0,1},{3,2},{4,5},{7,6},{8,9},{11,10},{12,13},{15,14},{16,17},{19,... | collective-permute-start | bytes 6291464 | tf_op jit(solution)/shard_map/ppermute | solution.py:80
  548.5 65.9 %collective-permute-start.49 = (bf16[3,64,2048]{2,1,0:T(8,128)(2,1)}, bf16[3,64,2048]{2,1,0:T(8,128)(2,1)S(1)}, u32[]{:S(2)}, u32[]{:S(2)}) collective-permute-start(bf16[3,64,2048]{2,1,0:T(8,128)(2,1)} %get-tuple-element.83.refs_1_), channel_id=1, source_target_pairs={{0,1},{3,2},{4,5},{7,6},{8,9},{11,10},{12,13},{15,14},{16,17},{19,... | collective-permute-start | bytes 2359304 | tf_op jit(solution)/shard_map/ppermute | solution.py:80
  599.7 71.2 %collective-permute-start.56 = (bf16[512,2048]{1,0:T(8,128)(2,1)}, bf16[512,2048]{1,0:T(8,128)(2,1)S(1)}, u32[]{:S(2)}, u32[]{:S(2)}) collective-permute-start(bf16[512,2048]{1,0:T(8,128)(2,1)} %add_convert_fusion), channel_id=1, source_target_pairs={{1,2},{2,1},{5,6},{6,5},{9,10},{10,9},{13,14},{14,13},{17,18},{18,... | collective-permute-start | bytes 6291464 | tf_op jit(solution)/shard_map/ppermute | solution.py:80
  603.2 39.3 %collective-permute-start.48 = (bf16[3,64,2048]{2,1,0:T(8,128)(2,1)S(1)}, bf16[3,64,2048]{2,1,0:T(8,128)(2,1)}, u32[]{:S(2)}, u32[]{:S(2)}) collective-permute-start(bf16[3,64,2048]{2,1,0:T(8,128)(2,1)S(1)} %copy-done.12), channel_id=1, source_target_pairs={{0,1},{3,2},{4,5},{7,6},{8,9},{11,10},{12,13},{15,14},{16,17},{19,... | collective-permute-start | bytes 2359304 | tf_op jit(solution)/shard_map/ppermute | solution.py:80
  615.6 53.1 %collective-permute-start.50 = (bf16[3,64,2048]{2,1,0:T(8,128)(2,1)}, bf16[3,64,2048]{2,1,0:T(8,128)(2,1)}, u32[]{:S(2)}, u32[]{:S(2)}) collective-permute-start(bf16[3,64,2048]{2,1,0:T(8,128)(2,1)} %add_convert_fusion.9), channel_id=1, source_target_pairs={{1,2},{2,1},{5,6},{6,5},{9,10},{10,9},{13,14},{14,13},{17,18},{18,... | collective-permute-start | bytes 2359304 | tf_op jit(solution)/shard_map/ppermute | solution.py:80
  641.2 41.7 %collective-permute-start.52 = (bf16[3,64,2048]{2,1,0:T(8,128)(2,1)}, bf16[3,64,2048]{2,1,0:T(8,128)(2,1)}, u32[]{:S(2)}, u32[]{:S(2)}) collective-permute-start(bf16[3,64,2048]{2,1,0:T(8,128)(2,1)} %get-tuple-element.86.refs_1_), channel_id=1, source_target_pairs={{0,1},{3,2},{4,5},{7,6},{8,9},{11,10},{12,13},{15,14},{16,17},{19,... | collective-permute-start | bytes 2359304 | tf_op jit(solution)/shard_map/ppermute | solution.py:80
  644.7 44.0 %collective-permute-start.54 = (bf16[3,64,2048]{2,1,0:T(8,128)(2,1)}, bf16[3,64,2048]{2,1,0:T(8,128)(2,1)}, u32[]{:S(2)}, u32[]{:S(2)}) collective-permute-start(bf16[3,64,2048]{2,1,0:T(8,128)(2,1)} %add_convert_fusion.7), channel_id=1, source_target_pairs={{1,2},{2,1},{5,6},{6,5},{9,10},{10,9},{13,14},{14,13},{17,18},{18,... | collective-permute-start | bytes 2359304 | tf_op jit(solution)/shard_map/ppermute | solution.py:80
  648.2 34.5 %all-to-all-start.4 = ((f32[4,512,16]{1,2,0:T(8,128)}), f32[4,512,16]{1,2,0:T(8,128)S(1)}, u32[]{:S(2)}, u32[]{:S(2)}) async-start(f32[4,512,16]{1,2,0:T(8,128)} %maximum_maximum_fusion), calls=%async_computation.4 | async-start | bytes 262144 | tf_op jit(solution)/shard_map/all_to_all | solution.py:994
  668.6 30.7 %collective-permute-start.51 = (bf16[3,64,2048]{2,1,0:T(8,128)(2,1)}, bf16[3,64,2048]{2,1,0:T(8,128)(2,1)}, u32[]{:S(2)}, u32[]{:S(2)}) collective-permute-start(bf16[3,64,2048]{2,1,0:T(8,128)(2,1)} %get-tuple-element.84.refs_1_), channel_id=1, source_target_pairs={{0,1},{3,2},{4,5},{7,6},{8,9},{11,10},{12,13},{15,14},{16,17},{19,... | collective-permute-start | bytes 2359304 | tf_op jit(solution)/shard_map/ppermute | solution.py:80
  685.5 20.4 %collective-permute-start.53 = (bf16[3,64,2048]{2,1,0:T(8,128)(2,1)}, bf16[3,64,2048]{2,1,0:T(8,128)(2,1)S(1)}, u32[]{:S(2)}, u32[]{:S(2)}) collective-permute-start(bf16[3,64,2048]{2,1,0:T(8,128)(2,1)} %add_convert_fusion.8), channel_id=1, source_target_pairs={{1,2},{2,1},{5,6},{6,5},{9,10},{10,9},{13,14},{14,13},{17,18},{18,... | collective-permute-start | bytes 2359304 | tf_op jit(solution)/shard_map/ppermute | solution.py:80
  688.8 24.4 %collective-permute-start.60 = (bf16[3,64,2048]{2,1,0:T(8,128)(2,1)S(1)}, bf16[3,64,2048]{2,1,0:T(8,128)(2,1)}, u32[]{:S(2)}, u32[]{:S(2)}) collective-permute-start(bf16[3,64,2048]{2,1,0:T(8,128)(2,1)S(1)} %copy-done.11), channel_id=1, source_target_pairs={{0,1},{3,2},{4,5},{7,6},{8,9},{11,10},{12,13},{15,14},{16,17},{19,... | collective-permute-start | bytes 2359304 | tf_op jit(solution)/shard_map/ppermute | solution.py:80
  693.5 18.4 %collective-permute-start.57 = (bf16[2,64,2048]{2,1,0:T(8,128)(2,1)}, bf16[2,64,2048]{2,1,0:T(8,128)(2,1)}, u32[]{:S(2)}, u32[]{:S(2)}) collective-permute-start(bf16[2,64,2048]{2,1,0:T(8,128)(2,1)} %mix_inward.8), channel_id=1, source_target_pairs={{1,0},{2,3},{5,4},{6,7},{9,8},{10,11},{13,12},{14,15},{17,16},{18,... | collective-permute-start | bytes 1572872 | tf_op jit(solution)/shard_map/ppermute | solution.py:80
  701.9 22.7 %collective-permute-start.62 = (bf16[3,64,2048]{2,1,0:T(8,128)(2,1)}, bf16[3,64,2048]{2,1,0:T(8,128)(2,1)}, u32[]{:S(2)}, u32[]{:S(2)}) collective-permute-start(bf16[3,64,2048]{2,1,0:T(8,128)(2,1)} %add_convert_fusion.5), channel_id=1, source_target_pairs={{1,2},{2,1},{5,6},{6,5},{9,10},{10,9},{13,14},{14,13},{17,18},{18,... | collective-permute-start | bytes 2359304 | tf_op jit(solution)/shard_map/ppermute | solution.py:80
  709.8 22.6 %collective-permute-start.67 = (bf16[2,64,2048]{2,1,0:T(8,128)(2,1)}, bf16[2,64,2048]{2,1,0:T(8,128)(2,1)}, u32[]{:S(2)}, u32[]{:S(2)}) collective-permute-start(bf16[2,64,2048]{2,1,0:T(8,128)(2,1)} %mix_inward.12), channel_id=1, source_target_pairs={{1,0},{2,3},{5,4},{6,7},{9,8},{10,11},{13,12},{14,15},{17,16},{18,... | collective-permute-start | bytes 1572872 | tf_op jit(solution)/shard_map/ppermute | solution.py:80
  711.9 39.1 %collective-permute-start.58 = (bf16[3,64,2048]{2,1,0:T(8,128)(2,1)S(1)}, bf16[3,64,2048]{2,1,0:T(8,128)(2,1)}, u32[]{:S(2)}, u32[]{:S(2)}) collective-permute-start(bf16[3,64,2048]{2,1,0:T(8,128)(2,1)S(1)} %copy-done.10), channel_id=1, source_target_pairs={{0,1},{3,2},{4,5},{7,6},{8,9},{11,10},{12,13},{15,14},{16,17},{19,... | collective-permute-start | bytes 2359304 | tf_op jit(solution)/shard_map/ppermute | solution.py:80
  715.6 35.4 %collective-permute-start.61 = (bf16[3,64,2048]{2,1,0:T(8,128)(2,1)}, bf16[3,64,2048]{2,1,0:T(8,128)(2,1)S(1)}, u32[]{:S(2)}, u32[]{:S(2)}) collective-permute-start(bf16[3,64,2048]{2,1,0:T(8,128)(2,1)} %add_convert_fusion.6), channel_id=1, source_target_pairs={{1,2},{2,1},{5,6},{6,5},{9,10},{10,9},{13,14},{14,13},{17,18},{18,... | collective-permute-start | bytes 2359304 | tf_op jit(solution)/shard_map/ppermute | solution.py:80
  727.4 23.6 %collective-permute-start.63 = (bf16[2,64,2048]{2,1,0:T(8,128)(2,1)}, bf16[2,64,2048]{2,1,0:T(8,128)(2,1)}, u32[]{:S(2)}, u32[]{:S(2)}) collective-permute-start(bf16[2,64,2048]{2,1,0:T(8,128)(2,1)} %mix_inward.10), channel_id=1, source_target_pairs={{1,0},{2,3},{5,4},{6,7},{9,8},{10,11},{13,12},{14,15},{17,16},{18,... | collective-permute-start | bytes 1572872 | tf_op jit(solution)/shard_map/ppermute | solution.py:80
  732.4 24.6 %collective-permute-start.68 = (bf16[3,64,2048]{2,1,0:T(8,128)(2,1)S(1)}, bf16[3,64,2048]{2,1,0:T(8,128)(2,1)S(1)}, u32[]{:S(2)}, u32[]{:S(2)}) collective-permute-start(bf16[3,64,2048]{2,1,0:T(8,128)(2,1)S(1)} %copy-done.9), channel_id=1, source_target_pairs={{0,1},{3,2},{4,5},{7,6},{8,9},{11,10},{12,13},{15,14},{16,17},{19,... | collective-permute-start | bytes 2359304 | tf_op jit(solution)/shard_map/ppermute | solution.py:80
  751.0 21.7 %collective-permute-start.64 = (bf16[3,64,2048]{2,1,0:T(8,128)(2,1)S(1)}, bf16[3,64,2048]{2,1,0:T(8,128)(2,1)S(1)}, u32[]{:S(2)}, u32[]{:S(2)}) collective-permute-start(bf16[3,64,2048]{2,1,0:T(8,128)(2,1)S(1)} %copy-done.8), channel_id=1, source_target_pairs={{0,1},{3,2},{4,5},{7,6},{8,9},{11,10},{12,13},{15,14},{16,17},{19,... | collective-permute-start | bytes 2359304 | tf_op jit(solution)/shard_map/ppermute | solution.py:80
  754.7 26.2 %collective-permute-start.71 = (bf16[3,64,2048]{2,1,0:T(8,128)(2,1)}, bf16[3,64,2048]{2,1,0:T(8,128)(2,1)}, u32[]{:S(2)}, u32[]{:S(2)}) collective-permute-start(bf16[3,64,2048]{2,1,0:T(8,128)(2,1)} %add_convert_fusion.2), channel_id=1, source_target_pairs={{1,2},{2,1},{5,6},{6,5},{9,10},{10,9},{13,14},{14,13},{17,18},{18,... | collective-permute-start | bytes 2359304 | tf_op jit(solution)/shard_map/ppermute | solution.py:80
  758.2 35.8 %collective-permute-start.69 = (bf16[3,64,2048]{2,1,0:T(8,128)(2,1)}, bf16[3,64,2048]{2,1,0:T(8,128)(2,1)S(1)}, u32[]{:S(2)}, u32[]{:S(2)}) collective-permute-start(bf16[3,64,2048]{2,1,0:T(8,128)(2,1)} %add_convert_fusion.3), channel_id=1, source_target_pairs={{1,2},{2,1},{5,6},{6,5},{9,10},{10,9},{13,14},{14,13},{17,18},{18,... | collective-permute-start | bytes 2359304 | tf_op jit(solution)/shard_map/ppermute | solution.py:80
  773.9 36.4 %collective-permute-start.65 = (bf16[3,64,2048]{2,1,0:T(8,128)(2,1)}, bf16[3,64,2048]{2,1,0:T(8,128)(2,1)S(1)}, u32[]{:S(2)}, u32[]{:S(2)}) collective-permute-start(bf16[3,64,2048]{2,1,0:T(8,128)(2,1)} %add_convert_fusion.4), channel_id=1, source_target_pairs={{1,2},{2,1},{5,6},{6,5},{9,10},{10,9},{13,14},{14,13},{17,18},{18,... | collective-permute-start | bytes 2359304 | tf_op jit(solution)/shard_map/ppermute | solution.py:80
  779.3 57.9 %collective-permute-start.73 = (bf16[2,64,2048]{2,1,0:T(8,128)(2,1)}, bf16[2,64,2048]{2,1,0:T(8,128)(2,1)S(1)}, u32[]{:S(2)}, u32[]{:S(2)}) collective-permute-start(bf16[2,64,2048]{2,1,0:T(8,128)(2,1)} %mix_inward.15), channel_id=1, source_target_pairs={{1,0},{2,3},{5,4},{6,7},{9,8},{10,11},{13,12},{14,15},{17,16},{18,... | collective-permute-start | bytes 1572872 | tf_op jit(solution)/shard_map/ppermute | solution.py:80
  783.7 57.9 %collective-permute-start.72 = (bf16[2,64,2048]{2,1,0:T(8,128)(2,1)}, bf16[2,64,2048]{2,1,0:T(8,128)(2,1)S(1)}, u32[]{:S(2)}, u32[]{:S(2)}) collective-permute-start(bf16[2,64,2048]{2,1,0:T(8,128)(2,1)} %mix_inward.14), channel_id=1, source_target_pairs={{1,0},{2,3},{5,4},{6,7},{9,8},{10,11},{13,12},{14,15},{17,16},{18,... | collective-permute-start | bytes 1572872 | tf_op jit(solution)/shard_map/ppermute | solution.py:80
  797.7 48.3 %collective-permute-start.70 = (bf16[2,64,2048]{2,1,0:T(8,128)(2,1)}, bf16[2,64,2048]{2,1,0:T(8,128)(2,1)S(1)}, u32[]{:S(2)}, u32[]{:S(2)}) collective-permute-start(bf16[2,64,2048]{2,1,0:T(8,128)(2,1)} %mix_inward.13), channel_id=1, source_target_pairs={{1,0},{2,3},{5,4},{6,7},{9,8},{10,11},{13,12},{14,15},{17,16},{18,... | collective-permute-start | bytes 1572872 | tf_op jit(solution)/shard_map/ppermute | solution.py:80
  813.9 36.6 %collective-permute-start.66 = (bf16[2,64,2048]{2,1,0:T(8,128)(2,1)}, bf16[2,64,2048]{2,1,0:T(8,128)(2,1)S(1)}, u32[]{:S(2)}, u32[]{:S(2)}) collective-permute-start(bf16[2,64,2048]{2,1,0:T(8,128)(2,1)} %mix_inward.11), channel_id=1, source_target_pairs={{1,0},{2,3},{5,4},{6,7},{9,8},{10,11},{13,12},{14,15},{17,16},{18,... | collective-permute-start | bytes 1572872 | tf_op jit(solution)/shard_map/ppermute | solution.py:80
  (77 other events, 1284.6 us)
Sparse Core Ops, SparseCore 0:
  14.0 44.3 all-gather.5
  481.5 48.9 reduce-scatter.6
  535.0 62.8 reduce-scatter.4
  601.3 71.2 reduce-scatter.10
  675.9 74.6 reduce-scatter.8

commit v3 on v2

--- a/solution.py
+++ b/solution.py
@@ -80,6 +80,12 @@
     return lax.ppermute(shard, "stream", pairs)
 
 
+def cost(microseconds):
+    return pl.CostEstimate(
+        flops=int(microseconds * 0.9e9), bytes_accessed=int(microseconds * 3e6), transcendentals=0
+    )
+
+
 def after(value, *others):
     return lax.optimization_barrier((value, *others))[0]
 
@@ -103,27 +109,52 @@
         index = lax.axis_index("dp")
         cut = self.cut
         half = shard.shape[cut] // 2
-        pieces = [(shard, 0, 0), (self.by_x, 2, 0), (self.by_y, 4, 0)]
+        shard, by_x, by_y = [gated(item, earlier) for item in (shard, self.by_x, self.by_y)]
+        pieces = [(shard, 0, 0), (by_x, 2, 0), (by_y, 4, 0)]
         if self.across is None:
-            low = lax.slice_in_dim(self.by_y, 0, half, axis=cut)
-            high = lax.slice_in_dim(self.by_x, half, 2 * half, axis=cut)
-            if earlier:
-                low, high = after(low, *earlier), after(high, *earlier)
+            low = lax.slice_in_dim(by_y, 0, half, axis=cut)
+            high = lax.slice_in_dim(by_x, half, 2 * half, axis=cut)
             pieces += [(partner(low, 2), 6, 0), (partner(high, 4), 6, half)]
         else:
             pieces.append((self.across, 6, 0))
         pieces += [(partner(piece, 1), code ^ 1, start) for piece, code, start in pieces]
-        whole = jnp.zeros((self.peers, *shard.shape), shard.dtype)
-        for piece, code, start in pieces:
-            place = [jnp.int32(0)] * (shard.ndim + 1)
-            place[0] = index ^ code
-            place[cut + 1] = jnp.int32(start)
-            whole = lax.dynamic_update_slice(whole, piece[None], place)
-        return whole
-
-
-def along_line(count, first, second, third):
-    ones, twos, threes = [], [], []
+        return put_together(pieces, shard, self.peers, cut, index)
+
+
+def put_together(pieces, shard, peers, cut, index):
+    codes = [(code, start) for _, code, start in pieces]
+    arrays = [piece for piece, _, _ in pieces]
+
+    def kernel(place, *refs):
+        out, sems = refs[-2:]
+        copies = []
+        for n, (code, start) in enumerate(codes):
+            size = refs[n].shape[cut]
+            span = tuple(
+                pl.ds(start, size) if dim == cut else slice(None) for dim in range(shard.ndim)
+            )
+            target = out.at[(place[0] ^ code, *span)]
+            copies.append(pltpu.make_async_copy(refs[n], target, sems.at[n]))
+        for copy in copies:
+            copy.start()
+        for copy in copies:
+            copy.wait()
+
+    anywhere = pl.BlockSpec(memory_space=pl.ANY)
+    size = peers * shard.size * shard.dtype.itemsize
+    return pl.pallas_call(
+        kernel,
+        in_specs=[pl.BlockSpec(memory_space=pltpu.SMEM)] + [anywhere] * len(arrays),
+        out_specs=anywhere,
+        out_shape=jax.ShapeDtypeStruct((peers, *shard.shape), shard.dtype),
+        scratch_shapes=[pltpu.SemaphoreType.DMA((len(arrays),))],
+        cost_estimate=cost(2 * size / 3e6),
+        name="put_together",
+    )(index.astype(jnp.int32).reshape(1), *arrays)
+
+
+def along_line(count, first, second, third, finish=None):
+    ones, twos, threes, ends = [], [], [], []
     for step in range(count + 2):
         if step < count:
             gates = []
@@ -132,12 +163,15 @@
             if step >= 3:
                 gates.append(twos[step - 3])
             if step >= 4:
-                gates.append(threes[step - 4])
+                gates.append(threes[step - 4] if finish is None else ends[step - 4])
             ones.append(line_hop(first(step, gates), OUTWARD))
         if 0 <= step - 1 < count:
             twos.append(line_hop(second(step - 1, ones[step - 1]), MIDDLE))
         if 0 <= step - 2 < count:
-            threes.append(line_hop(third(step - 2, ones[step - 2], twos[step - 2]), INWARD))
+            back = step - 2
+            threes.append(line_hop(third(back, ones[back], twos[back]), INWARD))
+            if finish is not None:
+                ends.append(finish(back, ones[back], twos[back], threes[back]))
     return ones, twos, threes
 
 
@@ -229,6 +263,7 @@
             jax.ShapeDtypeStruct((tokens, width), F32),
         ],
         scratch_shapes=[pltpu.VMEM((streams, sub, width), F32)],
+        cost_estimate=cost(22),
         name="make_streams",
     )(history, mix_rows, gains, biases)
 
@@ -266,6 +301,7 @@
         ],
         out_specs=pl.BlockSpec((2 * heads, 1, half, HD), lambda c: (0, c, 0, 0)),
         out_shape=jax.ShapeDtypeStruct((2 * heads, 3, half, HD), BF),
+        cost_estimate=cost(9),
         name="project",
     )(normed, w_heads, tables)
 
@@ -334,6 +370,7 @@
             jax.ShapeDtypeStruct((shards, half, HD), F32),
             jax.ShapeDtypeStruct((shards, half, 1), F32),
         ],
+        cost_estimate=cost(16),
         name="attend",
     )(first_key, side, own, other)
 
@@ -406,6 +443,7 @@
             jax.ShapeDtypeStruct((shards, 3, half, HD), BF),
             jax.ShapeDtypeStruct((shards, 2, half, HD), BF),
         ],
+        cost_estimate=cost(22),
         name="attend_back",
     )(first_key, side, own, other, grads, exact, norm)
 
@@ -484,6 +522,7 @@
             jax.ShapeDtypeStruct((3, 2, width), F32),
         ],
         scratch_shapes=[pltpu.VMEM((tokens, columns), BF), pltpu.VMEM((tokens, width), F32)],
+        cost_estimate=cost(18),
         name="heads_back",
     )(parts, w_heads, normed, unit, inv, gains[:, None, :], tables)
 
@@ -522,6 +561,7 @@
             jax.ShapeDtypeStruct((tokens, width), BF),
             jax.ShapeDtypeStruct((2, width), F32),
         ],
+        cost_estimate=cost(7),
         name="last_back",
     )(grad, unit, inv, gain, extra, flag)
 
@@ -559,6 +599,7 @@
         ],
         out_specs=pl.BlockSpec((streams, rows, entries), lambda i: (0, i, 0)),
         out_shape=jax.ShapeDtypeStruct((streams, tokens, entries), F32),
+        cost_estimate=cost(18),
         name="mixing_back",
     )(heads_part, last_part, history)
 
@@ -661,7 +702,9 @@
     def kernel(*refs):
         weights = refs[0][...]
         heads, lasts = refs[1 : 1 + groups], refs[1 + groups : 1 + 2 * groups]
-        out = refs[-1]
+        out = refs[-2] if final else refs[-1]
+        if final:
+            refs[-1][...] = jnp.zeros_like(refs[-1])
         columns = [weights[:, n : n + 1] for n in range(weights.shape[1])]
         for lane in range(0, width, lanes):
             span = slice(lane, lane + lanes)
@@ -694,8 +737,14 @@
             specs.append(pl.BlockSpec(memory_space=pl.ANY))
             args.append(whole)
             alias = {len(args) - 1: 0}
-        out_spec = pl.BlockSpec((each, block, width), lambda n: (0, i, 0))
-        out_shape = jax.ShapeDtypeStruct((each, coefficients.shape[0], width), F32)
+        out_spec = [
+            pl.BlockSpec((each, block, width), lambda n: (0, i, 0)),
+            pl.BlockSpec((8, 128), lambda n: (0, 0)),
+        ]
+        out_shape = [
+            jax.ShapeDtypeStruct((each, coefficients.shape[0], width), F32),
+            jax.ShapeDtypeStruct((8, 128), F32),
+        ]
     else:
         out_spec, out_shape = small, jax.ShapeDtypeStruct((each, block, width), BF)
     return pl.pallas_call(
@@ -705,6 +754,7 @@
         out_specs=out_spec,
         out_shape=out_shape,
         input_output_aliases=alias,
+        cost_estimate=cost(4 if final else 3),
         name="mix_final" if final else "mix_inward",
     )(*args)
 
@@ -731,6 +781,7 @@
         ],
         out_specs=[column, column],
         out_shape=[jax.ShapeDtypeStruct((tokens, units), BF)] * 2,
+        cost_estimate=cost(9),
         name="hidden_units",
     )(x, w_up)
 
@@ -759,6 +810,7 @@
         ],
         out_specs=pl.BlockSpec((tokens, cols), lambda n: (0, n)),
         out_shape=jax.ShapeDtypeStruct((tokens, shards * cols), F32),
+        cost_estimate=cost(13),
         name="merge_branches",
     )(attended, hidden, w_merge, w_down, stream, flag)
 
@@ -807,6 +859,7 @@
         out_specs=pl.BlockSpec((tokens, units), lambda n: (0, 0)),
         out_shape=jax.ShapeDtypeStruct((tokens, units), BF),
         scratch_shapes=[pltpu.VMEM((tokens, units), F32)],
+        cost_estimate=cost(13 if slope is not None else 7),
         name="back_through",
     )(*args)
 
@@ -839,11 +892,15 @@
     near = shards == 8 and heads_here * 2 == shards and tokens * shards == 2 * SEQ
 
     got_heads = Gathered(w_heads, direct=near)
-    got_up = Gathered(after(w_up, got_heads.shard))
-    got_merge = Gathered(w_merge)
     cotangent = lax.all_gather(out_cotangent, "stream", axis=1, tiled=True)
     lanes = jnp.concatenate([norm_gain, norm_bias]).astype(F32).reshape(tokens, -1)
     packed = lax.all_gather(jnp.concatenate([mixing[:, 0, :], lanes], axis=1), "stream", axis=0)
+    if near:
+        early = (got_heads.by_x, got_heads.by_y, got_heads.across)
+        history = after(history, *early)
+        w_up, w_merge = after(w_up, *early[:2]), after(w_merge, *early[:2])
+    got_up = Gathered(w_up)
+    got_merge = Gathered(w_merge)
     mix_all = packed[:, :, :entries]
     norms = packed[:, :, entries:].reshape(members, 2, width)
     gains, biases = norms[:, 0], norms[:, 1]
@@ -852,7 +909,7 @@
     normed, unit, inv, stream = make_streams(history, mix_rows, gains, biases)
     full_heads = got_heads.whole()
     positions = shard_offset[0] + jnp.arange(tokens, dtype=jnp.int32)
-    projected = project(normed, full_heads, rope_tables(positions, 1.0))
+    projected = project(after(normed, got_up.by_x, got_up.by_y), full_heads, rope_tables(positions, 1.0))
 
     first_rows = mixer_first.astype(F32).reshape(tokens, -1)
     second_flat = mixer_second[:, 0, :].astype(F32).reshape(-1)
@@ -880,8 +937,8 @@
         own = after(own, next_full, first_full, second_full, cotangent)
         got_down = Gathered(after(w_down, own))
         other = partner(own[:, 1:], 1)
-        full_up = got_up.whole()
-        full_merge = got_merge.whole()
+        full_up = got_up.whole(projected)
+        full_merge = got_merge.whole(projected)
         result, exact, level = attend(own, other, first_key, side)
         back = lax.all_to_all(result, "dp", 0, 0, tiled=True)
         attended = jnp.transpose(back.reshape(heads_here, tokens, HD), (1, 0, 2)).reshape(tokens, -1)
@@ -900,7 +957,7 @@
     share = merge_branches(attended, hidden, full_merge, full_down, stream, flags)
 
     inner = (member == 1) | (member == 2)
-    count = 4
+    count = 8
     rows = [lax.slice_in_dim(share, i * tokens // count, (i + 1) * tokens // count) for i in range(count)]
     totals = {}
 
@@ -941,34 +998,34 @@
     attended_grad = back_through(grad_out, full_merge, None)
     up_grad = back_through(grad_out, full_down, slope)
     merge_grad = dot_rows(attended, grad_out).astype(BF)
+    last_normed = dot_cols(up_grad, flat_up)
+    last_share, last_stats = last_back(
+        last_normed, unit[members - 1], inv, gains[members - 1 :], grad_out, flags
+    )
+    last_one = line_hop(last_share, OUTWARD)
+    last_two = line_hop((last_share.astype(F32) + last_one.astype(F32)).astype(BF), MIDDLE)
     if near:
         sent = attended_grad.reshape(tokens, heads_here, HD)
         sent = jnp.transpose(sent, (1, 0, 2)).reshape(shards, half, HD)
         grads = lax.all_to_all(sent, "dp", 0, 0, tiled=True)
-        grads = after(grads, up_grad)
+        grads = after(grads, last_share)
         kept_grads, given = attend_back(own, other, grads, exact, level, first_key, side)
         taken = partner(given, 1)
         summed = kept_grads[:, 1:].astype(F32) + taken.astype(F32)
         pair = jnp.concatenate([kept_grads[:, :1], summed.astype(BF)], axis=1)
         parts = lax.all_to_all(pair, "dp", 0, 0, tiled=True)
-        up_grad = after(up_grad, pair)
+        hidden = after(hidden, pair)
     else:
         grads = far_attend_back(split[0], attended_grad.reshape(tokens, heads_here, HD), kept)
         parts = grads.reshape(3, 2, half, heads_here, HD)
         parts = jnp.transpose(parts, (3, 1, 0, 2, 4)).reshape(2 * heads_here, 3, half, HD)
 
-    last_normed = dot_cols(up_grad, flat_up)
-    last_share, last_stats = last_back(
-        last_normed, unit[members - 1], inv, gains[members - 1 :], grad_out, flags
-    )
-    last_one = line_hop(last_share, OUTWARD)
-    down_grad = dot_rows(after(hidden, last_share), grad_out).astype(BF)
-    parts = after(parts, last_share, down_grad)
+    down_grad = dot_rows(hidden, grad_out).astype(BF)
+    parts = after(parts, last_one, down_grad)
     blocks = 8
     *pieces, heads_share, heads_grad, heads_stats = heads_back(
         parts, full_heads, normed, unit, inv, gains, rope_tables(positions, -1.0), blocks
     )
-    last_two = line_hop((last_share.astype(F32) + last_one.astype(F32)).astype(BF), MIDDLE)
     up_back = dot_rows(normed[members - 1], after(up_grad, heads_share)).astype(BF)
 
     grad_merge = lax.psum_scatter(merge_grad, "dp", scatter_dimension=1, tiled=True).astype(F32)
@@ -1000,6 +1057,8 @@
             )
             extra["all"] = jnp.sum(lax.all_gather(local, "dp", axis=0), axis=0)
             gates = gates + [extra["both"]]
+        if i == 2:
+            gates = gates + [last_two]
         if i == 7:
             gates = gates + [extra["all"]]
         return gated(pieces[i], gates)
@@ -1010,12 +1069,21 @@
     def third_hop(i, one, two):
         return mix_block(i, there, pieces[i], last_share, [two], [last_two], None, None)
 
-    ones, twos, threes = along_line(blocks, first_hop, second_hop, third_hop)
-    grad_history = None
-    for i in range(blocks):
-        grad_history = mix_block(
-            i, here, pieces[i], last_share, [ones[i], twos[i]], [last_one, last_two], threes[i], grad_history
+    def finish(i, one, two, three):
+        extra["history"], token = mix_block(
+            i,
+            here,
+            pieces[i],
+            last_share,
+            [one, two],
+            [last_one, last_two],
+            three,
+            extra.get("history"),
         )
+        return token
+
+    along_line(blocks, first_hop, second_hop, third_hop, finish)
+    grad_history = extra["history"]
 
     grad_mixing = extra["both"][:, :entries][:, None, :]
     sums = extra["all"]

time: 882 us -> 1570 us (1.78)
  the two profiles are of different devices: /device:TPU:8 before, /device:TPU:0 now
where the time goes in v3:
time: 1570 us; the launch traced here: 1560 us
  Pallas kernels  988 us (63%)
  waiting for transfers between devices  188 us (12%)
  starting transfers between devices  172 us (11%)
  blocking collectives  67.7 us (4%)
  local copies, waits for them, and re-layouts  47.3 us (3%)
  matrix products  42.1 us (3%)
  other arithmetic  41.8 us (3%)
  between operations  16.4 us (1%)
    pallas_call x4, Pallas kernels, put_together(): pl.pallas_call(kernel, in_specs=[pl.BlockSpec(memory_space=pltpu.SMEM)] +...  767 us
    ppermute x50, starting transfers between devices, line_hop(): return lax.ppermute(shard, 'stream', pairs)  126 us
    ppermute x50, waiting for transfers between devices, line_hop(): return lax.ppermute(shard, 'stream', pairs)  123 us
    pallas_call x16, Pallas kernels, mix_block(): pl.pallas_call(kernel, grid=(1,), in_specs=specs, out_specs=out_spec, out...  52.2 us
    ppermute x36, waiting for transfers between devices, partner(): return lax.ppermute(shard, 'dp', [(i, i ^ bit) for i in range(peers)])  48.5 us
  transfers between devices with their start and end apart: 96, of which 30 were waited for; matrix products, arithmetic and copies ran while one was open for 6% of the time, Pallas kernels for 43%

profile of v3, /device:TPU:0, one launch (start us, length us, event | category | flops | bytes accessed | tf_op | source)
XLA Modules:
  0.0 1563.1 jit_solution(11825235422907833737)
XLA Ops:
  13.6 14.6 all-gather
  34.4 12.5 collective-permute-done.1.refs_2_
  50.0 22.6 %make_streams.1 = (bf16[4,512,2048]{2,1,0:T(8,128)(2,1)}, bf16[4,512,2048]{2,1,0:T(8,128)(2,1)}, f32[512,4]{1,0:T(8,128)}, f32[512,2048]{1,0:T(8,128)}) custom-call(bf16[8,512,2048]{2,1,0:T(8,128)(2,1)} %hist.1, f32[512,32]{1,0:T(8,128)} %copy.145.mix, f32[4,2048]{1,0:T(4,128)} %get-tuple-element.245.gain, f32[4,2048]{1,0:T(4,128)} %get-tuple-element.244.bias), custom_call_target="tpu_custom_call" | custom-call | flops 19800000512 | bytes 66000000 | tf_op jit(solution)/shard_map/make_streams/pallas_call | solution.py:244
  72.5 191.8 %put_together.4.w = bf16[8,3,256,512]{3,2,1,0:T(8,128)(2,1)} custom-call(s32[1]{0:T(128)} %bitcast.5.place, bf16[3,256,512]{2,1,0:T(8,128)(2,1)} %refs_0_.1, bf16[3,256,512]{2,1,0:T(8,128)(2,1)} %copy-done.44, bf16[3,256,512]{2,1,0:T(8,128)(2,1)} %collective-permute-done.1.refs_2_, bf16[3,256,512]{2,1,0:T(8,128)(2,1)} %collective-permute-done.2.refs_3_, ...), custom_call_target="tpu_custom_call" | custom-call | flops 3774873600 | bytes 12582912 | tf_op jit(solution)/shard_map/put_together/pallas_call | solution.py:145
  264.4 9.2 project.1
  283.6 19.7 %collective-permute-done.18.refs_2_ = bf16[512,256]{1,0:T(8,128)(2,1)S(1)} collective-permute-done((bf16[512,256]{1,0:T(8,128)(2,1)}, bf16[512,256]{1,0:T(8,128)(2,1)S(1)}, u32[]{:S(2)}, u32[]{:S(2)}) %collective-permute-start.18) | collective-permute-done | bytes 262176 | tf_op jit(solution)/shard_map/ppermute | solution.py:76
  305.8 11.4 collective-permute-done.19.refs_3_
  318.6 3.8 collective-permute-done.20.refs_4_
  323.7 14.6 all-gather.2
  346.5 24.7 %all-gather.1 = s32[64,128]{1,0:T(8,128)S(1)} all-gather(s32[8,128]{1,0:T(8,128)S(1)} %broadcast_in_dim.51), channel_id=3, replica_groups=mesh['dp'=8,'stream'=4] {'dp'}, dimensions={0}, use_global_device_ids=true | all-gather | bytes 36864 | tf_op jit(solution)/shard_map/all_gather | solution.py:932
  372.0 64.7 %put_together.6.wm.refs_1_ = bf16[8,512,256]{2,1,0:T(8,128)(2,1)} custom-call(s32[1]{0:T(128)} %bitcast.5.place, bf16[512,256]{1,0:T(8,128)(2,1)} %refs_0_.3, bf16[512,256]{1,0:T(8,128)(2,1)} %collective-permute-done.17.refs_1_, bf16[512,256]{1,0:T(8,128)(2,1)} %copy-done.35, bf16[256,256]{1,0:T(8,128)(2,1)} %copy-done.47, bf16[256,256]{1,0:T(8,128)(2,1)} %copy-done.48, ...), custom_call_target="tpu_custom_call" | custom-call | flops 1258291200 | bytes 4194304 | tf_op jit(solution)/shard_map/put_together/pallas_call | solution.py:145
  436.7 255.3 %put_together.5 = bf16[8,256,2048]{2,1,0:T(8,128)(2,1)} custom-call(s32[1]{0:T(128)} %bitcast.5.place, bf16[256,2048]{1,0:T(8,128)(2,1)} %refs_0_.2, bf16[256,2048]{1,0:T(8,128)(2,1)} %collective-permute-done.3.refs_1_, bf16[256,2048]{1,0:T(8,128)(2,1)} %copy-done.27, bf16[128,2048]{1,0:T(8,128)(2,1)} %collective-permute-done.10.refs_3_, ...), custom_call_target="tpu_custom_call" | custom-call | flops 5033164800 | bytes 16777216 | tf_op jit(solution)/shard_map/put_together/pallas_call | solution.py:145
  697.9 22.5 %attend.1 = (bf16[8,256,128]{2,1,0:T(8,128)(2,1)}, f32[8,256,128]{2,1,0:T(8,128)}, f32[8,256,1]{2,1,0:T(8,128)}) custom-call(s32[8]{0:T(128)} %subtract_maximum_fusion.first, s32[1]{0:T(128)} %bitcast.7.part, bf16[8,3,256,128]{3,2,1,0:T(8,128)(2,1)} %copy-done.4, bf16[8,2,256,128]{3,2,1,0:T(8,128)(2,1)} %collective-permute-done.9.theirs), custom_call_target="tpu_custom_call" | custom-call | flops 14400000000 | bytes 48000000 | tf_op jit(solution)/shard_map/attend/pallas_call | solution.py:353
  720.4 5.8 all-to-all-start.1
  728.0 10.0 hidden_units.1
  741.3 255.3 %put_together.7.wd.refs_1_ = bf16[8,2048,256]{2,1,0:T(8,128)(2,1)} custom-call(s32[1]{0:T(128)} %bitcast.5.place, bf16[2048,256]{1,0:T(8,128)(2,1)} %refs_0_.4, bf16[2048,256]{1,0:T(8,128)(2,1)} %collective-permute-done.26.refs_1_, bf16[2048,256]{1,0:T(8,128)(2,1)} %collective-permute-done.27.refs_2_, bf16[1024,256]{1,0:T(8,128)(2,1)} %collective-permute-done.28.refs_3_, ...), custom_call_target="tpu_custom_call" | custom-call | flops 5033164800 | bytes 16777216 | tf_op jit(solution)/shard_map/put_together/pallas_call | solution.py:145
  996.6 13.1 merge_branches.1
  1012.3 4.1 collective-permute-start.35
  1017.7 5.4 collective-permute-done.35
  1023.8 4.3 collective-permute-done.38
  1028.2 8.5 collective-permute-start.44
  1038.0 5.3 collective-permute-done.44
  1046.3 5.6 collective-permute-done.37
  1051.9 5.9 collective-permute-start.47
  1057.7 3.8 collective-permute-done.47
  1066.7 3.8 collective-permute-done.40
  1070.4 6.5 collective-permute-start.50
  1077.5 4.0 collective-permute-done.50
  1081.5 4.4 collective-permute-start.56
  1092.4 6.9 collective-permute-done.43
  1111.6 9.9 collective-permute-done.49
  1134.9 7.2 back_through.2
  1142.1 13.3 back_through.3
  1155.5 10.6 fusion.43.g
  1170.5 6.4 last_back.1
  1180.9 29.6 %attend_back.1 = (bf16[8,3,256,128]{3,2,1,0:T(8,128)(2,1)}, bf16[8,2,256,128]{3,2,1,0:T(8,128)(2,1)}) custom-call(s32[8]{0:T(128)} %subtract_maximum_fusion.first, s32[1]{0:T(128)} %bitcast.7.part, bf16[8,3,256,128]{3,2,1,0:T(8,128)(2,1)} %copy-done.4, bf16[8,2,256,128]{3,2,1,0:T(8,128)(2,1)} %collective-permute-done.9.theirs, ...), custom_call_target="tpu_custom_call" | custom-call | flops 19800000512 | bytes 66000000 | tf_op jit(solution)/shard_map/attend_back/pallas_call | solution.py:427
  1215.6 4.4 convolution_convert_fusion.2
  1223.9 4.3 all-to-all-start.3
  1228.2 10.4 convolution_convert_fusion.1
  1238.6 20.6 %collective-permute-done.60.refs_5_ = bf16[512,2048]{1,0:T(8,128)(2,1)} collective-permute-done((bf16[512,2048]{1,0:T(8,128)(2,1)S(1)}, bf16[512,2048]{1,0:T(8,128)(2,1)}, u32[]{:S(2)}, u32[]{:S(2)}) %collective-permute-start.60) | collective-permute-done | bytes 2097184 | tf_op jit(solution)/shard_map/ppermute | solution.py:80
  1259.2 17.3 %heads_back.1 = (bf16[3,64,2048]{2,1,0:T(8,128)(2,1)}, bf16[3,64,2048]{2,1,0:T(8,128)(2,1)}, bf16[3,64,2048]{2,1,0:T(8,128)(2,1)}, bf16[3,64,2048]{2,1,0:T(8,128...) custom-call(bf16[8,3,256,128]{3,2,1,0:T(8,128)(2,1)} %all-to-all-don, ...), custom_call_target="tpu_custom_call" | custom-call | flops 16199999488 | bytes 54000000 | tf_op jit(solution)/shard_map/heads_back/pallas_call | solution.py:500
  1279.2 10.9 convolution_convert_fusion
  1293.3 4.0 add_convert_fusion
  1298.1 8.3 collective-permute-start.62
  1306.4 17.3 %mixing_back.1 = f32[4,512,8]{2,1,0:T(8,128)} custom-call(bf16[3,512,2048]{2,1,0:T(8,128)(2,1)} %get-tuple-element.121.first, bf16[512,2048]{1,0:T(8,128)(2,1)} %get-tuple-element.103.last.refs_3_.refs_4_, bf16[8,512,2048]{2,1,0:T(8,128)(2,1)} %hist.1), custom_call_target="tpu_custom_call" | custom-call | flops 16199999488 | bytes 54000000 | tf_op jit(solution)/shard_map/mixing_back/pallas_call | solution.py:592
  1333.7 4.8 collective-permute-start.61
  1338.5 12.7 all-to-all-done.4
  1361.6 13.8 all-gather.3
  1376.6 7.6 collective-permute-start.66
  1398.7 6.5 collective-permute-start.64
  1412.7 3.7 mix_final.8
  1416.5 6.3 collective-permute-done.64.refs_2_
  1429.6 8.9 collective-permute-done.70.refs_2_
  1440.4 3.7 mix_final.9
  1444.2 9.1 collective-permute-start.68
  1457.5 5.4 collective-permute-start.76
  1462.9 3.7 mix_final.10
  1475.6 5.7 collective-permute-start.72
  1481.4 3.7 mix_final.11
  1489.8 11.3 collective-permute-done.72.refs_2_
  1507.1 3.7 mix_final.12
  1520.2 3.9 collective-permute-done.80.refs_7_
  1528.5 4.7 collective-permute-done.78.refs_7_
  1537.7 6.0 collective-permute-done.74.refs_7_
  (395 shorter events, 227.1 us)
Async XLA Ops:
  7.2 334.5 %all-gather.6.cloned.1.call-start = ((), (), s32[]{:S(2)}) async-start(), calls=%async_computation.9 | async-start | bytes 2621440 | tf_op jit(solution)/shard_map/all_gather | solution.py:895
  7.2 27.2 %collective-permute-start = (bf16[3,256,512]{2,1,0:T(8,128)(2,1)}, bf16[3,256,512]{2,1,0:T(8,128)(2,1)S(1)}, u32[]{:S(2)}, u32[]{:S(2)}) collective-permute-start(bf16[3,256,512]{2,1,0:T(8,128)(2,1)} %refs_0_.1), channel_id=1, source_target_pairs={{0,8},{4,12},{8,0},{12,4},{16,24},{20,28},{24,16},{28,20},{1,9},{5... | collective-permute-start | bytes 2359304 | tf_op jit(solution)/shard_map/ppermute | solution.py:76
  10.3 36.6 %collective-permute-start.1 = (bf16[3,256,512]{2,1,0:T(8,128)(2,1)}, bf16[3,256,512]{2,1,0:T(8,128)(2,1)}, u32[]{:S(2)}, u32[]{:S(2)}) collective-permute-start(bf16[3,256,512]{2,1,0:T(8,128)(2,1)} %refs_0_.1), channel_id=1, source_target_pairs={{0,16},{4,20},{8,24},{12,28},{16,0},{20,4},{24,8},{28,12},{1,17},{... | collective-permute-start | bytes 2359304 | tf_op jit(solution)/shard_map/ppermute | solution.py:76
  11.8 37.7 %collective-permute-start.2 = (bf16[3,256,512]{2,1,0:T(8,128)(2,1)}, bf16[3,256,512]{2,1,0:T(8,128)(2,1)}, u32[]{:S(2)}, u32[]{:S(2)}) collective-permute-start(bf16[3,256,512]{2,1,0:T(8,128)(2,1)} %refs_0_.1), channel_id=1, source_target_pairs={{0,24},{4,28},{8,16},{12,20},{16,8},{20,12},{24,0},{28,4},{1,25},{... | collective-permute-start | bytes 2359304 | tf_op jit(solution)/shard_map/ppermute | solution.py:76
  11.8 38.1 %collective-permute-start.5 = (bf16[3,256,512]{2,1,0:T(8,128)(2,1)}, bf16[3,256,512]{2,1,0:T(8,128)(2,1)}, u32[]{:S(2)}, u32[]{:S(2)}) collective-permute-start(bf16[3,256,512]{2,1,0:T(8,128)(2,1)} %refs_0_.1), channel_id=1, source_target_pairs={{0,4},{4,0},{8,12},{12,8},{16,20},{20,16},{24,28},{28,24},{1,5},{5... | collective-permute-start | bytes 2359304 | tf_op jit(solution)/shard_map/ppermute | solution.py:76
  46.9 217.4 %collective-permute-start.3 = (bf16[256,2048]{1,0:T(8,128)(2,1)S(1)}, bf16[256,2048]{1,0:T(8,128)(2,1)}, u32[]{:S(2)}, u32[]{:S(2)}) collective-permute-start(bf16[256,2048]{1,0:T(8,128)(2,1)S(1)} %copy-done.42), channel_id=1, source_target_pairs={{0,8},{4,12},{8,0},{12,4},{16,24},{20,28},{24,16},{28,20},{1,9},{5... | collective-permute-start | bytes 3145736 | tf_op jit(solution)/shard_map/ppermute | solution.py:76
  46.9 217.5 %collective-permute-start.4 = (bf16[256,2048]{1,0:T(8,128)(2,1)S(1)}, bf16[256,2048]{1,0:T(8,128)(2,1)S(1)}, u32[]{:S(2)}, u32[]{:S(2)}) collective-permute-start(bf16[256,2048]{1,0:T(8,128)(2,1)S(1)} %copy-done.42), channel_id=1, source_target_pairs={{0,16},{4,20},{8,24},{12,28},{16,0},{20,4},{24,8},{28,12},{1,17},{... | collective-permute-start | bytes 3145736 | tf_op jit(solution)/shard_map/ppermute | solution.py:76
  49.4 23.1 %collective-permute-start.6 = (bf16[3,256,512]{2,1,0:T(8,128)(2,1)S(1)}, bf16[3,256,512]{2,1,0:T(8,128)(2,1)}, u32[]{:S(2)}, u32[]{:S(2)}) collective-permute-start(bf16[3,256,512]{2,1,0:T(8,128)(2,1)S(1)} %collective-permute-done.refs_1_), channel_id=1, source_target_pairs={{0,4},{4,0},{8,12},{12,8},{16,20},{20,16},{24,28},{28,24},{1,5},{5... | collective-permute-start | bytes 2359304 | tf_op jit(solution)/shard_map/ppermute | solution.py:76
  49.4 23.1 %collective-permute-start.7 = (bf16[3,256,512]{2,1,0:T(8,128)(2,1)}, bf16[3,256,512]{2,1,0:T(8,128)(2,1)}, u32[]{:S(2)}, u32[]{:S(2)}) collective-permute-start(bf16[3,256,512]{2,1,0:T(8,128)(2,1)} %collective-permute-done.1.refs_2_), channel_id=1, source_target_pairs={{0,4},{4,0},{8,12},{12,8},{16,20},{20,16},{24,28},{28,24},{1,5},{5... | collective-permute-start | bytes 2359304 | tf_op jit(solution)/shard_map/ppermute | solution.py:76
  49.9 22.6 %collective-permute-start.8 = (bf16[3,256,512]{2,1,0:T(8,128)(2,1)}, bf16[3,256,512]{2,1,0:T(8,128)(2,1)}, u32[]{:S(2)}, u32[]{:S(2)}) collective-permute-start(bf16[3,256,512]{2,1,0:T(8,128)(2,1)} %collective-permute-done.2.refs_3_), channel_id=1, source_target_pairs={{0,4},{4,0},{8,12},{12,8},{16,20},{20,16},{24,28},{28,24},{1,5},{5... | collective-permute-start | bytes 2359304 | tf_op jit(solution)/shard_map/ppermute | solution.py:76
  273.6 68.1 %all-to-all-start = ((bf16[8,3,256,128]{3,2,1,0:T(8,128)(2,1)}), bf16[8,3,256,128]{3,2,1,0:T(8,128)(2,1)S(1)}, u32[]{:S(2)}, u32[]{:S(2)}) async-start(bf16[8,3,256,128]{3,2,1,0:T(8,128)(2,1)} %project.1), calls=%async_computation | async-start | bytes 3145728 | tf_op jit(solution)/shard_map/all_to_all | solution.py:936
  277.2 26.1 %collective-permute-start.18 = (bf16[512,256]{1,0:T(8,128)(2,1)}, bf16[512,256]{1,0:T(8,128)(2,1)S(1)}, u32[]{:S(2)}, u32[]{:S(2)}) collective-permute-start(bf16[512,256]{1,0:T(8,128)(2,1)} %refs_0_.3), channel_id=1, source_target_pairs={{0,16},{4,20},{8,24},{12,28},{16,0},{20,4},{24,8},{28,12},{1,17},{... | collective-permute-start | bytes 786440 | tf_op jit(solution)/shard_map/ppermute | solution.py:76
  279.2 25.2 %collective-permute-start.17 = (bf16[512,256]{1,0:T(8,128)(2,1)}, bf16[512,256]{1,0:T(8,128)(2,1)}, u32[]{:S(2)}, u32[]{:S(2)}) collective-permute-start(bf16[512,256]{1,0:T(8,128)(2,1)} %refs_0_.3), channel_id=1, source_target_pairs={{0,8},{4,12},{8,0},{12,4},{16,24},{20,28},{24,16},{28,20},{1,9},{5... | collective-permute-start | bytes 786440 | tf_op jit(solution)/shard_map/ppermute | solution.py:76
  281.7 41.4 %collective-permute-start.10 = (bf16[128,2048]{1,0:T(8,128)(2,1)S(1)}, bf16[128,2048]{1,0:T(8,128)(2,1)}, u32[]{:S(2)}, u32[]{:S(2)}) collective-permute-start(bf16[128,2048]{1,0:T(8,128)(2,1)S(1)} %slice.134), channel_id=1, source_target_pairs={{0,8},{4,12},{8,0},{12,4},{16,24},{20,28},{24,16},{28,20},{1,9},{5... | collective-permute-start | bytes 1572872 | tf_op jit(solution)/shard_map/ppermute | solution.py:76
  283.4 39.8 %collective-permute-start.11 = (bf16[128,2048]{1,0:T(8,128)(2,1)S(1)}, bf16[128,2048]{1,0:T(8,128)(2,1)}, u32[]{:S(2)}, u32[]{:S(2)}) collective-permute-start(bf16[128,2048]{1,0:T(8,128)(2,1)S(1)} %slice.135), channel_id=1, source_target_pairs={{0,16},{4,20},{8,24},{12,28},{16,0},{20,4},{24,8},{28,12},{1,17},{... | collective-permute-start | bytes 1572872 | tf_op jit(solution)/shard_map/ppermute | solution.py:76
  304.3 18.1 %collective-permute-start.22 = (bf16[512,256]{1,0:T(8,128)(2,1)}, bf16[512,256]{1,0:T(8,128)(2,1)}, u32[]{:S(2)}, u32[]{:S(2)}) collective-permute-start(bf16[512,256]{1,0:T(8,128)(2,1)} %collective-permute-done.17.refs_1_), channel_id=1, source_target_pairs={{0,4},{4,0},{8,12},{12,8},{16,20},{20,16},{24,28},{28,24},{1,5},{5... | collective-permute-start | bytes 786440 | tf_op jit(solution)/shard_map/ppermute | solution.py:76
  304.3 39.0 %collective-permute-start.13 = (bf16[256,2048]{1,0:T(8,128)(2,1)}, bf16[256,2048]{1,0:T(8,128)(2,1)}, u32[]{:S(2)}, u32[]{:S(2)}) collective-permute-start(bf16[256,2048]{1,0:T(8,128)(2,1)} %collective-permute-done.3.refs_1_), channel_id=1, source_target_pairs={{0,4},{4,0},{8,12},{12,8},{16,20},{20,16},{24,28},{28,24},{1,5},{5... | collective-permute-start | bytes 3145736 | tf_op jit(solution)/shard_map/ppermute | solution.py:76
  323.1 18.7 %collective-permute-start.15 = (bf16[128,2048]{1,0:T(8,128)(2,1)}, bf16[128,2048]{1,0:T(8,128)(2,1)}, u32[]{:S(2)}, u32[]{:S(2)}) collective-permute-start(bf16[128,2048]{1,0:T(8,128)(2,1)} %collective-permute-done.10.refs_3_), channel_id=1, source_target_pairs={{0,4},{4,0},{8,12},{12,8},{16,20},{20,16},{24,28},{28,24},{1,5},{5... | collective-permute-start | bytes 1572872 | tf_op jit(solution)/shard_map/ppermute | solution.py:76
  323.2 19.6 %collective-permute-start.16 = (bf16[128,2048]{1,0:T(8,128)(2,1)}, bf16[128,2048]{1,0:T(8,128)(2,1)}, u32[]{:S(2)}, u32[]{:S(2)}) collective-permute-start(bf16[128,2048]{1,0:T(8,128)(2,1)} %collective-permute-done.11.refs_4_), channel_id=1, source_target_pairs={{0,4},{4,0},{8,12},{12,8},{16,20},{20,16},{24,28},{28,24},{1,5},{5... | collective-permute-start | bytes 1572872 | tf_op jit(solution)/shard_map/ppermute | solution.py:76
  340.1 96.7 %collective-permute-start.14 = (bf16[256,2048]{1,0:T(8,128)(2,1)}, bf16[256,2048]{1,0:T(8,128)(2,1)}, u32[]{:S(2)}, u32[]{:S(2)}) collective-permute-start(bf16[256,2048]{1,0:T(8,128)(2,1)} %copy-done.27), channel_id=1, source_target_pairs={{0,4},{4,0},{8,12},{12,8},{16,20},{20,16},{24,28},{28,24},{1,5},{5... | collective-permute-start | bytes 3145736 | tf_op jit(solution)/shard_map/ppermute | solution.py:76
  340.4 96.3 %collective-permute-start.12 = (bf16[256,2048]{1,0:T(8,128)(2,1)}, bf16[256,2048]{1,0:T(8,128)(2,1)}, u32[]{:S(2)}, u32[]{:S(2)}) collective-permute-start(bf16[256,2048]{1,0:T(8,128)(2,1)} %refs_0_.2), channel_id=1, source_target_pairs={{0,4},{4,0},{8,12},{12,8},{16,20},{20,16},{24,28},{28,24},{1,5},{5... | collective-permute-start | bytes 3145736 | tf_op jit(solution)/shard_map/ppermute | solution.py:76
  341.9 350.6 %collective-permute-start.27 = (bf16[2048,256]{1,0:T(8,128)(2,1)}, bf16[2048,256]{1,0:T(8,128)(2,1)}, u32[]{:S(2)}, u32[]{:S(2)}) collective-permute-start(bf16[2048,256]{1,0:T(8,128)(2,1)} %refs_0_.4), channel_id=1, source_target_pairs={{0,16},{4,20},{8,24},{12,28},{16,0},{20,4},{24,8},{28,12},{1,17},{... | collective-permute-start | bytes 3145736 | tf_op jit(solution)/shard_map/ppermute | solution.py:76
  342.8 352.3 %collective-permute-start.26 = (bf16[2048,256]{1,0:T(8,128)(2,1)}, bf16[2048,256]{1,0:T(8,128)(2,1)}, u32[]{:S(2)}, u32[]{:S(2)}) collective-permute-start(bf16[2048,256]{1,0:T(8,128)(2,1)} %refs_0_.4), channel_id=1, source_target_pairs={{0,8},{4,12},{8,0},{12,4},{16,24},{20,28},{24,16},{28,20},{1,9},{5... | collective-permute-start | bytes 3145736 | tf_op jit(solution)/shard_map/ppermute | solution.py:76
  343.4 354.0 %collective-permute-start.9 = (bf16[8,2,256,128]{3,2,1,0:T(8,128)(2,1)S(1)}, bf16[8,2,256,128]{3,2,1,0:T(8,128)(2,1)}, u32[]{:S(2)}, u32[]{:S(2)}) collective-permute-start(bf16[8,2,256,128]{3,2,1,0:T(8,128)(2,1)S(1)} %slice.132), channel_id=1, source_target_pairs={{0,4},{4,0},{8,12},{12,8},{16,20},{20,16},{24,28},{28,24},{1,5},{5... | collective-permute-start | bytes 3145736 | tf_op jit(solution)/shard_map/ppermute | solution.py:76
  692.1 47.2 %collective-permute-start.30 = (bf16[2048,256]{1,0:T(8,128)(2,1)}, bf16[2048,256]{1,0:T(8,128)(2,1)}, u32[]{:S(2)}, u32[]{:S(2)}) collective-permute-start(bf16[2048,256]{1,0:T(8,128)(2,1)} %refs_0_.4), channel_id=1, source_target_pairs={{0,4},{4,0},{8,12},{12,8},{16,20},{20,16},{24,28},{28,24},{1,5},{5... | collective-permute-start | bytes 3145736 | tf_op jit(solution)/shard_map/ppermute | solution.py:76
  693.6 32.6 %collective-permute-start.28 = (bf16[1024,256]{1,0:T(8,128)(2,1)S(1)}, bf16[1024,256]{1,0:T(8,128)(2,1)}, u32[]{:S(2)}, u32[]{:S(2)}) collective-permute-start(bf16[1024,256]{1,0:T(8,128)(2,1)S(1)} %slice.170), channel_id=1, source_target_pairs={{0,8},{4,12},{8,0},{12,4},{16,24},{20,28},{24,16},{28,20},{1,9},{5... | collective-permute-start | bytes 1572872 | tf_op jit(solution)/shard_map/ppermute | solution.py:76
  696.2 31.7 %collective-permute-start.29 = (bf16[1024,256]{1,0:T(8,128)(2,1)S(1)}, bf16[1024,256]{1,0:T(8,128)(2,1)}, u32[]{:S(2)}, u32[]{:S(2)}) collective-permute-start(bf16[1024,256]{1,0:T(8,128)(2,1)S(1)} %slice.171), channel_id=1, source_target_pairs={{0,16},{4,20},{8,24},{12,28},{16,0},{20,4},{24,8},{28,12},{1,17},{... | collective-permute-start | bytes 1572872 | tf_op jit(solution)/shard_map/ppermute | solution.py:76
  697.4 42.0 %collective-permute-start.31 = (bf16[2048,256]{1,0:T(8,128)(2,1)}, bf16[2048,256]{1,0:T(8,128)(2,1)}, u32[]{:S(2)}, u32[]{:S(2)}) collective-permute-start(bf16[2048,256]{1,0:T(8,128)(2,1)} %collective-permute-done.26.refs_1_), channel_id=1, source_target_pairs={{0,4},{4,0},{8,12},{12,8},{16,20},{20,16},{24,28},{28,24},{1,5},{5... | collective-permute-start | bytes 3145736 | tf_op jit(solution)/shard_map/ppermute | solution.py:76
  697.4 42.0 %collective-permute-start.32 = (bf16[2048,256]{1,0:T(8,128)(2,1)}, bf16[2048,256]{1,0:T(8,128)(2,1)S(1)}, u32[]{:S(2)}, u32[]{:S(2)}) collective-permute-start(bf16[2048,256]{1,0:T(8,128)(2,1)} %collective-permute-done.27.refs_2_), channel_id=1, source_target_pairs={{0,4},{4,0},{8,12},{12,8},{16,20},{20,16},{24,28},{28,24},{1,5},{5... | collective-permute-start | bytes 3145736 | tf_op jit(solution)/shard_map/ppermute | solution.py:76
  720.4 17.6 %all-to-all-start.1 = ((bf16[8,256,128]{2,1,0:T(8,128)(2,1)}), bf16[8,256,128]{2,1,0:T(8,128)(2,1)S(1)}, u32[]{:S(2)}, u32[]{:S(2)}) async-start(bf16[8,256,128]{2,1,0:T(8,128)(2,1)} %get-tuple-element.82), calls=%async_computation.1 | async-start | bytes 1048576 | tf_op jit(solution)/shard_map/all_to_all | solution.py:943
  1107.3 17.0 %collective-permute-start.52 = (bf16[64,2048]{1,0:T(8,128)(2,1)S(1)}, bf16[64,2048]{1,0:T(8,128)(2,1)S(1)}, u32[]{:S(2)}, u32[]{:S(2)}) collective-permute-start(bf16[64,2048]{1,0:T(8,128)(2,1)S(1)} %get-tuple-element.200), channel_id=1, source_target_pairs={{1,0},{2,3},{5,4},{6,7},{9,8},{10,11},{13,12},{14,15},{17,16},{18,... | collective-permute-start | bytes 786440 | tf_op jit(solution)/shard_map/ppermute | solution.py:80
  1108.6 18.5 %collective-permute-start.55 = (bf16[64,2048]{1,0:T(8,128)(2,1)S(1)}, bf16[64,2048]{1,0:T(8,128)(2,1)S(1)}, u32[]{:S(2)}, u32[]{:S(2)}) collective-permute-start(bf16[64,2048]{1,0:T(8,128)(2,1)S(1)} %get-tuple-element.199), channel_id=1, source_target_pairs={{1,0},{2,3},{5,4},{6,7},{9,8},{10,11},{13,12},{14,15},{17,16},{18,... | collective-permute-start | bytes 786440 | tf_op jit(solution)/shard_map/ppermute | solution.py:80
  1109.9 20.0 %collective-permute-start.58 = (bf16[64,2048]{1,0:T(8,128)(2,1)S(1)}, bf16[64,2048]{1,0:T(8,128)(2,1)S(1)}, u32[]{:S(2)}, u32[]{:S(2)}) collective-permute-start(bf16[64,2048]{1,0:T(8,128)(2,1)S(1)} %get-tuple-element.198), channel_id=1, source_target_pairs={{1,0},{2,3},{5,4},{6,7},{9,8},{10,11},{13,12},{14,15},{17,16},{18,... | collective-permute-start | bytes 786440 | tf_op jit(solution)/shard_map/ppermute | solution.py:80
  1170.5 217.0 %reduce-scatter.7.cloned.1.call-start = ((), (), s32[]{:S(2)}) async-start(), calls=%async_computation.11 | async-start | bytes 2359296 | tf_op jit(solution)/shard_map/reduce_scatter | solution.py:1031
  1212.6 46.6 %collective-permute-start.60 = (bf16[512,2048]{1,0:T(8,128)(2,1)S(1)}, bf16[512,2048]{1,0:T(8,128)(2,1)}, u32[]{:S(2)}, u32[]{:S(2)}) collective-permute-start(bf16[512,2048]{1,0:T(8,128)(2,1)S(1)} %copy-done), channel_id=1, source_target_pairs={{0,1},{3,2},{4,5},{7,6},{8,9},{11,10},{12,13},{15,14},{16,17},{19,... | collective-permute-start | bytes 6291464 | tf_op jit(solution)/shard_map/ppermute | solution.py:80
  1223.9 35.3 %all-to-all-start.3 = ((bf16[8,3,256,128]{3,2,1,0:T(8,128)(2,1)}), bf16[8,3,256,128]{3,2,1,0:T(8,128)(2,1)}, u32[]{:S(2)}, u32[]{:S(2)}) async-start(bf16[8,3,256,128]{3,2,1,0:T(8,128)(2,1)} %pad_maximum_fusion), calls=%async_computation.3 | async-start | bytes 3145728 | tf_op jit(solution)/shard_map/all_to_all | solution.py:1016
  1228.2 319.9 %reduce-scatter.5.cloned.1.call-start = ((), (), s32[]{:S(2)}) async-start(), calls=%async_computation.10 | async-start | bytes 7077888 | tf_op jit(solution)/shard_map/reduce_scatter | solution.py:1033
  1276.6 274.0 %reduce-scatter.11.cloned.1.call-start = ((), (), s32[]{:S(2)}) async-start(), calls=%async_computation.13 | async-start | bytes 9437184 | tf_op jit(solution)/shard_map/reduce_scatter | solution.py:1032
  1277.1 276.1 %reduce-scatter.9.cloned.1.call-start = ((), (), s32[]{:S(2)}) async-start(), calls=%async_computation.12 | async-start | bytes 9437184 | tf_op jit(solution)/shard_map/reduce_scatter | solution.py:1034
  1297.3 79.3 %collective-permute-start.65 = (bf16[512,2048]{1,0:T(8,128)(2,1)}, bf16[512,2048]{1,0:T(8,128)(2,1)S(1)}, u32[]{:S(2)}, u32[]{:S(2)}) collective-permute-start(bf16[512,2048]{1,0:T(8,128)(2,1)} %add_convert_fusion), channel_id=1, source_target_pairs={{1,2},{2,1},{5,6},{6,5},{9,10},{10,9},{13,14},{14,13},{17,18},{18,... | collective-permute-start | bytes 6291464 | tf_op jit(solution)/shard_map/ppermute | solution.py:80
  1298.1 56.1 %collective-permute-start.62 = (bf16[3,64,2048]{2,1,0:T(8,128)(2,1)}, bf16[3,64,2048]{2,1,0:T(8,128)(2,1)}, u32[]{:S(2)}, u32[]{:S(2)}) collective-permute-start(bf16[3,64,2048]{2,1,0:T(8,128)(2,1)} %get-tuple-element.115.refs_1_), channel_id=1, source_target_pairs={{0,1},{3,2},{4,5},{7,6},{8,9},{11,10},{12,13},{15,14},{16,17},{19,... | collective-permute-start | bytes 2359304 | tf_op jit(solution)/shard_map/ppermute | solution.py:80
  1328.6 22.5 %all-to-all-start.4 = ((f32[4,512,16]{1,2,0:T(8,128)}), f32[4,512,16]{1,2,0:T(8,128)S(1)}, u32[]{:S(2)}, u32[]{:S(2)}) async-start(f32[4,512,16]{1,2,0:T(8,128)} %maximum_maximum_fusion), calls=%async_computation.4 | async-start | bytes 262144 | tf_op jit(solution)/shard_map/all_to_all | solution.py:1051
  1333.7 24.9 %collective-permute-start.61 = (bf16[3,64,2048]{2,1,0:T(8,128)(2,1)S(1)}, bf16[3,64,2048]{2,1,0:T(8,128)(2,1)}, u32[]{:S(2)}, u32[]{:S(2)}) collective-permute-start(bf16[3,64,2048]{2,1,0:T(8,128)(2,1)S(1)} %copy-done.11), channel_id=1, source_target_pairs={{0,1},{3,2},{4,5},{7,6},{8,9},{11,10},{12,13},{15,14},{16,17},{19,... | collective-permute-start | bytes 2359304 | tf_op jit(solution)/shard_map/ppermute | solution.py:80
  1357.0 32.3 %collective-permute-start.63 = (bf16[3,64,2048]{2,1,0:T(8,128)(2,1)}, bf16[3,64,2048]{2,1,0:T(8,128)(2,1)}, u32[]{:S(2)}, u32[]{:S(2)}) collective-permute-start(bf16[3,64,2048]{2,1,0:T(8,128)(2,1)} %add_convert_fusion.9), channel_id=1, source_target_pairs={{1,2},{2,1},{5,6},{6,5},{9,10},{10,9},{13,14},{14,13},{17,18},{18,... | collective-permute-start | bytes 2359304 | tf_op jit(solution)/shard_map/ppermute | solution.py:80
  1360.9 32.7 %collective-permute-start.69 = (bf16[3,64,2048]{2,1,0:T(8,128)(2,1)}, bf16[3,64,2048]{2,1,0:T(8,128)(2,1)S(1)}, u32[]{:S(2)}, u32[]{:S(2)}) collective-permute-start(bf16[3,64,2048]{2,1,0:T(8,128)(2,1)} %add_convert_fusion.7), channel_id=1, source_target_pairs={{1,2},{2,1},{5,6},{6,5},{9,10},{10,9},{13,14},{14,13},{17,18},{18,... | collective-permute-start | bytes 2359304 | tf_op jit(solution)/shard_map/ppermute | solution.py:80
  1376.6 28.6 %collective-permute-start.66 = (bf16[3,64,2048]{2,1,0:T(8,128)(2,1)}, bf16[3,64,2048]{2,1,0:T(8,128)(2,1)}, u32[]{:S(2)}, u32[]{:S(2)}) collective-permute-start(bf16[3,64,2048]{2,1,0:T(8,128)(2,1)} %get-tuple-element.118.refs_1_), channel_id=1, source_target_pairs={{0,1},{3,2},{4,5},{7,6},{8,9},{11,10},{12,13},{15,14},{16,17},{19,... | collective-permute-start | bytes 2359304 | tf_op jit(solution)/shard_map/ppermute | solution.py:80
  1392.1 20.6 %collective-permute-start.85 = (bf16[2,64,2048]{2,1,0:T(8,128)(2,1)}, bf16[2,64,2048]{2,1,0:T(8,128)(2,1)}, u32[]{:S(2)}, u32[]{:S(2)}) collective-permute-start(bf16[2,64,2048]{2,1,0:T(8,128)(2,1)} %mix_inward.15), channel_id=1, source_target_pairs={{1,0},{2,3},{5,4},{6,7},{9,8},{10,11},{13,12},{14,15},{17,16},{18,... | collective-permute-start | bytes 1572872 | tf_op jit(solution)/shard_map/ppermute | solution.py:80
  1397.3 43.1 %collective-permute-start.84 = (bf16[2,64,2048]{2,1,0:T(8,128)(2,1)}, bf16[2,64,2048]{2,1,0:T(8,128)(2,1)}, u32[]{:S(2)}, u32[]{:S(2)}) collective-permute-start(bf16[2,64,2048]{2,1,0:T(8,128)(2,1)} %mix_inward.14), channel_id=1, source_target_pairs={{1,0},{2,3},{5,4},{6,7},{9,8},{10,11},{13,12},{14,15},{17,16},{18,... | collective-permute-start | bytes 1572872 | tf_op jit(solution)/shard_map/ppermute | solution.py:80
  1398.7 24.1 %collective-permute-start.64 = (bf16[3,64,2048]{2,1,0:T(8,128)(2,1)S(1)}, bf16[3,64,2048]{2,1,0:T(8,128)(2,1)S(1)}, u32[]{:S(2)}, u32[]{:S(2)}) collective-permute-start(bf16[3,64,2048]{2,1,0:T(8,128)(2,1)S(1)} %copy-done.10), channel_id=1, source_target_pairs={{0,1},{3,2},{4,5},{7,6},{8,9},{11,10},{12,13},{15,14},{16,17},{19,... | collective-permute-start | bytes 2359304 | tf_op jit(solution)/shard_map/ppermute | solution.py:80
  1407.8 17.8 %collective-permute-start.67 = (bf16[3,64,2048]{2,1,0:T(8,128)(2,1)}, bf16[3,64,2048]{2,1,0:T(8,128)(2,1)}, u32[]{:S(2)}, u32[]{:S(2)}) collective-permute-start(bf16[3,64,2048]{2,1,0:T(8,128)(2,1)} %add_convert_fusion.8), channel_id=1, source_target_pairs={{1,2},{2,1},{5,6},{6,5},{9,10},{10,9},{13,14},{14,13},{17,18},{18,... | collective-permute-start | bytes 2359304 | tf_op jit(solution)/shard_map/ppermute | solution.py:80
  1409.3 29.2 %collective-permute-start.70 = (bf16[3,64,2048]{2,1,0:T(8,128)(2,1)S(1)}, bf16[3,64,2048]{2,1,0:T(8,128)(2,1)S(1)}, u32[]{:S(2)}, u32[]{:S(2)}) collective-permute-start(bf16[3,64,2048]{2,1,0:T(8,128)(2,1)S(1)} %copy-done.9), channel_id=1, source_target_pairs={{0,1},{3,2},{4,5},{7,6},{8,9},{11,10},{12,13},{15,14},{16,17},{19,... | collective-permute-start | bytes 2359304 | tf_op jit(solution)/shard_map/ppermute | solution.py:80
  1424.0 29.2 %collective-permute-start.75 = (bf16[3,64,2048]{2,1,0:T(8,128)(2,1)}, bf16[3,64,2048]{2,1,0:T(8,128)(2,1)}, u32[]{:S(2)}, u32[]{:S(2)}) collective-permute-start(bf16[3,64,2048]{2,1,0:T(8,128)(2,1)} %add_convert_fusion.4), channel_id=1, source_target_pairs={{1,2},{2,1},{5,6},{6,5},{9,10},{10,9},{13,14},{14,13},{17,18},{18,... | collective-permute-start | bytes 2359304 | tf_op jit(solution)/shard_map/ppermute | solution.py:80
  1428.4 34.5 %collective-permute-start.83 = (bf16[2,64,2048]{2,1,0:T(8,128)(2,1)}, bf16[2,64,2048]{2,1,0:T(8,128)(2,1)}, u32[]{:S(2)}, u32[]{:S(2)}) collective-permute-start(bf16[2,64,2048]{2,1,0:T(8,128)(2,1)} %mix_inward.13), channel_id=1, source_target_pairs={{1,0},{2,3},{5,4},{6,7},{9,8},{10,11},{13,12},{14,15},{17,16},{18,... | collective-permute-start | bytes 1572872 | tf_op jit(solution)/shard_map/ppermute | solution.py:80
  1439.7 26.8 %collective-permute-start.71 = (bf16[3,64,2048]{2,1,0:T(8,128)(2,1)}, bf16[3,64,2048]{2,1,0:T(8,128)(2,1)S(1)}, u32[]{:S(2)}, u32[]{:S(2)}) collective-permute-start(bf16[3,64,2048]{2,1,0:T(8,128)(2,1)} %add_convert_fusion.6), channel_id=1, source_target_pairs={{1,2},{2,1},{5,6},{6,5},{9,10},{10,9},{13,14},{14,13},{17,18},{18,... | collective-permute-start | bytes 2359304 | tf_op jit(solution)/shard_map/ppermute | solution.py:80
  1444.2 27.6 %collective-permute-start.68 = (bf16[3,64,2048]{2,1,0:T(8,128)(2,1)S(1)}, bf16[3,64,2048]{2,1,0:T(8,128)(2,1)}, u32[]{:S(2)}, u32[]{:S(2)}) collective-permute-start(bf16[3,64,2048]{2,1,0:T(8,128)(2,1)S(1)} %copy-done.8), channel_id=1, source_target_pairs={{0,1},{3,2},{4,5},{7,6},{8,9},{11,10},{12,13},{15,14},{16,17},{19,... | collective-permute-start | bytes 2359304 | tf_op jit(solution)/shard_map/ppermute | solution.py:80
  1456.2 25.2 %collective-permute-start.82 = (bf16[2,64,2048]{2,1,0:T(8,128)(2,1)}, bf16[2,64,2048]{2,1,0:T(8,128)(2,1)}, u32[]{:S(2)}, u32[]{:S(2)}) collective-permute-start(bf16[2,64,2048]{2,1,0:T(8,128)(2,1)} %mix_inward.12), channel_id=1, source_target_pairs={{1,0},{2,3},{5,4},{6,7},{9,8},{10,11},{13,12},{14,15},{17,16},{18,... | collective-permute-start | bytes 1572872 | tf_op jit(solution)/shard_map/ppermute | solution.py:80
  1457.5 29.6 %collective-permute-start.76 = (bf16[3,64,2048]{2,1,0:T(8,128)(2,1)S(1)}, bf16[3,64,2048]{2,1,0:T(8,128)(2,1)S(1)}, u32[]{:S(2)}, u32[]{:S(2)}) collective-permute-start(bf16[3,64,2048]{2,1,0:T(8,128)(2,1)S(1)} %copy-done.7), channel_id=1, source_target_pairs={{0,1},{3,2},{4,5},{7,6},{8,9},{11,10},{12,13},{15,14},{16,17},{19,... | collective-permute-start | bytes 2359304 | tf_op jit(solution)/shard_map/ppermute | solution.py:80
  1470.3 36.8 %collective-permute-start.81 = (bf16[2,64,2048]{2,1,0:T(8,128)(2,1)}, bf16[2,64,2048]{2,1,0:T(8,128)(2,1)}, u32[]{:S(2)}, u32[]{:S(2)}) collective-permute-start(bf16[2,64,2048]{2,1,0:T(8,128)(2,1)} %mix_inward.11), channel_id=1, source_target_pairs={{1,0},{2,3},{5,4},{6,7},{9,8},{10,11},{13,12},{14,15},{17,16},{18,... | collective-permute-start | bytes 1572872 | tf_op jit(solution)/shard_map/ppermute | solution.py:80
  1474.1 28.9 %collective-permute-start.79 = (bf16[3,64,2048]{2,1,0:T(8,128)(2,1)}, bf16[3,64,2048]{2,1,0:T(8,128)(2,1)}, u32[]{:S(2)}, u32[]{:S(2)}) collective-permute-start(bf16[3,64,2048]{2,1,0:T(8,128)(2,1)} %add_convert_fusion.2), channel_id=1, source_target_pairs={{1,2},{2,1},{5,6},{6,5},{9,10},{10,9},{13,14},{14,13},{17,18},{18,... | collective-permute-start | bytes 2359304 | tf_op jit(solution)/shard_map/ppermute | solution.py:80
  1475.6 25.5 %collective-permute-start.72 = (bf16[3,64,2048]{2,1,0:T(8,128)(2,1)S(1)}, bf16[3,64,2048]{2,1,0:T(8,128)(2,1)S(1)}, u32[]{:S(2)}, u32[]{:S(2)}) collective-permute-start(bf16[3,64,2048]{2,1,0:T(8,128)(2,1)S(1)} %copy-done.6), channel_id=1, source_target_pairs={{0,1},{3,2},{4,5},{7,6},{8,9},{11,10},{12,13},{15,14},{16,17},{19,... | collective-permute-start | bytes 2359304 | tf_op jit(solution)/shard_map/ppermute | solution.py:80
  1488.3 22.5 %collective-permute-start.77 = (bf16[3,64,2048]{2,1,0:T(8,128)(2,1)}, bf16[3,64,2048]{2,1,0:T(8,128)(2,1)}, u32[]{:S(2)}, u32[]{:S(2)}) collective-permute-start(bf16[3,64,2048]{2,1,0:T(8,128)(2,1)} %add_convert_fusion.3), channel_id=1, source_target_pairs={{1,2},{2,1},{5,6},{6,5},{9,10},{10,9},{13,14},{14,13},{17,18},{18,... | collective-permute-start | bytes 2359304 | tf_op jit(solution)/shard_map/ppermute | solution.py:80
  1505.8 18.2 %collective-permute-start.80 = (bf16[2,64,2048]{2,1,0:T(8,128)(2,1)}, bf16[2,64,2048]{2,1,0:T(8,128)(2,1)S(1)}, u32[]{:S(2)}, u32[]{:S(2)}) collective-permute-start(bf16[2,64,2048]{2,1,0:T(8,128)(2,1)} %mix_inward.10), channel_id=1, source_target_pairs={{1,0},{2,3},{5,4},{6,7},{9,8},{10,11},{13,12},{14,15},{17,16},{18,... | collective-permute-start | bytes 1572872 | tf_op jit(solution)/shard_map/ppermute | solution.py:80
  1513.6 19.6 %collective-permute-start.78 = (bf16[2,64,2048]{2,1,0:T(8,128)(2,1)}, bf16[2,64,2048]{2,1,0:T(8,128)(2,1)S(1)}, u32[]{:S(2)}, u32[]{:S(2)}) collective-permute-start(bf16[2,64,2048]{2,1,0:T(8,128)(2,1)} %mix_inward.9), channel_id=1, source_target_pairs={{1,0},{2,3},{5,4},{6,7},{9,8},{10,11},{13,12},{14,15},{17,16},{18,... | collective-permute-start | bytes 1572872 | tf_op jit(solution)/shard_map/ppermute | solution.py:80
  1518.6 25.0 %collective-permute-start.74 = (bf16[2,64,2048]{2,1,0:T(8,128)(2,1)}, bf16[2,64,2048]{2,1,0:T(8,128)(2,1)S(1)}, u32[]{:S(2)}, u32[]{:S(2)}) collective-permute-start(bf16[2,64,2048]{2,1,0:T(8,128)(2,1)} %mix_inward.8), channel_id=1, source_target_pairs={{1,0},{2,3},{5,4},{6,7},{9,8},{10,11},{13,12},{14,15},{17,16},{18,... | collective-permute-start | bytes 1572872 | tf_op jit(solution)/shard_map/ppermute | solution.py:80
  (84 other events, 1587.0 us)
Sparse Core Ops, SparseCore 0:
  11.9 48.2 all-gather.5
  1220.1 45.5 reduce-scatter.6
  1276.7 63.6 reduce-scatter.4
  1343.7 72.4 reduce-scatter.10
  1419.5 71.5 reduce-scatter.8

commit v4 on v3

--- a/solution.py
+++ b/solution.py
@@ -126,18 +126,24 @@
     arrays = [piece for piece, _, _ in pieces]
 
     def kernel(place, *refs):
-        out, sems = refs[-2:]
-        copies = []
+        out, held, sems, sent = refs[-4:]
+        owners = {}
         for n, (code, start) in enumerate(codes):
             size = refs[n].shape[cut]
             span = tuple(
                 pl.ds(start, size) if dim == cut else slice(None) for dim in range(shard.ndim)
             )
-            target = out.at[(place[0] ^ code, *span)]
-            copies.append(pltpu.make_async_copy(refs[n], target, sems.at[n]))
-        for copy in copies:
+            copy = pltpu.make_async_copy(refs[n], held.at[(code, *span)], sems.at[n])
             copy.start()
-        for copy in copies:
+            owners.setdefault(code, []).append(copy)
+        leaving = []
+        for code, copies in owners.items():
+            for copy in copies:
+                copy.wait()
+            copy = pltpu.make_async_copy(held.at[code], out.at[place[0] ^ code], sent.at[code])
+            copy.start()
+            leaving.append(copy)
+        for copy in leaving:
             copy.wait()
 
     anywhere = pl.BlockSpec(memory_space=pl.ANY)
@@ -147,7 +153,11 @@
         in_specs=[pl.BlockSpec(memory_space=pltpu.SMEM)] + [anywhere] * len(arrays),
         out_specs=anywhere,
         out_shape=jax.ShapeDtypeStruct((peers, *shard.shape), shard.dtype),
-        scratch_shapes=[pltpu.SemaphoreType.DMA((len(arrays),))],
+        scratch_shapes=[
+            pltpu.VMEM((peers, *shard.shape), shard.dtype),
+            pltpu.SemaphoreType.DMA((len(arrays),)),
+            pltpu.SemaphoreType.DMA((peers,)),
+        ],
         cost_estimate=cost(2 * size / 3e6),
         name="put_together",
     )(index.astype(jnp.int32).reshape(1), *arrays)

time: 1570 us -> 814 us (0.52)
  Pallas kernels: 988 us -> 234 us
    pallas_call x4, Pallas kernels: 767 us -> 21.2 us  [put_together(): pl.pallas_call(kernel, in_specs=[pl.BlockSpec(memory_space=pltpu.SMEM)] +...]
  transfers between devices with their start and end apart: 96 -> 96, of which waited for: 30 -> 30; matrix products, arithmetic and copies ran while one was open for 6% -> 12% of each run, Pallas kernels for 43% -> 21%
where the time goes in v4:
time: 814 us; the launch traced here: 808 us
  Pallas kernels  234 us (29%)
  waiting for transfers between devices  187 us (23%)
  starting transfers between devices  172 us (21%)
  blocking collectives  67.6 us (8%)
  local copies, waits for them, and re-layouts  47.2 us (6%)
  matrix products  42.1 us (5%)
  other arithmetic  41.8 us (5%)
  between operations  16.4 us (2%)
    ppermute x50, starting transfers between devices, line_hop(): return lax.ppermute(shard, 'stream', pairs)  125 us
    ppermute x50, waiting for transfers between devices, line_hop(): return lax.ppermute(shard, 'stream', pairs)  122 us
    pallas_call x16, Pallas kernels, mix_block(): pl.pallas_call(kernel, grid=(1,), in_specs=specs, out_specs=out_spec, out...  52.2 us
    ppermute x36, waiting for transfers between devices, partner(): return lax.ppermute(shard, 'dp', [(i, i ^ bit) for i in range(peers)])  48.5 us
    dot_general x4, matrix products, dot_rows(): lax.dot_general(left, right, (((0,), (0,)), ((), ())), preferred_element_...  27.5 us
    ppermute x36, starting transfers between devices, partner(): return lax.ppermute(shard, 'dp', [(i, i ^ bit) for i in range(peers)])  25.5 us
    pallas_call x1, Pallas kernels, attend_back(): pl.pallas_call(kernel, grid_spec=pltpu.PrefetchScalarGridSpec(num_scalar_...  25.3 us
    all_gather x1, blocking collectives, body(): offsets = lax.all_gather(spread, 'dp', axis=0)[:, 0, 0]  24.7 us
  transfers between devices with their start and end apart: 96, of which 30 were waited for; matrix products, arithmetic and copies ran while one was open for 12% of the time, Pallas kernels for 21%

profile of v4, /device:TPU:0, one launch (start us, length us, event | category | flops | bytes accessed | tf_op | source)
XLA Modules:
  0.0 808.2 jit_solution(10577056085022430994)
XLA Ops:
  13.6 14.6 %all-gather = f32[2048,16]{0,1:T(8,128)S(1)} all-gather(f32[512,16]{0,1:T(8,128)S(1)} %pad_maximum_fusion.5), channel_id=2, replica_groups=mesh['dp'=8,'stream'=4] {'stream'}, dimensions={0}, use_global_device_ids=true | all-gather | bytes 163840 | tf_op jit(solution)/shard_map/all_gather | solution.py:907
  34.4 12.5 %collective-permute-done.1.refs_2_ = bf16[3,256,512]{2,1,0:T(8,128)(2,1)} collective-permute-done((bf16[3,256,512]{2,1,0:T(8,128)(2,1)}, bf16[3,256,512]{2,1,0:T(8,128)(2,1)}, u32[]{:S(2)}, u32[]{:S(2)}) %collective-permute-start.1) | collective-permute-done | bytes 786464 | tf_op jit(solution)/shard_map/ppermute | solution.py:76
  50.0 22.6 %make_streams.1 = (bf16[4,512,2048]{2,1,0:T(8,128)(2,1)}, bf16[4,512,2048]{2,1,0:T(8,128)(2,1)}, f32[512,4]{1,0:T(8,128)}, f32[512,2048]{1,0:T(8,128)}) custom-call(bf16[8,512,2048]{2,1,0:T(8,128)(2,1)} %hist.1, f32[512,32]{1,0:T(8,128)} %copy.145.mix, f32[4,2048]{1,0:T(4,128)} %get-tuple-element.245.gain, f32[4,2048]{1,0:T(4,128)} %get-tuple-element.244.bias), custom_call_target="tpu_custom_call" | custom-call | flops 19800000512 | bytes 66000000 | tf_op jit(solution)/shard_map/make_streams/pallas_call | solution.py:254
  72.5 5.6 put_together.4.w
  78.2 9.2 %project.1 = bf16[8,3,256,128]{3,2,1,0:T(8,128)(2,1)} custom-call(bf16[4,512,2048]{2,1,0:T(8,128)(2,1)} %get-tuple-element.78.x, bf16[8,3,256,512]{3,2,1,0:T(8,128)(2,1)} %put_together.4.w, f32[3,512,128]{2,1,0:T(8,128)} %get-tuple-element.223.table), custom_call_target="tpu_custom_call" | custom-call | flops 8099999744 | bytes 27000000 | tf_op jit(solution)/shard_map/project/pallas_call | solution.py:304
  97.4 19.7 %collective-permute-done.18.refs_2_ = bf16[512,256]{1,0:T(8,128)(2,1)S(1)} collective-permute-done((bf16[512,256]{1,0:T(8,128)(2,1)}, bf16[512,256]{1,0:T(8,128)(2,1)S(1)}, u32[]{:S(2)}, u32[]{:S(2)}) %collective-permute-start.18) | collective-permute-done | bytes 262176 | tf_op jit(solution)/shard_map/ppermute | solution.py:76
  119.6 11.4 %collective-permute-done.19.refs_3_ = bf16[256,256]{1,0:T(8,128)(2,1)S(1)} collective-permute-done((bf16[256,256]{1,0:T(8,128)(2,1)S(1)}, bf16[256,256]{1,0:T(8,128)(2,1)S(1)}, u32[]{:S(2)}, u32[]{:S(2)}) %collective-permute-start.19) | collective-permute-done | bytes 131104 | tf_op jit(solution)/shard_map/ppermute | solution.py:76
  132.4 3.8 collective-permute-done.20.refs_4_
  137.5 14.6 %all-gather.2 = f32[2048,46]{0,1:T(8,128)S(1)} all-gather(f32[512,46]{0,1:T(8,128)S(1)} %pad_maximum_fusion.3), channel_id=4, replica_groups=mesh['dp'=8,'stream'=4] {'stream'}, dimensions={0}, use_global_device_ids=true | all-gather | bytes 471040 | tf_op jit(solution)/shard_map/all_gather | solution.py:932
  160.3 24.7 %all-gather.1 = s32[64,128]{1,0:T(8,128)S(1)} all-gather(s32[8,128]{1,0:T(8,128)S(1)} %broadcast_in_dim.51), channel_id=3, replica_groups=mesh['dp'=8,'stream'=4] {'dp'}, dimensions={0}, use_global_device_ids=true | all-gather | bytes 36864 | tf_op jit(solution)/shard_map/all_gather | solution.py:942
  188.3 6.6 put_together.5
  200.5 19.1 %attend.1 = (bf16[8,256,128]{2,1,0:T(8,128)(2,1)}, f32[8,256,128]{2,1,0:T(8,128)}, f32[8,256,1]{2,1,0:T(8,128)}) custom-call(s32[8]{0:T(128)} %subtract_maximum_fusion.first, s32[1]{0:T(128)} %bitcast.7.part, bf16[8,3,256,128]{3,2,1,0:T(8,128)(2,1)} %copy-done.4, bf16[8,2,256,128]{3,2,1,0:T(8,128)(2,1)} %collective-permute-done.9.theirs), custom_call_target="tpu_custom_call" | custom-call | flops 14400000000 | bytes 48000000 | tf_op jit(solution)/shard_map/attend/pallas_call | solution.py:363
  219.6 5.7 all-to-all-start.1
  227.1 10.0 %hidden_units.1 = (bf16[512,2048]{1,0:T(8,128)(2,1)}, bf16[512,2048]{1,0:T(8,128)(2,1)}) custom-call(bf16[512,2048]{1,0:T(8,128)(2,1)} %slice_bitcast_fusion.1.x_ref, bf16[2048,2048]{1,0:T(8,128)(2,1)} %bitcast.111), custom_call_target="tpu_custom_call" | custom-call | flops 8099999744 | bytes 27000000 | tf_op jit(solution)/shard_map/hidden_units/pallas_call | solution.py:785
  240.3 6.6 put_together.7.wd.refs_1_
  246.9 13.1 %merge_branches.1 = f32[512,2048]{1,0:T(8,128)} custom-call(bf16[512,512]{1,0:T(8,128)(2,1)} %bitcast.101, bf16[512,2048]{1,0:T(8,128)(2,1)} %get-tuple-element.109.h, bf16[8,512,256]{2,1,0:T(8,128)(2,1)} %put_together.6.wm.refs_1_, bf16[8,2048,256]{2,1,0:T(8,128)(2,1)} %put_together.7.wd.refs_1_, f32[512,2048]{1,0:T(8,128)} %get-tuple-element.93.st, ...), custom_call_target="tpu_custom_call" | custom-call | flops 11699999744 | bytes 39000000 | tf_op jit(solution)/shard_map/merge_branches/pallas_call | solution.py:810
  262.7 4.1 collective-permute-start.35
  268.1 5.3 collective-permute-done.35
  274.2 4.2 collective-permute-done.38
  278.4 8.4 %collective-permute-start.44 = (bf16[64,2048]{1,0:T(8,128)(2,1)S(1)}, bf16[64,2048]{1,0:T(8,128)(2,1)S(1)}, u32[]{:S(2)}, u32[]{:S(2)}) collective-permute-start(bf16[64,2048]{1,0:T(8,128)(2,1)S(1)} %get-tuple-element.95), channel_id=1, source_target_pairs={{0,1},{3,2},{4,5},{7,6},{8,9},{11,10},{12,13},{15,14},{16,17},{19,... | collective-permute-start | bytes 786440 | tf_op jit(solution)/shard_map/ppermute | solution.py:80
  288.1 5.2 collective-permute-done.44
  296.2 5.6 collective-permute-done.37
  301.8 5.9 collective-permute-start.47
  307.7 3.8 collective-permute-done.47
  316.6 3.7 collective-permute-done.40
  320.3 6.5 collective-permute-start.50
  327.5 3.8 collective-permute-done.50
  331.3 4.4 collective-permute-start.56
  342.2 6.9 collective-permute-done.43
  361.5 9.9 %collective-permute-done.49 = bf16[64,2048]{1,0:T(8,128)(2,1)S(1)} collective-permute-done((bf16[64,2048]{1,0:T(8,128)(2,1)S(1)}, bf16[64,2048]{1,0:T(8,128)(2,1)S(1)}, u32[]{:S(2)}, u32[]{:S(2)}) %collective-permute-start.49) | collective-permute-done | bytes 262176 | tf_op jit(solution)/shard_map/ppermute | solution.py:80
  384.8 7.2 back_through.2
  392.0 13.3 %back_through.3 = bf16[512,2048]{1,0:T(8,128)(2,1)} custom-call(bf16[512,2048]{1,0:T(8,128)(2,1)} %fusion.3.refs_0_.e, bf16[8,2048,256]{2,1,0:T(8,128)(2,1)} %put_together.7.wd.refs_1_, bf16[512,2048]{1,0:T(8,128)(2,1)} %get-tuple-element.100.refs_2_), custom_call_target="tpu_custom_call" | custom-call | flops 11699999744 | bytes 39000000 | tf_op jit(solution)/shard_map/back_through/pallas_call | solution.py:865
  405.3 10.6 %fusion.43.g = f32[512,2048]{1,0:T(8,128)} fusion(bf16[512,2048]{1,0:T(8,128)(2,1)} %back_through.3, bf16[2048,2048]{1,0:T(8,128)(2,1)} %bitcast.112), kind=kOutput, calls=%fused_computation.147 | convolution fusion | flops 4294967296 | bytes 14680064 | tf_op jit(solution)/shard_map/dot_general | solution.py:71
  420.4 6.4 last_back.1
  430.8 25.3 %attend_back.1 = (bf16[8,3,256,128]{3,2,1,0:T(8,128)(2,1)}, bf16[8,2,256,128]{3,2,1,0:T(8,128)(2,1)}) custom-call(s32[8]{0:T(128)} %subtract_maximum_fusion.first, s32[1]{0:T(128)} %bitcast.7.part, bf16[8,3,256,128]{3,2,1,0:T(8,128)(2,1)} %copy-done.4, bf16[8,2,256,128]{3,2,1,0:T(8,128)(2,1)} %collective-permute-done.9.theirs, ...), custom_call_target="tpu_custom_call" | custom-call | flops 19800000512 | bytes 66000000 | tf_op jit(solution)/shard_map/attend_back/pallas_call | solution.py:437
  460.9 4.4 convolution_convert_fusion.2
  469.2 4.3 all-to-all-start.3
  473.6 10.4 %convolution_convert_fusion.1 = bf16[2048,2048]{1,0:T(8,128)(2,1)} fusion(bf16[512,2048]{1,0:T(8,128)(2,1)} %get-tuple-element.109.h, bf16[512,2048]{1,0:T(8,128)(2,1)} %fusion.3.refs_0_.e), kind=kOutput, calls=%fused_computation.1 | convolution fusion | flops 4299161600 | bytes 12582912 | tf_op jit(solution)/shard_map/dot_general | solution.py:67
  484.0 20.6 %collective-permute-done.60.refs_5_ = bf16[512,2048]{1,0:T(8,128)(2,1)} collective-permute-done((bf16[512,2048]{1,0:T(8,128)(2,1)S(1)}, bf16[512,2048]{1,0:T(8,128)(2,1)}, u32[]{:S(2)}, u32[]{:S(2)}) %collective-permute-start.60) | collective-permute-done | bytes 2097184 | tf_op jit(solution)/shard_map/ppermute | solution.py:80
  504.5 17.3 %heads_back.1 = (bf16[3,64,2048]{2,1,0:T(8,128)(2,1)}, bf16[3,64,2048]{2,1,0:T(8,128)(2,1)}, bf16[3,64,2048]{2,1,0:T(8,128)(2,1)}, bf16[3,64,2048]{2,1,0:T(8,128...) custom-call(bf16[8,3,256,128]{3,2,1,0:T(8,128)(2,1)} %all-to-all-don, ...), custom_call_target="tpu_custom_call" | custom-call | flops 16199999488 | bytes 54000000 | tf_op jit(solution)/shard_map/heads_back/pallas_call | solution.py:510
  524.5 11.0 %convolution_convert_fusion = bf16[2048,2048]{1,0:T(8,128)(2,1)} fusion(bf16[512,2048]{1,0:T(8,128)(2,1)} %back_through.3, bf16[4,512,2048]{2,1,0:T(8,128)(2,1)} %get-tuple-element.78.x), kind=kOutput, calls=%fused_computation | convolution fusion | flops 4299161600 | bytes 12582912 | tf_op jit(solution)/shard_map/dot_general | solution.py:67
  538.7 4.0 add_convert_fusion
  543.5 8.1 %collective-permute-start.62 = (bf16[3,64,2048]{2,1,0:T(8,128)(2,1)}, bf16[3,64,2048]{2,1,0:T(8,128)(2,1)}, u32[]{:S(2)}, u32[]{:S(2)}) collective-permute-start(bf16[3,64,2048]{2,1,0:T(8,128)(2,1)} %get-tuple-element.115.refs_1_), channel_id=1, source_target_pairs={{0,1},{3,2},{4,5},{7,6},{8,9},{11,10},{12,13},{15,14},{16,17},{19,... | collective-permute-start | bytes 2359304 | tf_op jit(solution)/shard_map/ppermute | solution.py:80
  551.6 17.3 %mixing_back.1 = f32[4,512,8]{2,1,0:T(8,128)} custom-call(bf16[3,512,2048]{2,1,0:T(8,128)(2,1)} %get-tuple-element.121.first, bf16[512,2048]{1,0:T(8,128)(2,1)} %get-tuple-element.103.last.refs_3_.refs_4_, bf16[8,512,2048]{2,1,0:T(8,128)(2,1)} %hist.1), custom_call_target="tpu_custom_call" | custom-call | flops 16199999488 | bytes 54000000 | tf_op jit(solution)/shard_map/mixing_back/pallas_call | solution.py:602
  578.9 4.8 collective-permute-start.61
  583.7 12.7 %all-to-all-done.4 = f32[4,512,16]{1,2,0:T(8,128)S(1)} async-done(((f32[4,512,16]{1,2,0:T(8,128)}), f32[4,512,16]{1,2,0:T(8,128)S(1)}, u32[]{:S(2)}, u32[]{:S(2)}) %all-to-all-start.4) | async-done | bytes 131104 | tf_op jit(solution)/shard_map/all_to_all | solution.py:1061
  606.8 13.7 %all-gather.3 = f32[4096,45]{0,1:T(8,128)S(1)} all-gather(f32[512,45]{0,1:T(8,128)S(1)} %pad_maximum_fusion.4), channel_id=5, replica_groups=mesh['dp'=8,'stream'=4] {'dp'}, dimensions={0}, use_global_device_ids=true | all-gather | bytes 829440 | tf_op jit(solution)/shard_map/all_gather | solution.py:1068
  621.9 7.7 collective-permute-start.66
  644.0 6.5 collective-permute-start.64
  657.9 3.7 mix_final.8
  661.7 6.4 collective-permute-done.64.refs_2_
  674.9 8.9 %collective-permute-done.70.refs_2_ = bf16[3,64,2048]{2,1,0:T(8,128)(2,1)S(1)} collective-permute-done((bf16[3,64,2048]{2,1,0:T(8,128)(2,1)S(1)}, bf16[3,64,2048]{2,1,0:T(8,128)(2,1)S(1)}, u32[]{:S(2)}, u32[]{:S(2)}) %collective-permute-start.70) | collective-permute-done | bytes 786464 | tf_op jit(solution)/shard_map/ppermute | solution.py:80
  685.7 3.7 mix_final.9
  689.4 9.0 %collective-permute-start.68 = (bf16[3,64,2048]{2,1,0:T(8,128)(2,1)S(1)}, bf16[3,64,2048]{2,1,0:T(8,128)(2,1)}, u32[]{:S(2)}, u32[]{:S(2)}) collective-permute-start(bf16[3,64,2048]{2,1,0:T(8,128)(2,1)S(1)} %copy-done.8), channel_id=1, source_target_pairs={{0,1},{3,2},{4,5},{7,6},{8,9},{11,10},{12,13},{15,14},{16,17},{19,... | collective-permute-start | bytes 2359304 | tf_op jit(solution)/shard_map/ppermute | solution.py:80
  702.7 5.4 collective-permute-start.76
  708.0 3.7 mix_final.10
  720.8 5.7 collective-permute-start.72
  726.6 3.7 mix_final.11
  735.0 11.3 %collective-permute-done.72.refs_2_ = bf16[3,64,2048]{2,1,0:T(8,128)(2,1)S(1)} collective-permute-done((bf16[3,64,2048]{2,1,0:T(8,128)(2,1)S(1)}, bf16[3,64,2048]{2,1,0:T(8,128)(2,1)S(1)}, u32[]{:S(2)}, u32[]{:S(2)}) %collective-permute-start.72) | collective-permute-done | bytes 786464 | tf_op jit(solution)/shard_map/ppermute | solution.py:80
  752.3 3.7 mix_final.12
  765.3 3.9 collective-permute-done.80.refs_7_
  770.0 3.6 mix_final.13
  773.7 4.5 collective-permute-done.78.refs_7_
  782.7 6.1 collective-permute-done.74.refs_7_
  (395 shorter events, 225.6 us)
Async XLA Ops:
  7.2 148.3 %all-gather.6.cloned.1.call-start = ((), (), s32[]{:S(2)}) async-start(), calls=%async_computation.9 | async-start | bytes 2621440 | tf_op jit(solution)/shard_map/all_gather | solution.py:905
  7.2 27.2 %collective-permute-start = (bf16[3,256,512]{2,1,0:T(8,128)(2,1)}, bf16[3,256,512]{2,1,0:T(8,128)(2,1)S(1)}, u32[]{:S(2)}, u32[]{:S(2)}) collective-permute-start(bf16[3,256,512]{2,1,0:T(8,128)(2,1)} %refs_0_.1), channel_id=1, source_target_pairs={{0,8},{4,12},{8,0},{12,4},{16,24},{20,28},{24,16},{28,20},{1,9},{5... | collective-permute-start | bytes 2359304 | tf_op jit(solution)/shard_map/ppermute | solution.py:76
  10.3 36.6 %collective-permute-start.1 = (bf16[3,256,512]{2,1,0:T(8,128)(2,1)}, bf16[3,256,512]{2,1,0:T(8,128)(2,1)}, u32[]{:S(2)}, u32[]{:S(2)}) collective-permute-start(bf16[3,256,512]{2,1,0:T(8,128)(2,1)} %refs_0_.1), channel_id=1, source_target_pairs={{0,16},{4,20},{8,24},{12,28},{16,0},{20,4},{24,8},{28,12},{1,17},{... | collective-permute-start | bytes 2359304 | tf_op jit(solution)/shard_map/ppermute | solution.py:76
  11.8 37.7 %collective-permute-start.2 = (bf16[3,256,512]{2,1,0:T(8,128)(2,1)}, bf16[3,256,512]{2,1,0:T(8,128)(2,1)}, u32[]{:S(2)}, u32[]{:S(2)}) collective-permute-start(bf16[3,256,512]{2,1,0:T(8,128)(2,1)} %refs_0_.1), channel_id=1, source_target_pairs={{0,24},{4,28},{8,16},{12,20},{16,8},{20,12},{24,0},{28,4},{1,25},{... | collective-permute-start | bytes 2359304 | tf_op jit(solution)/shard_map/ppermute | solution.py:76
  11.8 38.1 %collective-permute-start.5 = (bf16[3,256,512]{2,1,0:T(8,128)(2,1)}, bf16[3,256,512]{2,1,0:T(8,128)(2,1)}, u32[]{:S(2)}, u32[]{:S(2)}) collective-permute-start(bf16[3,256,512]{2,1,0:T(8,128)(2,1)} %refs_0_.1), channel_id=1, source_target_pairs={{0,4},{4,0},{8,12},{12,8},{16,20},{20,16},{24,28},{28,24},{1,5},{5... | collective-permute-start | bytes 2359304 | tf_op jit(solution)/shard_map/ppermute | solution.py:76
  46.9 31.2 %collective-permute-start.3 = (bf16[256,2048]{1,0:T(8,128)(2,1)S(1)}, bf16[256,2048]{1,0:T(8,128)(2,1)}, u32[]{:S(2)}, u32[]{:S(2)}) collective-permute-start(bf16[256,2048]{1,0:T(8,128)(2,1)S(1)} %copy-done.42), channel_id=1, source_target_pairs={{0,8},{4,12},{8,0},{12,4},{16,24},{20,28},{24,16},{28,20},{1,9},{5... | collective-permute-start | bytes 3145736 | tf_op jit(solution)/shard_map/ppermute | solution.py:76
  46.9 31.3 %collective-permute-start.4 = (bf16[256,2048]{1,0:T(8,128)(2,1)S(1)}, bf16[256,2048]{1,0:T(8,128)(2,1)S(1)}, u32[]{:S(2)}, u32[]{:S(2)}) collective-permute-start(bf16[256,2048]{1,0:T(8,128)(2,1)S(1)} %copy-done.42), channel_id=1, source_target_pairs={{0,16},{4,20},{8,24},{12,28},{16,0},{20,4},{24,8},{28,12},{1,17},{... | collective-permute-start | bytes 3145736 | tf_op jit(solution)/shard_map/ppermute | solution.py:76
  49.4 23.1 %collective-permute-start.6 = (bf16[3,256,512]{2,1,0:T(8,128)(2,1)S(1)}, bf16[3,256,512]{2,1,0:T(8,128)(2,1)}, u32[]{:S(2)}, u32[]{:S(2)}) collective-permute-start(bf16[3,256,512]{2,1,0:T(8,128)(2,1)S(1)} %collective-permute-done.refs_1_), channel_id=1, source_target_pairs={{0,4},{4,0},{8,12},{12,8},{16,20},{20,16},{24,28},{28,24},{1,5},{5... | collective-permute-start | bytes 2359304 | tf_op jit(solution)/shard_map/ppermute | solution.py:76
  49.4 23.1 %collective-permute-start.7 = (bf16[3,256,512]{2,1,0:T(8,128)(2,1)}, bf16[3,256,512]{2,1,0:T(8,128)(2,1)}, u32[]{:S(2)}, u32[]{:S(2)}) collective-permute-start(bf16[3,256,512]{2,1,0:T(8,128)(2,1)} %collective-permute-done.1.refs_2_), channel_id=1, source_target_pairs={{0,4},{4,0},{8,12},{12,8},{16,20},{20,16},{24,28},{28,24},{1,5},{5... | collective-permute-start | bytes 2359304 | tf_op jit(solution)/shard_map/ppermute | solution.py:76
  49.9 22.6 %collective-permute-start.8 = (bf16[3,256,512]{2,1,0:T(8,128)(2,1)}, bf16[3,256,512]{2,1,0:T(8,128)(2,1)}, u32[]{:S(2)}, u32[]{:S(2)}) collective-permute-start(bf16[3,256,512]{2,1,0:T(8,128)(2,1)} %collective-permute-done.2.refs_3_), channel_id=1, source_target_pairs={{0,4},{4,0},{8,12},{12,8},{16,20},{20,16},{24,28},{28,24},{1,5},{5... | collective-permute-start | bytes 2359304 | tf_op jit(solution)/shard_map/ppermute | solution.py:76
  87.4 68.1 %all-to-all-start = ((bf16[8,3,256,128]{3,2,1,0:T(8,128)(2,1)}), bf16[8,3,256,128]{3,2,1,0:T(8,128)(2,1)S(1)}, u32[]{:S(2)}, u32[]{:S(2)}) async-start(bf16[8,3,256,128]{3,2,1,0:T(8,128)(2,1)} %project.1), calls=%async_computation | async-start | bytes 3145728 | tf_op jit(solution)/shard_map/all_to_all | solution.py:946
  91.0 26.1 %collective-permute-start.18 = (bf16[512,256]{1,0:T(8,128)(2,1)}, bf16[512,256]{1,0:T(8,128)(2,1)S(1)}, u32[]{:S(2)}, u32[]{:S(2)}) collective-permute-start(bf16[512,256]{1,0:T(8,128)(2,1)} %refs_0_.3), channel_id=1, source_target_pairs={{0,16},{4,20},{8,24},{12,28},{16,0},{20,4},{24,8},{28,12},{1,17},{... | collective-permute-start | bytes 786440 | tf_op jit(solution)/shard_map/ppermute | solution.py:76
  93.0 25.2 %collective-permute-start.17 = (bf16[512,256]{1,0:T(8,128)(2,1)}, bf16[512,256]{1,0:T(8,128)(2,1)}, u32[]{:S(2)}, u32[]{:S(2)}) collective-permute-start(bf16[512,256]{1,0:T(8,128)(2,1)} %refs_0_.3), channel_id=1, source_target_pairs={{0,8},{4,12},{8,0},{12,4},{16,24},{20,28},{24,16},{28,20},{1,9},{5... | collective-permute-start | bytes 786440 | tf_op jit(solution)/shard_map/ppermute | solution.py:76
  95.5 41.4 %collective-permute-start.10 = (bf16[128,2048]{1,0:T(8,128)(2,1)S(1)}, bf16[128,2048]{1,0:T(8,128)(2,1)}, u32[]{:S(2)}, u32[]{:S(2)}) collective-permute-start(bf16[128,2048]{1,0:T(8,128)(2,1)S(1)} %slice.134), channel_id=1, source_target_pairs={{0,8},{4,12},{8,0},{12,4},{16,24},{20,28},{24,16},{28,20},{1,9},{5... | collective-permute-start | bytes 1572872 | tf_op jit(solution)/shard_map/ppermute | solution.py:76
  97.2 39.8 %collective-permute-start.11 = (bf16[128,2048]{1,0:T(8,128)(2,1)S(1)}, bf16[128,2048]{1,0:T(8,128)(2,1)}, u32[]{:S(2)}, u32[]{:S(2)}) collective-permute-start(bf16[128,2048]{1,0:T(8,128)(2,1)S(1)} %slice.135), channel_id=1, source_target_pairs={{0,16},{4,20},{8,24},{12,28},{16,0},{20,4},{24,8},{28,12},{1,17},{... | collective-permute-start | bytes 1572872 | tf_op jit(solution)/shard_map/ppermute | solution.py:76
  118.1 18.1 %collective-permute-start.22 = (bf16[512,256]{1,0:T(8,128)(2,1)}, bf16[512,256]{1,0:T(8,128)(2,1)}, u32[]{:S(2)}, u32[]{:S(2)}) collective-permute-start(bf16[512,256]{1,0:T(8,128)(2,1)} %collective-permute-done.17.refs_1_), channel_id=1, source_target_pairs={{0,4},{4,0},{8,12},{12,8},{16,20},{20,16},{24,28},{28,24},{1,5},{5... | collective-permute-start | bytes 786440 | tf_op jit(solution)/shard_map/ppermute | solution.py:76
  118.1 39.0 %collective-permute-start.13 = (bf16[256,2048]{1,0:T(8,128)(2,1)}, bf16[256,2048]{1,0:T(8,128)(2,1)}, u32[]{:S(2)}, u32[]{:S(2)}) collective-permute-start(bf16[256,2048]{1,0:T(8,128)(2,1)} %collective-permute-done.3.refs_1_), channel_id=1, source_target_pairs={{0,4},{4,0},{8,12},{12,8},{16,20},{20,16},{24,28},{28,24},{1,5},{5... | collective-permute-start | bytes 3145736 | tf_op jit(solution)/shard_map/ppermute | solution.py:76
  136.9 18.7 %collective-permute-start.15 = (bf16[128,2048]{1,0:T(8,128)(2,1)}, bf16[128,2048]{1,0:T(8,128)(2,1)}, u32[]{:S(2)}, u32[]{:S(2)}) collective-permute-start(bf16[128,2048]{1,0:T(8,128)(2,1)} %collective-permute-done.10.refs_3_), channel_id=1, source_target_pairs={{0,4},{4,0},{8,12},{12,8},{16,20},{20,16},{24,28},{28,24},{1,5},{5... | collective-permute-start | bytes 1572872 | tf_op jit(solution)/shard_map/ppermute | solution.py:76
  137.0 19.6 %collective-permute-start.16 = (bf16[128,2048]{1,0:T(8,128)(2,1)}, bf16[128,2048]{1,0:T(8,128)(2,1)}, u32[]{:S(2)}, u32[]{:S(2)}) collective-permute-start(bf16[128,2048]{1,0:T(8,128)(2,1)} %collective-permute-done.11.refs_4_), channel_id=1, source_target_pairs={{0,4},{4,0},{8,12},{12,8},{16,20},{20,16},{24,28},{28,24},{1,5},{5... | collective-permute-start | bytes 1572872 | tf_op jit(solution)/shard_map/ppermute | solution.py:76
  153.8 34.4 %collective-permute-start.14 = (bf16[256,2048]{1,0:T(8,128)(2,1)}, bf16[256,2048]{1,0:T(8,128)(2,1)}, u32[]{:S(2)}, u32[]{:S(2)}) collective-permute-start(bf16[256,2048]{1,0:T(8,128)(2,1)} %copy-done.27), channel_id=1, source_target_pairs={{0,4},{4,0},{8,12},{12,8},{16,20},{20,16},{24,28},{28,24},{1,5},{5... | collective-permute-start | bytes 3145736 | tf_op jit(solution)/shard_map/ppermute | solution.py:76
  154.2 34.1 %collective-permute-start.12 = (bf16[256,2048]{1,0:T(8,128)(2,1)}, bf16[256,2048]{1,0:T(8,128)(2,1)}, u32[]{:S(2)}, u32[]{:S(2)}) collective-permute-start(bf16[256,2048]{1,0:T(8,128)(2,1)} %refs_0_.2), channel_id=1, source_target_pairs={{0,4},{4,0},{8,12},{12,8},{16,20},{20,16},{24,28},{28,24},{1,5},{5... | collective-permute-start | bytes 3145736 | tf_op jit(solution)/shard_map/ppermute | solution.py:76
  155.6 39.5 %collective-permute-start.27 = (bf16[2048,256]{1,0:T(8,128)(2,1)}, bf16[2048,256]{1,0:T(8,128)(2,1)}, u32[]{:S(2)}, u32[]{:S(2)}) collective-permute-start(bf16[2048,256]{1,0:T(8,128)(2,1)} %refs_0_.4), channel_id=1, source_target_pairs={{0,16},{4,20},{8,24},{12,28},{16,0},{20,4},{24,8},{28,12},{1,17},{... | collective-permute-start | bytes 3145736 | tf_op jit(solution)/shard_map/ppermute | solution.py:76
  156.6 41.1 %collective-permute-start.26 = (bf16[2048,256]{1,0:T(8,128)(2,1)}, bf16[2048,256]{1,0:T(8,128)(2,1)}, u32[]{:S(2)}, u32[]{:S(2)}) collective-permute-start(bf16[2048,256]{1,0:T(8,128)(2,1)} %refs_0_.4), channel_id=1, source_target_pairs={{0,8},{4,12},{8,0},{12,4},{16,24},{20,28},{24,16},{28,20},{1,9},{5... | collective-permute-start | bytes 3145736 | tf_op jit(solution)/shard_map/ppermute | solution.py:76
  157.2 42.9 %collective-permute-start.9 = (bf16[8,2,256,128]{3,2,1,0:T(8,128)(2,1)S(1)}, bf16[8,2,256,128]{3,2,1,0:T(8,128)(2,1)}, u32[]{:S(2)}, u32[]{:S(2)}) collective-permute-start(bf16[8,2,256,128]{3,2,1,0:T(8,128)(2,1)S(1)} %slice.132), channel_id=1, source_target_pairs={{0,4},{4,0},{8,12},{12,8},{16,20},{20,16},{24,28},{28,24},{1,5},{5... | collective-permute-start | bytes 3145736 | tf_op jit(solution)/shard_map/ppermute | solution.py:76
  194.9 43.5 %collective-permute-start.30 = (bf16[2048,256]{1,0:T(8,128)(2,1)}, bf16[2048,256]{1,0:T(8,128)(2,1)}, u32[]{:S(2)}, u32[]{:S(2)}) collective-permute-start(bf16[2048,256]{1,0:T(8,128)(2,1)} %refs_0_.4), channel_id=1, source_target_pairs={{0,4},{4,0},{8,12},{12,8},{16,20},{20,16},{24,28},{28,24},{1,5},{5... | collective-permute-start | bytes 3145736 | tf_op jit(solution)/shard_map/ppermute | solution.py:76
  196.2 29.1 %collective-permute-start.28 = (bf16[1024,256]{1,0:T(8,128)(2,1)S(1)}, bf16[1024,256]{1,0:T(8,128)(2,1)}, u32[]{:S(2)}, u32[]{:S(2)}) collective-permute-start(bf16[1024,256]{1,0:T(8,128)(2,1)S(1)} %slice.170), channel_id=1, source_target_pairs={{0,8},{4,12},{8,0},{12,4},{16,24},{20,28},{24,16},{28,20},{1,9},{5... | collective-permute-start | bytes 1572872 | tf_op jit(solution)/shard_map/ppermute | solution.py:76
  198.8 28.1 %collective-permute-start.29 = (bf16[1024,256]{1,0:T(8,128)(2,1)S(1)}, bf16[1024,256]{1,0:T(8,128)(2,1)}, u32[]{:S(2)}, u32[]{:S(2)}) collective-permute-start(bf16[1024,256]{1,0:T(8,128)(2,1)S(1)} %slice.171), channel_id=1, source_target_pairs={{0,16},{4,20},{8,24},{12,28},{16,0},{20,4},{24,8},{28,12},{1,17},{... | collective-permute-start | bytes 1572872 | tf_op jit(solution)/shard_map/ppermute | solution.py:76
  200.0 38.4 %collective-permute-start.31 = (bf16[2048,256]{1,0:T(8,128)(2,1)}, bf16[2048,256]{1,0:T(8,128)(2,1)}, u32[]{:S(2)}, u32[]{:S(2)}) collective-permute-start(bf16[2048,256]{1,0:T(8,128)(2,1)} %collective-permute-done.26.refs_1_), channel_id=1, source_target_pairs={{0,4},{4,0},{8,12},{12,8},{16,20},{20,16},{24,28},{28,24},{1,5},{5... | collective-permute-start | bytes 3145736 | tf_op jit(solution)/shard_map/ppermute | solution.py:76
  200.0 38.4 %collective-permute-start.32 = (bf16[2048,256]{1,0:T(8,128)(2,1)}, bf16[2048,256]{1,0:T(8,128)(2,1)S(1)}, u32[]{:S(2)}, u32[]{:S(2)}) collective-permute-start(bf16[2048,256]{1,0:T(8,128)(2,1)} %collective-permute-done.27.refs_2_), channel_id=1, source_target_pairs={{0,4},{4,0},{8,12},{12,8},{16,20},{20,16},{24,28},{28,24},{1,5},{5... | collective-permute-start | bytes 3145736 | tf_op jit(solution)/shard_map/ppermute | solution.py:76
  219.6 17.5 %all-to-all-start.1 = ((bf16[8,256,128]{2,1,0:T(8,128)(2,1)}), bf16[8,256,128]{2,1,0:T(8,128)(2,1)S(1)}, u32[]{:S(2)}, u32[]{:S(2)}) async-start(bf16[8,256,128]{2,1,0:T(8,128)(2,1)} %get-tuple-element.82), calls=%async_computation.1 | async-start | bytes 1048576 | tf_op jit(solution)/shard_map/all_to_all | solution.py:953
  357.2 17.0 %collective-permute-start.52 = (bf16[64,2048]{1,0:T(8,128)(2,1)S(1)}, bf16[64,2048]{1,0:T(8,128)(2,1)S(1)}, u32[]{:S(2)}, u32[]{:S(2)}) collective-permute-start(bf16[64,2048]{1,0:T(8,128)(2,1)S(1)} %get-tuple-element.200), channel_id=1, source_target_pairs={{1,0},{2,3},{5,4},{6,7},{9,8},{10,11},{13,12},{14,15},{17,16},{18,... | collective-permute-start | bytes 786440 | tf_op jit(solution)/shard_map/ppermute | solution.py:80
  358.5 18.5 %collective-permute-start.55 = (bf16[64,2048]{1,0:T(8,128)(2,1)S(1)}, bf16[64,2048]{1,0:T(8,128)(2,1)S(1)}, u32[]{:S(2)}, u32[]{:S(2)}) collective-permute-start(bf16[64,2048]{1,0:T(8,128)(2,1)S(1)} %get-tuple-element.199), channel_id=1, source_target_pairs={{1,0},{2,3},{5,4},{6,7},{9,8},{10,11},{13,12},{14,15},{17,16},{18,... | collective-permute-start | bytes 786440 | tf_op jit(solution)/shard_map/ppermute | solution.py:80
  359.8 20.0 %collective-permute-start.58 = (bf16[64,2048]{1,0:T(8,128)(2,1)S(1)}, bf16[64,2048]{1,0:T(8,128)(2,1)S(1)}, u32[]{:S(2)}, u32[]{:S(2)}) collective-permute-start(bf16[64,2048]{1,0:T(8,128)(2,1)S(1)} %get-tuple-element.198), channel_id=1, source_target_pairs={{1,0},{2,3},{5,4},{6,7},{9,8},{10,11},{13,12},{14,15},{17,16},{18,... | collective-permute-start | bytes 786440 | tf_op jit(solution)/shard_map/ppermute | solution.py:80
  420.3 212.5 %reduce-scatter.7.cloned.1.call-start = ((), (), s32[]{:S(2)}) async-start(), calls=%async_computation.11 | async-start | bytes 2359296 | tf_op jit(solution)/shard_map/reduce_scatter | solution.py:1041
  457.9 46.6 %collective-permute-start.60 = (bf16[512,2048]{1,0:T(8,128)(2,1)S(1)}, bf16[512,2048]{1,0:T(8,128)(2,1)}, u32[]{:S(2)}, u32[]{:S(2)}) collective-permute-start(bf16[512,2048]{1,0:T(8,128)(2,1)S(1)} %copy-done), channel_id=1, source_target_pairs={{0,1},{3,2},{4,5},{7,6},{8,9},{11,10},{12,13},{15,14},{16,17},{19,... | collective-permute-start | bytes 6291464 | tf_op jit(solution)/shard_map/ppermute | solution.py:80
  469.2 35.3 %all-to-all-start.3 = ((bf16[8,3,256,128]{3,2,1,0:T(8,128)(2,1)}), bf16[8,3,256,128]{3,2,1,0:T(8,128)(2,1)}, u32[]{:S(2)}, u32[]{:S(2)}) async-start(bf16[8,3,256,128]{3,2,1,0:T(8,128)(2,1)} %pad_maximum_fusion), calls=%async_computation.3 | async-start | bytes 3145728 | tf_op jit(solution)/shard_map/all_to_all | solution.py:1026
  473.5 319.7 %reduce-scatter.5.cloned.1.call-start = ((), (), s32[]{:S(2)}) async-start(), calls=%async_computation.10 | async-start | bytes 7077888 | tf_op jit(solution)/shard_map/reduce_scatter | solution.py:1043
  521.9 273.8 %reduce-scatter.11.cloned.1.call-start = ((), (), s32[]{:S(2)}) async-start(), calls=%async_computation.13 | async-start | bytes 9437184 | tf_op jit(solution)/shard_map/reduce_scatter | solution.py:1042
  522.5 275.9 %reduce-scatter.9.cloned.1.call-start = ((), (), s32[]{:S(2)}) async-start(), calls=%async_computation.12 | async-start | bytes 9437184 | tf_op jit(solution)/shard_map/reduce_scatter | solution.py:1044
  542.7 79.2 %collective-permute-start.65 = (bf16[512,2048]{1,0:T(8,128)(2,1)}, bf16[512,2048]{1,0:T(8,128)(2,1)S(1)}, u32[]{:S(2)}, u32[]{:S(2)}) collective-permute-start(bf16[512,2048]{1,0:T(8,128)(2,1)} %add_convert_fusion), channel_id=1, source_target_pairs={{1,2},{2,1},{5,6},{6,5},{9,10},{10,9},{13,14},{14,13},{17,18},{18,... | collective-permute-start | bytes 6291464 | tf_op jit(solution)/shard_map/ppermute | solution.py:80
  543.5 56.0 %collective-permute-start.62 = (bf16[3,64,2048]{2,1,0:T(8,128)(2,1)}, bf16[3,64,2048]{2,1,0:T(8,128)(2,1)}, u32[]{:S(2)}, u32[]{:S(2)}) collective-permute-start(bf16[3,64,2048]{2,1,0:T(8,128)(2,1)} %get-tuple-element.115.refs_1_), channel_id=1, source_target_pairs={{0,1},{3,2},{4,5},{7,6},{8,9},{11,10},{12,13},{15,14},{16,17},{19,... | collective-permute-start | bytes 2359304 | tf_op jit(solution)/shard_map/ppermute | solution.py:80
  573.8 22.6 %all-to-all-start.4 = ((f32[4,512,16]{1,2,0:T(8,128)}), f32[4,512,16]{1,2,0:T(8,128)S(1)}, u32[]{:S(2)}, u32[]{:S(2)}) async-start(f32[4,512,16]{1,2,0:T(8,128)} %maximum_maximum_fusion), calls=%async_computation.4 | async-start | bytes 262144 | tf_op jit(solution)/shard_map/all_to_all | solution.py:1061
  578.9 24.9 %collective-permute-start.61 = (bf16[3,64,2048]{2,1,0:T(8,128)(2,1)S(1)}, bf16[3,64,2048]{2,1,0:T(8,128)(2,1)}, u32[]{:S(2)}, u32[]{:S(2)}) collective-permute-start(bf16[3,64,2048]{2,1,0:T(8,128)(2,1)S(1)} %copy-done.11), channel_id=1, source_target_pairs={{0,1},{3,2},{4,5},{7,6},{8,9},{11,10},{12,13},{15,14},{16,17},{19,... | collective-permute-start | bytes 2359304 | tf_op jit(solution)/shard_map/ppermute | solution.py:80
  602.2 32.3 %collective-permute-start.63 = (bf16[3,64,2048]{2,1,0:T(8,128)(2,1)}, bf16[3,64,2048]{2,1,0:T(8,128)(2,1)}, u32[]{:S(2)}, u32[]{:S(2)}) collective-permute-start(bf16[3,64,2048]{2,1,0:T(8,128)(2,1)} %add_convert_fusion.9), channel_id=1, source_target_pairs={{1,2},{2,1},{5,6},{6,5},{9,10},{10,9},{13,14},{14,13},{17,18},{18,... | collective-permute-start | bytes 2359304 | tf_op jit(solution)/shard_map/ppermute | solution.py:80
  606.1 32.7 %collective-permute-start.69 = (bf16[3,64,2048]{2,1,0:T(8,128)(2,1)}, bf16[3,64,2048]{2,1,0:T(8,128)(2,1)S(1)}, u32[]{:S(2)}, u32[]{:S(2)}) collective-permute-start(bf16[3,64,2048]{2,1,0:T(8,128)(2,1)} %add_convert_fusion.7), channel_id=1, source_target_pairs={{1,2},{2,1},{5,6},{6,5},{9,10},{10,9},{13,14},{14,13},{17,18},{18,... | collective-permute-start | bytes 2359304 | tf_op jit(solution)/shard_map/ppermute | solution.py:80
  621.9 28.6 %collective-permute-start.66 = (bf16[3,64,2048]{2,1,0:T(8,128)(2,1)}, bf16[3,64,2048]{2,1,0:T(8,128)(2,1)}, u32[]{:S(2)}, u32[]{:S(2)}) collective-permute-start(bf16[3,64,2048]{2,1,0:T(8,128)(2,1)} %get-tuple-element.118.refs_1_), channel_id=1, source_target_pairs={{0,1},{3,2},{4,5},{7,6},{8,9},{11,10},{12,13},{15,14},{16,17},{19,... | collective-permute-start | bytes 2359304 | tf_op jit(solution)/shard_map/ppermute | solution.py:80
  637.4 20.5 %collective-permute-start.85 = (bf16[2,64,2048]{2,1,0:T(8,128)(2,1)}, bf16[2,64,2048]{2,1,0:T(8,128)(2,1)}, u32[]{:S(2)}, u32[]{:S(2)}) collective-permute-start(bf16[2,64,2048]{2,1,0:T(8,128)(2,1)} %mix_inward.15), channel_id=1, source_target_pairs={{1,0},{2,3},{5,4},{6,7},{9,8},{10,11},{13,12},{14,15},{17,16},{18,... | collective-permute-start | bytes 1572872 | tf_op jit(solution)/shard_map/ppermute | solution.py:80
  642.6 43.1 %collective-permute-start.84 = (bf16[2,64,2048]{2,1,0:T(8,128)(2,1)}, bf16[2,64,2048]{2,1,0:T(8,128)(2,1)}, u32[]{:S(2)}, u32[]{:S(2)}) collective-permute-start(bf16[2,64,2048]{2,1,0:T(8,128)(2,1)} %mix_inward.14), channel_id=1, source_target_pairs={{1,0},{2,3},{5,4},{6,7},{9,8},{10,11},{13,12},{14,15},{17,16},{18,... | collective-permute-start | bytes 1572872 | tf_op jit(solution)/shard_map/ppermute | solution.py:80
  644.0 24.1 %collective-permute-start.64 = (bf16[3,64,2048]{2,1,0:T(8,128)(2,1)S(1)}, bf16[3,64,2048]{2,1,0:T(8,128)(2,1)S(1)}, u32[]{:S(2)}, u32[]{:S(2)}) collective-permute-start(bf16[3,64,2048]{2,1,0:T(8,128)(2,1)S(1)} %copy-done.10), channel_id=1, source_target_pairs={{0,1},{3,2},{4,5},{7,6},{8,9},{11,10},{12,13},{15,14},{16,17},{19,... | collective-permute-start | bytes 2359304 | tf_op jit(solution)/shard_map/ppermute | solution.py:80
  653.0 17.8 %collective-permute-start.67 = (bf16[3,64,2048]{2,1,0:T(8,128)(2,1)}, bf16[3,64,2048]{2,1,0:T(8,128)(2,1)}, u32[]{:S(2)}, u32[]{:S(2)}) collective-permute-start(bf16[3,64,2048]{2,1,0:T(8,128)(2,1)} %add_convert_fusion.8), channel_id=1, source_target_pairs={{1,2},{2,1},{5,6},{6,5},{9,10},{10,9},{13,14},{14,13},{17,18},{18,... | collective-permute-start | bytes 2359304 | tf_op jit(solution)/shard_map/ppermute | solution.py:80
  654.6 29.2 %collective-permute-start.70 = (bf16[3,64,2048]{2,1,0:T(8,128)(2,1)S(1)}, bf16[3,64,2048]{2,1,0:T(8,128)(2,1)S(1)}, u32[]{:S(2)}, u32[]{:S(2)}) collective-permute-start(bf16[3,64,2048]{2,1,0:T(8,128)(2,1)S(1)} %copy-done.9), channel_id=1, source_target_pairs={{0,1},{3,2},{4,5},{7,6},{8,9},{11,10},{12,13},{15,14},{16,17},{19,... | collective-permute-start | bytes 2359304 | tf_op jit(solution)/shard_map/ppermute | solution.py:80
  669.3 29.2 %collective-permute-start.75 = (bf16[3,64,2048]{2,1,0:T(8,128)(2,1)}, bf16[3,64,2048]{2,1,0:T(8,128)(2,1)}, u32[]{:S(2)}, u32[]{:S(2)}) collective-permute-start(bf16[3,64,2048]{2,1,0:T(8,128)(2,1)} %add_convert_fusion.4), channel_id=1, source_target_pairs={{1,2},{2,1},{5,6},{6,5},{9,10},{10,9},{13,14},{14,13},{17,18},{18,... | collective-permute-start | bytes 2359304 | tf_op jit(solution)/shard_map/ppermute | solution.py:80
  673.6 34.4 %collective-permute-start.83 = (bf16[2,64,2048]{2,1,0:T(8,128)(2,1)}, bf16[2,64,2048]{2,1,0:T(8,128)(2,1)}, u32[]{:S(2)}, u32[]{:S(2)}) collective-permute-start(bf16[2,64,2048]{2,1,0:T(8,128)(2,1)} %mix_inward.13), channel_id=1, source_target_pairs={{1,0},{2,3},{5,4},{6,7},{9,8},{10,11},{13,12},{14,15},{17,16},{18,... | collective-permute-start | bytes 1572872 | tf_op jit(solution)/shard_map/ppermute | solution.py:80
  685.0 26.7 %collective-permute-start.71 = (bf16[3,64,2048]{2,1,0:T(8,128)(2,1)}, bf16[3,64,2048]{2,1,0:T(8,128)(2,1)S(1)}, u32[]{:S(2)}, u32[]{:S(2)}) collective-permute-start(bf16[3,64,2048]{2,1,0:T(8,128)(2,1)} %add_convert_fusion.6), channel_id=1, source_target_pairs={{1,2},{2,1},{5,6},{6,5},{9,10},{10,9},{13,14},{14,13},{17,18},{18,... | collective-permute-start | bytes 2359304 | tf_op jit(solution)/shard_map/ppermute | solution.py:80
  689.4 27.5 %collective-permute-start.68 = (bf16[3,64,2048]{2,1,0:T(8,128)(2,1)S(1)}, bf16[3,64,2048]{2,1,0:T(8,128)(2,1)}, u32[]{:S(2)}, u32[]{:S(2)}) collective-permute-start(bf16[3,64,2048]{2,1,0:T(8,128)(2,1)S(1)} %copy-done.8), channel_id=1, source_target_pairs={{0,1},{3,2},{4,5},{7,6},{8,9},{11,10},{12,13},{15,14},{16,17},{19,... | collective-permute-start | bytes 2359304 | tf_op jit(solution)/shard_map/ppermute | solution.py:80
  701.4 25.2 %collective-permute-start.82 = (bf16[2,64,2048]{2,1,0:T(8,128)(2,1)}, bf16[2,64,2048]{2,1,0:T(8,128)(2,1)}, u32[]{:S(2)}, u32[]{:S(2)}) collective-permute-start(bf16[2,64,2048]{2,1,0:T(8,128)(2,1)} %mix_inward.12), channel_id=1, source_target_pairs={{1,0},{2,3},{5,4},{6,7},{9,8},{10,11},{13,12},{14,15},{17,16},{18,... | collective-permute-start | bytes 1572872 | tf_op jit(solution)/shard_map/ppermute | solution.py:80
  702.7 29.6 %collective-permute-start.76 = (bf16[3,64,2048]{2,1,0:T(8,128)(2,1)S(1)}, bf16[3,64,2048]{2,1,0:T(8,128)(2,1)S(1)}, u32[]{:S(2)}, u32[]{:S(2)}) collective-permute-start(bf16[3,64,2048]{2,1,0:T(8,128)(2,1)S(1)} %copy-done.7), channel_id=1, source_target_pairs={{0,1},{3,2},{4,5},{7,6},{8,9},{11,10},{12,13},{15,14},{16,17},{19,... | collective-permute-start | bytes 2359304 | tf_op jit(solution)/shard_map/ppermute | solution.py:80
  715.5 36.8 %collective-permute-start.81 = (bf16[2,64,2048]{2,1,0:T(8,128)(2,1)}, bf16[2,64,2048]{2,1,0:T(8,128)(2,1)}, u32[]{:S(2)}, u32[]{:S(2)}) collective-permute-start(bf16[2,64,2048]{2,1,0:T(8,128)(2,1)} %mix_inward.11), channel_id=1, source_target_pairs={{1,0},{2,3},{5,4},{6,7},{9,8},{10,11},{13,12},{14,15},{17,16},{18,... | collective-permute-start | bytes 1572872 | tf_op jit(solution)/shard_map/ppermute | solution.py:80
  719.3 28.9 %collective-permute-start.79 = (bf16[3,64,2048]{2,1,0:T(8,128)(2,1)}, bf16[3,64,2048]{2,1,0:T(8,128)(2,1)}, u32[]{:S(2)}, u32[]{:S(2)}) collective-permute-start(bf16[3,64,2048]{2,1,0:T(8,128)(2,1)} %add_convert_fusion.2), channel_id=1, source_target_pairs={{1,2},{2,1},{5,6},{6,5},{9,10},{10,9},{13,14},{14,13},{17,18},{18,... | collective-permute-start | bytes 2359304 | tf_op jit(solution)/shard_map/ppermute | solution.py:80
  720.8 25.5 %collective-permute-start.72 = (bf16[3,64,2048]{2,1,0:T(8,128)(2,1)S(1)}, bf16[3,64,2048]{2,1,0:T(8,128)(2,1)S(1)}, u32[]{:S(2)}, u32[]{:S(2)}) collective-permute-start(bf16[3,64,2048]{2,1,0:T(8,128)(2,1)S(1)} %copy-done.6), channel_id=1, source_target_pairs={{0,1},{3,2},{4,5},{7,6},{8,9},{11,10},{12,13},{15,14},{16,17},{19,... | collective-permute-start | bytes 2359304 | tf_op jit(solution)/shard_map/ppermute | solution.py:80
  733.5 22.5 %collective-permute-start.77 = (bf16[3,64,2048]{2,1,0:T(8,128)(2,1)}, bf16[3,64,2048]{2,1,0:T(8,128)(2,1)}, u32[]{:S(2)}, u32[]{:S(2)}) collective-permute-start(bf16[3,64,2048]{2,1,0:T(8,128)(2,1)} %add_convert_fusion.3), channel_id=1, source_target_pairs={{1,2},{2,1},{5,6},{6,5},{9,10},{10,9},{13,14},{14,13},{17,18},{18,... | collective-permute-start | bytes 2359304 | tf_op jit(solution)/shard_map/ppermute | solution.py:80
  751.0 18.2 %collective-permute-start.80 = (bf16[2,64,2048]{2,1,0:T(8,128)(2,1)}, bf16[2,64,2048]{2,1,0:T(8,128)(2,1)S(1)}, u32[]{:S(2)}, u32[]{:S(2)}) collective-permute-start(bf16[2,64,2048]{2,1,0:T(8,128)(2,1)} %mix_inward.10), channel_id=1, source_target_pairs={{1,0},{2,3},{5,4},{6,7},{9,8},{10,11},{13,12},{14,15},{17,16},{18,... | collective-permute-start | bytes 1572872 | tf_op jit(solution)/shard_map/ppermute | solution.py:80
  758.8 19.5 %collective-permute-start.78 = (bf16[2,64,2048]{2,1,0:T(8,128)(2,1)}, bf16[2,64,2048]{2,1,0:T(8,128)(2,1)S(1)}, u32[]{:S(2)}, u32[]{:S(2)}) collective-permute-start(bf16[2,64,2048]{2,1,0:T(8,128)(2,1)} %mix_inward.9), channel_id=1, source_target_pairs={{1,0},{2,3},{5,4},{6,7},{9,8},{10,11},{13,12},{14,15},{17,16},{18,... | collective-permute-start | bytes 1572872 | tf_op jit(solution)/shard_map/ppermute | solution.py:80
  763.8 24.9 %collective-permute-start.74 = (bf16[2,64,2048]{2,1,0:T(8,128)(2,1)}, bf16[2,64,2048]{2,1,0:T(8,128)(2,1)S(1)}, u32[]{:S(2)}, u32[]{:S(2)}) collective-permute-start(bf16[2,64,2048]{2,1,0:T(8,128)(2,1)} %mix_inward.8), channel_id=1, source_target_pairs={{1,0},{2,3},{5,4},{6,7},{9,8},{10,11},{13,12},{14,15},{17,16},{18,... | collective-permute-start | bytes 1572872 | tf_op jit(solution)/shard_map/ppermute | solution.py:80
  (84 other events, 1017.1 us)
Sparse Core Ops, SparseCore 0:
  11.9 48.2 all-gather.5
  465.4 45.4 reduce-scatter.6
  522.0 63.5 reduce-scatter.4
  588.9 72.4 reduce-scatter.10
  664.7 71.4 reduce-scatter.8

commit v5 on v4

--- a/solution.py
+++ b/solution.py
@@ -116,7 +116,7 @@
             high = lax.slice_in_dim(by_x, half, 2 * half, axis=cut)
             pieces += [(partner(low, 2), 6, 0), (partner(high, 4), 6, half)]
         else:
-            pieces.append((self.across, 6, 0))
+            pieces.append((gated(self.across, earlier), 6, 0))
         pieces += [(partner(piece, 1), code ^ 1, start) for piece, code, start in pieces]
         return put_together(pieces, shard, self.peers, cut, index)
 
@@ -576,10 +576,12 @@
     )(grad, unit, inv, gain, extra, flag)
 
 
-def mixing_back(heads_part, last_part, history):
+def mixing_back(heads_part, last_part, history, which, of):
     entries, tokens, width = history.shape
     streams = heads_part.shape[0] + 1
-    rows, sub, lanes = min(64, tokens), 16, 256
+    rows, sub, lanes = min(64, tokens // of), 16, 256
+    steps = tokens // of // rows
+    base = which * steps
 
     def kernel(first, last, hist, out):
         def step(r, carry):
@@ -601,15 +603,15 @@
 
     return pl.pallas_call(
         kernel,
-        grid=(tokens // rows,),
+        grid=(steps,),
         in_specs=[
-            pl.BlockSpec((streams - 1, rows, width), lambda i: (0, i, 0)),
-            pl.BlockSpec((rows, width), lambda i: (i, 0)),
-            pl.BlockSpec((entries, rows, width), lambda i: (0, i, 0)),
+            pl.BlockSpec((streams - 1, rows, width), lambda i: (0, base + i, 0)),
+            pl.BlockSpec((rows, width), lambda i: (base + i, 0)),
+            pl.BlockSpec((entries, rows, width), lambda i: (0, base + i, 0)),
         ],
         out_specs=pl.BlockSpec((streams, rows, entries), lambda i: (0, i, 0)),
-        out_shape=jax.ShapeDtypeStruct((streams, tokens, entries), F32),
-        cost_estimate=cost(18),
+        out_shape=jax.ShapeDtypeStruct((streams, tokens // of, entries), F32),
+        cost_estimate=cost(18 / of),
         name="mixing_back",
     )(heads_part, last_part, history)
 
@@ -904,51 +906,50 @@
     got_heads = Gathered(w_heads, direct=near)
     cotangent = lax.all_gather(out_cotangent, "stream", axis=1, tiled=True)
     lanes = jnp.concatenate([norm_gain, norm_bias]).astype(F32).reshape(tokens, -1)
-    packed = lax.all_gather(jnp.concatenate([mixing[:, 0, :], lanes], axis=1), "stream", axis=0)
-    if near:
-        early = (got_heads.by_x, got_heads.by_y, got_heads.across)
-        history = after(history, *early)
-        w_up, w_merge = after(w_up, *early[:2]), after(w_merge, *early[:2])
-    got_up = Gathered(w_up)
-    got_merge = Gathered(w_merge)
-    mix_all = packed[:, :, :entries]
-    norms = packed[:, :, entries:].reshape(members, 2, width)
-    gains, biases = norms[:, 0], norms[:, 1]
-    mix_rows = jnp.transpose(mix_all, (1, 0, 2)).reshape(tokens, members * entries)
-
-    normed, unit, inv, stream = make_streams(history, mix_rows, gains, biases)
-    full_heads = got_heads.whole()
-    positions = shard_offset[0] + jnp.arange(tokens, dtype=jnp.int32)
-    projected = project(after(normed, got_up.by_x, got_up.by_y), full_heads, rope_tables(positions, 1.0))
-
     first_rows = mixer_first.astype(F32).reshape(tokens, -1)
     second_flat = mixer_second[:, 0, :].astype(F32).reshape(-1)
     hidden_count = mixer_second.shape[0]
     lines = -(-second_flat.shape[0] // tokens)
     second_rows = jnp.pad(second_flat, (0, lines * tokens - second_flat.shape[0]))
-    rest = jnp.concatenate(
-        [next_cotangent[:, 0, :], first_rows, second_rows.reshape(tokens, lines)], axis=1
-    )
-    rest = lax.all_gather(after(rest, projected), "stream", axis=0)
     outputs = next_cotangent.shape[2]
-    cut = outputs + first_rows.shape[1]
-    next_full = rest[:, :, :outputs]
-    first_full = rest[:, :, outputs:cut].astype(BF).reshape(width, -1)
-    second_full = rest[:, :, cut:].reshape(members, -1)[:, : second_flat.shape[0]]
+    arrays = [mixing[:, 0, :], lanes, next_cotangent[:, 0, :], first_rows]
+    arrays.append(second_rows.reshape(tokens, lines))
+    packed = lax.all_gather(jnp.concatenate(arrays, axis=1), "stream", axis=0)
+    parts, place = [], 0
+    for array in arrays:
+        parts.append(packed[:, :, place : place + array.shape[1]])
+        place += array.shape[1]
+    mix_all, norms, next_full, first_full, second_full = parts
+    norms = norms.reshape(members, 2, width)
+    first_full = first_full.astype(BF).reshape(width, -1)
+    second_full = second_full.reshape(members, -1)[:, : second_flat.shape[0]]
     second_full = second_full.reshape(members, hidden_count, outputs)
-
     if near:
-        spread = after(jnp.broadcast_to(shard_offset[:, None], (8, 128)), projected)
+        spread = jnp.broadcast_to(shard_offset[:, None], (8, 128))
         offsets = lax.all_gather(spread, "dp", axis=0)[:, 0, 0]
+        early = (got_heads.by_x, got_heads.by_y, got_heads.across)
+        history = after(history, *early, offsets)
+        w_up, w_merge = after(w_up, *early[:2]), after(w_merge, *early[:2])
+    got_up = Gathered(w_up)
+    got_merge = Gathered(w_merge, direct=near)
+    gains, biases = norms[:, 0], norms[:, 1]
+    mix_rows = jnp.transpose(mix_all, (1, 0, 2)).reshape(tokens, members * entries)
+
+    normed, unit, inv, stream = make_streams(history, mix_rows, gains, biases)
+    full_heads = got_heads.whole()
+    positions = shard_offset[0] + jnp.arange(tokens, dtype=jnp.int32)
+    projected = project(after(normed, got_up.by_x, got_up.by_y), full_heads, rope_tables(positions, 1.0))
+
+    if near:
         side = (index % 2).astype(jnp.int32).reshape(1)
         place = jnp.arange(shards, dtype=jnp.int32)
         first_key = jnp.maximum(place - offsets // tokens, 0).astype(jnp.int32)
         own = lax.all_to_all(projected, "dp", 0, 0, tiled=True)
-        own = after(own, next_full, first_full, second_full, cotangent)
         got_down = Gathered(after(w_down, own))
         other = partner(own[:, 1:], 1)
         full_up = got_up.whole(projected)
-        full_merge = got_merge.whole(projected)
+        full_merge = got_merge.whole(own)
+        own = after(own, cotangent)
         result, exact, level = attend(own, other, first_key, side)
         back = lax.all_to_all(result, "dp", 0, 0, tiled=True)
         attended = jnp.transpose(back.reshape(heads_here, tokens, HD), (1, 0, 2)).reshape(tokens, -1)
@@ -1007,13 +1008,14 @@
 
     attended_grad = back_through(grad_out, full_merge, None)
     up_grad = back_through(grad_out, full_down, slope)
-    merge_grad = dot_rows(attended, grad_out).astype(BF)
-    last_normed = dot_cols(up_grad, flat_up)
+    down_grad = dot_rows(hidden, grad_out).astype(BF)
+    last_normed = dot_cols(after(up_grad, down_grad), flat_up)
     last_share, last_stats = last_back(
         last_normed, unit[members - 1], inv, gains[members - 1 :], grad_out, flags
     )
     last_one = line_hop(last_share, OUTWARD)
-    last_two = line_hop((last_share.astype(F32) + last_one.astype(F32)).astype(BF), MIDDLE)
+    last_sum = (last_share.astype(F32) + last_one.astype(F32)).astype(BF)
+    last_two = line_hop(last_sum, MIDDLE)
     if near:
         sent = attended_grad.reshape(tokens, heads_here, HD)
         sent = jnp.transpose(sent, (1, 0, 2)).reshape(shards, half, HD)
@@ -1023,20 +1025,22 @@
         taken = partner(given, 1)
         summed = kept_grads[:, 1:].astype(F32) + taken.astype(F32)
         pair = jnp.concatenate([kept_grads[:, :1], summed.astype(BF)], axis=1)
+        pair = after(pair, last_one)
         parts = lax.all_to_all(pair, "dp", 0, 0, tiled=True)
-        hidden = after(hidden, pair)
+        late_grad, late_up = after(grad_out, pair), after(up_grad, pair)
     else:
+        late_grad, late_up = grad_out, up_grad
         grads = far_attend_back(split[0], attended_grad.reshape(tokens, heads_here, HD), kept)
         parts = grads.reshape(3, 2, half, heads_here, HD)
         parts = jnp.transpose(parts, (3, 1, 0, 2, 4)).reshape(2 * heads_here, 3, half, HD)
 
-    down_grad = dot_rows(hidden, grad_out).astype(BF)
-    parts = after(parts, last_one, down_grad)
+    up_back = dot_rows(normed[members - 1], late_up).astype(BF)
+    merge_grad = dot_rows(attended, late_grad).astype(BF)
+    parts = after(parts, up_back, merge_grad, last_sum)
     blocks = 8
     *pieces, heads_share, heads_grad, heads_stats = heads_back(
         parts, full_heads, normed, unit, inv, gains, rope_tables(positions, -1.0), blocks
     )
-    up_back = dot_rows(normed[members - 1], after(up_grad, heads_share)).astype(BF)
 
     grad_merge = lax.psum_scatter(merge_grad, "dp", scatter_dimension=1, tiled=True).astype(F32)
     grad_down = lax.psum_scatter(down_grad, "dp", scatter_dimension=1, tiled=True).astype(F32)
@@ -1054,24 +1058,29 @@
     extra = {}
 
     def first_hop(i, gates):
+        gates = list(gates)
         if i == 1:
-            mix_parts = mixing_back(heads_share, last_share, history)
-            stats = jnp.concatenate([heads_stats, last_stats[None]])
-            both = jnp.concatenate([mix_parts, stats.reshape(members, tokens, -1)], axis=2)
-            extra["both"] = jnp.sum(lax.all_to_all(both, "stream", 0, 0, tiled=True), axis=0)
-        if i == 4:
-            sums = extra["both"][:, entries:]
-            second_sums = jnp.pad(second_local.reshape(-1), (0, lines * tokens - second_flat.shape[0]))
-            local = jnp.concatenate(
-                [sums, first_local.reshape(tokens, -1), second_sums.reshape(tokens, lines)], axis=1
-            )
-            extra["all"] = jnp.sum(lax.all_gather(local, "dp", axis=0), axis=0)
-            gates = gates + [extra["both"]]
+            gates.append(grad_down)
         if i == 2:
-            gates = gates + [last_two]
+            gates.append(last_two)
+        if i == 5:
+            gates.append(grad_up)
         if i == 7:
-            gates = gates + [extra["all"]]
+            gates.append(grad_merge)
         return gated(pieces[i], gates)
+
+    def small_sums():
+        stats = jnp.concatenate([heads_stats, last_stats[None]]).reshape(members, tokens, -1)
+        both = jnp.concatenate([jnp.concatenate(mixes, axis=1), stats], axis=2)
+        both = jnp.sum(lax.all_to_all(both, "stream", 0, 0, tiled=True), axis=0)
+        second_sums = jnp.pad(second_local.reshape(-1), (0, lines * tokens - second_flat.shape[0]))
+        local = [both[:, entries:], first_local.reshape(tokens, -1), second_sums.reshape(tokens, lines)]
+        everyone = lax.all_gather(jnp.concatenate(local, axis=1), "dp", axis=0)
+        return both[:, :entries], jnp.sum(everyone, axis=0)
+
+    mixes = []
+    quarters = 4
+    quarter = tokens // quarters
 
     def second_hop(i, one):
         return (pieces[i].astype(F32) + one.astype(F32)).astype(BF)
@@ -1080,6 +1089,12 @@
         return mix_block(i, there, pieces[i], last_share, [two], [last_two], None, None)
 
     def finish(i, one, two, three):
+        if i in (0, 1, 2, 3):
+            mixes.append(mixing_back(heads_share, last_share, after(history, two), i, quarters))
+        if i == 3:
+            extra["both"], extra["all"] = small_sums()
+        if i == 5:
+            three = after(three, extra["both"], extra["all"])
         extra["history"], token = mix_block(
             i,
             here,
@@ -1095,7 +1110,7 @@
     along_line(blocks, first_hop, second_hop, third_hop, finish)
     grad_history = extra["history"]
 
-    grad_mixing = extra["both"][:, :entries][:, None, :]
+    grad_mixing = extra["both"][:, None, :]
     sums = extra["all"]
     spans = 2 * width // tokens
     stats = sums[:, :spans].reshape(2, width)

time: 814 us -> 834 us (1.025); the launches traced: 808 us -> 819 us
  starting transfers between devices: 172 us -> 185 us
  local copies, waits for them, and re-layouts: 47.2 us -> 56.5 us
  waiting for transfers between devices: 187 us -> 196 us
  matrix products: 42.1 us -> 33.6 us
    all_gather x4 -> x2, blocking collectives: 67.6 us -> 28.7 us  [the longest x1 18.4 us: body(): packed = lax.all_gather(jnp.concatenate(arrays, axis=1), 'stream', axis=0)]
    unnamed x0 -> x1, blocking collectives: none -> 33.6 us
    all_to_all x1, waiting for transfers between devices: 12.7 us -> 1.33 us  [small_sums(): both = jnp.sum(lax.all_to_all(both, 'stream', 0, 0, tiled=True), axis=0)]
    ppermute x36 -> x34, waiting for transfers between devices: 48.5 us -> 59.3 us  [partner(): return lax.ppermute(shard, 'dp', [(i, i ^ bit) for i in range(peers)])]
    ppermute x50, starting transfers between devices: 125 us -> 136 us  [line_hop(): return lax.ppermute(shard, 'stream', pairs)]
    ppermute x50, waiting for transfers between devices: 122 us -> 132 us  [line_hop(): return lax.ppermute(shard, 'stream', pairs)]
    pallas_call x1 -> x4, Pallas kernels: 17.3 us -> 24.6 us  [mixing_back(): pl.pallas_call(kernel, grid=(steps,), in_specs=[pl.BlockSpec((streams - 1...]
    unnamed x114 -> x130, local copies, waits for them, and re-layouts: 14.9 us -> 20.8 us
  transfers between devices with their start and end apart: 96 -> 94, of which waited for: 30 -> 31; matrix products, arithmetic and copies ran while one was open for 12% -> 12% of each run, Pallas kernels for 21% -> 25%
where the time goes in v5:
time: 834 us; the launch traced here: 819 us
  Pallas kernels  230 us (28%)
  waiting for transfers between devices  196 us (24%)
  starting transfers between devices  185 us (22%)
  blocking collectives  62.3 us (7%)
  local copies, waits for them, and re-layouts  56.5 us (7%)
  other arithmetic  39 us (5%)
  matrix products  33.6 us (4%)
  between operations  16.4 us (2%)
    ppermute x50, starting transfers between devices, line_hop(): return lax.ppermute(shard, 'stream', pairs)  136 us
    ppermute x50, waiting for transfers between devices, line_hop(): return lax.ppermute(shard, 'stream', pairs)  132 us
    ppermute x34, waiting for transfers between devices, partner(): return lax.ppermute(shard, 'dp', [(i, i ^ bit) for i in range(peers)])  59.3 us
    pallas_call x16, Pallas kernels, mix_block(): pl.pallas_call(kernel, grid=(1,), in_specs=specs, out_specs=out_spec, out...  51.7 us
    unnamed x1, blocking collectives  33.6 us
    ppermute x34, starting transfers between devices, partner(): return lax.ppermute(shard, 'dp', [(i, i ^ bit) for i in range(peers)])  25.3 us
    pallas_call x4, Pallas kernels, mixing_back(): pl.pallas_call(kernel, grid=(steps,), in_specs=[pl.BlockSpec((streams - 1...  24.6 us
    pallas_call x1, Pallas kernels, make_streams(): pl.pallas_call(kernel, grid=(tokens // rows,), in_specs=[pl.BlockSpec((en...  22.6 us
  transfers between devices with their start and end apart: 94, of which 31 were waited for; matrix products, arithmetic and copies ran while one was open for 12% of the time, Pallas kernels for 25%

profile of v5, /device:TPU:0, one launch (start us, length us, event | category | flops | bytes accessed | tf_op | source)
XLA Modules:
  0.0 819.3 jit_solution(12682121594344460499)
XLA Ops:
  7.2 4.0 collective-permute-start.2
  14.6 33.6 %all-reduce.2 = s32[8]{0:T(128)S(1)} all-reduce(s32[8]{0:T(128)S(1)} %dynamic-update-slice), channel_id=3, replica_groups=mesh['dp'=8,'stream'=4] {'dp'}, use_global_device_ids=true, to_apply=%add.2 | all-reduce | flops 8 | bytes 64
  52.5 18.4 %all-gather.1 = f32[2048,62]{0,1:T(8,128)S(1)} all-gather(f32[512,62]{0,1:T(8,128)S(1)} %concatenate.30), channel_id=4, replica_groups=mesh['dp'=8,'stream'=4] {'stream'}, dimensions={0}, use_global_device_ids=true | all-gather | bytes 634880 | tf_op jit(solution)/shard_map/all_gather | solution.py:917
  80.4 22.6 %make_streams.1 = (bf16[4,512,2048]{2,1,0:T(8,128)(2,1)}, bf16[4,512,2048]{2,1,0:T(8,128)(2,1)}, f32[512,4]{1,0:T(8,128)}, f32[512,2048]{1,0:T(8,128)}) custom-call(bf16[8,512,2048]{2,1,0:T(8,128)(2,1)} %hist.4, f32[512,32]{1,0:T(8,128)} %copy.75.mix, f32[4,2048]{1,0:T(4,128)} %get-tuple-element.235.gain, f32[4,2048]{1,0:T(4,128)} %get-tuple-element.234.bias), custom_call_target="tpu_custom_call" | custom-call | flops 19800000512 | bytes 66000000 | tf_op jit(solution)/shard_map/make_streams/pallas_call | solution.py:254
  104.1 5.6 put_together.4.w
  109.7 8.8 %project.1 = bf16[8,3,256,128]{3,2,1,0:T(8,128)(2,1)} custom-call(bf16[4,512,2048]{2,1,0:T(8,128)(2,1)} %get-tuple-element.85.x, bf16[8,3,256,512]{3,2,1,0:T(8,128)(2,1)} %put_together.4.w, f32[3,512,128]{2,1,0:T(8,128)} %get-tuple-element.214.table), custom_call_target="tpu_custom_call" | custom-call | flops 8099999744 | bytes 27000000 | tf_op jit(solution)/shard_map/project/pallas_call | solution.py:304
  118.5 3.7 all-to-all-start
  128.1 26.0 %collective-permute-done.10.refs_3_ = bf16[128,2048]{1,0:T(8,128)(2,1)S(1)} collective-permute-done((bf16[128,2048]{1,0:T(8,128)(2,1)S(1)}, bf16[128,2048]{1,0:T(8,128)(2,1)S(1)}, u32[]{:S(2)}, u32[]{:S(2)}) %collective-permute-start.10) | collective-permute-done | bytes 524320 | tf_op jit(solution)/shard_map/ppermute | solution.py:76
  156.1 4.2 collective-permute-done.19.refs_3_
  160.8 5.0 collective-permute-done.18.refs_2_
  173.8 20.2 %collective-permute-done.25.refs_2_ = bf16[2048,256]{1,0:T(8,128)(2,1)} collective-permute-done((bf16[2048,256]{1,0:T(8,128)(2,1)}, bf16[2048,256]{1,0:T(8,128)(2,1)}, u32[]{:S(2)}, u32[]{:S(2)}) %collective-permute-start.25) | collective-permute-done | bytes 1048608 | tf_op jit(solution)/shard_map/ppermute | solution.py:76
  194.5 6.5 put_together.5
  206.1 14.2 %attend.1 = (bf16[8,256,128]{2,1,0:T(8,128)(2,1)}, f32[8,256,128]{2,1,0:T(8,128)}, f32[8,256,1]{2,1,0:T(8,128)}) custom-call(s32[8]{0:T(128)} %subtract_maximum_fusion.first, s32[1]{0:T(128)} %bitcast.1.part, bf16[8,3,256,128]{3,2,1,0:T(8,128)(2,1)} %copy-done.5, bf16[8,2,256,128]{3,2,1,0:T(8,128)(2,1)} %collective-permute-done.9.theirs), custom_call_target="tpu_custom_call" | custom-call | flops 14400000000 | bytes 48000000 | tf_op jit(solution)/shard_map/attend/pallas_call | solution.py:363
  220.3 6.0 all-to-all-start.1
  227.7 10.0 %hidden_units.1 = (bf16[512,2048]{1,0:T(8,128)(2,1)}, bf16[512,2048]{1,0:T(8,128)(2,1)}) custom-call(bf16[512,2048]{1,0:T(8,128)(2,1)} %slice_bitcast_fusion.1.x_ref, bf16[2048,2048]{1,0:T(8,128)(2,1)} %bitcast.107), custom_call_target="tpu_custom_call" | custom-call | flops 8099999744 | bytes 27000000 | tf_op jit(solution)/shard_map/hidden_units/pallas_call | solution.py:787
  243.4 6.5 put_together.7.wd.refs_1_
  249.9 13.1 %merge_branches.1 = f32[512,2048]{1,0:T(8,128)} custom-call(bf16[512,512]{1,0:T(8,128)(2,1)} %bitcast.98, bf16[512,2048]{1,0:T(8,128)(2,1)} %get-tuple-element.91.h, bf16[8,512,256]{2,1,0:T(8,128)(2,1)} %put_together.6.wm.refs_1_, bf16[8,2048,256]{2,1,0:T(8,128)(2,1)} %put_together.7.wd.refs_1_, f32[512,2048]{1,0:T(8,128)} %get-tuple-element.99.st, ...), custom_call_target="tpu_custom_call" | custom-call | flops 11699999744 | bytes 39000000 | tf_op jit(solution)/shard_map/merge_branches/pallas_call | solution.py:812
  268.2 5.3 collective-permute-done.33
  274.3 4.6 collective-permute-done.36
  279.0 8.8 %collective-permute-start.42 = (bf16[64,2048]{1,0:T(8,128)(2,1)S(1)}, bf16[64,2048]{1,0:T(8,128)(2,1)S(1)}, u32[]{:S(2)}, u32[]{:S(2)}) collective-permute-start(bf16[64,2048]{1,0:T(8,128)(2,1)S(1)} %get-tuple-element.101), channel_id=1, source_target_pairs={{0,1},{3,2},{4,5},{7,6},{8,9},{11,10},{12,13},{15,14},{16,17},{19,... | collective-permute-start | bytes 786440 | tf_op jit(solution)/shard_map/ppermute | solution.py:80
  289.1 5.3 collective-permute-done.42
  297.8 8.2 %collective-permute-done.35 = bf16[64,2048]{1,0:T(8,128)(2,1)S(1)} collective-permute-done((bf16[64,2048]{1,0:T(8,128)(2,1)S(1)}, bf16[64,2048]{1,0:T(8,128)(2,1)S(1)}, u32[]{:S(2)}, u32[]{:S(2)}) %collective-permute-start.35) | collective-permute-done | bytes 262176 | tf_op jit(solution)/shard_map/ppermute | solution.py:80
  308.1 3.8 collective-permute-done.45
  316.4 7.8 collective-permute-done.38
  327.6 3.8 collective-permute-done.48
  331.5 4.4 collective-permute-start.54
  342.8 6.9 collective-permute-done.41
  361.6 10.3 %collective-permute-done.47 = bf16[64,2048]{1,0:T(8,128)(2,1)S(1)} collective-permute-done((bf16[64,2048]{1,0:T(8,128)(2,1)S(1)}, bf16[64,2048]{1,0:T(8,128)(2,1)S(1)}, u32[]{:S(2)}, u32[]{:S(2)}) %collective-permute-start.47) | collective-permute-done | bytes 262176 | tf_op jit(solution)/shard_map/ppermute | solution.py:80
  372.0 8.3 %collective-permute-done.50 = bf16[64,2048]{1,0:T(8,128)(2,1)S(1)} collective-permute-done((bf16[64,2048]{1,0:T(8,128)(2,1)S(1)}, bf16[64,2048]{1,0:T(8,128)(2,1)S(1)}, u32[]{:S(2)}, u32[]{:S(2)}) %collective-permute-start.50) | collective-permute-done | bytes 262176 | tf_op jit(solution)/shard_map/ppermute | solution.py:80
  384.5 6.9 convolution_convert_fusion.1
  395.2 7.6 back_through.2
  404.8 3.9 all-to-all-start.2
  408.7 13.4 %back_through.3 = bf16[512,2048]{1,0:T(8,128)(2,1)} custom-call(bf16[512,2048]{1,0:T(8,128)(2,1)} %copy-done.55, bf16[8,2048,256]{2,1,0:T(8,128)(2,1)} %put_together.7.wd.refs_1_, bf16[512,2048]{1,0:T(8,128)(2,1)} %get-tuple-element.106.refs_2_), custom_call_target="tpu_custom_call" | custom-call | flops 11699999744 | bytes 39000000 | tf_op jit(solution)/shard_map/back_through/pallas_call | solution.py:867
  422.2 11.0 %fusion.46.g = f32[512,2048]{1,0:T(8,128)} fusion(bf16[512,2048]{1,0:T(8,128)(2,1)} %back_through.3, bf16[2048,2048]{1,0:T(8,128)(2,1)} %bitcast.108), kind=kOutput, calls=%fused_computation.144 | convolution fusion | flops 4294967296 | bytes 14680064 | tf_op jit(solution)/shard_map/dot_general | solution.py:71
  433.2 6.5 last_back.1
  442.0 19.1 %attend_back.1 = (bf16[8,3,256,128]{3,2,1,0:T(8,128)(2,1)}, bf16[8,2,256,128]{3,2,1,0:T(8,128)(2,1)}) custom-call(s32[8]{0:T(128)} %subtract_maximum_fusion.first, s32[1]{0:T(128)} %bitcast.1.part, bf16[8,3,256,128]{3,2,1,0:T(8,128)(2,1)} %copy-done.5, bf16[8,2,256,128]{3,2,1,0:T(8,128)(2,1)} %collective-permute-done.9.theirs, ...), custom_call_target="tpu_custom_call" | custom-call | flops 19800000512 | bytes 66000000 | tf_op jit(solution)/shard_map/attend_back/pallas_call | solution.py:437
  461.2 4.5 collective-permute-start.57
  470.9 16.3 %collective-permute-done.58.refs_5_ = bf16[512,2048]{1,0:T(8,128)(2,1)S(1)} collective-permute-done((bf16[512,2048]{1,0:T(8,128)(2,1)}, bf16[512,2048]{1,0:T(8,128)(2,1)S(1)}, u32[]{:S(2)}, u32[]{:S(2)}) %collective-permute-start.58) | collective-permute-done | bytes 2097184 | tf_op jit(solution)/shard_map/ppermute | solution.py:80
  487.2 4.3 all-to-all-start.3
  491.5 4.2 convolution_convert_fusion.2
  497.4 3.8 add_convert_fusion
  501.2 8.5 %convolution_convert_fusion = bf16[2048,2048]{1,0:T(8,128)(2,1)} fusion(bf16[512,2048]{1,0:T(8,128)(2,1)S(1)} %copy-done.57, bf16[4,512,2048]{2,1,0:T(8,128)(2,1)} %get-tuple-element.85.x), kind=kOutput, calls=%fused_computation | convolution fusion | flops 4299161600 | bytes 12582912 | tf_op jit(solution)/shard_map/dot_general | solution.py:67
  512.5 17.2 %heads_back.1 = (bf16[3,64,2048]{2,1,0:T(8,128)(2,1)}, bf16[3,64,2048]{2,1,0:T(8,128)(2,1)}, bf16[3,64,2048]{2,1,0:T(8,128)(2,1)}, bf16[3,64,2048]{2,1,0:T(8,128...) custom-call(bf16[8,3,256,128]{3,2,1,0:T(8,128)(2,1)} %all-to-all-don, ...), custom_call_target="tpu_custom_call" | custom-call | flops 16199999488 | bytes 54000000 | tf_op jit(solution)/shard_map/heads_back/pallas_call | solution.py:510
  531.3 7.2 collective-permute-start.60
  538.5 14.3 %collective-permute-done.60.refs_2_ = bf16[3,64,2048]{2,1,0:T(8,128)(2,1)} collective-permute-done((bf16[3,64,2048]{2,1,0:T(8,128)(2,1)}, bf16[3,64,2048]{2,1,0:T(8,128)(2,1)}, u32[]{:S(2)}, u32[]{:S(2)}) %collective-permute-start.60) | collective-permute-done | bytes 786464 | tf_op jit(solution)/shard_map/ppermute | solution.py:80
  558.9 27.4 %collective-permute-start.64 = (bf16[3,64,2048]{2,1,0:T(8,128)(2,1)S(1)}, bf16[3,64,2048]{2,1,0:T(8,128)(2,1)}, u32[]{:S(2)}, u32[]{:S(2)}) collective-permute-start(bf16[3,64,2048]{2,1,0:T(8,128)(2,1)S(1)} %copy-done.12), channel_id=1, source_target_pairs={{0,1},{3,2},{4,5},{7,6},{8,9},{11,10},{12,13},{15,14},{16,17},{19,... | collective-permute-start | bytes 2359304 | tf_op jit(solution)/shard_map/ppermute | solution.py:80
  599.5 7.8 collective-permute-start.59
  609.6 6.1 mixing_back.4
  624.4 3.6 mix_final.8
  628.1 12.3 %collective-permute-start.62 = (bf16[3,64,2048]{2,1,0:T(8,128)(2,1)S(1)}, bf16[3,64,2048]{2,1,0:T(8,128)(2,1)S(1)}, u32[]{:S(2)}, u32[]{:S(2)}) collective-permute-start(bf16[3,64,2048]{2,1,0:T(8,128)(2,1)S(1)} %copy-done.11), channel_id=1, source_target_pairs={{0,1},{3,2},{4,5},{7,6},{8,9},{11,10},{12,13},{15,14},{16,17},{19,... | collective-permute-start | bytes 2359304 | tf_op jit(solution)/shard_map/ppermute | solution.py:80
  640.4 6.1 mixing_back.6
  662.1 6.4 mixing_back.5
  669.7 7.2 collective-permute-start.68
  680.3 4.3 collective-permute-start.66
  691.9 6.0 mixing_back.7
  703.8 5.6 all-to-all-start.4
  712.1 5.8 collective-permute-start.74
  719.3 10.4 %all-gather.2 = f32[4096,45]{0,1:T(8,128)S(1)} all-gather(f32[512,45]{0,1:T(8,128)S(1)} %pad_maximum_fusion.3), channel_id=5, replica_groups=mesh['dp'=8,'stream'=4] {'dp'}, dimensions={0}, use_global_device_ids=true | all-gather | bytes 829440 | tf_op jit(solution)/shard_map/all_gather | solution.py:1078
  741.7 3.7 mix_final.11
  751.3 7.3 collective-permute-done.70.refs_2_
  765.0 3.7 mix_final.12
  773.6 7.4 collective-permute-done.78.refs_7_
  786.0 3.7 mix_final.13
  796.1 11.8 %collective-permute-done.72.refs_7_ = bf16[2,64,2048]{2,1,0:T(8,128)(2,1)S(1)} collective-permute-done((bf16[2,64,2048]{2,1,0:T(8,128)(2,1)}, bf16[2,64,2048]{2,1,0:T(8,128)(2,1)S(1)}, u32[]{:S(2)}, u32[]{:S(2)}) %collective-permute-start.72) | collective-permute-done | bytes 524320 | tf_op jit(solution)/shard_map/ppermute | solution.py:80
  (405 shorter events, 221.8 us)
Async XLA Ops:
  7.2 193.8 %all-gather.5.cloned.1.call-start = ((), (), s32[]{:S(2)}) async-start(), calls=%async_computation.9 | async-start | bytes 2621440 | tf_op jit(solution)/shard_map/all_gather | solution.py:907
  7.2 72.6 %collective-permute-start.2 = (bf16[3,256,512]{2,1,0:T(8,128)(2,1)}, bf16[3,256,512]{2,1,0:T(8,128)(2,1)S(1)}, u32[]{:S(2)}, u32[]{:S(2)}) collective-permute-start(bf16[3,256,512]{2,1,0:T(8,128)(2,1)} %refs_0_.1), channel_id=1, source_target_pairs={{0,24},{4,28},{8,16},{12,20},{16,8},{20,12},{24,0},{28,4},{1,25},{... | collective-permute-start | bytes 2359304 | tf_op jit(solution)/shard_map/ppermute | solution.py:76
  11.2 65.5 %collective-permute-start.1 = (bf16[3,256,512]{2,1,0:T(8,128)(2,1)}, bf16[3,256,512]{2,1,0:T(8,128)(2,1)}, u32[]{:S(2)}, u32[]{:S(2)}) collective-permute-start(bf16[3,256,512]{2,1,0:T(8,128)(2,1)} %refs_0_.1), channel_id=1, source_target_pairs={{0,16},{4,20},{8,24},{12,28},{16,0},{20,4},{24,8},{28,12},{1,17},{... | collective-permute-start | bytes 2359304 | tf_op jit(solution)/shard_map/ppermute | solution.py:76
  11.7 65.0 %collective-permute-start = (bf16[3,256,512]{2,1,0:T(8,128)(2,1)}, bf16[3,256,512]{2,1,0:T(8,128)(2,1)}, u32[]{:S(2)}, u32[]{:S(2)}) collective-permute-start(bf16[3,256,512]{2,1,0:T(8,128)(2,1)} %refs_0_.1), channel_id=1, source_target_pairs={{0,8},{4,12},{8,0},{12,4},{16,24},{20,28},{24,16},{28,20},{1,9},{5... | collective-permute-start | bytes 2359304 | tf_op jit(solution)/shard_map/ppermute | solution.py:76
  11.9 68.4 %collective-permute-start.5 = (bf16[3,256,512]{2,1,0:T(8,128)(2,1)}, bf16[3,256,512]{2,1,0:T(8,128)(2,1)}, u32[]{:S(2)}, u32[]{:S(2)}) collective-permute-start(bf16[3,256,512]{2,1,0:T(8,128)(2,1)} %refs_0_.1), channel_id=1, source_target_pairs={{0,4},{4,0},{8,12},{12,8},{16,20},{20,16},{24,28},{28,24},{1,5},{5... | collective-permute-start | bytes 2359304 | tf_op jit(solution)/shard_map/ppermute | solution.py:76
  76.7 32.9 %collective-permute-start.4 = (bf16[256,2048]{1,0:T(8,128)(2,1)}, bf16[256,2048]{1,0:T(8,128)(2,1)}, u32[]{:S(2)}, u32[]{:S(2)}) collective-permute-start(bf16[256,2048]{1,0:T(8,128)(2,1)} %refs_0_.2), channel_id=1, source_target_pairs={{0,16},{4,20},{8,24},{12,28},{16,0},{20,4},{24,8},{28,12},{1,17},{... | collective-permute-start | bytes 3145736 | tf_op jit(solution)/shard_map/ppermute | solution.py:76
  78.2 31.5 %collective-permute-start.3 = (bf16[256,2048]{1,0:T(8,128)(2,1)}, bf16[256,2048]{1,0:T(8,128)(2,1)}, u32[]{:S(2)}, u32[]{:S(2)}) collective-permute-start(bf16[256,2048]{1,0:T(8,128)(2,1)} %refs_0_.2), channel_id=1, source_target_pairs={{0,8},{4,12},{8,0},{12,4},{16,24},{20,28},{24,16},{28,20},{1,9},{5... | collective-permute-start | bytes 3145736 | tf_op jit(solution)/shard_map/ppermute | solution.py:76
  79.8 23.2 %collective-permute-start.8 = (bf16[3,256,512]{2,1,0:T(8,128)(2,1)S(1)}, bf16[3,256,512]{2,1,0:T(8,128)(2,1)S(1)}, u32[]{:S(2)}, u32[]{:S(2)}) collective-permute-start(bf16[3,256,512]{2,1,0:T(8,128)(2,1)S(1)} %collective-permute-done.2.refs_3_), channel_id=1, source_target_pairs={{0,4},{4,0},{8,12},{12,8},{16,20},{20,16},{24,28},{28,24},{1,5},{5... | collective-permute-start | bytes 2359304 | tf_op jit(solution)/shard_map/ppermute | solution.py:76
  79.8 23.2 %collective-permute-start.7 = (bf16[3,256,512]{2,1,0:T(8,128)(2,1)}, bf16[3,256,512]{2,1,0:T(8,128)(2,1)S(1)}, u32[]{:S(2)}, u32[]{:S(2)}) collective-permute-start(bf16[3,256,512]{2,1,0:T(8,128)(2,1)} %collective-permute-done.1.refs_2_), channel_id=1, source_target_pairs={{0,4},{4,0},{8,12},{12,8},{16,20},{20,16},{24,28},{28,24},{1,5},{5... | collective-permute-start | bytes 2359304 | tf_op jit(solution)/shard_map/ppermute | solution.py:76
  80.3 22.7 %collective-permute-start.6 = (bf16[3,256,512]{2,1,0:T(8,128)(2,1)}, bf16[3,256,512]{2,1,0:T(8,128)(2,1)}, u32[]{:S(2)}, u32[]{:S(2)}) collective-permute-start(bf16[3,256,512]{2,1,0:T(8,128)(2,1)} %collective-permute-done.refs_1_), channel_id=1, source_target_pairs={{0,4},{4,0},{8,12},{12,8},{16,20},{20,16},{24,28},{28,24},{1,5},{5... | collective-permute-start | bytes 2359304 | tf_op jit(solution)/shard_map/ppermute | solution.py:76
  118.5 42.3 %all-to-all-start = ((bf16[8,3,256,128]{3,2,1,0:T(8,128)(2,1)}), bf16[8,3,256,128]{3,2,1,0:T(8,128)(2,1)S(1)}, u32[]{:S(2)}, u32[]{:S(2)}) async-start(bf16[8,3,256,128]{3,2,1,0:T(8,128)(2,1)} %project.1), calls=%async_computation | async-start | bytes 3145728 | tf_op jit(solution)/shard_map/all_to_all | solution.py:947
  123.3 30.8 %collective-permute-start.10 = (bf16[128,2048]{1,0:T(8,128)(2,1)S(1)}, bf16[128,2048]{1,0:T(8,128)(2,1)S(1)}, u32[]{:S(2)}, u32[]{:S(2)}) collective-permute-start(bf16[128,2048]{1,0:T(8,128)(2,1)S(1)} %slice.124), channel_id=1, source_target_pairs={{0,8},{4,12},{8,0},{12,4},{16,24},{20,28},{24,16},{28,20},{1,9},{5... | collective-permute-start | bytes 1572872 | tf_op jit(solution)/shard_map/ppermute | solution.py:76
  126.4 27.7 %collective-permute-start.11 = (bf16[128,2048]{1,0:T(8,128)(2,1)S(1)}, bf16[128,2048]{1,0:T(8,128)(2,1)S(1)}, u32[]{:S(2)}, u32[]{:S(2)}) collective-permute-start(bf16[128,2048]{1,0:T(8,128)(2,1)S(1)} %slice.125), channel_id=1, source_target_pairs={{0,16},{4,20},{8,24},{12,28},{16,0},{20,4},{24,8},{28,12},{1,17},{... | collective-permute-start | bytes 1572872 | tf_op jit(solution)/shard_map/ppermute | solution.py:76
  127.9 41.5 %collective-permute-start.12 = (bf16[256,2048]{1,0:T(8,128)(2,1)}, bf16[256,2048]{1,0:T(8,128)(2,1)}, u32[]{:S(2)}, u32[]{:S(2)}) collective-permute-start(bf16[256,2048]{1,0:T(8,128)(2,1)} %refs_0_.2), channel_id=1, source_target_pairs={{0,4},{4,0},{8,12},{12,8},{16,20},{20,16},{24,28},{28,24},{1,5},{5... | collective-permute-start | bytes 3145736 | tf_op jit(solution)/shard_map/ppermute | solution.py:76
  127.9 32.3 %collective-permute-start.19 = (bf16[512,256]{1,0:T(8,128)(2,1)S(1)}, bf16[512,256]{1,0:T(8,128)(2,1)}, u32[]{:S(2)}, u32[]{:S(2)}) collective-permute-start(bf16[512,256]{1,0:T(8,128)(2,1)S(1)} %copy-done.52), channel_id=1, source_target_pairs={{0,24},{4,28},{8,16},{12,20},{16,8},{20,12},{24,0},{28,4},{1,25},{... | collective-permute-start | bytes 786440 | tf_op jit(solution)/shard_map/ppermute | solution.py:76
  168.1 25.9 %collective-permute-start.25 = (bf16[2048,256]{1,0:T(8,128)(2,1)}, bf16[2048,256]{1,0:T(8,128)(2,1)}, u32[]{:S(2)}, u32[]{:S(2)}) collective-permute-start(bf16[2048,256]{1,0:T(8,128)(2,1)} %refs_0_.4), channel_id=1, source_target_pairs={{0,16},{4,20},{8,24},{12,28},{16,0},{20,4},{24,8},{28,12},{1,17},{... | collective-permute-start | bytes 3145736 | tf_op jit(solution)/shard_map/ppermute | solution.py:76
  168.6 25.7 %collective-permute-start.24 = (bf16[2048,256]{1,0:T(8,128)(2,1)}, bf16[2048,256]{1,0:T(8,128)(2,1)}, u32[]{:S(2)}, u32[]{:S(2)}) collective-permute-start(bf16[2048,256]{1,0:T(8,128)(2,1)} %refs_0_.4), channel_id=1, source_target_pairs={{0,8},{4,12},{8,0},{12,4},{16,24},{20,28},{24,16},{28,20},{1,9},{5... | collective-permute-start | bytes 3145736 | tf_op jit(solution)/shard_map/ppermute | solution.py:76
  169.4 36.1 %collective-permute-start.9 = (bf16[8,2,256,128]{3,2,1,0:T(8,128)(2,1)S(1)}, bf16[8,2,256,128]{3,2,1,0:T(8,128)(2,1)}, u32[]{:S(2)}, u32[]{:S(2)}) collective-permute-start(bf16[8,2,256,128]{3,2,1,0:T(8,128)(2,1)S(1)} %slice.157), channel_id=1, source_target_pairs={{0,4},{4,0},{8,12},{12,8},{16,20},{20,16},{24,28},{28,24},{1,5},{5... | collective-permute-start | bytes 3145736 | tf_op jit(solution)/shard_map/ppermute | solution.py:76
  173.2 29.9 %collective-permute-start.20 = (bf16[512,256]{1,0:T(8,128)(2,1)S(1)}, bf16[512,256]{1,0:T(8,128)(2,1)S(1)}, u32[]{:S(2)}, u32[]{:S(2)}) collective-permute-start(bf16[512,256]{1,0:T(8,128)(2,1)S(1)} %copy-done.52), channel_id=1, source_target_pairs={{0,4},{4,0},{8,12},{12,8},{16,20},{20,16},{24,28},{28,24},{1,5},{5... | collective-permute-start | bytes 786440 | tf_op jit(solution)/shard_map/ppermute | solution.py:76
  173.7 29.8 %collective-permute-start.21 = (bf16[512,256]{1,0:T(8,128)(2,1)}, bf16[512,256]{1,0:T(8,128)(2,1)S(1)}, u32[]{:S(2)}, u32[]{:S(2)}) collective-permute-start(bf16[512,256]{1,0:T(8,128)(2,1)} %collective-permute-done.17.refs_1_), channel_id=1, source_target_pairs={{0,4},{4,0},{8,12},{12,8},{16,20},{20,16},{24,28},{28,24},{1,5},{5... | collective-permute-start | bytes 786440 | tf_op jit(solution)/shard_map/ppermute | solution.py:76
  203.2 38.3 %collective-permute-start.28 = (bf16[2048,256]{1,0:T(8,128)(2,1)}, bf16[2048,256]{1,0:T(8,128)(2,1)}, u32[]{:S(2)}, u32[]{:S(2)}) collective-permute-start(bf16[2048,256]{1,0:T(8,128)(2,1)} %refs_0_.4), channel_id=1, source_target_pairs={{0,4},{4,0},{8,12},{12,8},{16,20},{20,16},{24,28},{28,24},{1,5},{5... | collective-permute-start | bytes 3145736 | tf_op jit(solution)/shard_map/ppermute | solution.py:76
  203.5 23.0 %collective-permute-start.26 = (bf16[1024,256]{1,0:T(8,128)(2,1)S(1)}, bf16[1024,256]{1,0:T(8,128)(2,1)}, u32[]{:S(2)}, u32[]{:S(2)}) collective-permute-start(bf16[1024,256]{1,0:T(8,128)(2,1)S(1)} %slice.158), channel_id=1, source_target_pairs={{0,8},{4,12},{8,0},{12,4},{16,24},{20,28},{24,16},{28,20},{1,9},{5... | collective-permute-start | bytes 1572872 | tf_op jit(solution)/shard_map/ppermute | solution.py:76
  204.3 23.4 %collective-permute-start.27 = (bf16[1024,256]{1,0:T(8,128)(2,1)S(1)}, bf16[1024,256]{1,0:T(8,128)(2,1)}, u32[]{:S(2)}, u32[]{:S(2)}) collective-permute-start(bf16[1024,256]{1,0:T(8,128)(2,1)S(1)} %slice.159), channel_id=1, source_target_pairs={{0,16},{4,20},{8,24},{12,28},{16,0},{20,4},{24,8},{28,12},{1,17},{... | collective-permute-start | bytes 1572872 | tf_op jit(solution)/shard_map/ppermute | solution.py:76
  205.6 35.9 %collective-permute-start.30 = (bf16[2048,256]{1,0:T(8,128)(2,1)}, bf16[2048,256]{1,0:T(8,128)(2,1)}, u32[]{:S(2)}, u32[]{:S(2)}) collective-permute-start(bf16[2048,256]{1,0:T(8,128)(2,1)} %collective-permute-done.25.refs_2_), channel_id=1, source_target_pairs={{0,4},{4,0},{8,12},{12,8},{16,20},{20,16},{24,28},{28,24},{1,5},{5... | collective-permute-start | bytes 3145736 | tf_op jit(solution)/shard_map/ppermute | solution.py:76
  205.6 35.9 %collective-permute-start.29 = (bf16[2048,256]{1,0:T(8,128)(2,1)}, bf16[2048,256]{1,0:T(8,128)(2,1)S(1)}, u32[]{:S(2)}, u32[]{:S(2)}) collective-permute-start(bf16[2048,256]{1,0:T(8,128)(2,1)} %collective-permute-done.24.refs_1_), channel_id=1, source_target_pairs={{0,4},{4,0},{8,12},{12,8},{16,20},{20,16},{24,28},{28,24},{1,5},{5... | collective-permute-start | bytes 3145736 | tf_op jit(solution)/shard_map/ppermute | solution.py:76
  220.3 19.9 %all-to-all-start.1 = ((bf16[8,256,128]{2,1,0:T(8,128)(2,1)}), bf16[8,256,128]{2,1,0:T(8,128)(2,1)S(1)}, u32[]{:S(2)}, u32[]{:S(2)}) async-start(bf16[8,256,128]{2,1,0:T(8,128)(2,1)} %get-tuple-element.87), calls=%async_computation.1 | async-start | bytes 1048576 | tf_op jit(solution)/shard_map/all_to_all | solution.py:954
  226.2 370.6 %reduce-scatter.5.cloned.1.call-start = ((), (), s32[]{:S(2)}) async-start(), calls=%async_computation.10 | async-start | bytes 9437184 | tf_op jit(solution)/shard_map/reduce_scatter | solution.py:1046
  226.5 15.0 %collective-permute-start.31 = (bf16[1024,256]{1,0:T(8,128)(2,1)}, bf16[1024,256]{1,0:T(8,128)(2,1)S(1)}, u32[]{:S(2)}, u32[]{:S(2)}) collective-permute-start(bf16[1024,256]{1,0:T(8,128)(2,1)} %collective-permute-done.26.refs_3_), channel_id=1, source_target_pairs={{0,4},{4,0},{8,12},{12,8},{16,20},{20,16},{24,28},{28,24},{1,5},{5... | collective-permute-start | bytes 1572872 | tf_op jit(solution)/shard_map/ppermute | solution.py:76
  279.0 15.5 %collective-permute-start.42 = (bf16[64,2048]{1,0:T(8,128)(2,1)S(1)}, bf16[64,2048]{1,0:T(8,128)(2,1)S(1)}, u32[]{:S(2)}, u32[]{:S(2)}) collective-permute-start(bf16[64,2048]{1,0:T(8,128)(2,1)S(1)} %get-tuple-element.101), channel_id=1, source_target_pairs={{0,1},{3,2},{4,5},{7,6},{8,9},{11,10},{12,13},{15,14},{16,17},{19,... | collective-permute-start | bytes 786440 | tf_op jit(solution)/shard_map/ppermute | solution.py:80
  356.4 15.6 %collective-permute-start.47 = (bf16[64,2048]{1,0:T(8,128)(2,1)S(1)}, bf16[64,2048]{1,0:T(8,128)(2,1)S(1)}, u32[]{:S(2)}, u32[]{:S(2)}) collective-permute-start(bf16[64,2048]{1,0:T(8,128)(2,1)S(1)} %get-tuple-element.191), channel_id=1, source_target_pairs={{1,0},{2,3},{5,4},{6,7},{9,8},{10,11},{13,12},{14,15},{17,16},{18,... | collective-permute-start | bytes 786440 | tf_op jit(solution)/shard_map/ppermute | solution.py:80
  357.7 22.8 %collective-permute-start.56 = (bf16[64,2048]{1,0:T(8,128)(2,1)S(1)}, bf16[64,2048]{1,0:T(8,128)(2,1)S(1)}, u32[]{:S(2)}, u32[]{:S(2)}) collective-permute-start(bf16[64,2048]{1,0:T(8,128)(2,1)S(1)} %get-tuple-element.188), channel_id=1, source_target_pairs={{1,0},{2,3},{5,4},{6,7},{9,8},{10,11},{13,12},{14,15},{17,16},{18,... | collective-permute-start | bytes 786440 | tf_op jit(solution)/shard_map/ppermute | solution.py:80
  359.0 21.4 %collective-permute-start.53 = (bf16[64,2048]{1,0:T(8,128)(2,1)S(1)}, bf16[64,2048]{1,0:T(8,128)(2,1)S(1)}, u32[]{:S(2)}, u32[]{:S(2)}) collective-permute-start(bf16[64,2048]{1,0:T(8,128)(2,1)S(1)} %get-tuple-element.189), channel_id=1, source_target_pairs={{1,0},{2,3},{5,4},{6,7},{9,8},{10,11},{13,12},{14,15},{17,16},{18,... | collective-permute-start | bytes 786440 | tf_op jit(solution)/shard_map/ppermute | solution.py:80
  360.3 20.0 %collective-permute-start.50 = (bf16[64,2048]{1,0:T(8,128)(2,1)S(1)}, bf16[64,2048]{1,0:T(8,128)(2,1)S(1)}, u32[]{:S(2)}, u32[]{:S(2)}) collective-permute-start(bf16[64,2048]{1,0:T(8,128)(2,1)S(1)} %get-tuple-element.190), channel_id=1, source_target_pairs={{1,0},{2,3},{5,4},{6,7},{9,8},{10,11},{13,12},{14,15},{17,16},{18,... | collective-permute-start | bytes 786440 | tf_op jit(solution)/shard_map/ppermute | solution.py:80
  404.8 36.4 %all-to-all-start.2 = ((bf16[8,256,128]{2,1,0:T(8,128)(2,1)}), bf16[8,256,128]{2,1,0:T(8,128)(2,1)S(1)}, u32[]{:S(2)}, u32[]{:S(2)}) async-start(bf16[8,256,128]{2,1,0:T(8,128)(2,1)} %bitcast.20), calls=%async_computation.2 | async-start | bytes 1048576 | tf_op jit(solution)/shard_map/all_to_all | solution.py:1022
  439.7 47.4 %collective-permute-start.58 = (bf16[512,2048]{1,0:T(8,128)(2,1)}, bf16[512,2048]{1,0:T(8,128)(2,1)S(1)}, u32[]{:S(2)}, u32[]{:S(2)}) collective-permute-start(bf16[512,2048]{1,0:T(8,128)(2,1)} %get-tuple-element.110.refs_3_.last.refs_4_), channel_id=1, source_target_pairs={{0,1},{3,2},{4,5},{7,6},{8,9},{11,10},{12,13},{15,14},{16,17},{19,... | collective-permute-start | bytes 6291464 | tf_op jit(solution)/shard_map/ppermute | solution.py:80
  487.2 25.3 %all-to-all-start.3 = ((bf16[8,3,256,128]{3,2,1,0:T(8,128)(2,1)}), bf16[8,3,256,128]{3,2,1,0:T(8,128)(2,1)}, u32[]{:S(2)}, u32[]{:S(2)}) async-start(bf16[8,3,256,128]{3,2,1,0:T(8,128)(2,1)} %pad_maximum_fusion), calls=%async_computation.3 | async-start | bytes 3145728 | tf_op jit(solution)/shard_map/all_to_all | solution.py:1029
  491.5 126.1 %reduce-scatter.9.cloned.1.call-start = ((), (), s32[]{:S(2)}) async-start(), calls=%async_computation.12 | async-start | bytes 2359296 | tf_op jit(solution)/shard_map/reduce_scatter | solution.py:1045
  495.8 155.9 %reduce-scatter.11.cloned.1.call-start = ((), (), s32[]{:S(2)}) async-start(), calls=%async_computation.13 | async-start | bytes 7077888 | tf_op jit(solution)/shard_map/reduce_scatter | solution.py:1047
  529.7 147.7 %reduce-scatter.7.cloned.1.call-start = ((), (), s32[]{:S(2)}) async-start(), calls=%async_computation.11 | async-start | bytes 9437184 | tf_op jit(solution)/shard_map/reduce_scatter | solution.py:1048
  530.4 28.5 %collective-permute-start.63 = (bf16[512,2048]{1,0:T(8,128)(2,1)}, bf16[512,2048]{1,0:T(8,128)(2,1)S(1)}, u32[]{:S(2)}, u32[]{:S(2)}) collective-permute-start(bf16[512,2048]{1,0:T(8,128)(2,1)} %add_convert_fusion), channel_id=1, source_target_pairs={{1,2},{2,1},{5,6},{6,5},{9,10},{10,9},{13,14},{14,13},{17,18},{18,... | collective-permute-start | bytes 6291464 | tf_op jit(solution)/shard_map/ppermute | solution.py:80
  531.3 21.5 %collective-permute-start.60 = (bf16[3,64,2048]{2,1,0:T(8,128)(2,1)}, bf16[3,64,2048]{2,1,0:T(8,128)(2,1)}, u32[]{:S(2)}, u32[]{:S(2)}) collective-permute-start(bf16[3,64,2048]{2,1,0:T(8,128)(2,1)} %get-tuple-element.125.refs_1_), channel_id=1, source_target_pairs={{0,1},{3,2},{4,5},{7,6},{8,9},{11,10},{12,13},{15,14},{16,17},{19,... | collective-permute-start | bytes 2359304 | tf_op jit(solution)/shard_map/ppermute | solution.py:80
  555.5 37.0 %collective-permute-start.61 = (bf16[3,64,2048]{2,1,0:T(8,128)(2,1)}, bf16[3,64,2048]{2,1,0:T(8,128)(2,1)}, u32[]{:S(2)}, u32[]{:S(2)}) collective-permute-start(bf16[3,64,2048]{2,1,0:T(8,128)(2,1)} %add_convert_fusion.9), channel_id=1, source_target_pairs={{1,2},{2,1},{5,6},{6,5},{9,10},{10,9},{13,14},{14,13},{17,18},{18,... | collective-permute-start | bytes 2359304 | tf_op jit(solution)/shard_map/ppermute | solution.py:80
  558.9 48.4 %collective-permute-start.64 = (bf16[3,64,2048]{2,1,0:T(8,128)(2,1)S(1)}, bf16[3,64,2048]{2,1,0:T(8,128)(2,1)}, u32[]{:S(2)}, u32[]{:S(2)}) collective-permute-start(bf16[3,64,2048]{2,1,0:T(8,128)(2,1)S(1)} %copy-done.12), channel_id=1, source_target_pairs={{0,1},{3,2},{4,5},{7,6},{8,9},{11,10},{12,13},{15,14},{16,17},{19,... | collective-permute-start | bytes 2359304 | tf_op jit(solution)/shard_map/ppermute | solution.py:80
  595.4 29.1 %collective-permute-start.83 = (bf16[2,64,2048]{2,1,0:T(8,128)(2,1)}, bf16[2,64,2048]{2,1,0:T(8,128)(2,1)}, u32[]{:S(2)}, u32[]{:S(2)}) collective-permute-start(bf16[2,64,2048]{2,1,0:T(8,128)(2,1)} %mix_inward.15), channel_id=1, source_target_pairs={{1,0},{2,3},{5,4},{6,7},{9,8},{10,11},{13,12},{14,15},{17,16},{18,... | collective-permute-start | bytes 1572872 | tf_op jit(solution)/shard_map/ppermute | solution.py:80
  599.5 21.8 %collective-permute-start.59 = (bf16[3,64,2048]{2,1,0:T(8,128)(2,1)S(1)}, bf16[3,64,2048]{2,1,0:T(8,128)(2,1)S(1)}, u32[]{:S(2)}, u32[]{:S(2)}) collective-permute-start(bf16[3,64,2048]{2,1,0:T(8,128)(2,1)S(1)} %copy-done.13), channel_id=1, source_target_pairs={{0,1},{3,2},{4,5},{7,6},{8,9},{11,10},{12,13},{15,14},{16,17},{19,... | collective-permute-start | bytes 2359304 | tf_op jit(solution)/shard_map/ppermute | solution.py:80
  623.4 30.9 %collective-permute-start.67 = (bf16[3,64,2048]{2,1,0:T(8,128)(2,1)}, bf16[3,64,2048]{2,1,0:T(8,128)(2,1)S(1)}, u32[]{:S(2)}, u32[]{:S(2)}) collective-permute-start(bf16[3,64,2048]{2,1,0:T(8,128)(2,1)} %add_convert_fusion.7), channel_id=1, source_target_pairs={{1,2},{2,1},{5,6},{6,5},{9,10},{10,9},{13,14},{14,13},{17,18},{18,... | collective-permute-start | bytes 2359304 | tf_op jit(solution)/shard_map/ppermute | solution.py:80
  628.1 31.1 %collective-permute-start.62 = (bf16[3,64,2048]{2,1,0:T(8,128)(2,1)S(1)}, bf16[3,64,2048]{2,1,0:T(8,128)(2,1)S(1)}, u32[]{:S(2)}, u32[]{:S(2)}) collective-permute-start(bf16[3,64,2048]{2,1,0:T(8,128)(2,1)S(1)} %copy-done.11), channel_id=1, source_target_pairs={{0,1},{3,2},{4,5},{7,6},{8,9},{11,10},{12,13},{15,14},{16,17},{19,... | collective-permute-start | bytes 2359304 | tf_op jit(solution)/shard_map/ppermute | solution.py:80
  650.4 37.8 %collective-permute-start.81 = (bf16[2,64,2048]{2,1,0:T(8,128)(2,1)}, bf16[2,64,2048]{2,1,0:T(8,128)(2,1)}, u32[]{:S(2)}, u32[]{:S(2)}) collective-permute-start(bf16[2,64,2048]{2,1,0:T(8,128)(2,1)} %mix_inward.13), channel_id=1, source_target_pairs={{1,0},{2,3},{5,4},{6,7},{9,8},{10,11},{13,12},{14,15},{17,16},{18,... | collective-permute-start | bytes 1572872 | tf_op jit(solution)/shard_map/ppermute | solution.py:80
  657.9 26.7 %collective-permute-start.82 = (bf16[2,64,2048]{2,1,0:T(8,128)(2,1)}, bf16[2,64,2048]{2,1,0:T(8,128)(2,1)}, u32[]{:S(2)}, u32[]{:S(2)}) collective-permute-start(bf16[2,64,2048]{2,1,0:T(8,128)(2,1)} %mix_inward.14), channel_id=1, source_target_pairs={{1,0},{2,3},{5,4},{6,7},{9,8},{10,11},{13,12},{14,15},{17,16},{18,... | collective-permute-start | bytes 1572872 | tf_op jit(solution)/shard_map/ppermute | solution.py:80
  660.5 31.4 %collective-permute-start.73 = (bf16[3,64,2048]{2,1,0:T(8,128)(2,1)}, bf16[3,64,2048]{2,1,0:T(8,128)(2,1)}, u32[]{:S(2)}, u32[]{:S(2)}) collective-permute-start(bf16[3,64,2048]{2,1,0:T(8,128)(2,1)} %add_convert_fusion.4), channel_id=1, source_target_pairs={{1,2},{2,1},{5,6},{6,5},{9,10},{10,9},{13,14},{14,13},{17,18},{18,... | collective-permute-start | bytes 2359304 | tf_op jit(solution)/shard_map/ppermute | solution.py:80
  669.7 39.7 %collective-permute-start.68 = (bf16[3,64,2048]{2,1,0:T(8,128)(2,1)S(1)}, bf16[3,64,2048]{2,1,0:T(8,128)(2,1)S(1)}, u32[]{:S(2)}, u32[]{:S(2)}) collective-permute-start(bf16[3,64,2048]{2,1,0:T(8,128)(2,1)S(1)} %copy-done.10), channel_id=1, source_target_pairs={{0,1},{3,2},{4,5},{7,6},{8,9},{11,10},{12,13},{15,14},{16,17},{19,... | collective-permute-start | bytes 2359304 | tf_op jit(solution)/shard_map/ppermute | solution.py:80
  680.3 54.1 %collective-permute-start.66 = (bf16[3,64,2048]{2,1,0:T(8,128)(2,1)S(1)}, bf16[3,64,2048]{2,1,0:T(8,128)(2,1)}, u32[]{:S(2)}, u32[]{:S(2)}) collective-permute-start(bf16[3,64,2048]{2,1,0:T(8,128)(2,1)S(1)} %copy-done.9), channel_id=1, source_target_pairs={{0,1},{3,2},{4,5},{7,6},{8,9},{11,10},{12,13},{15,14},{16,17},{19,... | collective-permute-start | bytes 2359304 | tf_op jit(solution)/shard_map/ppermute | solution.py:80
  701.7 40.0 %collective-permute-start.80 = (bf16[2,64,2048]{2,1,0:T(8,128)(2,1)}, bf16[2,64,2048]{2,1,0:T(8,128)(2,1)}, u32[]{:S(2)}, u32[]{:S(2)}) collective-permute-start(bf16[2,64,2048]{2,1,0:T(8,128)(2,1)} %mix_inward.12), channel_id=1, source_target_pairs={{1,0},{2,3},{5,4},{6,7},{9,8},{10,11},{13,12},{14,15},{17,16},{18,... | collective-permute-start | bytes 1572872 | tf_op jit(solution)/shard_map/ppermute | solution.py:80
  703.8 15.5 %all-to-all-start.4 = ((f32[4,512,16]{1,2,0:T(8,128)}), f32[4,512,16]{1,2,0:T(8,128)S(1)}, u32[]{:S(2)}, u32[]{:S(2)}) async-start(f32[4,512,16]{1,2,0:T(8,128)} %maximum_maximum_fusion), calls=%async_computation.7 | async-start | bytes 262144 | tf_op jit(solution)/shard_map/all_to_all | solution.py:1075
  710.6 27.7 %collective-permute-start.69 = (bf16[3,64,2048]{2,1,0:T(8,128)(2,1)}, bf16[3,64,2048]{2,1,0:T(8,128)(2,1)}, u32[]{:S(2)}, u32[]{:S(2)}) collective-permute-start(bf16[3,64,2048]{2,1,0:T(8,128)(2,1)} %add_convert_fusion.6), channel_id=1, source_target_pairs={{1,2},{2,1},{5,6},{6,5},{9,10},{10,9},{13,14},{14,13},{17,18},{18,... | collective-permute-start | bytes 2359304 | tf_op jit(solution)/shard_map/ppermute | solution.py:80
  712.1 37.3 %collective-permute-start.74 = (bf16[3,64,2048]{2,1,0:T(8,128)(2,1)S(1)}, bf16[3,64,2048]{2,1,0:T(8,128)(2,1)S(1)}, u32[]{:S(2)}, u32[]{:S(2)}) collective-permute-start(bf16[3,64,2048]{2,1,0:T(8,128)(2,1)S(1)} %copy-done.8), channel_id=1, source_target_pairs={{0,1},{3,2},{4,5},{7,6},{8,9},{11,10},{12,13},{15,14},{16,17},{19,... | collective-permute-start | bytes 2359304 | tf_op jit(solution)/shard_map/ppermute | solution.py:80
  736.7 24.1 %collective-permute-start.77 = (bf16[3,64,2048]{2,1,0:T(8,128)(2,1)}, bf16[3,64,2048]{2,1,0:T(8,128)(2,1)}, u32[]{:S(2)}, u32[]{:S(2)}) collective-permute-start(bf16[3,64,2048]{2,1,0:T(8,128)(2,1)} %add_convert_fusion.2), channel_id=1, source_target_pairs={{1,2},{2,1},{5,6},{6,5},{9,10},{10,9},{13,14},{14,13},{17,18},{18,... | collective-permute-start | bytes 2359304 | tf_op jit(solution)/shard_map/ppermute | solution.py:80
  738.3 20.4 %collective-permute-start.70 = (bf16[3,64,2048]{2,1,0:T(8,128)(2,1)S(1)}, bf16[3,64,2048]{2,1,0:T(8,128)(2,1)S(1)}, u32[]{:S(2)}, u32[]{:S(2)}) collective-permute-start(bf16[3,64,2048]{2,1,0:T(8,128)(2,1)S(1)} %copy-done.7), channel_id=1, source_target_pairs={{0,1},{3,2},{4,5},{7,6},{8,9},{11,10},{12,13},{15,14},{16,17},{19,... | collective-permute-start | bytes 2359304 | tf_op jit(solution)/shard_map/ppermute | solution.py:80
  748.2 16.8 %collective-permute-start.79 = (bf16[2,64,2048]{2,1,0:T(8,128)(2,1)}, bf16[2,64,2048]{2,1,0:T(8,128)(2,1)}, u32[]{:S(2)}, u32[]{:S(2)}) collective-permute-start(bf16[2,64,2048]{2,1,0:T(8,128)(2,1)} %mix_inward.11), channel_id=1, source_target_pairs={{1,0},{2,3},{5,4},{6,7},{9,8},{10,11},{13,12},{14,15},{17,16},{18,... | collective-permute-start | bytes 1572872 | tf_op jit(solution)/shard_map/ppermute | solution.py:80
  750.6 18.0 %collective-permute-start.75 = (bf16[3,64,2048]{2,1,0:T(8,128)(2,1)}, bf16[3,64,2048]{2,1,0:T(8,128)(2,1)S(1)}, u32[]{:S(2)}, u32[]{:S(2)}) collective-permute-start(bf16[3,64,2048]{2,1,0:T(8,128)(2,1)} %add_convert_fusion.3), channel_id=1, source_target_pairs={{1,2},{2,1},{5,6},{6,5},{9,10},{10,9},{13,14},{14,13},{17,18},{18,... | collective-permute-start | bytes 2359304 | tf_op jit(solution)/shard_map/ppermute | solution.py:80
  759.9 21.2 %collective-permute-start.71 = (bf16[3,64,2048]{2,1,0:T(8,128)(2,1)}, bf16[3,64,2048]{2,1,0:T(8,128)(2,1)S(1)}, u32[]{:S(2)}, u32[]{:S(2)}) collective-permute-start(bf16[3,64,2048]{2,1,0:T(8,128)(2,1)} %add_convert_fusion.5), channel_id=1, source_target_pairs={{1,2},{2,1},{5,6},{6,5},{9,10},{10,9},{13,14},{14,13},{17,18},{18,... | collective-permute-start | bytes 2359304 | tf_op jit(solution)/shard_map/ppermute | solution.py:80
  763.7 17.3 %collective-permute-start.78 = (bf16[2,64,2048]{2,1,0:T(8,128)(2,1)}, bf16[2,64,2048]{2,1,0:T(8,128)(2,1)S(1)}, u32[]{:S(2)}, u32[]{:S(2)}) collective-permute-start(bf16[2,64,2048]{2,1,0:T(8,128)(2,1)} %mix_inward.10), channel_id=1, source_target_pairs={{1,0},{2,3},{5,4},{6,7},{9,8},{10,11},{13,12},{14,15},{17,16},{18,... | collective-permute-start | bytes 1572872 | tf_op jit(solution)/shard_map/ppermute | solution.py:80
  772.3 19.3 %collective-permute-start.76 = (bf16[2,64,2048]{2,1,0:T(8,128)(2,1)}, bf16[2,64,2048]{2,1,0:T(8,128)(2,1)S(1)}, u32[]{:S(2)}, u32[]{:S(2)}) collective-permute-start(bf16[2,64,2048]{2,1,0:T(8,128)(2,1)} %mix_inward.9), channel_id=1, source_target_pairs={{1,0},{2,3},{5,4},{6,7},{9,8},{10,11},{13,12},{14,15},{17,16},{18,... | collective-permute-start | bytes 1572872 | tf_op jit(solution)/shard_map/ppermute | solution.py:80
  784.7 23.1 %collective-permute-start.72 = (bf16[2,64,2048]{2,1,0:T(8,128)(2,1)}, bf16[2,64,2048]{2,1,0:T(8,128)(2,1)S(1)}, u32[]{:S(2)}, u32[]{:S(2)}) collective-permute-start(bf16[2,64,2048]{2,1,0:T(8,128)(2,1)} %mix_inward.8), channel_id=1, source_target_pairs={{1,0},{2,3},{5,4},{6,7},{9,8},{10,11},{13,12},{14,15},{17,16},{18,... | collective-permute-start | bytes 1572872 | tf_op jit(solution)/shard_map/ppermute | solution.py:80
  (89 other events, 1193.0 us)
Sparse Core Ops, SparseCore 0:
  12.0 49.6 all-gather.4
  391.5 69.8 reduce-scatter.4
  495.9 41.7 reduce-scatter.8
  540.9 61.7 reduce-scatter.10
  606.0 71.3 reduce-scatter.6
